TPU v7x, 512 devices: a whole 4x8x8 slice. The times are simulated.
512 devices in a mesh: phase: 16 (over z, core), rows: 32 (over y, x).
Axes of the slice: x: 4, y: 8, z: 8, core: 2. Of those that a mesh axis runs over, the one named last changes fastest.
Arguments:
- start: bfloat16 [16, 32768, 256], P('phase', 'rows')
- blocks: bfloat16 [16, 256, 4, 128, 128], P('phase', 'rows')
- cols: int32 [16, 256, 4], P('phase', 'rows'), may hold values from 0 to 255, as said below
- counts: int32 [16, 256], P('phase', 'rows'), may hold values from 1 to 4, as said below
Outputs:
- basis: float32 [16, 32768, 256], P('phase', 'rows')
- factor: float32 [16, 256, 256], P('phase')
Inputs may be any that keep to these rules, and one draw needn't show every extreme that they name: cols[q, i, 0] = i; the other slots of block row i name distinct block rows (i + o) mod 256 with 1 <= |o| <= 2. Block row i of section q uses its first counts[q, i] slots; every section has a block row that uses all 4.
All inputs are finite; a program needn't handle non-finite values.
Results may differ from a plain program's by a relative error of at most 0.012.
Values may be sent and summed in bfloat16 or wider, within the bound.
No kernel may reach another device: no remote copies, remote signals or barrier semaphores. Data moves between devices by JAX's collectives and lax.ppermute only.
A program may use at most 64 MiB of HBM per device.

v0:
```python
import jax
import jax.numpy as jnp
from jax import lax
from jax.sharding import PartitionSpec as P

HB = 2


def with_halo(array, sides, width):
    for axis, dim in sides:
        peers, length = (lax.axis_size(axis), array.shape[dim])
        up = [(i, (i + 1) % peers) for i in range(peers)]
        down = [(j, i) for i, j in up]
        last = lax.slice_in_dim(array, length - width, length, axis=dim)
        leading = lax.slice_in_dim(array, 0, width, axis=dim)
        before = lax.ppermute(last, axis, up)
        after = lax.ppermute(leading, axis, down)
        array = jnp.concatenate([before, array, after], axis=dim)
    return array


def passed_along(value, axis, steps):
    count = lax.axis_size(axis)
    pairs = [(source, (source + steps) % count) for source in range(count)]
    return lax.ppermute(value, axis, pairs)


def body(start, blocks, cols, counts):
    block_rows = blocks.shape[1]
    slot_count = blocks.shape[2]
    tile_size = blocks.shape[3]
    rows_here = start.shape[1]
    owners = lax.axis_size("rows")
    sections = lax.axis_size("phase")
    total_blocks = block_rows * owners
    first_block = lax.axis_index("rows") * block_rows
    local_index = jnp.mod(cols[0] - first_block + HB, total_blocks)
    live_slots = jnp.arange(slot_count, dtype=jnp.int32)[None, :] < counts[0][:, None]
    zero_value = jnp.zeros((), jnp.bfloat16)
    kept_blocks = jnp.where(live_slots[:, :, None, None], blocks[0], zero_value)
    rim_rows = HB * tile_size

    def advance(current):
        columns = current.shape[1]
        extended = with_halo(current, (("rows", 0),), rim_rows)
        row_tiles = extended.reshape(block_rows + 2 * HB, tile_size, columns)
        picked = row_tiles[local_index]
        product = jnp.einsum(
            "ijab,ijbk->iak", kept_blocks, picked, preferred_element_type=jnp.float32
        )
        return product.reshape(rows_here, columns).astype(jnp.bfloat16)

    def turn_one(turn_index, current):
        return passed_along(advance(current), "phase", 1)

    arrived = lax.fori_loop(0, sections, turn_one, start[0])
    gram_term = lax.dot_general(
        arrived, arrived, (((0,), (0,)), ((), ())), preferred_element_type=jnp.float32
    )
    gram_total = lax.psum(gram_term.astype(jnp.bfloat16), "rows").astype(jnp.float32) / (
        rows_here * owners
    )
    lower_factor = jnp.linalg.cholesky(gram_total)
    basis_out = jax.scipy.linalg.solve_triangular(
        lower_factor, arrived.astype(jnp.float32).T, lower=True
    ).T
    return (basis_out[None], lower_factor.T[None])


def solution(mesh):
    placed = (
        P("phase", "rows", None),
        P("phase", "rows", None, None, None),
        P("phase", "rows", None),
        P("phase", "rows"),
    )
    return jax.shard_map(
        body,
        mesh=mesh,
        in_specs=placed,
        out_specs=(P("phase", "rows", None), P("phase", None, None)),
        check_vma=False,
    )
```

profile of v0, /device:TPU:10, one launch (start us, length us, event | category | flops | bytes accessed | tf_op | source)
XLA Modules:
  0.0 633.7 jit_solution(17564700713426844968)
XLA Ops:
  10.4 392.7 %while.11 = (s32[]{:T(128)}, bf16[1024,256]{1,0:T(8,128)(2,1)S(1)}, s32[8,4]{0,1:T(4,128)S(1)}, bf16[8,4,128,128]{3,2,1,0:T(8,128)(2,1)}, s32[]{:T(128)}) while((s32[]{:T(128)}, bf16[1024,256]{1,0:T(8,128)(2,1)S(1)}, s32[8,4]{0,1:T(4,128)S(1)}, bf16[8,4,128,128]{3,2,1,0:T(8,128)(2,1)}, s32[]{:T(128)}) %tuple.54), condition=%wide.region_1.2_spmd, body=%wide.region_0.1_spmd.sunk | while | flops 271058016 | bytes 13112501 | solution.py:56
  23.1 14.5 %collective-permute-done.2 = bf16[1024,256]{1,0:T(8,128)(2,1)S(1)} collective-permute-done((bf16[1024,256]{1,0:T(8,128)(2,1)S(1)}, bf16[1024,256]{1,0:T(8,128)(2,1)S(1)}, u32[]{:S(2)}, u32[]{:S(2)}) %collective-permute-start.2) | collective-permute-done | bytes 524320 | tf_op jit(solution)/shard_map/while/body/eval_jaxpr/ppermute | solution.py:25
  37.6 5.2 collective-permute-start
  45.3 4.4 collective-permute-done.1
  52.2 9.8 %collective-permute-done.2 = bf16[1024,256]{1,0:T(8,128)(2,1)S(1)} collective-permute-done((bf16[1024,256]{1,0:T(8,128)(2,1)S(1)}, bf16[1024,256]{1,0:T(8,128)(2,1)S(1)}, u32[]{:S(2)}, u32[]{:S(2)}) %collective-permute-start.2) | collective-permute-done | bytes 524320 | tf_op jit(solution)/shard_map/while/body/eval_jaxpr/ppermute | solution.py:25
  75.4 9.8 %collective-permute-done.2 = bf16[1024,256]{1,0:T(8,128)(2,1)S(1)} collective-permute-done((bf16[1024,256]{1,0:T(8,128)(2,1)S(1)}, bf16[1024,256]{1,0:T(8,128)(2,1)S(1)}, u32[]{:S(2)}, u32[]{:S(2)}) %collective-permute-start.2) | collective-permute-done | bytes 524320 | tf_op jit(solution)/shard_map/while/body/eval_jaxpr/ppermute | solution.py:25
  85.2 4.5 collective-permute-start
  92.3 4.4 collective-permute-done.1
  99.2 9.8 %collective-permute-done.2 = bf16[1024,256]{1,0:T(8,128)(2,1)S(1)} collective-permute-done((bf16[1024,256]{1,0:T(8,128)(2,1)S(1)}, bf16[1024,256]{1,0:T(8,128)(2,1)S(1)}, u32[]{:S(2)}, u32[]{:S(2)}) %collective-permute-start.2) | collective-permute-done | bytes 524320 | tf_op jit(solution)/shard_map/while/body/eval_jaxpr/ppermute | solution.py:25
  109.0 6.0 collective-permute-start
  117.5 4.4 collective-permute-done.1
  124.4 9.8 %collective-permute-done.2 = bf16[1024,256]{1,0:T(8,128)(2,1)S(1)} collective-permute-done((bf16[1024,256]{1,0:T(8,128)(2,1)S(1)}, bf16[1024,256]{1,0:T(8,128)(2,1)S(1)}, u32[]{:S(2)}, u32[]{:S(2)}) %collective-permute-start.2) | collective-permute-done | bytes 524320 | tf_op jit(solution)/shard_map/while/body/eval_jaxpr/ppermute | solution.py:25
  134.2 5.2 collective-permute-start
  142.0 4.4 collective-permute-done.1
  148.8 9.8 %collective-permute-done.2 = bf16[1024,256]{1,0:T(8,128)(2,1)S(1)} collective-permute-done((bf16[1024,256]{1,0:T(8,128)(2,1)S(1)}, bf16[1024,256]{1,0:T(8,128)(2,1)S(1)}, u32[]{:S(2)}, u32[]{:S(2)}) %collective-permute-start.2) | collective-permute-done | bytes 524320 | tf_op jit(solution)/shard_map/while/body/eval_jaxpr/ppermute | solution.py:25
  158.7 5.2 collective-permute-start
  166.4 4.4 collective-permute-done.1
  173.3 9.8 %collective-permute-done.2 = bf16[1024,256]{1,0:T(8,128)(2,1)S(1)} collective-permute-done((bf16[1024,256]{1,0:T(8,128)(2,1)S(1)}, bf16[1024,256]{1,0:T(8,128)(2,1)S(1)}, u32[]{:S(2)}, u32[]{:S(2)}) %collective-permute-start.2) | collective-permute-done | bytes 524320 | tf_op jit(solution)/shard_map/while/body/eval_jaxpr/ppermute | solution.py:25
  183.1 5.3 collective-permute-start
  190.9 4.4 collective-permute-done.1
  197.7 9.8 %collective-permute-done.2 = bf16[1024,256]{1,0:T(8,128)(2,1)S(1)} collective-permute-done((bf16[1024,256]{1,0:T(8,128)(2,1)S(1)}, bf16[1024,256]{1,0:T(8,128)(2,1)S(1)}, u32[]{:S(2)}, u32[]{:S(2)}) %collective-permute-start.2) | collective-permute-done | bytes 524320 | tf_op jit(solution)/shard_map/while/body/eval_jaxpr/ppermute | solution.py:25
  207.6 5.2 collective-permute-start
  215.3 4.4 collective-permute-done.1
  222.2 9.8 %collective-permute-done.2 = bf16[1024,256]{1,0:T(8,128)(2,1)S(1)} collective-permute-done((bf16[1024,256]{1,0:T(8,128)(2,1)S(1)}, bf16[1024,256]{1,0:T(8,128)(2,1)S(1)}, u32[]{:S(2)}, u32[]{:S(2)}) %collective-permute-start.2) | collective-permute-done | bytes 524320 | tf_op jit(solution)/shard_map/while/body/eval_jaxpr/ppermute | solution.py:25
  232.0 5.3 collective-permute-start
  239.8 4.4 collective-permute-done.1
  246.6 9.8 %collective-permute-done.2 = bf16[1024,256]{1,0:T(8,128)(2,1)S(1)} collective-permute-done((bf16[1024,256]{1,0:T(8,128)(2,1)S(1)}, bf16[1024,256]{1,0:T(8,128)(2,1)S(1)}, u32[]{:S(2)}, u32[]{:S(2)}) %collective-permute-start.2) | collective-permute-done | bytes 524320 | tf_op jit(solution)/shard_map/while/body/eval_jaxpr/ppermute | solution.py:25
  256.5 5.2 collective-permute-start
  264.2 4.4 collective-permute-done.1
  271.1 9.8 %collective-permute-done.2 = bf16[1024,256]{1,0:T(8,128)(2,1)S(1)} collective-permute-done((bf16[1024,256]{1,0:T(8,128)(2,1)S(1)}, bf16[1024,256]{1,0:T(8,128)(2,1)S(1)}, u32[]{:S(2)}, u32[]{:S(2)}) %collective-permute-start.2) | collective-permute-done | bytes 524320 | tf_op jit(solution)/shard_map/while/body/eval_jaxpr/ppermute | solution.py:25
  280.9 5.3 collective-permute-start
  288.7 4.4 collective-permute-done.1
  295.5 9.8 %collective-permute-done.2 = bf16[1024,256]{1,0:T(8,128)(2,1)S(1)} collective-permute-done((bf16[1024,256]{1,0:T(8,128)(2,1)S(1)}, bf16[1024,256]{1,0:T(8,128)(2,1)S(1)}, u32[]{:S(2)}, u32[]{:S(2)}) %collective-permute-start.2) | collective-permute-done | bytes 524320 | tf_op jit(solution)/shard_map/while/body/eval_jaxpr/ppermute | solution.py:25
  305.3 5.2 collective-permute-start
  313.1 4.4 collective-permute-done.1
  320.0 9.8 %collective-permute-done.2 = bf16[1024,256]{1,0:T(8,128)(2,1)S(1)} collective-permute-done((bf16[1024,256]{1,0:T(8,128)(2,1)S(1)}, bf16[1024,256]{1,0:T(8,128)(2,1)S(1)}, u32[]{:S(2)}, u32[]{:S(2)}) %collective-permute-start.2) | collective-permute-done | bytes 524320 | tf_op jit(solution)/shard_map/while/body/eval_jaxpr/ppermute | solution.py:25
  329.8 5.3 collective-permute-start
  337.5 4.4 collective-permute-done.1
  344.4 9.8 %collective-permute-done.2 = bf16[1024,256]{1,0:T(8,128)(2,1)S(1)} collective-permute-done((bf16[1024,256]{1,0:T(8,128)(2,1)S(1)}, bf16[1024,256]{1,0:T(8,128)(2,1)S(1)}, u32[]{:S(2)}, u32[]{:S(2)}) %collective-permute-start.2) | collective-permute-done | bytes 524320 | tf_op jit(solution)/shard_map/while/body/eval_jaxpr/ppermute | solution.py:25
  354.2 5.2 collective-permute-start
  368.9 9.8 %collective-permute-done.2 = bf16[1024,256]{1,0:T(8,128)(2,1)S(1)} collective-permute-done((bf16[1024,256]{1,0:T(8,128)(2,1)S(1)}, bf16[1024,256]{1,0:T(8,128)(2,1)S(1)}, u32[]{:S(2)}, u32[]{:S(2)}) %collective-permute-start.2) | collective-permute-done | bytes 524320 | tf_op jit(solution)/shard_map/while/body/eval_jaxpr/ppermute | solution.py:25
  378.7 5.3 collective-permute-start
  393.3 9.8 %collective-permute-done.2 = bf16[1024,256]{1,0:T(8,128)(2,1)S(1)} collective-permute-done((bf16[1024,256]{1,0:T(8,128)(2,1)S(1)}, bf16[1024,256]{1,0:T(8,128)(2,1)S(1)}, u32[]{:S(2)}, u32[]{:S(2)}) %collective-permute-start.2) | collective-permute-done | bytes 524320 | tf_op jit(solution)/shard_map/while/body/eval_jaxpr/ppermute | solution.py:25
  404.2 156.6 %all-reduce.3.cloned.1.call-done = bf16[256,256]{0,1:T(8,128)(2,1)} async-done(((bf16[256,256]{0,1:T(8,128)(2,1)}), bf16[256,256]{0,1:T(8,128)(2,1)}) %all-reduce.3.cloned.1.call-update) | async-done | bytes 131088 | tf_op jit(solution)/shard_map/psum | solution.py:60
  562.8 11.7 %cholesky.50 = f32[128,128]{1,0:T(8,128)S(1)} custom-call(f32[128,128]{1,0:T(8,128)S(1)} %cholesky.118), custom_call_target="Cholesky" | custom-call | tf_op jit(solution)/shard_map/jit(cholesky)/cholesky | solution.py:63
  574.6 9.8 %custom-call.15 = f32[1,128,128]{1,2,0:T(8,128)S(1)} custom-call(f32[1,128,128]{2,1,0:T(8,128)S(1)} %get-tuple-element.62), custom_call_target="InvertDiagBlocksLowerTriangular" | custom-call | tf_op jit(solution)/shard_map/jit(cholesky)/cholesky | solution.py:63
  584.9 11.7 %cholesky.105 = f32[128,128]{1,0:T(8,128)S(1)} custom-call(f32[128,128]{1,0:T(8,128)S(1)} %convolution_subtract_fusion.1), custom_call_target="Cholesky" | custom-call | tf_op jit(solution)/shard_map/jit(cholesky)/cholesky | solution.py:63
  602.7 19.9 %custom-call.16 = f32[2,128,128]{1,2,0:T(8,128)S(1)} custom-call(f32[2,128,128]{2,1,0:T(8,128)S(1)} %get-tuple-element.32), custom_call_target="InvertDiagBlocksLowerTriangular" | custom-call | tf_op jit(solution)/shard_map/jit(_solve_triangular)/triangular_solve | solution.py:64
  (219 shorter events, 124.3 us)
Async XLA Ops:
  7.2 553.6 %all-reduce.3.cloned.1.call-start = ((), (), s32[]{:S(2)}) async-start(), calls=%async_computation | async-start | bytes 262144 | tf_op jit(solution)/shard_map/psum | solution.py:60
  10.4 7.1 %collective-permute-start = (bf16[256,256]{1,0:T(8,128)(2,1)S(1)}, bf16[256,256]{1,0:T(8,128)(2,1)S(1)}, u32[]{:S(2)}, u32[]{:S(2)}) collective-permute-start(bf16[256,256]{1,0:T(8,128)(2,1)S(1)} %get-tuple-element.117), channel_id=1, source_target_pairs={{1,0},{2,1},{3,2},{4,3},{5,4},{6,5},{7,6},{8,7},{9,8},{10,9},{11,1... | collective-permute-start | bytes 393224 | tf_op jit(solution)/shard_map/while/body/eval_jaxpr/ppermute | solution.py:17
  12.9 7.8 %collective-permute-start.1 = (bf16[256,256]{1,0:T(8,128)(2,1)S(1)}, bf16[256,256]{1,0:T(8,128)(2,1)S(1)}, u32[]{:S(2)}, u32[]{:S(2)}) collective-permute-start(bf16[256,256]{1,0:T(8,128)(2,1)S(1)} %get-tuple-element.118), channel_id=1, source_target_pairs={{0,1},{1,2},{2,3},{3,4},{4,5},{5,6},{6,7},{7,8},{8,9},{9,10},{10,1... | collective-permute-start | bytes 393224 | tf_op jit(solution)/shard_map/while/body/eval_jaxpr/ppermute | solution.py:16
  23.1 14.5 %collective-permute-start.2 = (bf16[1024,256]{1,0:T(8,128)(2,1)S(1)}, bf16[1024,256]{1,0:T(8,128)(2,1)S(1)}, u32[]{:S(2)}, u32[]{:S(2)}) collective-permute-start(bf16[1024,256]{1,0:T(8,128)(2,1)S(1)} %bitcast.85), channel_id=1, source_target_pairs={{0,32},{32,64},{64,96},{96,128},{128,160},{160,192},{192,224},{224... | collective-permute-start | bytes 1572872 | tf_op jit(solution)/shard_map/while/body/eval_jaxpr/ppermute | solution.py:25
  37.6 7.7 %collective-permute-start = (bf16[256,256]{1,0:T(8,128)(2,1)S(1)}, bf16[256,256]{1,0:T(8,128)(2,1)S(1)}, u32[]{:S(2)}, u32[]{:S(2)}) collective-permute-start(bf16[256,256]{1,0:T(8,128)(2,1)S(1)} %get-tuple-element.117), channel_id=1, source_target_pairs={{1,0},{2,1},{3,2},{4,3},{5,4},{6,5},{7,6},{8,7},{9,8},{10,9},{11,1... | collective-permute-start | bytes 393224 | tf_op jit(solution)/shard_map/while/body/eval_jaxpr/ppermute | solution.py:17
  42.8 6.9 %collective-permute-start.1 = (bf16[256,256]{1,0:T(8,128)(2,1)S(1)}, bf16[256,256]{1,0:T(8,128)(2,1)S(1)}, u32[]{:S(2)}, u32[]{:S(2)}) collective-permute-start(bf16[256,256]{1,0:T(8,128)(2,1)S(1)} %get-tuple-element.118), channel_id=1, source_target_pairs={{0,1},{1,2},{2,3},{3,4},{4,5},{5,6},{6,7},{7,8},{8,9},{9,10},{10,1... | collective-permute-start | bytes 393224 | tf_op jit(solution)/shard_map/while/body/eval_jaxpr/ppermute | solution.py:16
  52.2 9.8 %collective-permute-start.2 = (bf16[1024,256]{1,0:T(8,128)(2,1)S(1)}, bf16[1024,256]{1,0:T(8,128)(2,1)S(1)}, u32[]{:S(2)}, u32[]{:S(2)}) collective-permute-start(bf16[1024,256]{1,0:T(8,128)(2,1)S(1)} %bitcast.85), channel_id=1, source_target_pairs={{0,32},{32,64},{64,96},{96,128},{128,160},{160,192},{192,224},{224... | collective-permute-start | bytes 1572872 | tf_op jit(solution)/shard_map/while/body/eval_jaxpr/ppermute | solution.py:25
  62.0 6.9 %collective-permute-start = (bf16[256,256]{1,0:T(8,128)(2,1)S(1)}, bf16[256,256]{1,0:T(8,128)(2,1)S(1)}, u32[]{:S(2)}, u32[]{:S(2)}) collective-permute-start(bf16[256,256]{1,0:T(8,128)(2,1)S(1)} %get-tuple-element.117), channel_id=1, source_target_pairs={{1,0},{2,1},{3,2},{4,3},{5,4},{6,5},{7,6},{8,7},{9,8},{10,9},{11,1... | collective-permute-start | bytes 393224 | tf_op jit(solution)/shard_map/while/body/eval_jaxpr/ppermute | solution.py:17
  66.1 6.9 %collective-permute-start.1 = (bf16[256,256]{1,0:T(8,128)(2,1)S(1)}, bf16[256,256]{1,0:T(8,128)(2,1)S(1)}, u32[]{:S(2)}, u32[]{:S(2)}) collective-permute-start(bf16[256,256]{1,0:T(8,128)(2,1)S(1)} %get-tuple-element.118), channel_id=1, source_target_pairs={{0,1},{1,2},{2,3},{3,4},{4,5},{5,6},{6,7},{7,8},{8,9},{9,10},{10,1... | collective-permute-start | bytes 393224 | tf_op jit(solution)/shard_map/while/body/eval_jaxpr/ppermute | solution.py:16
  75.4 9.8 %collective-permute-start.2 = (bf16[1024,256]{1,0:T(8,128)(2,1)S(1)}, bf16[1024,256]{1,0:T(8,128)(2,1)S(1)}, u32[]{:S(2)}, u32[]{:S(2)}) collective-permute-start(bf16[1024,256]{1,0:T(8,128)(2,1)S(1)} %bitcast.85), channel_id=1, source_target_pairs={{0,32},{32,64},{64,96},{96,128},{128,160},{160,192},{192,224},{224... | collective-permute-start | bytes 1572872 | tf_op jit(solution)/shard_map/while/body/eval_jaxpr/ppermute | solution.py:25
  85.2 7.0 %collective-permute-start = (bf16[256,256]{1,0:T(8,128)(2,1)S(1)}, bf16[256,256]{1,0:T(8,128)(2,1)S(1)}, u32[]{:S(2)}, u32[]{:S(2)}) collective-permute-start(bf16[256,256]{1,0:T(8,128)(2,1)S(1)} %get-tuple-element.117), channel_id=1, source_target_pairs={{1,0},{2,1},{3,2},{4,3},{5,4},{6,5},{7,6},{8,7},{9,8},{10,9},{11,1... | collective-permute-start | bytes 393224 | tf_op jit(solution)/shard_map/while/body/eval_jaxpr/ppermute | solution.py:17
  89.8 6.9 %collective-permute-start.1 = (bf16[256,256]{1,0:T(8,128)(2,1)S(1)}, bf16[256,256]{1,0:T(8,128)(2,1)S(1)}, u32[]{:S(2)}, u32[]{:S(2)}) collective-permute-start(bf16[256,256]{1,0:T(8,128)(2,1)S(1)} %get-tuple-element.118), channel_id=1, source_target_pairs={{0,1},{1,2},{2,3},{3,4},{4,5},{5,6},{6,7},{7,8},{8,9},{9,10},{10,1... | collective-permute-start | bytes 393224 | tf_op jit(solution)/shard_map/while/body/eval_jaxpr/ppermute | solution.py:16
  99.1 9.8 %collective-permute-start.2 = (bf16[1024,256]{1,0:T(8,128)(2,1)S(1)}, bf16[1024,256]{1,0:T(8,128)(2,1)S(1)}, u32[]{:S(2)}, u32[]{:S(2)}) collective-permute-start(bf16[1024,256]{1,0:T(8,128)(2,1)S(1)} %bitcast.85), channel_id=1, source_target_pairs={{0,32},{32,64},{64,96},{96,128},{128,160},{160,192},{192,224},{224... | collective-permute-start | bytes 1572872 | tf_op jit(solution)/shard_map/while/body/eval_jaxpr/ppermute | solution.py:25
  109.0 8.5 %collective-permute-start = (bf16[256,256]{1,0:T(8,128)(2,1)S(1)}, bf16[256,256]{1,0:T(8,128)(2,1)S(1)}, u32[]{:S(2)}, u32[]{:S(2)}) collective-permute-start(bf16[256,256]{1,0:T(8,128)(2,1)S(1)} %get-tuple-element.117), channel_id=1, source_target_pairs={{1,0},{2,1},{3,2},{4,3},{5,4},{6,5},{7,6},{8,7},{9,8},{10,9},{11,1... | collective-permute-start | bytes 393224 | tf_op jit(solution)/shard_map/while/body/eval_jaxpr/ppermute | solution.py:17
  115.0 6.9 %collective-permute-start.1 = (bf16[256,256]{1,0:T(8,128)(2,1)S(1)}, bf16[256,256]{1,0:T(8,128)(2,1)S(1)}, u32[]{:S(2)}, u32[]{:S(2)}) collective-permute-start(bf16[256,256]{1,0:T(8,128)(2,1)S(1)} %get-tuple-element.118), channel_id=1, source_target_pairs={{0,1},{1,2},{2,3},{3,4},{4,5},{5,6},{6,7},{7,8},{8,9},{9,10},{10,1... | collective-permute-start | bytes 393224 | tf_op jit(solution)/shard_map/while/body/eval_jaxpr/ppermute | solution.py:16
  124.4 9.8 %collective-permute-start.2 = (bf16[1024,256]{1,0:T(8,128)(2,1)S(1)}, bf16[1024,256]{1,0:T(8,128)(2,1)S(1)}, u32[]{:S(2)}, u32[]{:S(2)}) collective-permute-start(bf16[1024,256]{1,0:T(8,128)(2,1)S(1)} %bitcast.85), channel_id=1, source_target_pairs={{0,32},{32,64},{64,96},{96,128},{128,160},{160,192},{192,224},{224... | collective-permute-start | bytes 1572872 | tf_op jit(solution)/shard_map/while/body/eval_jaxpr/ppermute | solution.py:25
  134.2 7.8 %collective-permute-start = (bf16[256,256]{1,0:T(8,128)(2,1)S(1)}, bf16[256,256]{1,0:T(8,128)(2,1)S(1)}, u32[]{:S(2)}, u32[]{:S(2)}) collective-permute-start(bf16[256,256]{1,0:T(8,128)(2,1)S(1)} %get-tuple-element.117), channel_id=1, source_target_pairs={{1,0},{2,1},{3,2},{4,3},{5,4},{6,5},{7,6},{8,7},{9,8},{10,9},{11,1... | collective-permute-start | bytes 393224 | tf_op jit(solution)/shard_map/while/body/eval_jaxpr/ppermute | solution.py:17
  139.5 6.9 %collective-permute-start.1 = (bf16[256,256]{1,0:T(8,128)(2,1)S(1)}, bf16[256,256]{1,0:T(8,128)(2,1)S(1)}, u32[]{:S(2)}, u32[]{:S(2)}) collective-permute-start(bf16[256,256]{1,0:T(8,128)(2,1)S(1)} %get-tuple-element.118), channel_id=1, source_target_pairs={{0,1},{1,2},{2,3},{3,4},{4,5},{5,6},{6,7},{7,8},{8,9},{9,10},{10,1... | collective-permute-start | bytes 393224 | tf_op jit(solution)/shard_map/while/body/eval_jaxpr/ppermute | solution.py:16
  148.8 9.8 %collective-permute-start.2 = (bf16[1024,256]{1,0:T(8,128)(2,1)S(1)}, bf16[1024,256]{1,0:T(8,128)(2,1)S(1)}, u32[]{:S(2)}, u32[]{:S(2)}) collective-permute-start(bf16[1024,256]{1,0:T(8,128)(2,1)S(1)} %bitcast.85), channel_id=1, source_target_pairs={{0,32},{32,64},{64,96},{96,128},{128,160},{160,192},{192,224},{224... | collective-permute-start | bytes 1572872 | tf_op jit(solution)/shard_map/while/body/eval_jaxpr/ppermute | solution.py:25
  158.7 7.7 %collective-permute-start = (bf16[256,256]{1,0:T(8,128)(2,1)S(1)}, bf16[256,256]{1,0:T(8,128)(2,1)S(1)}, u32[]{:S(2)}, u32[]{:S(2)}) collective-permute-start(bf16[256,256]{1,0:T(8,128)(2,1)S(1)} %get-tuple-element.117), channel_id=1, source_target_pairs={{1,0},{2,1},{3,2},{4,3},{5,4},{6,5},{7,6},{8,7},{9,8},{10,9},{11,1... | collective-permute-start | bytes 393224 | tf_op jit(solution)/shard_map/while/body/eval_jaxpr/ppermute | solution.py:17
  163.9 6.9 %collective-permute-start.1 = (bf16[256,256]{1,0:T(8,128)(2,1)S(1)}, bf16[256,256]{1,0:T(8,128)(2,1)S(1)}, u32[]{:S(2)}, u32[]{:S(2)}) collective-permute-start(bf16[256,256]{1,0:T(8,128)(2,1)S(1)} %get-tuple-element.118), channel_id=1, source_target_pairs={{0,1},{1,2},{2,3},{3,4},{4,5},{5,6},{6,7},{7,8},{8,9},{9,10},{10,1... | collective-permute-start | bytes 393224 | tf_op jit(solution)/shard_map/while/body/eval_jaxpr/ppermute | solution.py:16
  173.3 9.8 %collective-permute-start.2 = (bf16[1024,256]{1,0:T(8,128)(2,1)S(1)}, bf16[1024,256]{1,0:T(8,128)(2,1)S(1)}, u32[]{:S(2)}, u32[]{:S(2)}) collective-permute-start(bf16[1024,256]{1,0:T(8,128)(2,1)S(1)} %bitcast.85), channel_id=1, source_target_pairs={{0,32},{32,64},{64,96},{96,128},{128,160},{160,192},{192,224},{224... | collective-permute-start | bytes 1572872 | tf_op jit(solution)/shard_map/while/body/eval_jaxpr/ppermute | solution.py:25
  183.1 7.8 %collective-permute-start = (bf16[256,256]{1,0:T(8,128)(2,1)S(1)}, bf16[256,256]{1,0:T(8,128)(2,1)S(1)}, u32[]{:S(2)}, u32[]{:S(2)}) collective-permute-start(bf16[256,256]{1,0:T(8,128)(2,1)S(1)} %get-tuple-element.117), channel_id=1, source_target_pairs={{1,0},{2,1},{3,2},{4,3},{5,4},{6,5},{7,6},{8,7},{9,8},{10,9},{11,1... | collective-permute-start | bytes 393224 | tf_op jit(solution)/shard_map/while/body/eval_jaxpr/ppermute | solution.py:17
  188.4 6.9 %collective-permute-start.1 = (bf16[256,256]{1,0:T(8,128)(2,1)S(1)}, bf16[256,256]{1,0:T(8,128)(2,1)S(1)}, u32[]{:S(2)}, u32[]{:S(2)}) collective-permute-start(bf16[256,256]{1,0:T(8,128)(2,1)S(1)} %get-tuple-element.118), channel_id=1, source_target_pairs={{0,1},{1,2},{2,3},{3,4},{4,5},{5,6},{6,7},{7,8},{8,9},{9,10},{10,1... | collective-permute-start | bytes 393224 | tf_op jit(solution)/shard_map/while/body/eval_jaxpr/ppermute | solution.py:16
  197.7 9.8 %collective-permute-start.2 = (bf16[1024,256]{1,0:T(8,128)(2,1)S(1)}, bf16[1024,256]{1,0:T(8,128)(2,1)S(1)}, u32[]{:S(2)}, u32[]{:S(2)}) collective-permute-start(bf16[1024,256]{1,0:T(8,128)(2,1)S(1)} %bitcast.85), channel_id=1, source_target_pairs={{0,32},{32,64},{64,96},{96,128},{128,160},{160,192},{192,224},{224... | collective-permute-start | bytes 1572872 | tf_op jit(solution)/shard_map/while/body/eval_jaxpr/ppermute | solution.py:25
  207.6 7.7 %collective-permute-start = (bf16[256,256]{1,0:T(8,128)(2,1)S(1)}, bf16[256,256]{1,0:T(8,128)(2,1)S(1)}, u32[]{:S(2)}, u32[]{:S(2)}) collective-permute-start(bf16[256,256]{1,0:T(8,128)(2,1)S(1)} %get-tuple-element.117), channel_id=1, source_target_pairs={{1,0},{2,1},{3,2},{4,3},{5,4},{6,5},{7,6},{8,7},{9,8},{10,9},{11,1... | collective-permute-start | bytes 393224 | tf_op jit(solution)/shard_map/while/body/eval_jaxpr/ppermute | solution.py:17
  212.8 6.9 %collective-permute-start.1 = (bf16[256,256]{1,0:T(8,128)(2,1)S(1)}, bf16[256,256]{1,0:T(8,128)(2,1)S(1)}, u32[]{:S(2)}, u32[]{:S(2)}) collective-permute-start(bf16[256,256]{1,0:T(8,128)(2,1)S(1)} %get-tuple-element.118), channel_id=1, source_target_pairs={{0,1},{1,2},{2,3},{3,4},{4,5},{5,6},{6,7},{7,8},{8,9},{9,10},{10,1... | collective-permute-start | bytes 393224 | tf_op jit(solution)/shard_map/while/body/eval_jaxpr/ppermute | solution.py:16
  222.1 9.8 %collective-permute-start.2 = (bf16[1024,256]{1,0:T(8,128)(2,1)S(1)}, bf16[1024,256]{1,0:T(8,128)(2,1)S(1)}, u32[]{:S(2)}, u32[]{:S(2)}) collective-permute-start(bf16[1024,256]{1,0:T(8,128)(2,1)S(1)} %bitcast.85), channel_id=1, source_target_pairs={{0,32},{32,64},{64,96},{96,128},{128,160},{160,192},{192,224},{224... | collective-permute-start | bytes 1572872 | tf_op jit(solution)/shard_map/while/body/eval_jaxpr/ppermute | solution.py:25
  232.0 7.8 %collective-permute-start = (bf16[256,256]{1,0:T(8,128)(2,1)S(1)}, bf16[256,256]{1,0:T(8,128)(2,1)S(1)}, u32[]{:S(2)}, u32[]{:S(2)}) collective-permute-start(bf16[256,256]{1,0:T(8,128)(2,1)S(1)} %get-tuple-element.117), channel_id=1, source_target_pairs={{1,0},{2,1},{3,2},{4,3},{5,4},{6,5},{7,6},{8,7},{9,8},{10,9},{11,1... | collective-permute-start | bytes 393224 | tf_op jit(solution)/shard_map/while/body/eval_jaxpr/ppermute | solution.py:17
  237.3 6.9 %collective-permute-start.1 = (bf16[256,256]{1,0:T(8,128)(2,1)S(1)}, bf16[256,256]{1,0:T(8,128)(2,1)S(1)}, u32[]{:S(2)}, u32[]{:S(2)}) collective-permute-start(bf16[256,256]{1,0:T(8,128)(2,1)S(1)} %get-tuple-element.118), channel_id=1, source_target_pairs={{0,1},{1,2},{2,3},{3,4},{4,5},{5,6},{6,7},{7,8},{8,9},{9,10},{10,1... | collective-permute-start | bytes 393224 | tf_op jit(solution)/shard_map/while/body/eval_jaxpr/ppermute | solution.py:16
  246.6 9.8 %collective-permute-start.2 = (bf16[1024,256]{1,0:T(8,128)(2,1)S(1)}, bf16[1024,256]{1,0:T(8,128)(2,1)S(1)}, u32[]{:S(2)}, u32[]{:S(2)}) collective-permute-start(bf16[1024,256]{1,0:T(8,128)(2,1)S(1)} %bitcast.85), channel_id=1, source_target_pairs={{0,32},{32,64},{64,96},{96,128},{128,160},{160,192},{192,224},{224... | collective-permute-start | bytes 1572872 | tf_op jit(solution)/shard_map/while/body/eval_jaxpr/ppermute | solution.py:25
  256.5 7.7 %collective-permute-start = (bf16[256,256]{1,0:T(8,128)(2,1)S(1)}, bf16[256,256]{1,0:T(8,128)(2,1)S(1)}, u32[]{:S(2)}, u32[]{:S(2)}) collective-permute-start(bf16[256,256]{1,0:T(8,128)(2,1)S(1)} %get-tuple-element.117), channel_id=1, source_target_pairs={{1,0},{2,1},{3,2},{4,3},{5,4},{6,5},{7,6},{8,7},{9,8},{10,9},{11,1... | collective-permute-start | bytes 393224 | tf_op jit(solution)/shard_map/while/body/eval_jaxpr/ppermute | solution.py:17
  261.7 6.9 %collective-permute-start.1 = (bf16[256,256]{1,0:T(8,128)(2,1)S(1)}, bf16[256,256]{1,0:T(8,128)(2,1)S(1)}, u32[]{:S(2)}, u32[]{:S(2)}) collective-permute-start(bf16[256,256]{1,0:T(8,128)(2,1)S(1)} %get-tuple-element.118), channel_id=1, source_target_pairs={{0,1},{1,2},{2,3},{3,4},{4,5},{5,6},{6,7},{7,8},{8,9},{9,10},{10,1... | collective-permute-start | bytes 393224 | tf_op jit(solution)/shard_map/while/body/eval_jaxpr/ppermute | solution.py:16
  271.0 9.8 %collective-permute-start.2 = (bf16[1024,256]{1,0:T(8,128)(2,1)S(1)}, bf16[1024,256]{1,0:T(8,128)(2,1)S(1)}, u32[]{:S(2)}, u32[]{:S(2)}) collective-permute-start(bf16[1024,256]{1,0:T(8,128)(2,1)S(1)} %bitcast.85), channel_id=1, source_target_pairs={{0,32},{32,64},{64,96},{96,128},{128,160},{160,192},{192,224},{224... | collective-permute-start | bytes 1572872 | tf_op jit(solution)/shard_map/while/body/eval_jaxpr/ppermute | solution.py:25
  280.9 7.8 %collective-permute-start = (bf16[256,256]{1,0:T(8,128)(2,1)S(1)}, bf16[256,256]{1,0:T(8,128)(2,1)S(1)}, u32[]{:S(2)}, u32[]{:S(2)}) collective-permute-start(bf16[256,256]{1,0:T(8,128)(2,1)S(1)} %get-tuple-element.117), channel_id=1, source_target_pairs={{1,0},{2,1},{3,2},{4,3},{5,4},{6,5},{7,6},{8,7},{9,8},{10,9},{11,1... | collective-permute-start | bytes 393224 | tf_op jit(solution)/shard_map/while/body/eval_jaxpr/ppermute | solution.py:17
  286.2 6.9 %collective-permute-start.1 = (bf16[256,256]{1,0:T(8,128)(2,1)S(1)}, bf16[256,256]{1,0:T(8,128)(2,1)S(1)}, u32[]{:S(2)}, u32[]{:S(2)}) collective-permute-start(bf16[256,256]{1,0:T(8,128)(2,1)S(1)} %get-tuple-element.118), channel_id=1, source_target_pairs={{0,1},{1,2},{2,3},{3,4},{4,5},{5,6},{6,7},{7,8},{8,9},{9,10},{10,1... | collective-permute-start | bytes 393224 | tf_op jit(solution)/shard_map/while/body/eval_jaxpr/ppermute | solution.py:16
  295.5 9.8 %collective-permute-start.2 = (bf16[1024,256]{1,0:T(8,128)(2,1)S(1)}, bf16[1024,256]{1,0:T(8,128)(2,1)S(1)}, u32[]{:S(2)}, u32[]{:S(2)}) collective-permute-start(bf16[1024,256]{1,0:T(8,128)(2,1)S(1)} %bitcast.85), channel_id=1, source_target_pairs={{0,32},{32,64},{64,96},{96,128},{128,160},{160,192},{192,224},{224... | collective-permute-start | bytes 1572872 | tf_op jit(solution)/shard_map/while/body/eval_jaxpr/ppermute | solution.py:25
  305.3 7.7 %collective-permute-start = (bf16[256,256]{1,0:T(8,128)(2,1)S(1)}, bf16[256,256]{1,0:T(8,128)(2,1)S(1)}, u32[]{:S(2)}, u32[]{:S(2)}) collective-permute-start(bf16[256,256]{1,0:T(8,128)(2,1)S(1)} %get-tuple-element.117), channel_id=1, source_target_pairs={{1,0},{2,1},{3,2},{4,3},{5,4},{6,5},{7,6},{8,7},{9,8},{10,9},{11,1... | collective-permute-start | bytes 393224 | tf_op jit(solution)/shard_map/while/body/eval_jaxpr/ppermute | solution.py:17
  310.6 6.9 %collective-permute-start.1 = (bf16[256,256]{1,0:T(8,128)(2,1)S(1)}, bf16[256,256]{1,0:T(8,128)(2,1)S(1)}, u32[]{:S(2)}, u32[]{:S(2)}) collective-permute-start(bf16[256,256]{1,0:T(8,128)(2,1)S(1)} %get-tuple-element.118), channel_id=1, source_target_pairs={{0,1},{1,2},{2,3},{3,4},{4,5},{5,6},{6,7},{7,8},{8,9},{9,10},{10,1... | collective-permute-start | bytes 393224 | tf_op jit(solution)/shard_map/while/body/eval_jaxpr/ppermute | solution.py:16
  319.9 9.8 %collective-permute-start.2 = (bf16[1024,256]{1,0:T(8,128)(2,1)S(1)}, bf16[1024,256]{1,0:T(8,128)(2,1)S(1)}, u32[]{:S(2)}, u32[]{:S(2)}) collective-permute-start(bf16[1024,256]{1,0:T(8,128)(2,1)S(1)} %bitcast.85), channel_id=1, source_target_pairs={{0,32},{32,64},{64,96},{96,128},{128,160},{160,192},{192,224},{224... | collective-permute-start | bytes 1572872 | tf_op jit(solution)/shard_map/while/body/eval_jaxpr/ppermute | solution.py:25
  329.8 7.8 %collective-permute-start = (bf16[256,256]{1,0:T(8,128)(2,1)S(1)}, bf16[256,256]{1,0:T(8,128)(2,1)S(1)}, u32[]{:S(2)}, u32[]{:S(2)}) collective-permute-start(bf16[256,256]{1,0:T(8,128)(2,1)S(1)} %get-tuple-element.117), channel_id=1, source_target_pairs={{1,0},{2,1},{3,2},{4,3},{5,4},{6,5},{7,6},{8,7},{9,8},{10,9},{11,1... | collective-permute-start | bytes 393224 | tf_op jit(solution)/shard_map/while/body/eval_jaxpr/ppermute | solution.py:17
  335.0 6.9 %collective-permute-start.1 = (bf16[256,256]{1,0:T(8,128)(2,1)S(1)}, bf16[256,256]{1,0:T(8,128)(2,1)S(1)}, u32[]{:S(2)}, u32[]{:S(2)}) collective-permute-start(bf16[256,256]{1,0:T(8,128)(2,1)S(1)} %get-tuple-element.118), channel_id=1, source_target_pairs={{0,1},{1,2},{2,3},{3,4},{4,5},{5,6},{6,7},{7,8},{8,9},{9,10},{10,1... | collective-permute-start | bytes 393224 | tf_op jit(solution)/shard_map/while/body/eval_jaxpr/ppermute | solution.py:16
  344.4 9.8 %collective-permute-start.2 = (bf16[1024,256]{1,0:T(8,128)(2,1)S(1)}, bf16[1024,256]{1,0:T(8,128)(2,1)S(1)}, u32[]{:S(2)}, u32[]{:S(2)}) collective-permute-start(bf16[1024,256]{1,0:T(8,128)(2,1)S(1)} %bitcast.85), channel_id=1, source_target_pairs={{0,32},{32,64},{64,96},{96,128},{128,160},{160,192},{192,224},{224... | collective-permute-start | bytes 1572872 | tf_op jit(solution)/shard_map/while/body/eval_jaxpr/ppermute | solution.py:25
  354.2 7.7 %collective-permute-start = (bf16[256,256]{1,0:T(8,128)(2,1)S(1)}, bf16[256,256]{1,0:T(8,128)(2,1)S(1)}, u32[]{:S(2)}, u32[]{:S(2)}) collective-permute-start(bf16[256,256]{1,0:T(8,128)(2,1)S(1)} %get-tuple-element.117), channel_id=1, source_target_pairs={{1,0},{2,1},{3,2},{4,3},{5,4},{6,5},{7,6},{8,7},{9,8},{10,9},{11,1... | collective-permute-start | bytes 393224 | tf_op jit(solution)/shard_map/while/body/eval_jaxpr/ppermute | solution.py:17
  359.5 6.9 %collective-permute-start.1 = (bf16[256,256]{1,0:T(8,128)(2,1)S(1)}, bf16[256,256]{1,0:T(8,128)(2,1)S(1)}, u32[]{:S(2)}, u32[]{:S(2)}) collective-permute-start(bf16[256,256]{1,0:T(8,128)(2,1)S(1)} %get-tuple-element.118), channel_id=1, source_target_pairs={{0,1},{1,2},{2,3},{3,4},{4,5},{5,6},{6,7},{7,8},{8,9},{9,10},{10,1... | collective-permute-start | bytes 393224 | tf_op jit(solution)/shard_map/while/body/eval_jaxpr/ppermute | solution.py:16
  368.8 9.8 %collective-permute-start.2 = (bf16[1024,256]{1,0:T(8,128)(2,1)S(1)}, bf16[1024,256]{1,0:T(8,128)(2,1)S(1)}, u32[]{:S(2)}, u32[]{:S(2)}) collective-permute-start(bf16[1024,256]{1,0:T(8,128)(2,1)S(1)} %bitcast.85), channel_id=1, source_target_pairs={{0,32},{32,64},{64,96},{96,128},{128,160},{160,192},{192,224},{224... | collective-permute-start | bytes 1572872 | tf_op jit(solution)/shard_map/while/body/eval_jaxpr/ppermute | solution.py:25
  378.7 7.8 %collective-permute-start = (bf16[256,256]{1,0:T(8,128)(2,1)S(1)}, bf16[256,256]{1,0:T(8,128)(2,1)S(1)}, u32[]{:S(2)}, u32[]{:S(2)}) collective-permute-start(bf16[256,256]{1,0:T(8,128)(2,1)S(1)} %get-tuple-element.117), channel_id=1, source_target_pairs={{1,0},{2,1},{3,2},{4,3},{5,4},{6,5},{7,6},{8,7},{9,8},{10,9},{11,1... | collective-permute-start | bytes 393224 | tf_op jit(solution)/shard_map/while/body/eval_jaxpr/ppermute | solution.py:17
  393.3 9.8 %collective-permute-start.2 = (bf16[1024,256]{1,0:T(8,128)(2,1)S(1)}, bf16[1024,256]{1,0:T(8,128)(2,1)S(1)}, u32[]{:S(2)}, u32[]{:S(2)}) collective-permute-start(bf16[1024,256]{1,0:T(8,128)(2,1)S(1)} %bitcast.85), channel_id=1, source_target_pairs={{0,32},{32,64},{64,96},{96,128},{128,160},{160,192},{192,224},{224... | collective-permute-start | bytes 1572872 | tf_op jit(solution)/shard_map/while/body/eval_jaxpr/ppermute | solution.py:25
  (3 other events, 13.2 us)
Sparse Core Ops, SparseCore 0:
  404.3 156.4 all-reduce.2
where the time goes:
time: 636 us; the launch traced here: 634 us
  waiting for transfers between devices  393 us (62%)
  starting transfers between devices  112 us (18%)
  other arithmetic  60 us (9%)
  matrix products  31.2 us (5%)
  local copies, waits for them, and re-layouts  20.1 us (3%)
  between operations  15.5 us (2%)
    ppermute x16, waiting for transfers between devices, passed_along(): return lax.ppermute(value, axis, pairs)  161 us
    psum x1, waiting for transfers between devices, body(): lax.psum(gram_term.astype(jnp.bfloat16), 'rows').astype(jnp.float32)  157 us
    ppermute x16, starting transfers between devices, with_halo(): after = lax.ppermute(leading, axis, down)  79.9 us
    ppermute x16, waiting for transfers between devices, with_halo(): before = lax.ppermute(last, axis, up)  68.2 us
    another operation x6, other arithmetic, body(): lower_factor = jnp.linalg.cholesky(gram_total)  34 us
    ppermute x16, starting transfers between devices, with_halo(): before = lax.ppermute(last, axis, up)  32.2 us
    dot_general x16, matrix products, advance(): jnp.einsum('ijab,ijbk->iak', kept_blocks, picked, preferred_element_type=...  27.7 us
    another operation x2, other arithmetic, body(): jax.scipy.linalg.solve_triangular(lower_factor, arrived.astype(jnp.float3...  19.9 us
  transfers between devices with their start and end apart: 49, of which 49 were waited for; matrix products, arithmetic and copies ran while one was open for 0% of the time, Pallas kernels for 0%

commit v1 on v0

--- a/solution.py
+++ b/solution.py
@@ -1,9 +1,94 @@
 import jax
 import jax.numpy as jnp
 from jax import lax
+from jax.experimental import pallas as pl
+from jax.experimental.pallas import tpu as pltpu
 from jax.sharding import PartitionSpec as P
 
 HB = 2
+NB = 16
+
+def factor_kernel(gram_ref, arrived_ref, basis_ref, factor_ref, a_ref, w_ref):
+    size = gram_ref.shape[0]
+    a_ref[...] = gram_ref[...]
+    row_i = lax.broadcasted_iota(jnp.int32, (size, size), 0)
+    col_i = lax.broadcasted_iota(jnp.int32, (size, size), 1)
+    w_ref[...] = jnp.where(row_i == col_i, 1.0, 0.0)
+    lanes = 128
+    sub = lax.broadcasted_iota(jnp.int32, (NB, lanes), 0)
+    wide_row = lax.broadcasted_iota(jnp.int32, (NB, size), 0)
+    wide_col = lax.broadcasted_iota(jnp.int32, (NB, size), 1)
+    for first in range(0, size, NB):
+        panel = a_ref[first : first + NB, :]
+        other = w_ref[first : first + NB, :]
+        columns = [
+            jnp.broadcast_to(panel[:, first + k : first + k + 1], (NB, lanes))
+            for k in range(NB)
+        ]
+        pivots = jnp.zeros((NB, lanes), jnp.float32)
+        for j in range(NB):
+            column = columns[j]
+            pivot = jnp.broadcast_to(column[j : j + 1, :], (NB, lanes))
+            pivots = jnp.where(sub == j, pivot, pivots)
+            if j == NB - 1:
+                break
+            scaled = jnp.where(sub > j, column / pivot, 0.0)
+            for k in range(j + 1, NB):
+                columns[k] = columns[k] - scaled * jnp.broadcast_to(
+                    column[k : k + 1, :], (NB, lanes)
+                )
+            both = jnp.concatenate([scaled] * (size // lanes), axis=1)
+            panel = panel - both * jnp.broadcast_to(panel[j : j + 1, :], (NB, size))
+            other = other - both * jnp.broadcast_to(other[j : j + 1, :], (NB, size))
+        scale = 1.0 / jnp.sqrt(pivots)
+        both = jnp.concatenate([scale] * (size // lanes), axis=1)
+        upper = jnp.where(wide_col >= wide_row + first, panel * both, 0.0)
+        other = other * both
+        factor_ref[first : first + NB, :] = upper
+        w_ref[first : first + NB, :] = other
+        rest = first + NB
+        if rest < size:
+            right = jnp.concatenate([upper, other], axis=1)
+            change = lax.dot_general(
+                upper, right, (((0,), (0,)), ((), ())),
+                preferred_element_type=jnp.float32, precision=lax.Precision.HIGHEST,
+            )
+            a_ref[rest:, :] = a_ref[rest:, :] - change[rest:, :size]
+            w_ref[rest:, :] = w_ref[rest:, :] - change[rest:, size:]
+    w = w_ref[...]
+    high = w.astype(jnp.bfloat16)
+    low = (w - high.astype(jnp.float32)).astype(jnp.bfloat16)
+    dims = (((1,), (1,)), ((), ()))
+    for piece in range(0, arrived_ref.shape[0], 256):
+        rows = arrived_ref[piece : piece + 256, :]
+        basis_ref[piece : piece + 256, :] = lax.dot_general(
+            rows, high, dims, preferred_element_type=jnp.float32
+        ) + lax.dot_general(rows, low, dims, preferred_element_type=jnp.float32)
+
+def finish(gram, arrived):
+    size = gram.shape[0]
+    vmem = pl.BlockSpec(memory_space=pltpu.VMEM)
+    return pl.pallas_call(
+        factor_kernel,
+        out_shape=(
+            jax.ShapeDtypeStruct(arrived.shape, jnp.float32),
+            jax.ShapeDtypeStruct((size, size), jnp.float32),
+        ),
+        in_specs=[vmem, vmem],
+        out_specs=(vmem, vmem),
+        scratch_shapes=[pltpu.VMEM((size, size), jnp.float32), pltpu.VMEM((size, size), jnp.float32)],
+        name="factor_solve",
+    )(gram, arrived)
+
+
+def sum_over_rows(term):
+    owners = lax.axis_size("rows")
+    size = term.shape[0]
+    pieces = term.reshape(owners, size // owners, size)
+    pieces = lax.all_to_all(pieces, "rows", 0, 0, tiled=True)
+    mine = jnp.sum(pieces.astype(jnp.float32), axis=0, keepdims=True)
+    copies = jnp.broadcast_to(mine, (owners, size // owners, size))
+    return lax.all_to_all(copies, "rows", 0, 0, tiled=True).reshape(size, size)
 
 
 def with_halo(array, sides, width):
@@ -57,14 +142,9 @@
     gram_term = lax.dot_general(
         arrived, arrived, (((0,), (0,)), ((), ())), preferred_element_type=jnp.float32
     )
-    gram_total = lax.psum(gram_term.astype(jnp.bfloat16), "rows").astype(jnp.float32) / (
-        rows_here * owners
-    )
-    lower_factor = jnp.linalg.cholesky(gram_total)
-    basis_out = jax.scipy.linalg.solve_triangular(
-        lower_factor, arrived.astype(jnp.float32).T, lower=True
-    ).T
-    return (basis_out[None], lower_factor.T[None])
+    gram_total = sum_over_rows(gram_term.astype(jnp.bfloat16)) / (rows_here * owners)
+    basis_out, upper_factor = finish(gram_total, arrived)
+    return (basis_out[None], upper_factor[None])
 
 
 def solution(mesh):

time: 636 us -> 453 us (0.71)
  the two profiles are of different devices: /device:TPU:10 before, /device:TPU:8 now
where the time goes in v1:
time: 453 us; the launch traced here: 451 us
  waiting for transfers between devices  258 us (57%)
  starting transfers between devices  94.4 us (21%)
  blocking collectives  34.4 us (8%)
  matrix products  28 us (6%)
  Pallas kernels  15.6 us (3%)
  local copies, waits for them, and re-layouts  13.8 us (3%)
  other arithmetic  5.58 us (1%)
    ppermute x16, waiting for transfers between devices, passed_along(): return lax.ppermute(value, axis, pairs)  161 us
    ppermute x16, waiting for transfers between devices, with_halo(): before = lax.ppermute(last, axis, up)  83.8 us
    ppermute x16, starting transfers between devices, with_halo(): after = lax.ppermute(leading, axis, down)  50 us
    ppermute x16, starting transfers between devices, with_halo(): before = lax.ppermute(last, axis, up)  44.1 us
    dot_general x16, matrix products, advance(): jnp.einsum('ijab,ijbk->iak', kept_blocks, picked, preferred_element_type=...  27.7 us
    all_to_all x1, blocking collectives, sum_over_rows(): pieces = lax.all_to_all(pieces, 'rows', 0, 0, tiled=True)  19.4 us
    pallas_call x1, Pallas kernels, finish(): pl.pallas_call(factor_kernel, out_shape=(jax.ShapeDtypeStruct(arrived.sha...  15.6 us
    all_to_all x1, blocking collectives, sum_over_rows(): return lax.all_to_all(copies, 'rows', 0, 0, tiled=True).reshape(size, size)  15 us
  transfers between devices with their start and end apart: 48, of which 48 were waited for; matrix products, arithmetic and copies ran while one was open for 1% of the time, Pallas kernels for 0%

profile of v1, /device:TPU:8, one launch (start us, length us, event | category | flops | bytes accessed | tf_op | source)
XLA Modules:
  0.0 451.0 jit_solution(506401213931956102)
XLA Ops:
  4.5 395.5 %while.10 = (s32[]{:T(128)}, bf16[1024,256]{1,0:T(8,128)(2,1)S(1)}, s32[8,4]{0,1:T(4,128)S(1)}, bf16[8,4,128,128]{3,2,1,0:T(8,128)(2,1)}, s32[]{:T(128)}) while((s32[]{:T(128)}, bf16[1024,256]{1,0:T(8,128)(2,1)S(1)}, s32[8,4]{0,1:T(4,128)S(1)}, bf16[8,4,128,128]{3,2,1,0:T(8,128)(2,1)}, s32[]{:T(128)}) %tuple.28), condition=%wide.region_1.2_spmd, body=%wide.region_0.1_spmd.sunk | while | flops 271058016 | bytes 13112501 | solution.py:141
  4.5 4.6 %collective-permute-start = (bf16[256,256]{1,0:T(8,128)(2,1)S(1)}, bf16[256,256]{1,0:T(8,128)(2,1)S(1)}, u32[]{:S(2)}, u32[]{:S(2)}) collective-permute-start(bf16[256,256]{1,0:T(8,128)(2,1)S(1)} %get-tuple-element.66), channel_id=1, source_target_pairs={{1,0},{2,1},{3,2},{4,3},{5,4},{6,5},{7,6},{8,7},{9,8},{10,9},{11,1... | collective-permute-start | bytes 393224 | tf_op jit(solution)/shard_map/while/body/eval_jaxpr/ppermute | solution.py:102
  11.8 6.2 %collective-permute-done.1 = bf16[256,256]{1,0:T(8,128)(2,1)S(1)} collective-permute-done((bf16[256,256]{1,0:T(8,128)(2,1)S(1)}, bf16[256,256]{1,0:T(8,128)(2,1)S(1)}, u32[]{:S(2)}, u32[]{:S(2)}) %collective-permute-start.1) | collective-permute-done | bytes 131104 | tf_op jit(solution)/shard_map/while/body/eval_jaxpr/ppermute | solution.py:101
  20.5 13.9 %collective-permute-done.2 = bf16[1024,256]{1,0:T(8,128)(2,1)S(1)} collective-permute-done((bf16[1024,256]{1,0:T(8,128)(2,1)S(1)}, bf16[1024,256]{1,0:T(8,128)(2,1)S(1)}, u32[]{:S(2)}, u32[]{:S(2)}) %collective-permute-start.2) | collective-permute-done | bytes 524320 | tf_op jit(solution)/shard_map/while/body/eval_jaxpr/ppermute | solution.py:110
  36.4 3.9 collective-permute-start.1
  41.3 4.0 collective-permute-done.1
  47.9 9.8 %collective-permute-done.2 = bf16[1024,256]{1,0:T(8,128)(2,1)S(1)} collective-permute-done((bf16[1024,256]{1,0:T(8,128)(2,1)S(1)}, bf16[1024,256]{1,0:T(8,128)(2,1)S(1)}, u32[]{:S(2)}, u32[]{:S(2)}) %collective-permute-start.2) | collective-permute-done | bytes 524320 | tf_op jit(solution)/shard_map/while/body/eval_jaxpr/ppermute | solution.py:110
  59.7 3.8 collective-permute-start.1
  64.5 4.5 %collective-permute-done.1 = bf16[256,256]{1,0:T(8,128)(2,1)S(1)} collective-permute-done((bf16[256,256]{1,0:T(8,128)(2,1)S(1)}, bf16[256,256]{1,0:T(8,128)(2,1)S(1)}, u32[]{:S(2)}, u32[]{:S(2)}) %collective-permute-start.1) | collective-permute-done | bytes 131104 | tf_op jit(solution)/shard_map/while/body/eval_jaxpr/ppermute | solution.py:101
  71.6 9.8 %collective-permute-done.2 = bf16[1024,256]{1,0:T(8,128)(2,1)S(1)} collective-permute-done((bf16[1024,256]{1,0:T(8,128)(2,1)S(1)}, bf16[1024,256]{1,0:T(8,128)(2,1)S(1)}, u32[]{:S(2)}, u32[]{:S(2)}) %collective-permute-start.2) | collective-permute-done | bytes 524320 | tf_op jit(solution)/shard_map/while/body/eval_jaxpr/ppermute | solution.py:110
  81.4 3.9 collective-permute-start
  88.3 6.0 %collective-permute-done.1 = bf16[256,256]{1,0:T(8,128)(2,1)S(1)} collective-permute-done((bf16[256,256]{1,0:T(8,128)(2,1)S(1)}, bf16[256,256]{1,0:T(8,128)(2,1)S(1)}, u32[]{:S(2)}, u32[]{:S(2)}) %collective-permute-start.1) | collective-permute-done | bytes 131104 | tf_op jit(solution)/shard_map/while/body/eval_jaxpr/ppermute | solution.py:101
  96.8 9.8 %collective-permute-done.2 = bf16[1024,256]{1,0:T(8,128)(2,1)S(1)} collective-permute-done((bf16[1024,256]{1,0:T(8,128)(2,1)S(1)}, bf16[1024,256]{1,0:T(8,128)(2,1)S(1)}, u32[]{:S(2)}, u32[]{:S(2)}) %collective-permute-start.2) | collective-permute-done | bytes 524320 | tf_op jit(solution)/shard_map/while/body/eval_jaxpr/ppermute | solution.py:110
  106.6 3.1 collective-permute-start
  113.5 5.3 %collective-permute-done.1 = bf16[256,256]{1,0:T(8,128)(2,1)S(1)} collective-permute-done((bf16[256,256]{1,0:T(8,128)(2,1)S(1)}, bf16[256,256]{1,0:T(8,128)(2,1)S(1)}, u32[]{:S(2)}, u32[]{:S(2)}) %collective-permute-start.1) | collective-permute-done | bytes 131104 | tf_op jit(solution)/shard_map/while/body/eval_jaxpr/ppermute | solution.py:101
  121.3 9.8 %collective-permute-done.2 = bf16[1024,256]{1,0:T(8,128)(2,1)S(1)} collective-permute-done((bf16[1024,256]{1,0:T(8,128)(2,1)S(1)}, bf16[1024,256]{1,0:T(8,128)(2,1)S(1)}, u32[]{:S(2)}, u32[]{:S(2)}) %collective-permute-start.2) | collective-permute-done | bytes 524320 | tf_op jit(solution)/shard_map/while/body/eval_jaxpr/ppermute | solution.py:110
  138.0 5.2 %collective-permute-done.1 = bf16[256,256]{1,0:T(8,128)(2,1)S(1)} collective-permute-done((bf16[256,256]{1,0:T(8,128)(2,1)S(1)}, bf16[256,256]{1,0:T(8,128)(2,1)S(1)}, u32[]{:S(2)}, u32[]{:S(2)}) %collective-permute-start.1) | collective-permute-done | bytes 131104 | tf_op jit(solution)/shard_map/while/body/eval_jaxpr/ppermute | solution.py:101
  145.7 9.8 %collective-permute-done.2 = bf16[1024,256]{1,0:T(8,128)(2,1)S(1)} collective-permute-done((bf16[1024,256]{1,0:T(8,128)(2,1)S(1)}, bf16[1024,256]{1,0:T(8,128)(2,1)S(1)}, u32[]{:S(2)}, u32[]{:S(2)}) %collective-permute-start.2) | collective-permute-done | bytes 524320 | tf_op jit(solution)/shard_map/while/body/eval_jaxpr/ppermute | solution.py:110
  162.4 5.2 %collective-permute-done.1 = bf16[256,256]{1,0:T(8,128)(2,1)S(1)} collective-permute-done((bf16[256,256]{1,0:T(8,128)(2,1)S(1)}, bf16[256,256]{1,0:T(8,128)(2,1)S(1)}, u32[]{:S(2)}, u32[]{:S(2)}) %collective-permute-start.1) | collective-permute-done | bytes 131104 | tf_op jit(solution)/shard_map/while/body/eval_jaxpr/ppermute | solution.py:101
  170.2 9.8 %collective-permute-done.2 = bf16[1024,256]{1,0:T(8,128)(2,1)S(1)} collective-permute-done((bf16[1024,256]{1,0:T(8,128)(2,1)S(1)}, bf16[1024,256]{1,0:T(8,128)(2,1)S(1)}, u32[]{:S(2)}, u32[]{:S(2)}) %collective-permute-start.2) | collective-permute-done | bytes 524320 | tf_op jit(solution)/shard_map/while/body/eval_jaxpr/ppermute | solution.py:110
  180.0 3.1 collective-permute-start
  186.8 5.2 %collective-permute-done.1 = bf16[256,256]{1,0:T(8,128)(2,1)S(1)} collective-permute-done((bf16[256,256]{1,0:T(8,128)(2,1)S(1)}, bf16[256,256]{1,0:T(8,128)(2,1)S(1)}, u32[]{:S(2)}, u32[]{:S(2)}) %collective-permute-start.1) | collective-permute-done | bytes 131104 | tf_op jit(solution)/shard_map/while/body/eval_jaxpr/ppermute | solution.py:101
  194.6 9.8 %collective-permute-done.2 = bf16[1024,256]{1,0:T(8,128)(2,1)S(1)} collective-permute-done((bf16[1024,256]{1,0:T(8,128)(2,1)S(1)}, bf16[1024,256]{1,0:T(8,128)(2,1)S(1)}, u32[]{:S(2)}, u32[]{:S(2)}) %collective-permute-start.2) | collective-permute-done | bytes 524320 | tf_op jit(solution)/shard_map/while/body/eval_jaxpr/ppermute | solution.py:110
  204.4 3.1 collective-permute-start
  211.3 5.2 %collective-permute-done.1 = bf16[256,256]{1,0:T(8,128)(2,1)S(1)} collective-permute-done((bf16[256,256]{1,0:T(8,128)(2,1)S(1)}, bf16[256,256]{1,0:T(8,128)(2,1)S(1)}, u32[]{:S(2)}, u32[]{:S(2)}) %collective-permute-start.1) | collective-permute-done | bytes 131104 | tf_op jit(solution)/shard_map/while/body/eval_jaxpr/ppermute | solution.py:101
  219.0 9.8 %collective-permute-done.2 = bf16[1024,256]{1,0:T(8,128)(2,1)S(1)} collective-permute-done((bf16[1024,256]{1,0:T(8,128)(2,1)S(1)}, bf16[1024,256]{1,0:T(8,128)(2,1)S(1)}, u32[]{:S(2)}, u32[]{:S(2)}) %collective-permute-start.2) | collective-permute-done | bytes 524320 | tf_op jit(solution)/shard_map/while/body/eval_jaxpr/ppermute | solution.py:110
  228.9 3.1 collective-permute-start
  235.7 5.2 %collective-permute-done.1 = bf16[256,256]{1,0:T(8,128)(2,1)S(1)} collective-permute-done((bf16[256,256]{1,0:T(8,128)(2,1)S(1)}, bf16[256,256]{1,0:T(8,128)(2,1)S(1)}, u32[]{:S(2)}, u32[]{:S(2)}) %collective-permute-start.1) | collective-permute-done | bytes 131104 | tf_op jit(solution)/shard_map/while/body/eval_jaxpr/ppermute | solution.py:101
  243.5 9.8 %collective-permute-done.2 = bf16[1024,256]{1,0:T(8,128)(2,1)S(1)} collective-permute-done((bf16[1024,256]{1,0:T(8,128)(2,1)S(1)}, bf16[1024,256]{1,0:T(8,128)(2,1)S(1)}, u32[]{:S(2)}, u32[]{:S(2)}) %collective-permute-start.2) | collective-permute-done | bytes 524320 | tf_op jit(solution)/shard_map/while/body/eval_jaxpr/ppermute | solution.py:110
  260.2 5.2 %collective-permute-done.1 = bf16[256,256]{1,0:T(8,128)(2,1)S(1)} collective-permute-done((bf16[256,256]{1,0:T(8,128)(2,1)S(1)}, bf16[256,256]{1,0:T(8,128)(2,1)S(1)}, u32[]{:S(2)}, u32[]{:S(2)}) %collective-permute-start.1) | collective-permute-done | bytes 131104 | tf_op jit(solution)/shard_map/while/body/eval_jaxpr/ppermute | solution.py:101
  267.9 9.8 %collective-permute-done.2 = bf16[1024,256]{1,0:T(8,128)(2,1)S(1)} collective-permute-done((bf16[1024,256]{1,0:T(8,128)(2,1)S(1)}, bf16[1024,256]{1,0:T(8,128)(2,1)S(1)}, u32[]{:S(2)}, u32[]{:S(2)}) %collective-permute-start.2) | collective-permute-done | bytes 524320 | tf_op jit(solution)/shard_map/while/body/eval_jaxpr/ppermute | solution.py:110
  277.7 3.1 collective-permute-start
  284.6 5.2 %collective-permute-done.1 = bf16[256,256]{1,0:T(8,128)(2,1)S(1)} collective-permute-done((bf16[256,256]{1,0:T(8,128)(2,1)S(1)}, bf16[256,256]{1,0:T(8,128)(2,1)S(1)}, u32[]{:S(2)}, u32[]{:S(2)}) %collective-permute-start.1) | collective-permute-done | bytes 131104 | tf_op jit(solution)/shard_map/while/body/eval_jaxpr/ppermute | solution.py:101
  292.4 9.8 %collective-permute-done.2 = bf16[1024,256]{1,0:T(8,128)(2,1)S(1)} collective-permute-done((bf16[1024,256]{1,0:T(8,128)(2,1)S(1)}, bf16[1024,256]{1,0:T(8,128)(2,1)S(1)}, u32[]{:S(2)}, u32[]{:S(2)}) %collective-permute-start.2) | collective-permute-done | bytes 524320 | tf_op jit(solution)/shard_map/while/body/eval_jaxpr/ppermute | solution.py:110
  302.2 3.1 collective-permute-start
  309.1 5.2 %collective-permute-done.1 = bf16[256,256]{1,0:T(8,128)(2,1)S(1)} collective-permute-done((bf16[256,256]{1,0:T(8,128)(2,1)S(1)}, bf16[256,256]{1,0:T(8,128)(2,1)S(1)}, u32[]{:S(2)}, u32[]{:S(2)}) %collective-permute-start.1) | collective-permute-done | bytes 131104 | tf_op jit(solution)/shard_map/while/body/eval_jaxpr/ppermute | solution.py:101
  316.8 9.8 %collective-permute-done.2 = bf16[1024,256]{1,0:T(8,128)(2,1)S(1)} collective-permute-done((bf16[1024,256]{1,0:T(8,128)(2,1)S(1)}, bf16[1024,256]{1,0:T(8,128)(2,1)S(1)}, u32[]{:S(2)}, u32[]{:S(2)}) %collective-permute-start.2) | collective-permute-done | bytes 524320 | tf_op jit(solution)/shard_map/while/body/eval_jaxpr/ppermute | solution.py:110
  326.6 3.1 collective-permute-start
  333.5 5.2 %collective-permute-done.1 = bf16[256,256]{1,0:T(8,128)(2,1)S(1)} collective-permute-done((bf16[256,256]{1,0:T(8,128)(2,1)S(1)}, bf16[256,256]{1,0:T(8,128)(2,1)S(1)}, u32[]{:S(2)}, u32[]{:S(2)}) %collective-permute-start.1) | collective-permute-done | bytes 131104 | tf_op jit(solution)/shard_map/while/body/eval_jaxpr/ppermute | solution.py:101
  341.3 9.8 %collective-permute-done.2 = bf16[1024,256]{1,0:T(8,128)(2,1)S(1)} collective-permute-done((bf16[1024,256]{1,0:T(8,128)(2,1)S(1)}, bf16[1024,256]{1,0:T(8,128)(2,1)S(1)}, u32[]{:S(2)}, u32[]{:S(2)}) %collective-permute-start.2) | collective-permute-done | bytes 524320 | tf_op jit(solution)/shard_map/while/body/eval_jaxpr/ppermute | solution.py:110
  357.9 5.2 %collective-permute-done.1 = bf16[256,256]{1,0:T(8,128)(2,1)S(1)} collective-permute-done((bf16[256,256]{1,0:T(8,128)(2,1)S(1)}, bf16[256,256]{1,0:T(8,128)(2,1)S(1)}, u32[]{:S(2)}, u32[]{:S(2)}) %collective-permute-start.1) | collective-permute-done | bytes 131104 | tf_op jit(solution)/shard_map/while/body/eval_jaxpr/ppermute | solution.py:101
  365.7 9.8 %collective-permute-done.2 = bf16[1024,256]{1,0:T(8,128)(2,1)S(1)} collective-permute-done((bf16[1024,256]{1,0:T(8,128)(2,1)S(1)}, bf16[1024,256]{1,0:T(8,128)(2,1)S(1)}, u32[]{:S(2)}, u32[]{:S(2)}) %collective-permute-start.2) | collective-permute-done | bytes 524320 | tf_op jit(solution)/shard_map/while/body/eval_jaxpr/ppermute | solution.py:110
  375.5 3.1 collective-permute-start
  382.4 5.2 %collective-permute-done.1 = bf16[256,256]{1,0:T(8,128)(2,1)S(1)} collective-permute-done((bf16[256,256]{1,0:T(8,128)(2,1)S(1)}, bf16[256,256]{1,0:T(8,128)(2,1)S(1)}, u32[]{:S(2)}, u32[]{:S(2)}) %collective-permute-start.1) | collective-permute-done | bytes 131104 | tf_op jit(solution)/shard_map/while/body/eval_jaxpr/ppermute | solution.py:101
  390.1 9.8 %collective-permute-done.2 = bf16[1024,256]{1,0:T(8,128)(2,1)S(1)} collective-permute-done((bf16[1024,256]{1,0:T(8,128)(2,1)S(1)}, bf16[1024,256]{1,0:T(8,128)(2,1)S(1)}, u32[]{:S(2)}, u32[]{:S(2)}) %collective-permute-start.2) | collective-permute-done | bytes 524320 | tf_op jit(solution)/shard_map/while/body/eval_jaxpr/ppermute | solution.py:110
  400.3 19.4 %all_to_all.10 = bf16[32,8,256]{2,1,0:T(8,128)(2,1)S(1)} all-to-all(bf16[32,8,256]{2,1,0:T(8,128)(2,1)S(1)} %fusion.1), channel_id=1, replica_groups=mesh['phase'=16,'rows'=32] {'rows'}, dimensions={0} | all-to-all | bytes 262144 | tf_op jit(solution)/shard_map/all_to_all | solution.py:88
  419.8 15.0 %all_to_all.11 = f32[32,8,256]{2,1,0:T(8,128)S(1)} all-to-all(f32[32,8,256]{2,1,0:T(8,128)S(1)} %broadcast_in_dim.29), channel_id=1, replica_groups=mesh['phase'=16,'rows'=32] {'rows'}, dimensions={0} | all-to-all | bytes 524288 | tf_op jit(solution)/shard_map/all_to_all | solution.py:91
  435.5 15.6 %factor_solve.1 = (f32[1024,256]{1,0:T(8,128)}, f32[256,256]{1,0:T(8,128)}) custom-call(f32[256,256]{1,0:T(8,128)} %multiply_bitcast_fusion.gram_ref, bf16[1024,256]{1,0:T(8,128)(2,1)S(1)} %get-tuple-element.26.arrived_ref), custom_call_target="tpu_custom_call" | custom-call | tf_op jit(solution)/shard_map/factor_solve/pallas_call | solution.py:71
  (189 shorter events, 113.5 us)
Async XLA Ops:
  4.5 7.3 %collective-permute-start = (bf16[256,256]{1,0:T(8,128)(2,1)S(1)}, bf16[256,256]{1,0:T(8,128)(2,1)S(1)}, u32[]{:S(2)}, u32[]{:S(2)}) collective-permute-start(bf16[256,256]{1,0:T(8,128)(2,1)S(1)} %get-tuple-element.66), channel_id=1, source_target_pairs={{1,0},{2,1},{3,2},{4,3},{5,4},{6,5},{7,6},{8,7},{9,8},{10,9},{11,1... | collective-permute-start | bytes 393224 | tf_op jit(solution)/shard_map/while/body/eval_jaxpr/ppermute | solution.py:102
  9.0 9.0 %collective-permute-start.1 = (bf16[256,256]{1,0:T(8,128)(2,1)S(1)}, bf16[256,256]{1,0:T(8,128)(2,1)S(1)}, u32[]{:S(2)}, u32[]{:S(2)}) collective-permute-start(bf16[256,256]{1,0:T(8,128)(2,1)S(1)} %get-tuple-element.67), channel_id=1, source_target_pairs={{0,1},{1,2},{2,3},{3,4},{4,5},{5,6},{6,7},{7,8},{8,9},{9,10},{10,1... | collective-permute-start | bytes 393224 | tf_op jit(solution)/shard_map/while/body/eval_jaxpr/ppermute | solution.py:101
  20.5 13.9 %collective-permute-start.2 = (bf16[1024,256]{1,0:T(8,128)(2,1)S(1)}, bf16[1024,256]{1,0:T(8,128)(2,1)S(1)}, u32[]{:S(2)}, u32[]{:S(2)}) collective-permute-start(bf16[1024,256]{1,0:T(8,128)(2,1)S(1)} %bitcast.49), channel_id=1, source_target_pairs={{0,32},{32,64},{64,96},{96,128},{128,160},{160,192},{192,224},{224... | collective-permute-start | bytes 1572872 | tf_op jit(solution)/shard_map/while/body/eval_jaxpr/ppermute | solution.py:110
  34.4 6.9 %collective-permute-start = (bf16[256,256]{1,0:T(8,128)(2,1)S(1)}, bf16[256,256]{1,0:T(8,128)(2,1)S(1)}, u32[]{:S(2)}, u32[]{:S(2)}) collective-permute-start(bf16[256,256]{1,0:T(8,128)(2,1)S(1)} %get-tuple-element.66), channel_id=1, source_target_pairs={{1,0},{2,1},{3,2},{4,3},{5,4},{6,5},{7,6},{8,7},{9,8},{10,9},{11,1... | collective-permute-start | bytes 393224 | tf_op jit(solution)/shard_map/while/body/eval_jaxpr/ppermute | solution.py:102
  36.4 9.0 %collective-permute-start.1 = (bf16[256,256]{1,0:T(8,128)(2,1)S(1)}, bf16[256,256]{1,0:T(8,128)(2,1)S(1)}, u32[]{:S(2)}, u32[]{:S(2)}) collective-permute-start(bf16[256,256]{1,0:T(8,128)(2,1)S(1)} %get-tuple-element.67), channel_id=1, source_target_pairs={{0,1},{1,2},{2,3},{3,4},{4,5},{5,6},{6,7},{7,8},{8,9},{9,10},{10,1... | collective-permute-start | bytes 393224 | tf_op jit(solution)/shard_map/while/body/eval_jaxpr/ppermute | solution.py:101
  47.8 9.8 %collective-permute-start.2 = (bf16[1024,256]{1,0:T(8,128)(2,1)S(1)}, bf16[1024,256]{1,0:T(8,128)(2,1)S(1)}, u32[]{:S(2)}, u32[]{:S(2)}) collective-permute-start(bf16[1024,256]{1,0:T(8,128)(2,1)S(1)} %bitcast.49), channel_id=1, source_target_pairs={{0,32},{32,64},{64,96},{96,128},{128,160},{160,192},{192,224},{224... | collective-permute-start | bytes 1572872 | tf_op jit(solution)/shard_map/while/body/eval_jaxpr/ppermute | solution.py:110
  57.7 6.9 %collective-permute-start = (bf16[256,256]{1,0:T(8,128)(2,1)S(1)}, bf16[256,256]{1,0:T(8,128)(2,1)S(1)}, u32[]{:S(2)}, u32[]{:S(2)}) collective-permute-start(bf16[256,256]{1,0:T(8,128)(2,1)S(1)} %get-tuple-element.66), channel_id=1, source_target_pairs={{1,0},{2,1},{3,2},{4,3},{5,4},{6,5},{7,6},{8,7},{9,8},{10,9},{11,1... | collective-permute-start | bytes 393224 | tf_op jit(solution)/shard_map/while/body/eval_jaxpr/ppermute | solution.py:102
  59.7 9.3 %collective-permute-start.1 = (bf16[256,256]{1,0:T(8,128)(2,1)S(1)}, bf16[256,256]{1,0:T(8,128)(2,1)S(1)}, u32[]{:S(2)}, u32[]{:S(2)}) collective-permute-start(bf16[256,256]{1,0:T(8,128)(2,1)S(1)} %get-tuple-element.67), channel_id=1, source_target_pairs={{0,1},{1,2},{2,3},{3,4},{4,5},{5,6},{6,7},{7,8},{8,9},{9,10},{10,1... | collective-permute-start | bytes 393224 | tf_op jit(solution)/shard_map/while/body/eval_jaxpr/ppermute | solution.py:101
  71.6 9.8 %collective-permute-start.2 = (bf16[1024,256]{1,0:T(8,128)(2,1)S(1)}, bf16[1024,256]{1,0:T(8,128)(2,1)S(1)}, u32[]{:S(2)}, u32[]{:S(2)}) collective-permute-start(bf16[1024,256]{1,0:T(8,128)(2,1)S(1)} %bitcast.49), channel_id=1, source_target_pairs={{0,32},{32,64},{64,96},{96,128},{128,160},{160,192},{192,224},{224... | collective-permute-start | bytes 1572872 | tf_op jit(solution)/shard_map/while/body/eval_jaxpr/ppermute | solution.py:110
  81.4 6.9 %collective-permute-start = (bf16[256,256]{1,0:T(8,128)(2,1)S(1)}, bf16[256,256]{1,0:T(8,128)(2,1)S(1)}, u32[]{:S(2)}, u32[]{:S(2)}) collective-permute-start(bf16[256,256]{1,0:T(8,128)(2,1)S(1)} %get-tuple-element.66), channel_id=1, source_target_pairs={{1,0},{2,1},{3,2},{4,3},{5,4},{6,5},{7,6},{8,7},{9,8},{10,9},{11,1... | collective-permute-start | bytes 393224 | tf_op jit(solution)/shard_map/while/body/eval_jaxpr/ppermute | solution.py:102
  85.3 9.0 %collective-permute-start.1 = (bf16[256,256]{1,0:T(8,128)(2,1)S(1)}, bf16[256,256]{1,0:T(8,128)(2,1)S(1)}, u32[]{:S(2)}, u32[]{:S(2)}) collective-permute-start(bf16[256,256]{1,0:T(8,128)(2,1)S(1)} %get-tuple-element.67), channel_id=1, source_target_pairs={{0,1},{1,2},{2,3},{3,4},{4,5},{5,6},{6,7},{7,8},{8,9},{9,10},{10,1... | collective-permute-start | bytes 393224 | tf_op jit(solution)/shard_map/while/body/eval_jaxpr/ppermute | solution.py:101
  96.8 9.8 %collective-permute-start.2 = (bf16[1024,256]{1,0:T(8,128)(2,1)S(1)}, bf16[1024,256]{1,0:T(8,128)(2,1)S(1)}, u32[]{:S(2)}, u32[]{:S(2)}) collective-permute-start(bf16[1024,256]{1,0:T(8,128)(2,1)S(1)} %bitcast.49), channel_id=1, source_target_pairs={{0,32},{32,64},{64,96},{96,128},{128,160},{160,192},{192,224},{224... | collective-permute-start | bytes 1572872 | tf_op jit(solution)/shard_map/while/body/eval_jaxpr/ppermute | solution.py:110
  106.6 6.9 %collective-permute-start = (bf16[256,256]{1,0:T(8,128)(2,1)S(1)}, bf16[256,256]{1,0:T(8,128)(2,1)S(1)}, u32[]{:S(2)}, u32[]{:S(2)}) collective-permute-start(bf16[256,256]{1,0:T(8,128)(2,1)S(1)} %get-tuple-element.66), channel_id=1, source_target_pairs={{1,0},{2,1},{3,2},{4,3},{5,4},{6,5},{7,6},{8,7},{9,8},{10,9},{11,1... | collective-permute-start | bytes 393224 | tf_op jit(solution)/shard_map/while/body/eval_jaxpr/ppermute | solution.py:102
  109.8 9.0 %collective-permute-start.1 = (bf16[256,256]{1,0:T(8,128)(2,1)S(1)}, bf16[256,256]{1,0:T(8,128)(2,1)S(1)}, u32[]{:S(2)}, u32[]{:S(2)}) collective-permute-start(bf16[256,256]{1,0:T(8,128)(2,1)S(1)} %get-tuple-element.67), channel_id=1, source_target_pairs={{0,1},{1,2},{2,3},{3,4},{4,5},{5,6},{6,7},{7,8},{8,9},{9,10},{10,1... | collective-permute-start | bytes 393224 | tf_op jit(solution)/shard_map/while/body/eval_jaxpr/ppermute | solution.py:101
  121.3 9.8 %collective-permute-start.2 = (bf16[1024,256]{1,0:T(8,128)(2,1)S(1)}, bf16[1024,256]{1,0:T(8,128)(2,1)S(1)}, u32[]{:S(2)}, u32[]{:S(2)}) collective-permute-start(bf16[1024,256]{1,0:T(8,128)(2,1)S(1)} %bitcast.49), channel_id=1, source_target_pairs={{0,32},{32,64},{64,96},{96,128},{128,160},{160,192},{192,224},{224... | collective-permute-start | bytes 1572872 | tf_op jit(solution)/shard_map/while/body/eval_jaxpr/ppermute | solution.py:110
  131.1 6.9 %collective-permute-start = (bf16[256,256]{1,0:T(8,128)(2,1)S(1)}, bf16[256,256]{1,0:T(8,128)(2,1)S(1)}, u32[]{:S(2)}, u32[]{:S(2)}) collective-permute-start(bf16[256,256]{1,0:T(8,128)(2,1)S(1)} %get-tuple-element.66), channel_id=1, source_target_pairs={{1,0},{2,1},{3,2},{4,3},{5,4},{6,5},{7,6},{8,7},{9,8},{10,9},{11,1... | collective-permute-start | bytes 393224 | tf_op jit(solution)/shard_map/while/body/eval_jaxpr/ppermute | solution.py:102
  134.2 9.0 %collective-permute-start.1 = (bf16[256,256]{1,0:T(8,128)(2,1)S(1)}, bf16[256,256]{1,0:T(8,128)(2,1)S(1)}, u32[]{:S(2)}, u32[]{:S(2)}) collective-permute-start(bf16[256,256]{1,0:T(8,128)(2,1)S(1)} %get-tuple-element.67), channel_id=1, source_target_pairs={{0,1},{1,2},{2,3},{3,4},{4,5},{5,6},{6,7},{7,8},{8,9},{9,10},{10,1... | collective-permute-start | bytes 393224 | tf_op jit(solution)/shard_map/while/body/eval_jaxpr/ppermute | solution.py:101
  145.7 9.8 %collective-permute-start.2 = (bf16[1024,256]{1,0:T(8,128)(2,1)S(1)}, bf16[1024,256]{1,0:T(8,128)(2,1)S(1)}, u32[]{:S(2)}, u32[]{:S(2)}) collective-permute-start(bf16[1024,256]{1,0:T(8,128)(2,1)S(1)} %bitcast.49), channel_id=1, source_target_pairs={{0,32},{32,64},{64,96},{96,128},{128,160},{160,192},{192,224},{224... | collective-permute-start | bytes 1572872 | tf_op jit(solution)/shard_map/while/body/eval_jaxpr/ppermute | solution.py:110
  155.5 6.9 %collective-permute-start = (bf16[256,256]{1,0:T(8,128)(2,1)S(1)}, bf16[256,256]{1,0:T(8,128)(2,1)S(1)}, u32[]{:S(2)}, u32[]{:S(2)}) collective-permute-start(bf16[256,256]{1,0:T(8,128)(2,1)S(1)} %get-tuple-element.66), channel_id=1, source_target_pairs={{1,0},{2,1},{3,2},{4,3},{5,4},{6,5},{7,6},{8,7},{9,8},{10,9},{11,1... | collective-permute-start | bytes 393224 | tf_op jit(solution)/shard_map/while/body/eval_jaxpr/ppermute | solution.py:102
  158.7 9.0 %collective-permute-start.1 = (bf16[256,256]{1,0:T(8,128)(2,1)S(1)}, bf16[256,256]{1,0:T(8,128)(2,1)S(1)}, u32[]{:S(2)}, u32[]{:S(2)}) collective-permute-start(bf16[256,256]{1,0:T(8,128)(2,1)S(1)} %get-tuple-element.67), channel_id=1, source_target_pairs={{0,1},{1,2},{2,3},{3,4},{4,5},{5,6},{6,7},{7,8},{8,9},{9,10},{10,1... | collective-permute-start | bytes 393224 | tf_op jit(solution)/shard_map/while/body/eval_jaxpr/ppermute | solution.py:101
  170.1 9.8 %collective-permute-start.2 = (bf16[1024,256]{1,0:T(8,128)(2,1)S(1)}, bf16[1024,256]{1,0:T(8,128)(2,1)S(1)}, u32[]{:S(2)}, u32[]{:S(2)}) collective-permute-start(bf16[1024,256]{1,0:T(8,128)(2,1)S(1)} %bitcast.49), channel_id=1, source_target_pairs={{0,32},{32,64},{64,96},{96,128},{128,160},{160,192},{192,224},{224... | collective-permute-start | bytes 1572872 | tf_op jit(solution)/shard_map/while/body/eval_jaxpr/ppermute | solution.py:110
  180.0 6.9 %collective-permute-start = (bf16[256,256]{1,0:T(8,128)(2,1)S(1)}, bf16[256,256]{1,0:T(8,128)(2,1)S(1)}, u32[]{:S(2)}, u32[]{:S(2)}) collective-permute-start(bf16[256,256]{1,0:T(8,128)(2,1)S(1)} %get-tuple-element.66), channel_id=1, source_target_pairs={{1,0},{2,1},{3,2},{4,3},{5,4},{6,5},{7,6},{8,7},{9,8},{10,9},{11,1... | collective-permute-start | bytes 393224 | tf_op jit(solution)/shard_map/while/body/eval_jaxpr/ppermute | solution.py:102
  183.1 9.0 %collective-permute-start.1 = (bf16[256,256]{1,0:T(8,128)(2,1)S(1)}, bf16[256,256]{1,0:T(8,128)(2,1)S(1)}, u32[]{:S(2)}, u32[]{:S(2)}) collective-permute-start(bf16[256,256]{1,0:T(8,128)(2,1)S(1)} %get-tuple-element.67), channel_id=1, source_target_pairs={{0,1},{1,2},{2,3},{3,4},{4,5},{5,6},{6,7},{7,8},{8,9},{9,10},{10,1... | collective-permute-start | bytes 393224 | tf_op jit(solution)/shard_map/while/body/eval_jaxpr/ppermute | solution.py:101
  194.6 9.8 %collective-permute-start.2 = (bf16[1024,256]{1,0:T(8,128)(2,1)S(1)}, bf16[1024,256]{1,0:T(8,128)(2,1)S(1)}, u32[]{:S(2)}, u32[]{:S(2)}) collective-permute-start(bf16[1024,256]{1,0:T(8,128)(2,1)S(1)} %bitcast.49), channel_id=1, source_target_pairs={{0,32},{32,64},{64,96},{96,128},{128,160},{160,192},{192,224},{224... | collective-permute-start | bytes 1572872 | tf_op jit(solution)/shard_map/while/body/eval_jaxpr/ppermute | solution.py:110
  204.4 6.9 %collective-permute-start = (bf16[256,256]{1,0:T(8,128)(2,1)S(1)}, bf16[256,256]{1,0:T(8,128)(2,1)S(1)}, u32[]{:S(2)}, u32[]{:S(2)}) collective-permute-start(bf16[256,256]{1,0:T(8,128)(2,1)S(1)} %get-tuple-element.66), channel_id=1, source_target_pairs={{1,0},{2,1},{3,2},{4,3},{5,4},{6,5},{7,6},{8,7},{9,8},{10,9},{11,1... | collective-permute-start | bytes 393224 | tf_op jit(solution)/shard_map/while/body/eval_jaxpr/ppermute | solution.py:102
  207.6 9.0 %collective-permute-start.1 = (bf16[256,256]{1,0:T(8,128)(2,1)S(1)}, bf16[256,256]{1,0:T(8,128)(2,1)S(1)}, u32[]{:S(2)}, u32[]{:S(2)}) collective-permute-start(bf16[256,256]{1,0:T(8,128)(2,1)S(1)} %get-tuple-element.67), channel_id=1, source_target_pairs={{0,1},{1,2},{2,3},{3,4},{4,5},{5,6},{6,7},{7,8},{8,9},{9,10},{10,1... | collective-permute-start | bytes 393224 | tf_op jit(solution)/shard_map/while/body/eval_jaxpr/ppermute | solution.py:101
  219.0 9.8 %collective-permute-start.2 = (bf16[1024,256]{1,0:T(8,128)(2,1)S(1)}, bf16[1024,256]{1,0:T(8,128)(2,1)S(1)}, u32[]{:S(2)}, u32[]{:S(2)}) collective-permute-start(bf16[1024,256]{1,0:T(8,128)(2,1)S(1)} %bitcast.49), channel_id=1, source_target_pairs={{0,32},{32,64},{64,96},{96,128},{128,160},{160,192},{192,224},{224... | collective-permute-start | bytes 1572872 | tf_op jit(solution)/shard_map/while/body/eval_jaxpr/ppermute | solution.py:110
  228.9 6.9 %collective-permute-start = (bf16[256,256]{1,0:T(8,128)(2,1)S(1)}, bf16[256,256]{1,0:T(8,128)(2,1)S(1)}, u32[]{:S(2)}, u32[]{:S(2)}) collective-permute-start(bf16[256,256]{1,0:T(8,128)(2,1)S(1)} %get-tuple-element.66), channel_id=1, source_target_pairs={{1,0},{2,1},{3,2},{4,3},{5,4},{6,5},{7,6},{8,7},{9,8},{10,9},{11,1... | collective-permute-start | bytes 393224 | tf_op jit(solution)/shard_map/while/body/eval_jaxpr/ppermute | solution.py:102
  232.0 9.0 %collective-permute-start.1 = (bf16[256,256]{1,0:T(8,128)(2,1)S(1)}, bf16[256,256]{1,0:T(8,128)(2,1)S(1)}, u32[]{:S(2)}, u32[]{:S(2)}) collective-permute-start(bf16[256,256]{1,0:T(8,128)(2,1)S(1)} %get-tuple-element.67), channel_id=1, source_target_pairs={{0,1},{1,2},{2,3},{3,4},{4,5},{5,6},{6,7},{7,8},{8,9},{9,10},{10,1... | collective-permute-start | bytes 393224 | tf_op jit(solution)/shard_map/while/body/eval_jaxpr/ppermute | solution.py:101
  243.5 9.8 %collective-permute-start.2 = (bf16[1024,256]{1,0:T(8,128)(2,1)S(1)}, bf16[1024,256]{1,0:T(8,128)(2,1)S(1)}, u32[]{:S(2)}, u32[]{:S(2)}) collective-permute-start(bf16[1024,256]{1,0:T(8,128)(2,1)S(1)} %bitcast.49), channel_id=1, source_target_pairs={{0,32},{32,64},{64,96},{96,128},{128,160},{160,192},{192,224},{224... | collective-permute-start | bytes 1572872 | tf_op jit(solution)/shard_map/while/body/eval_jaxpr/ppermute | solution.py:110
  253.3 6.9 %collective-permute-start = (bf16[256,256]{1,0:T(8,128)(2,1)S(1)}, bf16[256,256]{1,0:T(8,128)(2,1)S(1)}, u32[]{:S(2)}, u32[]{:S(2)}) collective-permute-start(bf16[256,256]{1,0:T(8,128)(2,1)S(1)} %get-tuple-element.66), channel_id=1, source_target_pairs={{1,0},{2,1},{3,2},{4,3},{5,4},{6,5},{7,6},{8,7},{9,8},{10,9},{11,1... | collective-permute-start | bytes 393224 | tf_op jit(solution)/shard_map/while/body/eval_jaxpr/ppermute | solution.py:102
  256.4 9.0 %collective-permute-start.1 = (bf16[256,256]{1,0:T(8,128)(2,1)S(1)}, bf16[256,256]{1,0:T(8,128)(2,1)S(1)}, u32[]{:S(2)}, u32[]{:S(2)}) collective-permute-start(bf16[256,256]{1,0:T(8,128)(2,1)S(1)} %get-tuple-element.67), channel_id=1, source_target_pairs={{0,1},{1,2},{2,3},{3,4},{4,5},{5,6},{6,7},{7,8},{8,9},{9,10},{10,1... | collective-permute-start | bytes 393224 | tf_op jit(solution)/shard_map/while/body/eval_jaxpr/ppermute | solution.py:101
  267.9 9.8 %collective-permute-start.2 = (bf16[1024,256]{1,0:T(8,128)(2,1)S(1)}, bf16[1024,256]{1,0:T(8,128)(2,1)S(1)}, u32[]{:S(2)}, u32[]{:S(2)}) collective-permute-start(bf16[1024,256]{1,0:T(8,128)(2,1)S(1)} %bitcast.49), channel_id=1, source_target_pairs={{0,32},{32,64},{64,96},{96,128},{128,160},{160,192},{192,224},{224... | collective-permute-start | bytes 1572872 | tf_op jit(solution)/shard_map/while/body/eval_jaxpr/ppermute | solution.py:110
  277.7 6.9 %collective-permute-start = (bf16[256,256]{1,0:T(8,128)(2,1)S(1)}, bf16[256,256]{1,0:T(8,128)(2,1)S(1)}, u32[]{:S(2)}, u32[]{:S(2)}) collective-permute-start(bf16[256,256]{1,0:T(8,128)(2,1)S(1)} %get-tuple-element.66), channel_id=1, source_target_pairs={{1,0},{2,1},{3,2},{4,3},{5,4},{6,5},{7,6},{8,7},{9,8},{10,9},{11,1... | collective-permute-start | bytes 393224 | tf_op jit(solution)/shard_map/while/body/eval_jaxpr/ppermute | solution.py:102
  280.9 9.0 %collective-permute-start.1 = (bf16[256,256]{1,0:T(8,128)(2,1)S(1)}, bf16[256,256]{1,0:T(8,128)(2,1)S(1)}, u32[]{:S(2)}, u32[]{:S(2)}) collective-permute-start(bf16[256,256]{1,0:T(8,128)(2,1)S(1)} %get-tuple-element.67), channel_id=1, source_target_pairs={{0,1},{1,2},{2,3},{3,4},{4,5},{5,6},{6,7},{7,8},{8,9},{9,10},{10,1... | collective-permute-start | bytes 393224 | tf_op jit(solution)/shard_map/while/body/eval_jaxpr/ppermute | solution.py:101
  292.3 9.8 %collective-permute-start.2 = (bf16[1024,256]{1,0:T(8,128)(2,1)S(1)}, bf16[1024,256]{1,0:T(8,128)(2,1)S(1)}, u32[]{:S(2)}, u32[]{:S(2)}) collective-permute-start(bf16[1024,256]{1,0:T(8,128)(2,1)S(1)} %bitcast.49), channel_id=1, source_target_pairs={{0,32},{32,64},{64,96},{96,128},{128,160},{160,192},{192,224},{224... | collective-permute-start | bytes 1572872 | tf_op jit(solution)/shard_map/while/body/eval_jaxpr/ppermute | solution.py:110
  302.2 6.9 %collective-permute-start = (bf16[256,256]{1,0:T(8,128)(2,1)S(1)}, bf16[256,256]{1,0:T(8,128)(2,1)S(1)}, u32[]{:S(2)}, u32[]{:S(2)}) collective-permute-start(bf16[256,256]{1,0:T(8,128)(2,1)S(1)} %get-tuple-element.66), channel_id=1, source_target_pairs={{1,0},{2,1},{3,2},{4,3},{5,4},{6,5},{7,6},{8,7},{9,8},{10,9},{11,1... | collective-permute-start | bytes 393224 | tf_op jit(solution)/shard_map/while/body/eval_jaxpr/ppermute | solution.py:102
  305.3 9.0 %collective-permute-start.1 = (bf16[256,256]{1,0:T(8,128)(2,1)S(1)}, bf16[256,256]{1,0:T(8,128)(2,1)S(1)}, u32[]{:S(2)}, u32[]{:S(2)}) collective-permute-start(bf16[256,256]{1,0:T(8,128)(2,1)S(1)} %get-tuple-element.67), channel_id=1, source_target_pairs={{0,1},{1,2},{2,3},{3,4},{4,5},{5,6},{6,7},{7,8},{8,9},{9,10},{10,1... | collective-permute-start | bytes 393224 | tf_op jit(solution)/shard_map/while/body/eval_jaxpr/ppermute | solution.py:101
  316.8 9.8 %collective-permute-start.2 = (bf16[1024,256]{1,0:T(8,128)(2,1)S(1)}, bf16[1024,256]{1,0:T(8,128)(2,1)S(1)}, u32[]{:S(2)}, u32[]{:S(2)}) collective-permute-start(bf16[1024,256]{1,0:T(8,128)(2,1)S(1)} %bitcast.49), channel_id=1, source_target_pairs={{0,32},{32,64},{64,96},{96,128},{128,160},{160,192},{192,224},{224... | collective-permute-start | bytes 1572872 | tf_op jit(solution)/shard_map/while/body/eval_jaxpr/ppermute | solution.py:110
  326.6 6.9 %collective-permute-start = (bf16[256,256]{1,0:T(8,128)(2,1)S(1)}, bf16[256,256]{1,0:T(8,128)(2,1)S(1)}, u32[]{:S(2)}, u32[]{:S(2)}) collective-permute-start(bf16[256,256]{1,0:T(8,128)(2,1)S(1)} %get-tuple-element.66), channel_id=1, source_target_pairs={{1,0},{2,1},{3,2},{4,3},{5,4},{6,5},{7,6},{8,7},{9,8},{10,9},{11,1... | collective-permute-start | bytes 393224 | tf_op jit(solution)/shard_map/while/body/eval_jaxpr/ppermute | solution.py:102
  329.8 9.0 %collective-permute-start.1 = (bf16[256,256]{1,0:T(8,128)(2,1)S(1)}, bf16[256,256]{1,0:T(8,128)(2,1)S(1)}, u32[]{:S(2)}, u32[]{:S(2)}) collective-permute-start(bf16[256,256]{1,0:T(8,128)(2,1)S(1)} %get-tuple-element.67), channel_id=1, source_target_pairs={{0,1},{1,2},{2,3},{3,4},{4,5},{5,6},{6,7},{7,8},{8,9},{9,10},{10,1... | collective-permute-start | bytes 393224 | tf_op jit(solution)/shard_map/while/body/eval_jaxpr/ppermute | solution.py:101
  341.2 9.8 %collective-permute-start.2 = (bf16[1024,256]{1,0:T(8,128)(2,1)S(1)}, bf16[1024,256]{1,0:T(8,128)(2,1)S(1)}, u32[]{:S(2)}, u32[]{:S(2)}) collective-permute-start(bf16[1024,256]{1,0:T(8,128)(2,1)S(1)} %bitcast.49), channel_id=1, source_target_pairs={{0,32},{32,64},{64,96},{96,128},{128,160},{160,192},{192,224},{224... | collective-permute-start | bytes 1572872 | tf_op jit(solution)/shard_map/while/body/eval_jaxpr/ppermute | solution.py:110
  351.1 6.9 %collective-permute-start = (bf16[256,256]{1,0:T(8,128)(2,1)S(1)}, bf16[256,256]{1,0:T(8,128)(2,1)S(1)}, u32[]{:S(2)}, u32[]{:S(2)}) collective-permute-start(bf16[256,256]{1,0:T(8,128)(2,1)S(1)} %get-tuple-element.66), channel_id=1, source_target_pairs={{1,0},{2,1},{3,2},{4,3},{5,4},{6,5},{7,6},{8,7},{9,8},{10,9},{11,1... | collective-permute-start | bytes 393224 | tf_op jit(solution)/shard_map/while/body/eval_jaxpr/ppermute | solution.py:102
  354.2 9.0 %collective-permute-start.1 = (bf16[256,256]{1,0:T(8,128)(2,1)S(1)}, bf16[256,256]{1,0:T(8,128)(2,1)S(1)}, u32[]{:S(2)}, u32[]{:S(2)}) collective-permute-start(bf16[256,256]{1,0:T(8,128)(2,1)S(1)} %get-tuple-element.67), channel_id=1, source_target_pairs={{0,1},{1,2},{2,3},{3,4},{4,5},{5,6},{6,7},{7,8},{8,9},{9,10},{10,1... | collective-permute-start | bytes 393224 | tf_op jit(solution)/shard_map/while/body/eval_jaxpr/ppermute | solution.py:101
  365.7 9.8 %collective-permute-start.2 = (bf16[1024,256]{1,0:T(8,128)(2,1)S(1)}, bf16[1024,256]{1,0:T(8,128)(2,1)S(1)}, u32[]{:S(2)}, u32[]{:S(2)}) collective-permute-start(bf16[1024,256]{1,0:T(8,128)(2,1)S(1)} %bitcast.49), channel_id=1, source_target_pairs={{0,32},{32,64},{64,96},{96,128},{128,160},{160,192},{192,224},{224... | collective-permute-start | bytes 1572872 | tf_op jit(solution)/shard_map/while/body/eval_jaxpr/ppermute | solution.py:110
  375.5 6.9 %collective-permute-start = (bf16[256,256]{1,0:T(8,128)(2,1)S(1)}, bf16[256,256]{1,0:T(8,128)(2,1)S(1)}, u32[]{:S(2)}, u32[]{:S(2)}) collective-permute-start(bf16[256,256]{1,0:T(8,128)(2,1)S(1)} %get-tuple-element.66), channel_id=1, source_target_pairs={{1,0},{2,1},{3,2},{4,3},{5,4},{6,5},{7,6},{8,7},{9,8},{10,9},{11,1... | collective-permute-start | bytes 393224 | tf_op jit(solution)/shard_map/while/body/eval_jaxpr/ppermute | solution.py:102
  378.7 9.0 %collective-permute-start.1 = (bf16[256,256]{1,0:T(8,128)(2,1)S(1)}, bf16[256,256]{1,0:T(8,128)(2,1)S(1)}, u32[]{:S(2)}, u32[]{:S(2)}) collective-permute-start(bf16[256,256]{1,0:T(8,128)(2,1)S(1)} %get-tuple-element.67), channel_id=1, source_target_pairs={{0,1},{1,2},{2,3},{3,4},{4,5},{5,6},{6,7},{7,8},{8,9},{9,10},{10,1... | collective-permute-start | bytes 393224 | tf_op jit(solution)/shard_map/while/body/eval_jaxpr/ppermute | solution.py:101
  390.1 9.8 %collective-permute-start.2 = (bf16[1024,256]{1,0:T(8,128)(2,1)S(1)}, bf16[1024,256]{1,0:T(8,128)(2,1)S(1)}, u32[]{:S(2)}, u32[]{:S(2)}) collective-permute-start(bf16[1024,256]{1,0:T(8,128)(2,1)S(1)} %bitcast.49), channel_id=1, source_target_pairs={{0,32},{32,64},{64,96},{96,128},{128,160},{160,192},{192,224},{224... | collective-permute-start | bytes 1572872 | tf_op jit(solution)/shard_map/while/body/eval_jaxpr/ppermute | solution.py:110
  (1 other events, 3.8 us)

commit v2 on v1

--- a/solution.py
+++ b/solution.py
@@ -6,6 +6,79 @@
 from jax.sharding import PartitionSpec as P
 
 HB = 2
+TILE = 128
+HALF = 4 * TILE
+OPS = 16 * TILE
+DEAD = 7
+
+def visit_kernel(cur, ra, rb, first, second, out, wide, mid):
+    for n in range(4):
+        wide[(3 - n) * TILE : (4 - n) * TILE, :] = ra[n * TILE : (n + 1) * TILE, :]
+        wide[(15 - n) * TILE : (16 - n) * TILE, :] = rb[n * TILE : (n + 1) * TILE, :]
+    wide[4 * TILE : 12 * TILE, :] = cur[...]
+    zero = jnp.zeros((TILE, cur.shape[1]), cur.dtype)
+    wide[16 * TILE :, :] = zero
+    mid[12 * TILE :, :] = zero
+
+    def table_of(ref, start, count):
+        return ref[start : start + count, :TILE].astype(jnp.float32).astype(jnp.int32)
+
+    def row(ops, base, table, line, source, centre, sign, nothing):
+        def block(j):
+            if j == 0:
+                return source[centre * TILE : (centre + 1) * TILE, :]
+            value = jnp.max(table[line + j : line + j + 1, :])
+            place = jnp.where(value == DEAD, nothing, centre + sign * (value - 2))
+            return source[pl.ds(pl.multiple_of(place * TILE, TILE), TILE), :]
+
+        total = None
+        for pair in range(2):
+            left = ops[base + pair * TILE : base + (pair + 1) * TILE, :]
+            right = jnp.concatenate([block(2 * pair), block(2 * pair + 1)], axis=0)
+            part = jnp.dot(left, right, preferred_element_type=jnp.float32)
+            total = part if total is None else total + part
+        return total.astype(out.dtype)
+
+    near_a = table_of(ra, 2 * HALF, 16)
+    near_b = table_of(rb, 2 * HALF, 16)
+    own = table_of(first, OPS, 64)
+    for n in range(2):
+        c = -1 - n
+        mid[(c + 2) * TILE : (c + 3) * TILE, :] = row(
+            ra, HALF + n * 2 * TILE, near_a, n * 8, wide, c + 4, -1, 16
+        )
+        c = 9 - n
+        mid[(c + 2) * TILE : (c + 3) * TILE, :] = row(
+            rb, HALF + n * 2 * TILE, near_b, n * 8, wide, c + 4, -1, 16
+        )
+    for c in range(8):
+        mid[(c + 2) * TILE : (c + 3) * TILE, :] = row(
+            first, c * 2 * TILE, own, c * 8, wide, c + 4, 1, 16
+        )
+    other = table_of(second, OPS, 64)
+    for c in range(8):
+        out[c * TILE : (c + 1) * TILE, :] = row(
+            second, c * 2 * TILE, other, c * 8, mid, c + 2, 1, 12
+        )
+
+def visit(cur, ra, rb, first, second):
+    vmem = pl.BlockSpec(memory_space=pltpu.VMEM)
+    columns = cur.shape[1]
+    return pl.pallas_call(
+        visit_kernel,
+        out_shape=jax.ShapeDtypeStruct(cur.shape, cur.dtype),
+        in_specs=[vmem] * 5,
+        out_specs=vmem,
+        scratch_shapes=[
+            pltpu.VMEM((17 * TILE, columns), cur.dtype),
+            pltpu.VMEM((13 * TILE, columns), cur.dtype),
+        ],
+        compiler_params=pltpu.CompilerParams(vmem_limit_bytes=24 * 1024 * 1024),
+        cost_estimate=pl.CostEstimate(flops=700_000_000, bytes_accessed=4_000_000, transcendentals=0),
+        name="two_steps",
+    )(cur, ra, rb, first, second)
+
+
 NB = 16
 
 def factor_kernel(gram_ref, arrived_ref, basis_ref, factor_ref, a_ref, w_ref):
@@ -91,54 +164,59 @@
     return lax.all_to_all(copies, "rows", 0, 0, tiled=True).reshape(size, size)
 
 
-def with_halo(array, sides, width):
-    for axis, dim in sides:
-        peers, length = (lax.axis_size(axis), array.shape[dim])
-        up = [(i, (i + 1) % peers) for i in range(peers)]
-        down = [(j, i) for i, j in up]
-        last = lax.slice_in_dim(array, length - width, length, axis=dim)
-        leading = lax.slice_in_dim(array, 0, width, axis=dim)
-        before = lax.ppermute(last, axis, up)
-        after = lax.ppermute(leading, axis, down)
-        array = jnp.concatenate([before, array, after], axis=dim)
-    return array
-
-
-def passed_along(value, axis, steps):
-    count = lax.axis_size(axis)
-    pairs = [(source, (source + steps) % count) for source in range(count)]
-    return lax.ppermute(value, axis, pairs)
+def packed_operator(blocks, cols, counts, even):
+    block_rows, slots, tile, unused = blocks.shape
+    owners = lax.axis_size("rows")
+    total = block_rows * owners
+    index = lax.axis_index("rows") * block_rows + jnp.arange(block_rows, dtype=jnp.int32)
+    offset = jnp.mod(cols - index[:, None] + HB, total) - HB
+    offset = jnp.where(even, -offset, offset) + HB
+    live = jnp.arange(slots, dtype=jnp.int32)[None, :] < counts[:, None]
+    place = jnp.where(live, offset, DEAD)
+    place = jnp.where(even, place[::-1], place)
+    place = jnp.pad(place, ((0, 0), (0, 8 - slots)), constant_values=DEAD)
+    table = jnp.broadcast_to(
+        place.reshape(block_rows * 8, 1).astype(jnp.bfloat16), (block_rows * 8, 2 * tile)
+    )
+    paired = blocks.reshape(block_rows, 2, 2, tile, tile).transpose(0, 1, 3, 2, 4)
+    paired = jnp.where(even, paired[::-1], paired)
+    return jnp.concatenate([paired.reshape(block_rows * 2 * tile, 2 * tile), table], axis=0)
 
 
 def body(start, blocks, cols, counts):
-    block_rows = blocks.shape[1]
-    slot_count = blocks.shape[2]
-    tile_size = blocks.shape[3]
+    tile = blocks.shape[3]
     rows_here = start.shape[1]
+    columns = start.shape[2]
     owners = lax.axis_size("rows")
     sections = lax.axis_size("phase")
-    total_blocks = block_rows * owners
-    first_block = lax.axis_index("rows") * block_rows
-    local_index = jnp.mod(cols[0] - first_block + HB, total_blocks)
-    live_slots = jnp.arange(slot_count, dtype=jnp.int32)[None, :] < counts[0][:, None]
-    zero_value = jnp.zeros((), jnp.bfloat16)
-    kept_blocks = jnp.where(live_slots[:, :, None, None], blocks[0], zero_value)
-    rim_rows = HB * tile_size
-
-    def advance(current):
-        columns = current.shape[1]
-        extended = with_halo(current, (("rows", 0),), rim_rows)
-        row_tiles = extended.reshape(block_rows + 2 * HB, tile_size, columns)
-        picked = row_tiles[local_index]
-        product = jnp.einsum(
-            "ijab,ijbk->iak", kept_blocks, picked, preferred_element_type=jnp.float32
-        )
-        return product.reshape(rows_here, columns).astype(jnp.bfloat16)
-
-    def turn_one(turn_index, current):
-        return passed_along(advance(current), "phase", 1)
-
-    arrived = lax.fori_loop(0, sections, turn_one, start[0])
+    even = lax.axis_index("rows") % 2 == 0
+    first_core = lax.axis_index("phase") % 2 == 0
+    to_a = [(i, i ^ 1) for i in range(owners)]
+    to_b = [(i, (i + 1) % owners if i % 2 else (i - 1) % owners) for i in range(owners)]
+    back = [(i, (i - 2) % sections) for i in range(sections)]
+    mates = [(i, i ^ 1) for i in range(sections)]
+
+    def mirrored(rows):
+        tiles = rows.reshape(rows_here // tile, tile, columns)
+        return jnp.where(even, tiles[::-1], tiles).reshape(rows_here, columns)
+
+    travel = mirrored(start[0])
+    home = packed_operator(blocks[0], cols[0], counts[0], even)
+    here, ahead = home, lax.ppermute(home, "phase", back)
+    ops = rows_here * 2
+    visits = sections // 2
+    for turn in range(visits):
+        travel, here, ahead = lax.optimization_barrier((travel, here, ahead))
+        later = lax.ppermute(ahead, "phase", back) if turn + 2 < visits else home
+        a_side = jnp.concatenate([travel[:HALF], here[: 4 * tile], here[ops : ops + 16]], axis=0)
+        b_side = jnp.concatenate([travel[HALF:], here[ops - 4 * tile : ops], here[ops + 48 :]], axis=0)
+        from_a = lax.ppermute(a_side, "rows", to_a)
+        from_b = lax.ppermute(b_side, "rows", to_b)
+        other = lax.ppermute(jnp.where(first_core, ahead, here), "phase", mates)
+        travel = visit(travel, from_a, from_b, here, other)
+        here, ahead = ahead, later
+
+    arrived = mirrored(travel)
     gram_term = lax.dot_general(
         arrived, arrived, (((0,), (0,)), ((), ())), preferred_element_type=jnp.float32
     )

time: 453 us -> 309 us (0.68)
  waiting for transfers between devices: 258 us -> 145 us
  matrix products: 28 us -> 0.33 us
  blocking collectives: 34.4 us -> 18.3 us
  Pallas kernels: 15.6 us -> 26.9 us
  starting transfers between devices: 94.4 us -> 104 us
  local copies, waits for them, and re-layouts: 13.8 us -> 5.84 us
    ppermute x48 -> x31, waiting for transfers between devices: 258 us -> 136 us  [the longest x8 96.7 us: body(): from_b = lax.ppermute(b_side, 'rows', to_b)]
    dot_general x16 -> x0, matrix products: 27.7 us -> none  [advance(): jnp.einsum('ijab,ijbk->iak', kept_blocks, picked, preferred_element_type=...]
    all_to_all x1 -> x0, blocking collectives: 15 us -> none  [sum_over_rows(): return lax.all_to_all(copies, 'rows', 0, 0, tiled=True).reshape(size, size)]
    pallas_call x0 -> x8, Pallas kernels: none -> 11.2 us  [visit(): pl.pallas_call(visit_kernel, out_shape=jax.ShapeDtypeStruct(cur.shape, cu...]
    gather x16 -> x0, local copies, waits for them, and re-layouts: 10.9 us -> none  [advance(): picked = row_tiles[local_index]]
    all_to_all x0 -> x1, waiting for transfers between devices: none -> 9.81 us  [sum_over_rows(): return lax.all_to_all(copies, 'rows', 0, 0, tiled=True).reshape(size, size)]
    all_to_all x0 -> x1, starting transfers between devices: none -> 4.77 us  [sum_over_rows(): return lax.all_to_all(copies, 'rows', 0, 0, tiled=True).reshape(size, size)]
    ppermute x48 -> x31, starting transfers between devices: 94.4 us -> 99 us  [the longest x8 34.4 us: body(): from_b = lax.ppermute(b_side, 'rows', to_b)]
  transfers between devices with their start and end apart: 48 -> 32, of which waited for: 48 -> 19; matrix products, arithmetic and copies ran while one was open for 1% -> 1% of each run, Pallas kernels for 0% -> 3%
where the time goes in v2:
time: 309 us; the launch traced here: 307 us
  waiting for transfers between devices  145 us (47%)
  starting transfers between devices  104 us (34%)
  Pallas kernels  26.9 us (9%)
  blocking collectives  18.3 us (6%)
  local copies, waits for them, and re-layouts  5.84 us (2%)
  other arithmetic  5.33 us (2%)
    ppermute x8, waiting for transfers between devices, body(): from_b = lax.ppermute(b_side, 'rows', to_b)  96.7 us
    ppermute x8, starting transfers between devices, body(): from_b = lax.ppermute(b_side, 'rows', to_b)  34.4 us
    ppermute x1, waiting for transfers between devices, body(): here, ahead = (home, lax.ppermute(home, 'phase', back))  22.4 us
    ppermute x6, starting transfers between devices, body(): later = lax.ppermute(ahead, 'phase', back) if turn + 2 < visits else home  21.9 us
    all_to_all x1, blocking collectives, sum_over_rows(): pieces = lax.all_to_all(pieces, 'rows', 0, 0, tiled=True)  18.3 us
    ppermute x8, starting transfers between devices, body(): from_a = lax.ppermute(a_side, 'rows', to_a)  16.4 us
    pallas_call x1, Pallas kernels, finish(): pl.pallas_call(factor_kernel, out_shape=(jax.ShapeDtypeStruct(arrived.sha...  15.8 us
    ppermute x8, waiting for transfers between devices, body(): from_a = lax.ppermute(a_side, 'rows', to_a)  15.7 us
  transfers between devices with their start and end apart: 32, of which 19 were waited for; matrix products, arithmetic and copies ran while one was open for 1% of the time, Pallas kernels for 3%

profile of v2, /device:TPU:8, one launch (start us, length us, event | category | flops | bytes accessed | tf_op | source)
XLA Modules:
  0.0 307.4 jit_solution(14068699305728428959)
XLA Ops:
  2.3 2.3 copy.21
  6.3 10.9 %collective-permute-start = (bf16[2112,256]{1,0:T(8,128)(2,1)S(1)}, bf16[2112,256]{1,0:T(8,128)(2,1)S(1)}, u32[]{:S(2)}, u32[]{:S(2)}) collective-permute-start(bf16[2112,256]{1,0:T(8,128)(2,1)S(1)} %pad_maximum_fusion.first), channel_id=1, source_target_pairs={{0,448},{32,480},{64,0},{96,32},{128,64},{160,96},{192,128},{224,1... | collective-permute-start | bytes 3244040 | tf_op jit(solution)/shard_map/ppermute | solution.py:205
  17.9 22.4 %collective-permute-done.first = bf16[2112,256]{1,0:T(8,128)(2,1)S(1)} collective-permute-done((bf16[2112,256]{1,0:T(8,128)(2,1)S(1)}, bf16[2112,256]{1,0:T(8,128)(2,1)S(1)}, u32[]{:S(2)}, u32[]{:S(2)}) %collective-permute-start) | collective-permute-done | bytes 1081376 | tf_op jit(solution)/shard_map/ppermute | solution.py:205
  40.3 5.6 %collective-permute-start.4 = (bf16[2112,256]{1,0:T(8,128)(2,1)S(1)}, bf16[2112,256]{1,0:T(8,128)(2,1)S(1)}, u32[]{:S(2)}, u32[]{:S(2)}) collective-permute-start(bf16[2112,256]{1,0:T(8,128)(2,1)S(1)} %collective-permute-done.first), channel_id=1, source_target_pairs={{0,448},{32,480},{64,0},{96,32},{128,64},{160,96},{192,128},{224,1... | collective-permute-start | bytes 3244040 | tf_op jit(solution)/shard_map/ppermute | solution.py:210
  46.1 1.9 collective-permute-start.3
  48.1 4.6 %collective-permute-start.2 = (bf16[1040,256]{1,0:T(8,128)(2,1)S(1)}, bf16[1040,256]{1,0:T(8,128)(2,1)S(1)}, u32[]{:S(2)}, u32[]{:S(2)}) collective-permute-start(bf16[1040,256]{1,0:T(8,128)(2,1)S(1)} %pad_maximum_fusion.2), channel_id=1, source_target_pairs={{0,31},{1,2},{2,1},{3,4},{4,3},{5,6},{6,5},{7,8},{8,7},{9,10},{10,... | collective-permute-start | bytes 1597448 | tf_op jit(solution)/shard_map/ppermute | solution.py:214
  52.7 2.2 collective-permute-start.1
  55.0 11.6 %collective-permute-done.2.rb = bf16[1040,256]{1,0:T(8,128)(2,1)S(1)} collective-permute-done((bf16[1040,256]{1,0:T(8,128)(2,1)S(1)}, bf16[1040,256]{1,0:T(8,128)(2,1)S(1)}, u32[]{:S(2)}, u32[]{:S(2)}) %collective-permute-start.2) | collective-permute-done | bytes 532512 | tf_op jit(solution)/shard_map/ppermute | solution.py:214
  66.6 2.2 collective-permute-done.1.ra
  70.4 3.5 %collective-permute-start.8 = (bf16[2112,256]{1,0:T(8,128)(2,1)S(1)}, bf16[2112,256]{1,0:T(8,128)(2,1)S(1)}, u32[]{:S(2)}, u32[]{:S(2)}) collective-permute-start(bf16[2112,256]{1,0:T(8,128)(2,1)S(1)} %collective-permute-done.4.first), channel_id=1, source_target_pairs={{0,448},{32,480},{64,0},{96,32},{128,64},{160,96},{192,128},{224,1... | collective-permute-start | bytes 3244040 | tf_op jit(solution)/shard_map/ppermute | solution.py:210
  74.0 1.9 collective-permute-start.7
  76.0 4.6 %collective-permute-start.6 = (bf16[1040,256]{1,0:T(8,128)(2,1)S(1)}, bf16[1040,256]{1,0:T(8,128)(2,1)S(1)}, u32[]{:S(2)}, u32[]{:S(2)}) collective-permute-start(bf16[1040,256]{1,0:T(8,128)(2,1)S(1)} %pad_maximum_fusion.4), channel_id=1, source_target_pairs={{0,31},{1,2},{2,1},{3,4},{4,3},{5,6},{6,5},{7,8},{8,7},{9,10},{10,... | collective-permute-start | bytes 1597448 | tf_op jit(solution)/shard_map/ppermute | solution.py:214
  80.6 2.2 collective-permute-start.5
  82.8 11.6 %collective-permute-done.6.rb = bf16[1040,256]{1,0:T(8,128)(2,1)S(1)} collective-permute-done((bf16[1040,256]{1,0:T(8,128)(2,1)S(1)}, bf16[1040,256]{1,0:T(8,128)(2,1)S(1)}, u32[]{:S(2)}, u32[]{:S(2)}) %collective-permute-start.6) | collective-permute-done | bytes 532512 | tf_op jit(solution)/shard_map/ppermute | solution.py:214
  94.5 2.2 collective-permute-done.5.ra
  98.3 2.8 collective-permute-start.12
  101.1 1.9 collective-permute-start.11
  103.1 4.6 %collective-permute-start.10 = (bf16[1040,256]{1,0:T(8,128)(2,1)S(1)}, bf16[1040,256]{1,0:T(8,128)(2,1)S(1)}, u32[]{:S(2)}, u32[]{:S(2)}) collective-permute-start(bf16[1040,256]{1,0:T(8,128)(2,1)S(1)} %pad_maximum_fusion.6), channel_id=1, source_target_pairs={{0,31},{1,2},{2,1},{3,4},{4,3},{5,6},{6,5},{7,8},{8,7},{9,10},{10,... | collective-permute-start | bytes 1597448 | tf_op jit(solution)/shard_map/ppermute | solution.py:214
  107.7 2.2 collective-permute-start.9
  110.0 11.6 %collective-permute-done.10.rb = bf16[1040,256]{1,0:T(8,128)(2,1)S(1)} collective-permute-done((bf16[1040,256]{1,0:T(8,128)(2,1)S(1)}, bf16[1040,256]{1,0:T(8,128)(2,1)S(1)}, u32[]{:S(2)}, u32[]{:S(2)}) %collective-permute-start.10) | collective-permute-done | bytes 532512 | tf_op jit(solution)/shard_map/ppermute | solution.py:214
  121.6 2.2 collective-permute-done.9.ra
  125.5 3.4 %collective-permute-start.16 = (bf16[2112,256]{1,0:T(8,128)(2,1)S(1)}, bf16[2112,256]{1,0:T(8,128)(2,1)S(1)}, u32[]{:S(2)}, u32[]{:S(2)}) collective-permute-start(bf16[2112,256]{1,0:T(8,128)(2,1)S(1)} %collective-permute-done.12.first), channel_id=1, source_target_pairs={{0,448},{32,480},{64,0},{96,32},{128,64},{160,96},{192,128},{224,1... | collective-permute-start | bytes 3244040 | tf_op jit(solution)/shard_map/ppermute | solution.py:210
  128.9 1.9 collective-permute-start.15
  130.9 3.4 %collective-permute-start.14 = (bf16[1040,256]{1,0:T(8,128)(2,1)S(1)}, bf16[1040,256]{1,0:T(8,128)(2,1)S(1)}, u32[]{:S(2)}, u32[]{:S(2)}) collective-permute-start(bf16[1040,256]{1,0:T(8,128)(2,1)S(1)} %pad_maximum_fusion.8), channel_id=1, source_target_pairs={{0,31},{1,2},{2,1},{3,4},{4,3},{5,6},{6,5},{7,8},{8,7},{9,10},{10,... | collective-permute-start | bytes 1597448 | tf_op jit(solution)/shard_map/ppermute | solution.py:214
  134.4 2.0 collective-permute-start.13
  136.4 13.1 %collective-permute-done.14.rb = bf16[1040,256]{1,0:T(8,128)(2,1)S(1)} collective-permute-done((bf16[1040,256]{1,0:T(8,128)(2,1)S(1)}, bf16[1040,256]{1,0:T(8,128)(2,1)S(1)}, u32[]{:S(2)}, u32[]{:S(2)}) %collective-permute-start.14) | collective-permute-done | bytes 532512 | tf_op jit(solution)/shard_map/ppermute | solution.py:214
  152.6 3.6 %collective-permute-start.20 = (bf16[2112,256]{1,0:T(8,128)(2,1)S(1)}, bf16[2112,256]{1,0:T(8,128)(2,1)S(1)}, u32[]{:S(2)}, u32[]{:S(2)}) collective-permute-start(bf16[2112,256]{1,0:T(8,128)(2,1)S(1)} %collective-permute-done.16.first), channel_id=1, source_target_pairs={{0,448},{32,480},{64,0},{96,32},{128,64},{160,96},{192,128},{224,1... | collective-permute-start | bytes 3244040 | tf_op jit(solution)/shard_map/ppermute | solution.py:210
  156.2 1.9 collective-permute-start.19
  158.3 3.7 %collective-permute-start.18 = (bf16[1040,256]{1,0:T(8,128)(2,1)S(1)}, bf16[1040,256]{1,0:T(8,128)(2,1)S(1)}, u32[]{:S(2)}, u32[]{:S(2)}) collective-permute-start(bf16[1040,256]{1,0:T(8,128)(2,1)S(1)} %pad_maximum_fusion.10), channel_id=1, source_target_pairs={{0,31},{1,2},{2,1},{3,4},{4,3},{5,6},{6,5},{7,8},{8,7},{9,10},{10,... | collective-permute-start | bytes 1597448 | tf_op jit(solution)/shard_map/ppermute | solution.py:214
  162.0 1.9 collective-permute-start.17
  163.9 12.8 %collective-permute-done.18.rb = bf16[1040,256]{1,0:T(8,128)(2,1)S(1)} collective-permute-done((bf16[1040,256]{1,0:T(8,128)(2,1)S(1)}, bf16[1040,256]{1,0:T(8,128)(2,1)S(1)}, u32[]{:S(2)}, u32[]{:S(2)}) %collective-permute-start.18) | collective-permute-done | bytes 532512 | tf_op jit(solution)/shard_map/ppermute | solution.py:214
  179.7 3.0 collective-permute-start.24
  182.7 1.9 collective-permute-start.23
  184.7 5.3 %collective-permute-start.22 = (bf16[1040,256]{1,0:T(8,128)(2,1)S(1)}, bf16[1040,256]{1,0:T(8,128)(2,1)S(1)}, u32[]{:S(2)}, u32[]{:S(2)}) collective-permute-start(bf16[1040,256]{1,0:T(8,128)(2,1)S(1)} %pad_maximum_fusion.12), channel_id=1, source_target_pairs={{0,31},{1,2},{2,1},{3,4},{4,3},{5,6},{6,5},{7,8},{8,7},{9,10},{10,... | collective-permute-start | bytes 1597448 | tf_op jit(solution)/shard_map/ppermute | solution.py:214
  190.1 1.9 collective-permute-start.21
  192.0 11.2 %collective-permute-done.22.rb = bf16[1040,256]{1,0:T(8,128)(2,1)S(1)} collective-permute-done((bf16[1040,256]{1,0:T(8,128)(2,1)S(1)}, bf16[1040,256]{1,0:T(8,128)(2,1)S(1)}, u32[]{:S(2)}, u32[]{:S(2)}) %collective-permute-start.22) | collective-permute-done | bytes 532512 | tf_op jit(solution)/shard_map/ppermute | solution.py:214
  203.2 3.0 collective-permute-done.21.ra
  207.8 1.9 collective-permute-start.27
  209.8 4.2 %collective-permute-start.26 = (bf16[1040,256]{1,0:T(8,128)(2,1)S(1)}, bf16[1040,256]{1,0:T(8,128)(2,1)S(1)}, u32[]{:S(2)}, u32[]{:S(2)}) collective-permute-start(bf16[1040,256]{1,0:T(8,128)(2,1)S(1)} %pad_maximum_fusion.14), channel_id=1, source_target_pairs={{0,31},{1,2},{2,1},{3,4},{4,3},{5,6},{6,5},{7,8},{8,7},{9,10},{10,... | collective-permute-start | bytes 1597448 | tf_op jit(solution)/shard_map/ppermute | solution.py:214
  214.1 1.9 collective-permute-start.25
  216.0 12.3 %collective-permute-done.26.rb = bf16[1040,256]{1,0:T(8,128)(2,1)S(1)} collective-permute-done((bf16[1040,256]{1,0:T(8,128)(2,1)S(1)}, bf16[1040,256]{1,0:T(8,128)(2,1)S(1)}, u32[]{:S(2)}, u32[]{:S(2)}) %collective-permute-start.26) | collective-permute-done | bytes 532512 | tf_op jit(solution)/shard_map/ppermute | solution.py:214
  231.8 1.9 collective-permute-start.30
  233.8 4.1 %collective-permute-start.29 = (bf16[1040,256]{1,0:T(8,128)(2,1)S(1)}, bf16[1040,256]{1,0:T(8,128)(2,1)S(1)}, u32[]{:S(2)}, u32[]{:S(2)}) collective-permute-start(bf16[1040,256]{1,0:T(8,128)(2,1)S(1)} %pad_maximum_fusion.16), channel_id=1, source_target_pairs={{0,31},{1,2},{2,1},{3,4},{4,3},{5,6},{6,5},{7,8},{8,7},{9,10},{10,... | collective-permute-start | bytes 1597448 | tf_op jit(solution)/shard_map/ppermute | solution.py:214
  239.9 12.4 %collective-permute-done.29.rb = bf16[1040,256]{1,0:T(8,128)(2,1)S(1)} collective-permute-done((bf16[1040,256]{1,0:T(8,128)(2,1)S(1)}, bf16[1040,256]{1,0:T(8,128)(2,1)S(1)}, u32[]{:S(2)}, u32[]{:S(2)}) %collective-permute-start.29) | collective-permute-done | bytes 532512 | tf_op jit(solution)/shard_map/ppermute | solution.py:214
  256.2 18.3 %all_to_all.10 = bf16[32,8,256]{2,1,0:T(8,128)(2,1)S(1)} all-to-all(bf16[32,8,256]{2,1,0:T(8,128)(2,1)S(1)} %fusion.1), channel_id=1, replica_groups=mesh['phase'=16,'rows'=32] {'rows'}, dimensions={0} | all-to-all | bytes 262144 | tf_op jit(solution)/shard_map/all_to_all | solution.py:161
  275.3 4.8 %all-to-all-start.1 = ((f32[32,8,256]{2,1,0:T(8,128)}), f32[32,8,256]{2,1,0:T(8,128)S(1)}, u32[]{:S(2)}, u32[]{:S(2)}) async-start(f32[32,8,256]{2,1,0:T(8,128)} %broadcast_in_dim.25), calls=%async_computation.1 | async-start | bytes 524288 | tf_op jit(solution)/shard_map/all_to_all | solution.py:164
  281.1 9.8 %all-to-all-done.1 = f32[32,8,256]{2,1,0:T(8,128)S(1)} async-done(((f32[32,8,256]{2,1,0:T(8,128)}), f32[32,8,256]{2,1,0:T(8,128)S(1)}, u32[]{:S(2)}, u32[]{:S(2)}) %all-to-all-start.1) | async-done | bytes 262176 | tf_op jit(solution)/shard_map/all_to_all | solution.py:164
  291.7 15.8 %factor_solve.1 = (f32[1024,256]{1,0:T(8,128)}, f32[256,256]{1,0:T(8,128)}) custom-call(f32[256,256]{1,0:T(8,128)} %multiply_bitcast_fusion.gram_ref, bf16[1024,256]{1,0:T(8,128)(2,1)} %bitcast.44), custom_call_target="tpu_custom_call" | custom-call | tf_op jit(solution)/shard_map/factor_solve/pallas_call | solution.py:144
  (97 shorter events, 29.0 us)
Async XLA Ops:
  5.9 11.3 %copy-start = (bf16[1,1024,256]{2,1,0:T(8,128)(2,1)S(1)}, bf16[1,1024,256]{2,1,0:T(8,128)(2,1)}, u32[]{:S(2)}) copy-start(bf16[1,1024,256]{2,1,0:T(8,128)(2,1)} %param.4) | copy-start | bytes 1572868
  6.3 34.1 %collective-permute-start = (bf16[2112,256]{1,0:T(8,128)(2,1)S(1)}, bf16[2112,256]{1,0:T(8,128)(2,1)S(1)}, u32[]{:S(2)}, u32[]{:S(2)}) collective-permute-start(bf16[2112,256]{1,0:T(8,128)(2,1)S(1)} %pad_maximum_fusion.first), channel_id=1, source_target_pairs={{0,448},{32,480},{64,0},{96,32},{128,64},{160,96},{192,128},{224,1... | collective-permute-start | bytes 3244040 | tf_op jit(solution)/shard_map/ppermute | solution.py:205
  40.3 29.9 %collective-permute-start.4 = (bf16[2112,256]{1,0:T(8,128)(2,1)S(1)}, bf16[2112,256]{1,0:T(8,128)(2,1)S(1)}, u32[]{:S(2)}, u32[]{:S(2)}) collective-permute-start(bf16[2112,256]{1,0:T(8,128)(2,1)S(1)} %collective-permute-done.first), channel_id=1, source_target_pairs={{0,448},{32,480},{64,0},{96,32},{128,64},{160,96},{192,128},{224,1... | collective-permute-start | bytes 3244040 | tf_op jit(solution)/shard_map/ppermute | solution.py:210
  46.1 22.8 %collective-permute-start.3 = (bf16[2112,256]{1,0:T(8,128)(2,1)S(1)}, bf16[2112,256]{1,0:T(8,128)(2,1)S(1)}, u32[]{:S(2)}, u32[]{:S(2)}) collective-permute-start(bf16[2112,256]{1,0:T(8,128)(2,1)S(1)} %broadcast_select_fusion.8), channel_id=1, source_target_pairs={{0,32},{32,0},{64,96},{96,64},{128,160},{160,128},{192,224},{224,1... | collective-permute-start | bytes 3244040 | tf_op jit(solution)/shard_map/ppermute | solution.py:215
  48.1 18.5 %collective-permute-start.2 = (bf16[1040,256]{1,0:T(8,128)(2,1)S(1)}, bf16[1040,256]{1,0:T(8,128)(2,1)S(1)}, u32[]{:S(2)}, u32[]{:S(2)}) collective-permute-start(bf16[1040,256]{1,0:T(8,128)(2,1)S(1)} %pad_maximum_fusion.2), channel_id=1, source_target_pairs={{0,31},{1,2},{2,1},{3,4},{4,3},{5,6},{6,5},{7,8},{8,7},{9,10},{10,... | collective-permute-start | bytes 1597448 | tf_op jit(solution)/shard_map/ppermute | solution.py:214
  52.7 16.1 %collective-permute-start.1 = (bf16[1040,256]{1,0:T(8,128)(2,1)S(1)}, bf16[1040,256]{1,0:T(8,128)(2,1)S(1)}, u32[]{:S(2)}, u32[]{:S(2)}) collective-permute-start(bf16[1040,256]{1,0:T(8,128)(2,1)S(1)} %pad_maximum_fusion.1), channel_id=1, source_target_pairs={{0,1},{1,0},{2,3},{3,2},{4,5},{5,4},{6,7},{7,6},{8,9},{9,8},{10,11... | collective-permute-start | bytes 1597448 | tf_op jit(solution)/shard_map/ppermute | solution.py:213
  70.4 27.7 %collective-permute-start.8 = (bf16[2112,256]{1,0:T(8,128)(2,1)S(1)}, bf16[2112,256]{1,0:T(8,128)(2,1)S(1)}, u32[]{:S(2)}, u32[]{:S(2)}) collective-permute-start(bf16[2112,256]{1,0:T(8,128)(2,1)S(1)} %collective-permute-done.4.first), channel_id=1, source_target_pairs={{0,448},{32,480},{64,0},{96,32},{128,64},{160,96},{192,128},{224,1... | collective-permute-start | bytes 3244040 | tf_op jit(solution)/shard_map/ppermute | solution.py:210
  74.0 22.7 %collective-permute-start.7 = (bf16[2112,256]{1,0:T(8,128)(2,1)S(1)}, bf16[2112,256]{1,0:T(8,128)(2,1)S(1)}, u32[]{:S(2)}, u32[]{:S(2)}) collective-permute-start(bf16[2112,256]{1,0:T(8,128)(2,1)S(1)} %broadcast_select_fusion.7), channel_id=1, source_target_pairs={{0,32},{32,0},{64,96},{96,64},{128,160},{160,128},{192,224},{224,1... | collective-permute-start | bytes 3244040 | tf_op jit(solution)/shard_map/ppermute | solution.py:215
  76.0 18.5 %collective-permute-start.6 = (bf16[1040,256]{1,0:T(8,128)(2,1)S(1)}, bf16[1040,256]{1,0:T(8,128)(2,1)S(1)}, u32[]{:S(2)}, u32[]{:S(2)}) collective-permute-start(bf16[1040,256]{1,0:T(8,128)(2,1)S(1)} %pad_maximum_fusion.4), channel_id=1, source_target_pairs={{0,31},{1,2},{2,1},{3,4},{4,3},{5,6},{6,5},{7,8},{8,7},{9,10},{10,... | collective-permute-start | bytes 1597448 | tf_op jit(solution)/shard_map/ppermute | solution.py:214
  80.6 16.1 %collective-permute-start.5 = (bf16[1040,256]{1,0:T(8,128)(2,1)S(1)}, bf16[1040,256]{1,0:T(8,128)(2,1)S(1)}, u32[]{:S(2)}, u32[]{:S(2)}) collective-permute-start(bf16[1040,256]{1,0:T(8,128)(2,1)S(1)} %pad_maximum_fusion.3), channel_id=1, source_target_pairs={{0,1},{1,0},{2,3},{3,2},{4,5},{5,4},{6,7},{7,6},{8,9},{9,8},{10,11... | collective-permute-start | bytes 1597448 | tf_op jit(solution)/shard_map/ppermute | solution.py:213
  98.3 27.0 %collective-permute-start.12 = (bf16[2112,256]{1,0:T(8,128)(2,1)S(1)}, bf16[2112,256]{1,0:T(8,128)(2,1)S(1)}, u32[]{:S(2)}, u32[]{:S(2)}) collective-permute-start(bf16[2112,256]{1,0:T(8,128)(2,1)S(1)} %collective-permute-done.8.first), channel_id=1, source_target_pairs={{0,448},{32,480},{64,0},{96,32},{128,64},{160,96},{192,128},{224,1... | collective-permute-start | bytes 3244040 | tf_op jit(solution)/shard_map/ppermute | solution.py:210
  101.1 22.7 %collective-permute-start.11 = (bf16[2112,256]{1,0:T(8,128)(2,1)S(1)}, bf16[2112,256]{1,0:T(8,128)(2,1)S(1)}, u32[]{:S(2)}, u32[]{:S(2)}) collective-permute-start(bf16[2112,256]{1,0:T(8,128)(2,1)S(1)} %broadcast_select_fusion.6), channel_id=1, source_target_pairs={{0,32},{32,0},{64,96},{96,64},{128,160},{160,128},{192,224},{224,1... | collective-permute-start | bytes 3244040 | tf_op jit(solution)/shard_map/ppermute | solution.py:215
  103.1 18.5 %collective-permute-start.10 = (bf16[1040,256]{1,0:T(8,128)(2,1)S(1)}, bf16[1040,256]{1,0:T(8,128)(2,1)S(1)}, u32[]{:S(2)}, u32[]{:S(2)}) collective-permute-start(bf16[1040,256]{1,0:T(8,128)(2,1)S(1)} %pad_maximum_fusion.6), channel_id=1, source_target_pairs={{0,31},{1,2},{2,1},{3,4},{4,3},{5,6},{6,5},{7,8},{8,7},{9,10},{10,... | collective-permute-start | bytes 1597448 | tf_op jit(solution)/shard_map/ppermute | solution.py:214
  107.7 16.1 %collective-permute-start.9 = (bf16[1040,256]{1,0:T(8,128)(2,1)S(1)}, bf16[1040,256]{1,0:T(8,128)(2,1)S(1)}, u32[]{:S(2)}, u32[]{:S(2)}) collective-permute-start(bf16[1040,256]{1,0:T(8,128)(2,1)S(1)} %pad_maximum_fusion.5), channel_id=1, source_target_pairs={{0,1},{1,0},{2,3},{3,2},{4,5},{5,4},{6,7},{7,6},{8,9},{9,8},{10,11... | collective-permute-start | bytes 1597448 | tf_op jit(solution)/shard_map/ppermute | solution.py:213
  125.5 27.0 %collective-permute-start.16 = (bf16[2112,256]{1,0:T(8,128)(2,1)S(1)}, bf16[2112,256]{1,0:T(8,128)(2,1)S(1)}, u32[]{:S(2)}, u32[]{:S(2)}) collective-permute-start(bf16[2112,256]{1,0:T(8,128)(2,1)S(1)} %collective-permute-done.12.first), channel_id=1, source_target_pairs={{0,448},{32,480},{64,0},{96,32},{128,64},{160,96},{192,128},{224,1... | collective-permute-start | bytes 3244040 | tf_op jit(solution)/shard_map/ppermute | solution.py:210
  128.9 21.6 %collective-permute-start.15 = (bf16[2112,256]{1,0:T(8,128)(2,1)S(1)}, bf16[2112,256]{1,0:T(8,128)(2,1)S(1)}, u32[]{:S(2)}, u32[]{:S(2)}) collective-permute-start(bf16[2112,256]{1,0:T(8,128)(2,1)S(1)} %broadcast_select_fusion.5), channel_id=1, source_target_pairs={{0,32},{32,0},{64,96},{96,64},{128,160},{160,128},{192,224},{224,1... | collective-permute-start | bytes 3244040 | tf_op jit(solution)/shard_map/ppermute | solution.py:215
  130.9 18.5 %collective-permute-start.14 = (bf16[1040,256]{1,0:T(8,128)(2,1)S(1)}, bf16[1040,256]{1,0:T(8,128)(2,1)S(1)}, u32[]{:S(2)}, u32[]{:S(2)}) collective-permute-start(bf16[1040,256]{1,0:T(8,128)(2,1)S(1)} %pad_maximum_fusion.8), channel_id=1, source_target_pairs={{0,31},{1,2},{2,1},{3,4},{4,3},{5,6},{6,5},{7,8},{8,7},{9,10},{10,... | collective-permute-start | bytes 1597448 | tf_op jit(solution)/shard_map/ppermute | solution.py:214
  134.4 16.1 %collective-permute-start.13 = (bf16[1040,256]{1,0:T(8,128)(2,1)S(1)}, bf16[1040,256]{1,0:T(8,128)(2,1)S(1)}, u32[]{:S(2)}, u32[]{:S(2)}) collective-permute-start(bf16[1040,256]{1,0:T(8,128)(2,1)S(1)} %pad_maximum_fusion.7), channel_id=1, source_target_pairs={{0,1},{1,0},{2,3},{3,2},{4,5},{5,4},{6,7},{7,6},{8,9},{9,8},{10,11... | collective-permute-start | bytes 1597448 | tf_op jit(solution)/shard_map/ppermute | solution.py:213
  152.6 26.9 %collective-permute-start.20 = (bf16[2112,256]{1,0:T(8,128)(2,1)S(1)}, bf16[2112,256]{1,0:T(8,128)(2,1)S(1)}, u32[]{:S(2)}, u32[]{:S(2)}) collective-permute-start(bf16[2112,256]{1,0:T(8,128)(2,1)S(1)} %collective-permute-done.16.first), channel_id=1, source_target_pairs={{0,448},{32,480},{64,0},{96,32},{128,64},{160,96},{192,128},{224,1... | collective-permute-start | bytes 3244040 | tf_op jit(solution)/shard_map/ppermute | solution.py:210
  156.2 21.9 %collective-permute-start.19 = (bf16[2112,256]{1,0:T(8,128)(2,1)S(1)}, bf16[2112,256]{1,0:T(8,128)(2,1)S(1)}, u32[]{:S(2)}, u32[]{:S(2)}) collective-permute-start(bf16[2112,256]{1,0:T(8,128)(2,1)S(1)} %broadcast_select_fusion.4), channel_id=1, source_target_pairs={{0,32},{32,0},{64,96},{96,64},{128,160},{160,128},{192,224},{224,1... | collective-permute-start | bytes 3244040 | tf_op jit(solution)/shard_map/ppermute | solution.py:215
  158.3 18.5 %collective-permute-start.18 = (bf16[1040,256]{1,0:T(8,128)(2,1)S(1)}, bf16[1040,256]{1,0:T(8,128)(2,1)S(1)}, u32[]{:S(2)}, u32[]{:S(2)}) collective-permute-start(bf16[1040,256]{1,0:T(8,128)(2,1)S(1)} %pad_maximum_fusion.10), channel_id=1, source_target_pairs={{0,31},{1,2},{2,1},{3,4},{4,3},{5,6},{6,5},{7,8},{8,7},{9,10},{10,... | collective-permute-start | bytes 1597448 | tf_op jit(solution)/shard_map/ppermute | solution.py:214
  162.0 16.1 %collective-permute-start.17 = (bf16[1040,256]{1,0:T(8,128)(2,1)S(1)}, bf16[1040,256]{1,0:T(8,128)(2,1)S(1)}, u32[]{:S(2)}, u32[]{:S(2)}) collective-permute-start(bf16[1040,256]{1,0:T(8,128)(2,1)S(1)} %pad_maximum_fusion.9), channel_id=1, source_target_pairs={{0,1},{1,0},{2,3},{3,2},{4,5},{5,4},{6,7},{7,6},{8,9},{9,8},{10,11... | collective-permute-start | bytes 1597448 | tf_op jit(solution)/shard_map/ppermute | solution.py:213
  179.7 27.9 %collective-permute-start.24 = (bf16[2112,256]{1,0:T(8,128)(2,1)S(1)}, bf16[2112,256]{1,0:T(8,128)(2,1)S(1)}, u32[]{:S(2)}, u32[]{:S(2)}) collective-permute-start(bf16[2112,256]{1,0:T(8,128)(2,1)S(1)} %collective-permute-done.20.first), channel_id=1, source_target_pairs={{0,448},{32,480},{64,0},{96,32},{128,64},{160,96},{192,128},{224,1... | collective-permute-start | bytes 3244040 | tf_op jit(solution)/shard_map/ppermute | solution.py:210
  182.7 23.5 %collective-permute-start.23 = (bf16[2112,256]{1,0:T(8,128)(2,1)S(1)}, bf16[2112,256]{1,0:T(8,128)(2,1)S(1)}, u32[]{:S(2)}, u32[]{:S(2)}) collective-permute-start(bf16[2112,256]{1,0:T(8,128)(2,1)S(1)} %broadcast_select_fusion.3), channel_id=1, source_target_pairs={{0,32},{32,0},{64,96},{96,64},{128,160},{160,128},{192,224},{224,1... | collective-permute-start | bytes 3244040 | tf_op jit(solution)/shard_map/ppermute | solution.py:215
  184.7 18.5 %collective-permute-start.22 = (bf16[1040,256]{1,0:T(8,128)(2,1)S(1)}, bf16[1040,256]{1,0:T(8,128)(2,1)S(1)}, u32[]{:S(2)}, u32[]{:S(2)}) collective-permute-start(bf16[1040,256]{1,0:T(8,128)(2,1)S(1)} %pad_maximum_fusion.12), channel_id=1, source_target_pairs={{0,31},{1,2},{2,1},{3,4},{4,3},{5,6},{6,5},{7,8},{8,7},{9,10},{10,... | collective-permute-start | bytes 1597448 | tf_op jit(solution)/shard_map/ppermute | solution.py:214
  190.1 16.1 %collective-permute-start.21 = (bf16[1040,256]{1,0:T(8,128)(2,1)S(1)}, bf16[1040,256]{1,0:T(8,128)(2,1)S(1)}, u32[]{:S(2)}, u32[]{:S(2)}) collective-permute-start(bf16[1040,256]{1,0:T(8,128)(2,1)S(1)} %pad_maximum_fusion.11), channel_id=1, source_target_pairs={{0,1},{1,0},{2,3},{3,2},{4,5},{5,4},{6,7},{7,6},{8,9},{9,8},{10,11... | collective-permute-start | bytes 1597448 | tf_op jit(solution)/shard_map/ppermute | solution.py:213
  207.8 22.4 %collective-permute-start.27 = (bf16[2112,256]{1,0:T(8,128)(2,1)S(1)}, bf16[2112,256]{1,0:T(8,128)(2,1)S(1)}, u32[]{:S(2)}, u32[]{:S(2)}) collective-permute-start(bf16[2112,256]{1,0:T(8,128)(2,1)S(1)} %broadcast_select_fusion.2), channel_id=1, source_target_pairs={{0,32},{32,0},{64,96},{96,64},{128,160},{160,128},{192,224},{224,1... | collective-permute-start | bytes 3244040 | tf_op jit(solution)/shard_map/ppermute | solution.py:215
  209.8 18.5 %collective-permute-start.26 = (bf16[1040,256]{1,0:T(8,128)(2,1)S(1)}, bf16[1040,256]{1,0:T(8,128)(2,1)S(1)}, u32[]{:S(2)}, u32[]{:S(2)}) collective-permute-start(bf16[1040,256]{1,0:T(8,128)(2,1)S(1)} %pad_maximum_fusion.14), channel_id=1, source_target_pairs={{0,31},{1,2},{2,1},{3,4},{4,3},{5,6},{6,5},{7,8},{8,7},{9,10},{10,... | collective-permute-start | bytes 1597448 | tf_op jit(solution)/shard_map/ppermute | solution.py:214
  214.1 16.1 %collective-permute-start.25 = (bf16[1040,256]{1,0:T(8,128)(2,1)S(1)}, bf16[1040,256]{1,0:T(8,128)(2,1)S(1)}, u32[]{:S(2)}, u32[]{:S(2)}) collective-permute-start(bf16[1040,256]{1,0:T(8,128)(2,1)S(1)} %pad_maximum_fusion.13), channel_id=1, source_target_pairs={{0,1},{1,0},{2,3},{3,2},{4,5},{5,4},{6,7},{7,6},{8,9},{9,8},{10,11... | collective-permute-start | bytes 1597448 | tf_op jit(solution)/shard_map/ppermute | solution.py:213
  231.8 22.3 %collective-permute-start.30 = (bf16[2112,256]{1,0:T(8,128)(2,1)S(1)}, bf16[2112,256]{1,0:T(8,128)(2,1)S(1)}, u32[]{:S(2)}, u32[]{:S(2)}) collective-permute-start(bf16[2112,256]{1,0:T(8,128)(2,1)S(1)} %broadcast_select_fusion.1), channel_id=1, source_target_pairs={{0,32},{32,0},{64,96},{96,64},{128,160},{160,128},{192,224},{224,1... | collective-permute-start | bytes 3244040 | tf_op jit(solution)/shard_map/ppermute | solution.py:215
  233.8 18.5 %collective-permute-start.29 = (bf16[1040,256]{1,0:T(8,128)(2,1)S(1)}, bf16[1040,256]{1,0:T(8,128)(2,1)S(1)}, u32[]{:S(2)}, u32[]{:S(2)}) collective-permute-start(bf16[1040,256]{1,0:T(8,128)(2,1)S(1)} %pad_maximum_fusion.16), channel_id=1, source_target_pairs={{0,31},{1,2},{2,1},{3,4},{4,3},{5,6},{6,5},{7,8},{8,7},{9,10},{10,... | collective-permute-start | bytes 1597448 | tf_op jit(solution)/shard_map/ppermute | solution.py:214
  238.0 16.1 %collective-permute-start.28 = (bf16[1040,256]{1,0:T(8,128)(2,1)S(1)}, bf16[1040,256]{1,0:T(8,128)(2,1)S(1)}, u32[]{:S(2)}, u32[]{:S(2)}) collective-permute-start(bf16[1040,256]{1,0:T(8,128)(2,1)S(1)} %pad_maximum_fusion.15), channel_id=1, source_target_pairs={{0,1},{1,0},{2,3},{3,2},{4,5},{5,4},{6,7},{7,6},{8,9},{9,8},{10,11... | collective-permute-start | bytes 1597448 | tf_op jit(solution)/shard_map/ppermute | solution.py:213
  275.3 15.6 %all-to-all-start.1 = ((f32[32,8,256]{2,1,0:T(8,128)}), f32[32,8,256]{2,1,0:T(8,128)S(1)}, u32[]{:S(2)}, u32[]{:S(2)}) async-start(f32[32,8,256]{2,1,0:T(8,128)} %broadcast_in_dim.25), calls=%async_computation.1 | async-start | bytes 524288 | tf_op jit(solution)/shard_map/all_to_all | solution.py:164

commit v3 on v2

--- a/solution.py
+++ b/solution.py
@@ -5,13 +5,14 @@
 from jax.experimental.pallas import tpu as pltpu
 from jax.sharding import PartitionSpec as P
 
+
 HB = 2
 TILE = 128
 HALF = 4 * TILE
-OPS = 16 * TILE
 DEAD = 7
 
-def visit_kernel(cur, ra, rb, first, second, out, wide, mid):
+
+def visit_kernel(cur, ra, rb, rim_a, rim_b, first, second, out, wide, mid):
     for n in range(4):
         wide[(3 - n) * TILE : (4 - n) * TILE, :] = ra[n * TILE : (n + 1) * TILE, :]
         wide[(15 - n) * TILE : (16 - n) * TILE, :] = rb[n * TILE : (n + 1) * TILE, :]
@@ -20,54 +21,46 @@
     wide[16 * TILE :, :] = zero
     mid[12 * TILE :, :] = zero
 
-    def table_of(ref, start, count):
-        return ref[start : start + count, :TILE].astype(jnp.float32).astype(jnp.int32)
-
-    def row(ops, base, table, line, source, centre, sign, nothing):
+    def row(ops, n, source, centre, sign, nothing):
+        line = ops.shape[0] // (4 * TILE + 8) * 4 * TILE + n * 8
+        table = ops[line : line + 8, :].astype(jnp.float32).astype(jnp.int32)
+
         def block(j):
             if j == 0:
                 return source[centre * TILE : (centre + 1) * TILE, :]
-            value = jnp.max(table[line + j : line + j + 1, :])
+            value = jnp.max(table[j : j + 1, :])
             place = jnp.where(value == DEAD, nothing, centre + sign * (value - 2))
             return source[pl.ds(pl.multiple_of(place * TILE, TILE), TILE), :]
 
+        def slot(j):
+            return ops[(n * 4 + j) * TILE : (n * 4 + j + 1) * TILE, :]
+
         total = None
-        for pair in range(2):
-            left = ops[base + pair * TILE : base + (pair + 1) * TILE, :]
-            right = jnp.concatenate([block(2 * pair), block(2 * pair + 1)], axis=0)
+        for j in (0, 2):
+            left = jnp.concatenate([slot(j), slot(j + 1)], axis=1)
+            right = jnp.concatenate([block(j), block(j + 1)], axis=0)
             part = jnp.dot(left, right, preferred_element_type=jnp.float32)
             total = part if total is None else total + part
         return total.astype(out.dtype)
 
-    near_a = table_of(ra, 2 * HALF, 16)
-    near_b = table_of(rb, 2 * HALF, 16)
-    own = table_of(first, OPS, 64)
     for n in range(2):
-        c = -1 - n
-        mid[(c + 2) * TILE : (c + 3) * TILE, :] = row(
-            ra, HALF + n * 2 * TILE, near_a, n * 8, wide, c + 4, -1, 16
-        )
-        c = 9 - n
-        mid[(c + 2) * TILE : (c + 3) * TILE, :] = row(
-            rb, HALF + n * 2 * TILE, near_b, n * 8, wide, c + 4, -1, 16
-        )
+        c = 1 - n
+        mid[c * TILE : (c + 1) * TILE, :] = row(rim_a, n, wide, c + 2, -1, 16)
+        c = 11 - n
+        mid[c * TILE : (c + 1) * TILE, :] = row(rim_b, n, wide, c + 2, -1, 16)
     for c in range(8):
-        mid[(c + 2) * TILE : (c + 3) * TILE, :] = row(
-            first, c * 2 * TILE, own, c * 8, wide, c + 4, 1, 16
-        )
-    other = table_of(second, OPS, 64)
+        mid[(c + 2) * TILE : (c + 3) * TILE, :] = row(first, c, wide, c + 4, 1, 16)
     for c in range(8):
-        out[c * TILE : (c + 1) * TILE, :] = row(
-            second, c * 2 * TILE, other, c * 8, mid, c + 2, 1, 12
-        )
-
-def visit(cur, ra, rb, first, second):
+        out[c * TILE : (c + 1) * TILE, :] = row(second, c, mid, c + 2, 1, 12)
+
+
+def visit(cur, ra, rb, rim_a, rim_b, first, second):
     vmem = pl.BlockSpec(memory_space=pltpu.VMEM)
     columns = cur.shape[1]
     return pl.pallas_call(
         visit_kernel,
         out_shape=jax.ShapeDtypeStruct(cur.shape, cur.dtype),
-        in_specs=[vmem] * 5,
+        in_specs=[vmem] * 7,
         out_specs=vmem,
         scratch_shapes=[
             pltpu.VMEM((17 * TILE, columns), cur.dtype),
@@ -76,10 +69,11 @@
         compiler_params=pltpu.CompilerParams(vmem_limit_bytes=24 * 1024 * 1024),
         cost_estimate=pl.CostEstimate(flops=700_000_000, bytes_accessed=4_000_000, transcendentals=0),
         name="two_steps",
-    )(cur, ra, rb, first, second)
+    )(cur, ra, rb, rim_a, rim_b, first, second)
 
 
 NB = 16
+
 
 def factor_kernel(gram_ref, arrived_ref, basis_ref, factor_ref, a_ref, w_ref):
     size = gram_ref.shape[0]
@@ -121,22 +115,30 @@
         w_ref[first : first + NB, :] = other
         rest = first + NB
         if rest < size:
-            right = jnp.concatenate([upper, other], axis=1)
+            low_row = rest // lanes * lanes
+            low_lane = first // lanes * lanes
+            high_lane = low_lane + lanes
+            right = jnp.concatenate([upper[:, low_lane:], other[:, :high_lane]], axis=1)
             change = lax.dot_general(
-                upper, right, (((0,), (0,)), ((), ())),
+                upper[:, low_row:], right, (((0,), (0,)), ((), ())),
                 preferred_element_type=jnp.float32, precision=lax.Precision.HIGHEST,
-            )
-            a_ref[rest:, :] = a_ref[rest:, :] - change[rest:, :size]
-            w_ref[rest:, :] = w_ref[rest:, :] - change[rest:, size:]
+            )[rest - low_row :, :]
+            split = size - low_lane
+            a_ref[rest:, low_lane:] = a_ref[rest:, low_lane:] - change[:, :split]
+            w_ref[rest:, :high_lane] = w_ref[rest:, :high_lane] - change[:, split:]
     w = w_ref[...]
     high = w.astype(jnp.bfloat16)
     low = (w - high.astype(jnp.float32)).astype(jnp.bfloat16)
     dims = (((1,), (1,)), ((), ()))
-    for piece in range(0, arrived_ref.shape[0], 256):
-        rows = arrived_ref[piece : piece + 256, :]
-        basis_ref[piece : piece + 256, :] = lax.dot_general(
+
+    @pl.loop(0, arrived_ref.shape[0], step=256)
+    def _(piece):
+        at = pl.ds(pl.multiple_of(piece, 256), 256)
+        rows = arrived_ref[at, :]
+        basis_ref[at, :] = lax.dot_general(
             rows, high, dims, preferred_element_type=jnp.float32
         ) + lax.dot_general(rows, low, dims, preferred_element_type=jnp.float32)
+
 
 def finish(gram, arrived):
     size = gram.shape[0]
@@ -165,7 +167,7 @@
 
 
 def packed_operator(blocks, cols, counts, even):
-    block_rows, slots, tile, unused = blocks.shape
+    block_rows, slots, tile, _ = blocks.shape
     owners = lax.axis_size("rows")
     total = block_rows * owners
     index = lax.axis_index("rows") * block_rows + jnp.arange(block_rows, dtype=jnp.int32)
@@ -176,15 +178,14 @@
     place = jnp.where(even, place[::-1], place)
     place = jnp.pad(place, ((0, 0), (0, 8 - slots)), constant_values=DEAD)
     table = jnp.broadcast_to(
-        place.reshape(block_rows * 8, 1).astype(jnp.bfloat16), (block_rows * 8, 2 * tile)
-    )
-    paired = blocks.reshape(block_rows, 2, 2, tile, tile).transpose(0, 1, 3, 2, 4)
-    paired = jnp.where(even, paired[::-1], paired)
-    return jnp.concatenate([paired.reshape(block_rows * 2 * tile, 2 * tile), table], axis=0)
+        place.reshape(block_rows * 8, 1).astype(jnp.bfloat16), (block_rows * 8, tile)
+    )
+    blocks = jnp.where(even, blocks[::-1], blocks)
+    return jnp.concatenate([blocks.reshape(block_rows * slots * tile, tile), table], axis=0)
 
 
 def body(start, blocks, cols, counts):
-    tile = blocks.shape[3]
+    block_rows, slots, tile = blocks.shape[1:4]
     rows_here = start.shape[1]
     columns = start.shape[2]
     owners = lax.axis_size("rows")
@@ -194,27 +195,42 @@
     to_a = [(i, i ^ 1) for i in range(owners)]
     to_b = [(i, (i + 1) % owners if i % 2 else (i - 1) % owners) for i in range(owners)]
     back = [(i, (i - 2) % sections) for i in range(sections)]
+    ahead = [(i, (i + 2) % sections) for i in range(sections)]
     mates = [(i, i ^ 1) for i in range(sections)]
+    lines = block_rows * slots * tile
+    edge = HB * slots * tile
 
     def mirrored(rows):
         tiles = rows.reshape(rows_here // tile, tile, columns)
         return jnp.where(even, tiles[::-1], tiles).reshape(rows_here, columns)
 
+    def rims(operator):
+        a_side = jnp.concatenate([operator[:edge], operator[lines : lines + 8 * HB]], axis=0)
+        b_side = jnp.concatenate([operator[lines - edge : lines], operator[-8 * HB :]], axis=0)
+        return (lax.ppermute(a_side, "rows", to_a), lax.ppermute(b_side, "rows", to_b))
+
+    visits = sections // 2
+    far = visits // 2
+    home = packed_operator(blocks[0], cols[0], counts[0], even)
+    held = {0: home, visits: home}
+    held[1] = lax.ppermute(home, "phase", back)
+    held[visits - 1] = lax.ppermute(home, "phase", ahead)
     travel = mirrored(start[0])
-    home = packed_operator(blocks[0], cols[0], counts[0], even)
-    here, ahead = home, lax.ppermute(home, "phase", back)
-    ops = rows_here * 2
-    visits = sections // 2
+    rim = rims(home)
     for turn in range(visits):
-        travel, here, ahead = lax.optimization_barrier((travel, here, ahead))
-        later = lax.ppermute(ahead, "phase", back) if turn + 2 < visits else home
-        a_side = jnp.concatenate([travel[:HALF], here[: 4 * tile], here[ops : ops + 16]], axis=0)
-        b_side = jnp.concatenate([travel[HALF:], here[ops - 4 * tile : ops], here[ops + 48 :]], axis=0)
-        from_a = lax.ppermute(a_side, "rows", to_a)
-        from_b = lax.ppermute(b_side, "rows", to_b)
-        other = lax.ppermute(jnp.where(first_core, ahead, here), "phase", mates)
-        travel = visit(travel, from_a, from_b, here, other)
-        here, ahead = ahead, later
+        from_a = lax.ppermute(travel[:HALF], "rows", to_a)
+        from_b = lax.ppermute(travel[HALF:], "rows", to_b)
+        here, later, travel = lax.optimization_barrier((held[turn], held[turn + 1], travel))
+        if turn + 2 <= far:
+            held[turn + 2] = lax.ppermute(later, "phase", back)
+        end = visits - 1 - turn
+        if turn > 0 and end > far:
+            nearer, travel = lax.optimization_barrier((held[end + 1], travel))
+            held[end] = lax.ppermute(nearer, "phase", ahead)
+        other = lax.ppermute(jnp.where(first_core, later, here), "phase", mates)
+        next_rim = rims(later) if turn + 1 < visits else None
+        travel = visit(travel, from_a, from_b, *rim, here, other)
+        rim = next_rim
 
     arrived = mirrored(travel)
     gram_term = lax.dot_general(

time: 309 us -> 348 us (1.13)
  the two profiles are of different devices: /device:TPU:8 before, /device:TPU:64 now
where the time goes in v3:
time: 348 us; the launch traced here: 346 us
  starting transfers between devices  166 us (48%)
  waiting for transfers between devices  110 us (32%)
  Pallas kernels  27.5 us (8%)
  blocking collectives  14.9 us (4%)
  other arithmetic  13.5 us (4%)
  local copies, waits for them, and re-layouts  12.6 us (4%)
    ppermute x8, starting transfers between devices, rims(): lax.ppermute(b_side, 'rows', to_b)  38.3 us
    ppermute x8, waiting for transfers between devices, body(): from_b = lax.ppermute(travel[HALF:], 'rows', to_b)  38.3 us
    ppermute x8, starting transfers between devices, body(): from_b = lax.ppermute(travel[HALF:], 'rows', to_b)  35.2 us
    ppermute x8, starting transfers between devices, body(): from_a = lax.ppermute(travel[:HALF], 'rows', to_a)  25.9 us
    ppermute x8, waiting for transfers between devices, body(): from_a = lax.ppermute(travel[:HALF], 'rows', to_a)  23.2 us
    ppermute x3, starting transfers between devices, body(): held[turn + 2] = lax.ppermute(later, 'phase', back)  18 us
    ppermute x8, starting transfers between devices, rims(): lax.ppermute(a_side, 'rows', to_a)  16.8 us
    ppermute x8, starting transfers between devices, body(): other = lax.ppermute(jnp.where(first_core, later, here), 'phase', mates)  15.4 us
  transfers between devices with their start and end apart: 48, of which 24 were waited for; matrix products, arithmetic and copies ran while one was open for 5% of the time, Pallas kernels for 2%

profile of v3, /device:TPU:64, one launch (start us, length us, event | category | flops | bytes accessed | tf_op | source)
XLA Modules:
  0.0 346.3 jit_solution(17268077169378136173)
XLA Ops:
  6.5 6.9 %collective-permute-start.1 = (bf16[4160,128]{1,0:T(8,128)(2,1)S(1)}, bf16[4160,128]{1,0:T(8,128)(2,1)S(1)}, u32[]{:S(2)}, u32[]{:S(2)}) collective-permute-start(bf16[4160,128]{1,0:T(8,128)(2,1)S(1)} %pad_maximum_fusion.first), channel_id=1, source_target_pairs={{0,448},{32,480},{64,0},{96,32},{128,64},{160,96},{192,128},{224,1... | collective-permute-start | bytes 3194888 | tf_op jit(solution)/shard_map/ppermute | solution.py:216
  20.6 13.6 %collective-permute-done.1.first = bf16[4160,128]{1,0:T(8,128)(2,1)S(1)} collective-permute-done((bf16[4160,128]{1,0:T(8,128)(2,1)S(1)}, bf16[4160,128]{1,0:T(8,128)(2,1)S(1)}, u32[]{:S(2)}, u32[]{:S(2)}) %collective-permute-start.1) | collective-permute-done | bytes 1064992 | tf_op jit(solution)/shard_map/ppermute | solution.py:216
  34.3 7.6 %collective-permute-start.2 = (bf16[4160,128]{1,0:T(8,128)(2,1)S(1)}, bf16[4160,128]{1,0:T(8,128)(2,1)S(1)}, u32[]{:S(2)}, u32[]{:S(2)}) collective-permute-start(bf16[4160,128]{1,0:T(8,128)(2,1)S(1)} %collective-permute-done.1.first), channel_id=1, source_target_pairs={{0,448},{32,480},{64,0},{96,32},{128,64},{160,96},{192,128},{224,1... | collective-permute-start | bytes 3194888 | tf_op jit(solution)/shard_map/ppermute | solution.py:225
  45.9 3.4 collective-permute-start.5
  51.9 2.4 collective-permute-start.3
  56.4 7.6 %collective-permute-start.6 = (bf16[1040,128]{1,0:T(8,128)(2,1)}, bf16[1040,128]{1,0:T(8,128)(2,1)}, u32[]{:S(2)}, u32[]{:S(2)}) collective-permute-start(bf16[1040,128]{1,0:T(8,128)(2,1)} %pad_maximum_fusion.2), channel_id=1, source_target_pairs={{0,31},{1,2},{2,1},{3,4},{4,3},{5,6},{6,5},{7,8},{8,7},{9,10},{10,... | collective-permute-start | bytes 798728 | tf_op jit(solution)/shard_map/ppermute | solution.py:210
  65.7 4.3 %collective-permute-start.4 = (bf16[512,256]{1,0:T(8,128)(2,1)}, bf16[512,256]{1,0:T(8,128)(2,1)S(1)}, u32[]{:S(2)}, u32[]{:S(2)}) collective-permute-start(bf16[512,256]{1,0:T(8,128)(2,1)} %bitcast.44), channel_id=1, source_target_pairs={{0,31},{1,2},{2,1},{3,4},{4,3},{5,6},{6,5},{7,8},{8,7},{9,10},{10,... | collective-permute-start | bytes 786440 | tf_op jit(solution)/shard_map/ppermute | solution.py:222
  70.1 9.1 %collective-permute-done.4.rb = bf16[512,256]{1,0:T(8,128)(2,1)S(1)} collective-permute-done((bf16[512,256]{1,0:T(8,128)(2,1)}, bf16[512,256]{1,0:T(8,128)(2,1)S(1)}, u32[]{:S(2)}, u32[]{:S(2)}) %collective-permute-start.4) | collective-permute-done | bytes 262176 | tf_op jit(solution)/shard_map/ppermute | solution.py:222
  81.1 2.8 two_steps.8.cur
  83.9 5.6 %collective-permute-start.9 = (bf16[4160,128]{1,0:T(8,128)(2,1)S(1)}, bf16[4160,128]{1,0:T(8,128)(2,1)S(1)}, u32[]{:S(2)}, u32[]{:S(2)}) collective-permute-start(bf16[4160,128]{1,0:T(8,128)(2,1)S(1)} %collective-permute-done.2.first), channel_id=1, source_target_pairs={{0,448},{32,480},{64,0},{96,32},{128,64},{160,96},{192,128},{224,1... | collective-permute-start | bytes 3194888 | tf_op jit(solution)/shard_map/ppermute | solution.py:225
  93.6 4.1 %collective-permute-start.13 = (bf16[1040,128]{1,0:T(8,128)(2,1)S(1)}, bf16[1040,128]{1,0:T(8,128)(2,1)S(1)}, u32[]{:S(2)}, u32[]{:S(2)}) collective-permute-start(bf16[1040,128]{1,0:T(8,128)(2,1)S(1)} %pad_maximum_fusion.4), channel_id=1, source_target_pairs={{0,31},{1,2},{2,1},{3,4},{4,3},{5,6},{6,5},{7,8},{8,7},{9,10},{10,... | collective-permute-start | bytes 798728 | tf_op jit(solution)/shard_map/ppermute | solution.py:210
  97.8 9.4 %collective-permute-done.first = bf16[4160,128]{1,0:T(8,128)(2,1)S(1)} collective-permute-done((bf16[4160,128]{1,0:T(8,128)(2,1)S(1)}, bf16[4160,128]{1,0:T(8,128)(2,1)S(1)}, u32[]{:S(2)}, u32[]{:S(2)}) %collective-permute-start) | collective-permute-done | bytes 1064992 | tf_op jit(solution)/shard_map/ppermute | solution.py:217
  109.1 4.1 %collective-permute-start.11 = (bf16[512,256]{1,0:T(8,128)(2,1)S(1)}, bf16[512,256]{1,0:T(8,128)(2,1)S(1)}, u32[]{:S(2)}, u32[]{:S(2)}) collective-permute-start(bf16[512,256]{1,0:T(8,128)(2,1)S(1)} %get-tuple-element.104), channel_id=1, source_target_pairs={{0,31},{1,2},{2,1},{3,4},{4,3},{5,6},{6,5},{7,8},{8,7},{9,10},{10,... | collective-permute-start | bytes 786440 | tf_op jit(solution)/shard_map/ppermute | solution.py:222
  115.5 5.3 %collective-permute-done.11.rb = bf16[512,256]{1,0:T(8,128)(2,1)S(1)} collective-permute-done((bf16[512,256]{1,0:T(8,128)(2,1)S(1)}, bf16[512,256]{1,0:T(8,128)(2,1)S(1)}, u32[]{:S(2)}, u32[]{:S(2)}) %collective-permute-start.11) | collective-permute-done | bytes 262176 | tf_op jit(solution)/shard_map/ppermute | solution.py:222
  122.2 4.8 %collective-permute-start.16 = (bf16[4160,128]{1,0:T(8,128)(2,1)S(1)}, bf16[4160,128]{1,0:T(8,128)(2,1)S(1)}, u32[]{:S(2)}, u32[]{:S(2)}) collective-permute-start(bf16[4160,128]{1,0:T(8,128)(2,1)S(1)} %collective-permute-done.9.first), channel_id=1, source_target_pairs={{0,448},{32,480},{64,0},{96,32},{128,64},{160,96},{192,128},{224,1... | collective-permute-start | bytes 3194888 | tf_op jit(solution)/shard_map/ppermute | solution.py:225
  129.2 4.1 %collective-permute-start.20 = (bf16[1040,128]{1,0:T(8,128)(2,1)S(1)}, bf16[1040,128]{1,0:T(8,128)(2,1)S(1)}, u32[]{:S(2)}, u32[]{:S(2)}) collective-permute-start(bf16[1040,128]{1,0:T(8,128)(2,1)S(1)} %pad_maximum_fusion.6), channel_id=1, source_target_pairs={{0,31},{1,2},{2,1},{3,4},{4,3},{5,6},{6,5},{7,8},{8,7},{9,10},{10,... | collective-permute-start | bytes 798728 | tf_op jit(solution)/shard_map/ppermute | solution.py:210
  135.3 7.9 %collective-permute-done.20.rim_b = bf16[1040,128]{1,0:T(8,128)(2,1)S(1)} collective-permute-done((bf16[1040,128]{1,0:T(8,128)(2,1)S(1)}, bf16[1040,128]{1,0:T(8,128)(2,1)S(1)}, u32[]{:S(2)}, u32[]{:S(2)}) %collective-permute-start.20) | collective-permute-done | bytes 266272 | tf_op jit(solution)/shard_map/ppermute | solution.py:210
  145.1 4.1 %collective-permute-start.18 = (bf16[512,256]{1,0:T(8,128)(2,1)S(1)}, bf16[512,256]{1,0:T(8,128)(2,1)S(1)}, u32[]{:S(2)}, u32[]{:S(2)}) collective-permute-start(bf16[512,256]{1,0:T(8,128)(2,1)S(1)} %get-tuple-element.102), channel_id=1, source_target_pairs={{0,31},{1,2},{2,1},{3,4},{4,3},{5,6},{6,5},{7,8},{8,7},{9,10},{10,... | collective-permute-start | bytes 786440 | tf_op jit(solution)/shard_map/ppermute | solution.py:222
  152.9 5.3 %collective-permute-done.18.rb = bf16[512,256]{1,0:T(8,128)(2,1)S(1)} collective-permute-done((bf16[512,256]{1,0:T(8,128)(2,1)S(1)}, bf16[512,256]{1,0:T(8,128)(2,1)S(1)}, u32[]{:S(2)}, u32[]{:S(2)}) %collective-permute-start.18) | collective-permute-done | bytes 262176 | tf_op jit(solution)/shard_map/ppermute | solution.py:222
  161.7 4.1 %collective-permute-start.25 = (bf16[1040,128]{1,0:T(8,128)(2,1)S(1)}, bf16[1040,128]{1,0:T(8,128)(2,1)S(1)}, u32[]{:S(2)}, u32[]{:S(2)}) collective-permute-start(bf16[1040,128]{1,0:T(8,128)(2,1)S(1)} %pad_maximum_fusion.8), channel_id=1, source_target_pairs={{0,31},{1,2},{2,1},{3,4},{4,3},{5,6},{6,5},{7,8},{8,7},{9,10},{10,... | collective-permute-start | bytes 798728 | tf_op jit(solution)/shard_map/ppermute | solution.py:210
  167.8 3.9 %collective-permute-start.22 = (bf16[512,256]{1,0:T(8,128)(2,1)S(1)}, bf16[512,256]{1,0:T(8,128)(2,1)S(1)}, u32[]{:S(2)}, u32[]{:S(2)}) collective-permute-start(bf16[512,256]{1,0:T(8,128)(2,1)S(1)} %get-tuple-element.101), channel_id=1, source_target_pairs={{0,1},{1,0},{2,3},{3,2},{4,5},{5,4},{6,7},{7,6},{8,9},{9,8},{10,11... | collective-permute-start | bytes 786440 | tf_op jit(solution)/shard_map/ppermute | solution.py:221
  171.8 3.9 %collective-permute-done.25.rim_b = bf16[1040,128]{1,0:T(8,128)(2,1)S(1)} collective-permute-done((bf16[1040,128]{1,0:T(8,128)(2,1)S(1)}, bf16[1040,128]{1,0:T(8,128)(2,1)S(1)}, u32[]{:S(2)}, u32[]{:S(2)}) %collective-permute-start.25) | collective-permute-done | bytes 266272 | tf_op jit(solution)/shard_map/ppermute | solution.py:210
  175.7 4.3 %collective-permute-start.23 = (bf16[512,256]{1,0:T(8,128)(2,1)S(1)}, bf16[512,256]{1,0:T(8,128)(2,1)S(1)}, u32[]{:S(2)}, u32[]{:S(2)}) collective-permute-start(bf16[512,256]{1,0:T(8,128)(2,1)S(1)} %get-tuple-element.100), channel_id=1, source_target_pairs={{0,31},{1,2},{2,1},{3,4},{4,3},{5,6},{6,5},{7,8},{8,7},{9,10},{10,... | collective-permute-start | bytes 786440 | tf_op jit(solution)/shard_map/ppermute | solution.py:222
  181.9 6.9 %collective-permute-done.23.rb = bf16[512,256]{1,0:T(8,128)(2,1)S(1)} collective-permute-done((bf16[512,256]{1,0:T(8,128)(2,1)S(1)}, bf16[512,256]{1,0:T(8,128)(2,1)S(1)}, u32[]{:S(2)}, u32[]{:S(2)}) %collective-permute-start.23) | collective-permute-done | bytes 262176 | tf_op jit(solution)/shard_map/ppermute | solution.py:222
  192.3 4.1 %collective-permute-start.30 = (bf16[1040,128]{1,0:T(8,128)(2,1)S(1)}, bf16[1040,128]{1,0:T(8,128)(2,1)S(1)}, u32[]{:S(2)}, u32[]{:S(2)}) collective-permute-start(bf16[1040,128]{1,0:T(8,128)(2,1)S(1)} %pad_maximum_fusion.10), channel_id=1, source_target_pairs={{0,31},{1,2},{2,1},{3,4},{4,3},{5,6},{6,5},{7,8},{8,7},{9,10},{10,... | collective-permute-start | bytes 798728 | tf_op jit(solution)/shard_map/ppermute | solution.py:210
  198.5 3.9 %collective-permute-start.27 = (bf16[512,256]{1,0:T(8,128)(2,1)S(1)}, bf16[512,256]{1,0:T(8,128)(2,1)S(1)}, u32[]{:S(2)}, u32[]{:S(2)}) collective-permute-start(bf16[512,256]{1,0:T(8,128)(2,1)S(1)} %get-tuple-element.99), channel_id=1, source_target_pairs={{0,1},{1,0},{2,3},{3,2},{4,5},{5,4},{6,7},{7,6},{8,9},{9,8},{10,11... | collective-permute-start | bytes 786440 | tf_op jit(solution)/shard_map/ppermute | solution.py:221
  202.4 5.0 %collective-permute-start.28 = (bf16[512,256]{1,0:T(8,128)(2,1)S(1)}, bf16[512,256]{1,0:T(8,128)(2,1)S(1)}, u32[]{:S(2)}, u32[]{:S(2)}) collective-permute-start(bf16[512,256]{1,0:T(8,128)(2,1)S(1)} %get-tuple-element.98), channel_id=1, source_target_pairs={{0,31},{1,2},{2,1},{3,4},{4,3},{5,6},{6,5},{7,8},{8,7},{9,10},{10,... | collective-permute-start | bytes 786440 | tf_op jit(solution)/shard_map/ppermute | solution.py:222
  207.7 4.9 %collective-permute-done.27.ra = bf16[512,256]{1,0:T(8,128)(2,1)S(1)} collective-permute-done((bf16[512,256]{1,0:T(8,128)(2,1)S(1)}, bf16[512,256]{1,0:T(8,128)(2,1)S(1)}, u32[]{:S(2)}, u32[]{:S(2)}) %collective-permute-start.27) | collective-permute-done | bytes 262176 | tf_op jit(solution)/shard_map/ppermute | solution.py:221
  212.5 3.0 collective-permute-done.28.rb
  219.0 5.0 %collective-permute-start.35 = (bf16[1040,128]{1,0:T(8,128)(2,1)S(1)}, bf16[1040,128]{1,0:T(8,128)(2,1)S(1)}, u32[]{:S(2)}, u32[]{:S(2)}) collective-permute-start(bf16[1040,128]{1,0:T(8,128)(2,1)S(1)} %pad_maximum_fusion.12), channel_id=1, source_target_pairs={{0,31},{1,2},{2,1},{3,4},{4,3},{5,6},{6,5},{7,8},{8,7},{9,10},{10,... | collective-permute-start | bytes 798728 | tf_op jit(solution)/shard_map/ppermute | solution.py:210
  226.1 3.9 %collective-permute-start.32 = (bf16[512,256]{1,0:T(8,128)(2,1)S(1)}, bf16[512,256]{1,0:T(8,128)(2,1)S(1)}, u32[]{:S(2)}, u32[]{:S(2)}) collective-permute-start(bf16[512,256]{1,0:T(8,128)(2,1)S(1)} %get-tuple-element.97), channel_id=1, source_target_pairs={{0,1},{1,0},{2,3},{3,2},{4,5},{5,4},{6,7},{7,6},{8,9},{9,8},{10,11... | collective-permute-start | bytes 786440 | tf_op jit(solution)/shard_map/ppermute | solution.py:221
  230.0 4.1 %collective-permute-start.33 = (bf16[512,256]{1,0:T(8,128)(2,1)S(1)}, bf16[512,256]{1,0:T(8,128)(2,1)S(1)}, u32[]{:S(2)}, u32[]{:S(2)}) collective-permute-start(bf16[512,256]{1,0:T(8,128)(2,1)S(1)} %get-tuple-element.96), channel_id=1, source_target_pairs={{0,31},{1,2},{2,1},{3,4},{4,3},{5,6},{6,5},{7,8},{8,7},{9,10},{10,... | collective-permute-start | bytes 786440 | tf_op jit(solution)/shard_map/ppermute | solution.py:222
  235.3 4.9 %collective-permute-done.32.ra = bf16[512,256]{1,0:T(8,128)(2,1)S(1)} collective-permute-done((bf16[512,256]{1,0:T(8,128)(2,1)S(1)}, bf16[512,256]{1,0:T(8,128)(2,1)S(1)}, u32[]{:S(2)}, u32[]{:S(2)}) %collective-permute-start.32) | collective-permute-done | bytes 262176 | tf_op jit(solution)/shard_map/ppermute | solution.py:221
  240.1 3.0 collective-permute-done.33.rb
  246.6 4.1 %collective-permute-start.40 = (bf16[1040,128]{1,0:T(8,128)(2,1)S(1)}, bf16[1040,128]{1,0:T(8,128)(2,1)S(1)}, u32[]{:S(2)}, u32[]{:S(2)}) collective-permute-start(bf16[1040,128]{1,0:T(8,128)(2,1)S(1)} %pad_maximum_fusion.14), channel_id=1, source_target_pairs={{0,31},{1,2},{2,1},{3,4},{4,3},{5,6},{6,5},{7,8},{8,7},{9,10},{10,... | collective-permute-start | bytes 798728 | tf_op jit(solution)/shard_map/ppermute | solution.py:210
  252.8 3.9 %collective-permute-start.37 = (bf16[512,256]{1,0:T(8,128)(2,1)S(1)}, bf16[512,256]{1,0:T(8,128)(2,1)S(1)}, u32[]{:S(2)}, u32[]{:S(2)}) collective-permute-start(bf16[512,256]{1,0:T(8,128)(2,1)S(1)} %get-tuple-element.95), channel_id=1, source_target_pairs={{0,1},{1,0},{2,3},{3,2},{4,5},{5,4},{6,7},{7,6},{8,9},{9,8},{10,11... | collective-permute-start | bytes 786440 | tf_op jit(solution)/shard_map/ppermute | solution.py:221
  256.7 5.0 %collective-permute-start.38 = (bf16[512,256]{1,0:T(8,128)(2,1)S(1)}, bf16[512,256]{1,0:T(8,128)(2,1)S(1)}, u32[]{:S(2)}, u32[]{:S(2)}) collective-permute-start(bf16[512,256]{1,0:T(8,128)(2,1)S(1)} %get-tuple-element.94), channel_id=1, source_target_pairs={{0,31},{1,2},{2,1},{3,4},{4,3},{5,6},{6,5},{7,8},{8,7},{9,10},{10,... | collective-permute-start | bytes 786440 | tf_op jit(solution)/shard_map/ppermute | solution.py:222
  262.0 4.9 %collective-permute-done.37.ra = bf16[512,256]{1,0:T(8,128)(2,1)S(1)} collective-permute-done((bf16[512,256]{1,0:T(8,128)(2,1)S(1)}, bf16[512,256]{1,0:T(8,128)(2,1)S(1)}, u32[]{:S(2)}, u32[]{:S(2)}) %collective-permute-start.37) | collective-permute-done | bytes 262176 | tf_op jit(solution)/shard_map/ppermute | solution.py:221
  266.8 3.0 collective-permute-done.38.rb
  273.4 5.0 %collective-permute-start.45 = (bf16[1040,128]{1,0:T(8,128)(2,1)S(1)}, bf16[1040,128]{1,0:T(8,128)(2,1)S(1)}, u32[]{:S(2)}, u32[]{:S(2)}) collective-permute-start(bf16[1040,128]{1,0:T(8,128)(2,1)S(1)} %pad_maximum_fusion.16), channel_id=1, source_target_pairs={{0,31},{1,2},{2,1},{3,4},{4,3},{5,6},{6,5},{7,8},{8,7},{9,10},{10,... | collective-permute-start | bytes 798728 | tf_op jit(solution)/shard_map/ppermute | solution.py:210
  280.4 3.9 %collective-permute-start.42 = (bf16[512,256]{1,0:T(8,128)(2,1)S(1)}, bf16[512,256]{1,0:T(8,128)(2,1)S(1)}, u32[]{:S(2)}, u32[]{:S(2)}) collective-permute-start(bf16[512,256]{1,0:T(8,128)(2,1)S(1)} %get-tuple-element.93), channel_id=1, source_target_pairs={{0,1},{1,0},{2,3},{3,2},{4,5},{5,4},{6,7},{7,6},{8,9},{9,8},{10,11... | collective-permute-start | bytes 786440 | tf_op jit(solution)/shard_map/ppermute | solution.py:221
  284.3 4.1 %collective-permute-start.43 = (bf16[512,256]{1,0:T(8,128)(2,1)S(1)}, bf16[512,256]{1,0:T(8,128)(2,1)S(1)}, u32[]{:S(2)}, u32[]{:S(2)}) collective-permute-start(bf16[512,256]{1,0:T(8,128)(2,1)S(1)} %get-tuple-element.92), channel_id=1, source_target_pairs={{0,31},{1,2},{2,1},{3,4},{4,3},{5,6},{6,5},{7,8},{8,7},{9,10},{10,... | collective-permute-start | bytes 786440 | tf_op jit(solution)/shard_map/ppermute | solution.py:222
  289.6 4.9 %collective-permute-done.42.ra = bf16[512,256]{1,0:T(8,128)(2,1)S(1)} collective-permute-done((bf16[512,256]{1,0:T(8,128)(2,1)S(1)}, bf16[512,256]{1,0:T(8,128)(2,1)S(1)}, u32[]{:S(2)}, u32[]{:S(2)}) %collective-permute-start.42) | collective-permute-done | bytes 262176 | tf_op jit(solution)/shard_map/ppermute | solution.py:221
  294.5 3.0 collective-permute-done.43.rb
  299.6 14.9 %all_to_all.10 = bf16[32,8,256]{2,1,0:T(8,128)(2,1)S(1)} all-to-all(bf16[32,8,256]{2,1,0:T(8,128)(2,1)S(1)} %fusion.1), channel_id=1, replica_groups=mesh['phase'=16,'rows'=32] {'rows'}, dimensions={0} | all-to-all | bytes 262144 | tf_op jit(solution)/shard_map/all_to_all | solution.py:163
  315.3 4.1 %all-to-all-start.1 = ((f32[32,8,256]{2,1,0:T(8,128)}), f32[32,8,256]{2,1,0:T(8,128)S(1)}, u32[]{:S(2)}, u32[]{:S(2)}) async-start(f32[32,8,256]{2,1,0:T(8,128)} %broadcast_in_dim.31), calls=%async_computation.1 | async-start | bytes 524288 | tf_op jit(solution)/shard_map/all_to_all | solution.py:166
  320.5 10.6 %all-to-all-done.1 = f32[32,8,256]{2,1,0:T(8,128)S(1)} async-done(((f32[32,8,256]{2,1,0:T(8,128)}), f32[32,8,256]{2,1,0:T(8,128)S(1)}, u32[]{:S(2)}, u32[]{:S(2)}) %all-to-all-start.1) | async-done | bytes 262176 | tf_op jit(solution)/shard_map/all_to_all | solution.py:166
  331.7 14.6 %factor_solve.1 = (f32[1024,256]{1,0:T(8,128)}, f32[256,256]{1,0:T(8,128)}) custom-call(f32[256,256]{1,0:T(8,128)} %multiply_bitcast_fusion.gram_ref, bf16[1024,256]{1,0:T(8,128)(2,1)} %bitcast.38), custom_call_target="tpu_custom_call" | custom-call | tf_op jit(solution)/shard_map/factor_solve/pallas_call | solution.py:146
  (138 shorter events, 81.3 us)
Async XLA Ops:
  6.5 27.8 %collective-permute-start.1 = (bf16[4160,128]{1,0:T(8,128)(2,1)S(1)}, bf16[4160,128]{1,0:T(8,128)(2,1)S(1)}, u32[]{:S(2)}, u32[]{:S(2)}) collective-permute-start(bf16[4160,128]{1,0:T(8,128)(2,1)S(1)} %pad_maximum_fusion.first), channel_id=1, source_target_pairs={{0,448},{32,480},{64,0},{96,32},{128,64},{160,96},{192,128},{224,1... | collective-permute-start | bytes 3194888 | tf_op jit(solution)/shard_map/ppermute | solution.py:216
  34.3 49.7 %collective-permute-start.2 = (bf16[4160,128]{1,0:T(8,128)(2,1)S(1)}, bf16[4160,128]{1,0:T(8,128)(2,1)S(1)}, u32[]{:S(2)}, u32[]{:S(2)}) collective-permute-start(bf16[4160,128]{1,0:T(8,128)(2,1)S(1)} %collective-permute-done.1.first), channel_id=1, source_target_pairs={{0,448},{32,480},{64,0},{96,32},{128,64},{160,96},{192,128},{224,1... | collective-permute-start | bytes 3194888 | tf_op jit(solution)/shard_map/ppermute | solution.py:225
  43.0 38.1 %collective-permute-start.7 = (bf16[4160,128]{1,0:T(8,128)(2,1)}, bf16[4160,128]{1,0:T(8,128)(2,1)}, u32[]{:S(2)}, u32[]{:S(2)}) collective-permute-start(bf16[4160,128]{1,0:T(8,128)(2,1)} %broadcast_select_fusion.7), channel_id=1, source_target_pairs={{0,32},{32,0},{64,96},{96,64},{128,160},{160,128},{192,224},{224,1... | collective-permute-start | bytes 3194888 | tf_op jit(solution)/shard_map/ppermute | solution.py:230
  45.9 35.2 %collective-permute-start.5 = (bf16[1040,128]{1,0:T(8,128)(2,1)}, bf16[1040,128]{1,0:T(8,128)(2,1)S(1)}, u32[]{:S(2)}, u32[]{:S(2)}) collective-permute-start(bf16[1040,128]{1,0:T(8,128)(2,1)} %pad_maximum_fusion.1), channel_id=1, source_target_pairs={{0,1},{1,0},{2,3},{3,2},{4,5},{5,4},{6,7},{7,6},{8,9},{9,8},{10,11... | collective-permute-start | bytes 798728 | tf_op jit(solution)/shard_map/ppermute | solution.py:210
  51.9 13.9 %collective-permute-start.3 = (bf16[512,256]{1,0:T(8,128)(2,1)}, bf16[512,256]{1,0:T(8,128)(2,1)}, u32[]{:S(2)}, u32[]{:S(2)}) collective-permute-start(bf16[512,256]{1,0:T(8,128)(2,1)} %bitcast.43), channel_id=1, source_target_pairs={{0,1},{1,0},{2,3},{3,2},{4,5},{5,4},{6,7},{7,6},{8,9},{9,8},{10,11... | collective-permute-start | bytes 786440 | tf_op jit(solution)/shard_map/ppermute | solution.py:221
  56.4 24.7 %collective-permute-start.6 = (bf16[1040,128]{1,0:T(8,128)(2,1)}, bf16[1040,128]{1,0:T(8,128)(2,1)}, u32[]{:S(2)}, u32[]{:S(2)}) collective-permute-start(bf16[1040,128]{1,0:T(8,128)(2,1)} %pad_maximum_fusion.2), channel_id=1, source_target_pairs={{0,31},{1,2},{2,1},{3,4},{4,3},{5,6},{6,5},{7,8},{8,7},{9,10},{10,... | collective-permute-start | bytes 798728 | tf_op jit(solution)/shard_map/ppermute | solution.py:210
  65.7 13.4 %collective-permute-start.4 = (bf16[512,256]{1,0:T(8,128)(2,1)}, bf16[512,256]{1,0:T(8,128)(2,1)S(1)}, u32[]{:S(2)}, u32[]{:S(2)}) collective-permute-start(bf16[512,256]{1,0:T(8,128)(2,1)} %bitcast.44), channel_id=1, source_target_pairs={{0,31},{1,2},{2,1},{3,4},{4,3},{5,6},{6,5},{7,8},{8,7},{9,10},{10,... | collective-permute-start | bytes 786440 | tf_op jit(solution)/shard_map/ppermute | solution.py:222
  79.2 28.1 %collective-permute-start = (bf16[4160,128]{1,0:T(8,128)(2,1)S(1)}, bf16[4160,128]{1,0:T(8,128)(2,1)S(1)}, u32[]{:S(2)}, u32[]{:S(2)}) collective-permute-start(bf16[4160,128]{1,0:T(8,128)(2,1)S(1)} %pad_maximum_fusion.first), channel_id=1, source_target_pairs={{0,64},{32,96},{64,128},{96,160},{128,192},{160,224},{192,256},{22... | collective-permute-start | bytes 3194888 | tf_op jit(solution)/shard_map/ppermute | solution.py:217
  83.9 38.3 %collective-permute-start.9 = (bf16[4160,128]{1,0:T(8,128)(2,1)S(1)}, bf16[4160,128]{1,0:T(8,128)(2,1)S(1)}, u32[]{:S(2)}, u32[]{:S(2)}) collective-permute-start(bf16[4160,128]{1,0:T(8,128)(2,1)S(1)} %collective-permute-done.2.first), channel_id=1, source_target_pairs={{0,448},{32,480},{64,0},{96,32},{128,64},{160,96},{192,128},{224,1... | collective-permute-start | bytes 3194888 | tf_op jit(solution)/shard_map/ppermute | solution.py:225
  89.7 31.1 %collective-permute-start.14 = (bf16[4160,128]{1,0:T(8,128)(2,1)S(1)}, bf16[4160,128]{1,0:T(8,128)(2,1)S(1)}, u32[]{:S(2)}, u32[]{:S(2)}) collective-permute-start(bf16[4160,128]{1,0:T(8,128)(2,1)S(1)} %broadcast_select_fusion.6), channel_id=1, source_target_pairs={{0,32},{32,0},{64,96},{96,64},{128,160},{160,128},{192,224},{224,1... | collective-permute-start | bytes 3194888 | tf_op jit(solution)/shard_map/ppermute | solution.py:230
  91.6 17.5 %collective-permute-start.12 = (bf16[1040,128]{1,0:T(8,128)(2,1)S(1)}, bf16[1040,128]{1,0:T(8,128)(2,1)S(1)}, u32[]{:S(2)}, u32[]{:S(2)}) collective-permute-start(bf16[1040,128]{1,0:T(8,128)(2,1)S(1)} %pad_maximum_fusion.3), channel_id=1, source_target_pairs={{0,1},{1,0},{2,3},{3,2},{4,5},{5,4},{6,7},{7,6},{8,9},{9,8},{10,11... | collective-permute-start | bytes 798728 | tf_op jit(solution)/shard_map/ppermute | solution.py:210
  93.6 19.7 %collective-permute-start.13 = (bf16[1040,128]{1,0:T(8,128)(2,1)S(1)}, bf16[1040,128]{1,0:T(8,128)(2,1)S(1)}, u32[]{:S(2)}, u32[]{:S(2)}) collective-permute-start(bf16[1040,128]{1,0:T(8,128)(2,1)S(1)} %pad_maximum_fusion.4), channel_id=1, source_target_pairs={{0,31},{1,2},{2,1},{3,4},{4,3},{5,6},{6,5},{7,8},{8,7},{9,10},{10,... | collective-permute-start | bytes 798728 | tf_op jit(solution)/shard_map/ppermute | solution.py:210
  107.2 8.3 %collective-permute-start.10 = (bf16[512,256]{1,0:T(8,128)(2,1)S(1)}, bf16[512,256]{1,0:T(8,128)(2,1)S(1)}, u32[]{:S(2)}, u32[]{:S(2)}) collective-permute-start(bf16[512,256]{1,0:T(8,128)(2,1)S(1)} %get-tuple-element.105), channel_id=1, source_target_pairs={{0,1},{1,0},{2,3},{3,2},{4,5},{5,4},{6,7},{7,6},{8,9},{9,8},{10,11... | collective-permute-start | bytes 786440 | tf_op jit(solution)/shard_map/ppermute | solution.py:221
  109.1 11.6 %collective-permute-start.11 = (bf16[512,256]{1,0:T(8,128)(2,1)S(1)}, bf16[512,256]{1,0:T(8,128)(2,1)S(1)}, u32[]{:S(2)}, u32[]{:S(2)}) collective-permute-start(bf16[512,256]{1,0:T(8,128)(2,1)S(1)} %get-tuple-element.104), channel_id=1, source_target_pairs={{0,31},{1,2},{2,1},{3,4},{4,3},{5,6},{6,5},{7,8},{8,7},{9,10},{10,... | collective-permute-start | bytes 786440 | tf_op jit(solution)/shard_map/ppermute | solution.py:222
  113.3 31.8 %collective-permute-start.8 = (bf16[4160,128]{1,0:T(8,128)(2,1)S(1)}, bf16[4160,128]{1,0:T(8,128)(2,1)S(1)}, u32[]{:S(2)}, u32[]{:S(2)}) collective-permute-start(bf16[4160,128]{1,0:T(8,128)(2,1)S(1)} %collective-permute-done.first), channel_id=1, source_target_pairs={{0,64},{32,96},{64,128},{96,160},{128,192},{160,224},{192,256},{22... | collective-permute-start | bytes 3194888 | tf_op jit(solution)/shard_map/ppermute | solution.py:229
  122.2 37.4 %collective-permute-start.16 = (bf16[4160,128]{1,0:T(8,128)(2,1)S(1)}, bf16[4160,128]{1,0:T(8,128)(2,1)S(1)}, u32[]{:S(2)}, u32[]{:S(2)}) collective-permute-start(bf16[4160,128]{1,0:T(8,128)(2,1)S(1)} %collective-permute-done.9.first), channel_id=1, source_target_pairs={{0,448},{32,480},{64,0},{96,32},{128,64},{160,96},{192,128},{224,1... | collective-permute-start | bytes 3194888 | tf_op jit(solution)/shard_map/ppermute | solution.py:225
  127.2 31.0 %collective-permute-start.21 = (bf16[4160,128]{1,0:T(8,128)(2,1)S(1)}, bf16[4160,128]{1,0:T(8,128)(2,1)S(1)}, u32[]{:S(2)}, u32[]{:S(2)}) collective-permute-start(bf16[4160,128]{1,0:T(8,128)(2,1)S(1)} %broadcast_select_fusion.5), channel_id=1, source_target_pairs={{0,32},{32,0},{64,96},{96,64},{128,160},{160,128},{192,224},{224,1... | collective-permute-start | bytes 3194888 | tf_op jit(solution)/shard_map/ppermute | solution.py:230
  129.2 14.0 %collective-permute-start.20 = (bf16[1040,128]{1,0:T(8,128)(2,1)S(1)}, bf16[1040,128]{1,0:T(8,128)(2,1)S(1)}, u32[]{:S(2)}, u32[]{:S(2)}) collective-permute-start(bf16[1040,128]{1,0:T(8,128)(2,1)S(1)} %pad_maximum_fusion.6), channel_id=1, source_target_pairs={{0,31},{1,2},{2,1},{3,4},{4,3},{5,6},{6,5},{7,8},{8,7},{9,10},{10,... | collective-permute-start | bytes 798728 | tf_op jit(solution)/shard_map/ppermute | solution.py:210
  133.3 16.0 %collective-permute-start.19 = (bf16[1040,128]{1,0:T(8,128)(2,1)S(1)}, bf16[1040,128]{1,0:T(8,128)(2,1)S(1)}, u32[]{:S(2)}, u32[]{:S(2)}) collective-permute-start(bf16[1040,128]{1,0:T(8,128)(2,1)S(1)} %pad_maximum_fusion.5), channel_id=1, source_target_pairs={{0,1},{1,0},{2,3},{3,2},{4,5},{5,4},{6,7},{7,6},{8,9},{9,8},{10,11... | collective-permute-start | bytes 798728 | tf_op jit(solution)/shard_map/ppermute | solution.py:210
  143.2 9.7 %collective-permute-start.17 = (bf16[512,256]{1,0:T(8,128)(2,1)S(1)}, bf16[512,256]{1,0:T(8,128)(2,1)S(1)}, u32[]{:S(2)}, u32[]{:S(2)}) collective-permute-start(bf16[512,256]{1,0:T(8,128)(2,1)S(1)} %get-tuple-element.103), channel_id=1, source_target_pairs={{0,1},{1,0},{2,3},{3,2},{4,5},{5,4},{6,7},{7,6},{8,9},{9,8},{10,11... | collective-permute-start | bytes 786440 | tf_op jit(solution)/shard_map/ppermute | solution.py:221
  145.1 13.1 %collective-permute-start.18 = (bf16[512,256]{1,0:T(8,128)(2,1)S(1)}, bf16[512,256]{1,0:T(8,128)(2,1)S(1)}, u32[]{:S(2)}, u32[]{:S(2)}) collective-permute-start(bf16[512,256]{1,0:T(8,128)(2,1)S(1)} %get-tuple-element.102), channel_id=1, source_target_pairs={{0,31},{1,2},{2,1},{3,4},{4,3},{5,6},{6,5},{7,8},{8,7},{9,10},{10,... | collective-permute-start | bytes 786440 | tf_op jit(solution)/shard_map/ppermute | solution.py:222
  149.3 40.9 %collective-permute-start.15 = (bf16[4160,128]{1,0:T(8,128)(2,1)S(1)}, bf16[4160,128]{1,0:T(8,128)(2,1)S(1)}, u32[]{:S(2)}, u32[]{:S(2)}) collective-permute-start(bf16[4160,128]{1,0:T(8,128)(2,1)S(1)} %collective-permute-done.8.first), channel_id=1, source_target_pairs={{0,64},{32,96},{64,128},{96,160},{128,192},{160,224},{192,256},{22... | collective-permute-start | bytes 3194888 | tf_op jit(solution)/shard_map/ppermute | solution.py:229
  159.7 29.0 %collective-permute-start.26 = (bf16[4160,128]{1,0:T(8,128)(2,1)S(1)}, bf16[4160,128]{1,0:T(8,128)(2,1)S(1)}, u32[]{:S(2)}, u32[]{:S(2)}) collective-permute-start(bf16[4160,128]{1,0:T(8,128)(2,1)S(1)} %broadcast_select_fusion.4), channel_id=1, source_target_pairs={{0,32},{32,0},{64,96},{96,64},{128,160},{160,128},{192,224},{224,1... | collective-permute-start | bytes 3194888 | tf_op jit(solution)/shard_map/ppermute | solution.py:230
  161.7 14.0 %collective-permute-start.25 = (bf16[1040,128]{1,0:T(8,128)(2,1)S(1)}, bf16[1040,128]{1,0:T(8,128)(2,1)S(1)}, u32[]{:S(2)}, u32[]{:S(2)}) collective-permute-start(bf16[1040,128]{1,0:T(8,128)(2,1)S(1)} %pad_maximum_fusion.8), channel_id=1, source_target_pairs={{0,31},{1,2},{2,1},{3,4},{4,3},{5,6},{6,5},{7,8},{8,7},{9,10},{10,... | collective-permute-start | bytes 798728 | tf_op jit(solution)/shard_map/ppermute | solution.py:210
  165.9 14.2 %collective-permute-start.24 = (bf16[1040,128]{1,0:T(8,128)(2,1)S(1)}, bf16[1040,128]{1,0:T(8,128)(2,1)S(1)}, u32[]{:S(2)}, u32[]{:S(2)}) collective-permute-start(bf16[1040,128]{1,0:T(8,128)(2,1)S(1)} %pad_maximum_fusion.7), channel_id=1, source_target_pairs={{0,1},{1,0},{2,3},{3,2},{4,5},{5,4},{6,7},{7,6},{8,9},{9,8},{10,11... | collective-permute-start | bytes 798728 | tf_op jit(solution)/shard_map/ppermute | solution.py:210
  167.8 14.1 %collective-permute-start.22 = (bf16[512,256]{1,0:T(8,128)(2,1)S(1)}, bf16[512,256]{1,0:T(8,128)(2,1)S(1)}, u32[]{:S(2)}, u32[]{:S(2)}) collective-permute-start(bf16[512,256]{1,0:T(8,128)(2,1)S(1)} %get-tuple-element.101), channel_id=1, source_target_pairs={{0,1},{1,0},{2,3},{3,2},{4,5},{5,4},{6,7},{7,6},{8,9},{9,8},{10,11... | collective-permute-start | bytes 786440 | tf_op jit(solution)/shard_map/ppermute | solution.py:221
  175.7 13.1 %collective-permute-start.23 = (bf16[512,256]{1,0:T(8,128)(2,1)S(1)}, bf16[512,256]{1,0:T(8,128)(2,1)S(1)}, u32[]{:S(2)}, u32[]{:S(2)}) collective-permute-start(bf16[512,256]{1,0:T(8,128)(2,1)S(1)} %get-tuple-element.100), channel_id=1, source_target_pairs={{0,31},{1,2},{2,1},{3,4},{4,3},{5,6},{6,5},{7,8},{8,7},{9,10},{10,... | collective-permute-start | bytes 786440 | tf_op jit(solution)/shard_map/ppermute | solution.py:222
  190.4 25.1 %collective-permute-start.31 = (bf16[4160,128]{1,0:T(8,128)(2,1)S(1)}, bf16[4160,128]{1,0:T(8,128)(2,1)S(1)}, u32[]{:S(2)}, u32[]{:S(2)}) collective-permute-start(bf16[4160,128]{1,0:T(8,128)(2,1)S(1)} %broadcast_select_fusion.3), channel_id=1, source_target_pairs={{0,32},{32,0},{64,96},{96,64},{128,160},{160,128},{192,224},{224,1... | collective-permute-start | bytes 3194888 | tf_op jit(solution)/shard_map/ppermute | solution.py:230
  192.3 15.2 %collective-permute-start.30 = (bf16[1040,128]{1,0:T(8,128)(2,1)S(1)}, bf16[1040,128]{1,0:T(8,128)(2,1)S(1)}, u32[]{:S(2)}, u32[]{:S(2)}) collective-permute-start(bf16[1040,128]{1,0:T(8,128)(2,1)S(1)} %pad_maximum_fusion.10), channel_id=1, source_target_pairs={{0,31},{1,2},{2,1},{3,4},{4,3},{5,6},{6,5},{7,8},{8,7},{9,10},{10,... | collective-permute-start | bytes 798728 | tf_op jit(solution)/shard_map/ppermute | solution.py:210
  196.5 11.2 %collective-permute-start.29 = (bf16[1040,128]{1,0:T(8,128)(2,1)S(1)}, bf16[1040,128]{1,0:T(8,128)(2,1)S(1)}, u32[]{:S(2)}, u32[]{:S(2)}) collective-permute-start(bf16[1040,128]{1,0:T(8,128)(2,1)S(1)} %pad_maximum_fusion.9), channel_id=1, source_target_pairs={{0,1},{1,0},{2,3},{3,2},{4,5},{5,4},{6,7},{7,6},{8,9},{9,8},{10,11... | collective-permute-start | bytes 798728 | tf_op jit(solution)/shard_map/ppermute | solution.py:210
  198.5 14.1 %collective-permute-start.27 = (bf16[512,256]{1,0:T(8,128)(2,1)S(1)}, bf16[512,256]{1,0:T(8,128)(2,1)S(1)}, u32[]{:S(2)}, u32[]{:S(2)}) collective-permute-start(bf16[512,256]{1,0:T(8,128)(2,1)S(1)} %get-tuple-element.99), channel_id=1, source_target_pairs={{0,1},{1,0},{2,3},{3,2},{4,5},{5,4},{6,7},{7,6},{8,9},{9,8},{10,11... | collective-permute-start | bytes 786440 | tf_op jit(solution)/shard_map/ppermute | solution.py:221
  202.4 13.1 %collective-permute-start.28 = (bf16[512,256]{1,0:T(8,128)(2,1)S(1)}, bf16[512,256]{1,0:T(8,128)(2,1)S(1)}, u32[]{:S(2)}, u32[]{:S(2)}) collective-permute-start(bf16[512,256]{1,0:T(8,128)(2,1)S(1)} %get-tuple-element.98), channel_id=1, source_target_pairs={{0,31},{1,2},{2,1},{3,4},{4,3},{5,6},{6,5},{7,8},{8,7},{9,10},{10,... | collective-permute-start | bytes 786440 | tf_op jit(solution)/shard_map/ppermute | solution.py:222
  217.1 26.0 %collective-permute-start.36 = (bf16[4160,128]{1,0:T(8,128)(2,1)S(1)}, bf16[4160,128]{1,0:T(8,128)(2,1)S(1)}, u32[]{:S(2)}, u32[]{:S(2)}) collective-permute-start(bf16[4160,128]{1,0:T(8,128)(2,1)S(1)} %broadcast_select_fusion.2), channel_id=1, source_target_pairs={{0,32},{32,0},{64,96},{96,64},{128,160},{160,128},{192,224},{224,1... | collective-permute-start | bytes 3194888 | tf_op jit(solution)/shard_map/ppermute | solution.py:230
  219.0 15.2 %collective-permute-start.35 = (bf16[1040,128]{1,0:T(8,128)(2,1)S(1)}, bf16[1040,128]{1,0:T(8,128)(2,1)S(1)}, u32[]{:S(2)}, u32[]{:S(2)}) collective-permute-start(bf16[1040,128]{1,0:T(8,128)(2,1)S(1)} %pad_maximum_fusion.12), channel_id=1, source_target_pairs={{0,31},{1,2},{2,1},{3,4},{4,3},{5,6},{6,5},{7,8},{8,7},{9,10},{10,... | collective-permute-start | bytes 798728 | tf_op jit(solution)/shard_map/ppermute | solution.py:210
  224.1 11.2 %collective-permute-start.34 = (bf16[1040,128]{1,0:T(8,128)(2,1)S(1)}, bf16[1040,128]{1,0:T(8,128)(2,1)S(1)}, u32[]{:S(2)}, u32[]{:S(2)}) collective-permute-start(bf16[1040,128]{1,0:T(8,128)(2,1)S(1)} %pad_maximum_fusion.11), channel_id=1, source_target_pairs={{0,1},{1,0},{2,3},{3,2},{4,5},{5,4},{6,7},{7,6},{8,9},{9,8},{10,11... | collective-permute-start | bytes 798728 | tf_op jit(solution)/shard_map/ppermute | solution.py:210
  226.1 14.1 %collective-permute-start.32 = (bf16[512,256]{1,0:T(8,128)(2,1)S(1)}, bf16[512,256]{1,0:T(8,128)(2,1)S(1)}, u32[]{:S(2)}, u32[]{:S(2)}) collective-permute-start(bf16[512,256]{1,0:T(8,128)(2,1)S(1)} %get-tuple-element.97), channel_id=1, source_target_pairs={{0,1},{1,0},{2,3},{3,2},{4,5},{5,4},{6,7},{7,6},{8,9},{9,8},{10,11... | collective-permute-start | bytes 786440 | tf_op jit(solution)/shard_map/ppermute | solution.py:221
  230.0 13.1 %collective-permute-start.33 = (bf16[512,256]{1,0:T(8,128)(2,1)S(1)}, bf16[512,256]{1,0:T(8,128)(2,1)S(1)}, u32[]{:S(2)}, u32[]{:S(2)}) collective-permute-start(bf16[512,256]{1,0:T(8,128)(2,1)S(1)} %get-tuple-element.96), channel_id=1, source_target_pairs={{0,31},{1,2},{2,1},{3,4},{4,3},{5,6},{6,5},{7,8},{8,7},{9,10},{10,... | collective-permute-start | bytes 786440 | tf_op jit(solution)/shard_map/ppermute | solution.py:222
  244.7 25.1 %collective-permute-start.41 = (bf16[4160,128]{1,0:T(8,128)(2,1)S(1)}, bf16[4160,128]{1,0:T(8,128)(2,1)S(1)}, u32[]{:S(2)}, u32[]{:S(2)}) collective-permute-start(bf16[4160,128]{1,0:T(8,128)(2,1)S(1)} %broadcast_select_fusion.1), channel_id=1, source_target_pairs={{0,32},{32,0},{64,96},{96,64},{128,160},{160,128},{192,224},{224,1... | collective-permute-start | bytes 3194888 | tf_op jit(solution)/shard_map/ppermute | solution.py:230
  246.6 15.2 %collective-permute-start.40 = (bf16[1040,128]{1,0:T(8,128)(2,1)S(1)}, bf16[1040,128]{1,0:T(8,128)(2,1)S(1)}, u32[]{:S(2)}, u32[]{:S(2)}) collective-permute-start(bf16[1040,128]{1,0:T(8,128)(2,1)S(1)} %pad_maximum_fusion.14), channel_id=1, source_target_pairs={{0,31},{1,2},{2,1},{3,4},{4,3},{5,6},{6,5},{7,8},{8,7},{9,10},{10,... | collective-permute-start | bytes 798728 | tf_op jit(solution)/shard_map/ppermute | solution.py:210
  250.8 11.2 %collective-permute-start.39 = (bf16[1040,128]{1,0:T(8,128)(2,1)S(1)}, bf16[1040,128]{1,0:T(8,128)(2,1)S(1)}, u32[]{:S(2)}, u32[]{:S(2)}) collective-permute-start(bf16[1040,128]{1,0:T(8,128)(2,1)S(1)} %pad_maximum_fusion.13), channel_id=1, source_target_pairs={{0,1},{1,0},{2,3},{3,2},{4,5},{5,4},{6,7},{7,6},{8,9},{9,8},{10,11... | collective-permute-start | bytes 798728 | tf_op jit(solution)/shard_map/ppermute | solution.py:210
  252.8 14.1 %collective-permute-start.37 = (bf16[512,256]{1,0:T(8,128)(2,1)S(1)}, bf16[512,256]{1,0:T(8,128)(2,1)S(1)}, u32[]{:S(2)}, u32[]{:S(2)}) collective-permute-start(bf16[512,256]{1,0:T(8,128)(2,1)S(1)} %get-tuple-element.95), channel_id=1, source_target_pairs={{0,1},{1,0},{2,3},{3,2},{4,5},{5,4},{6,7},{7,6},{8,9},{9,8},{10,11... | collective-permute-start | bytes 786440 | tf_op jit(solution)/shard_map/ppermute | solution.py:221
  256.7 13.1 %collective-permute-start.38 = (bf16[512,256]{1,0:T(8,128)(2,1)S(1)}, bf16[512,256]{1,0:T(8,128)(2,1)S(1)}, u32[]{:S(2)}, u32[]{:S(2)}) collective-permute-start(bf16[512,256]{1,0:T(8,128)(2,1)S(1)} %get-tuple-element.94), channel_id=1, source_target_pairs={{0,31},{1,2},{2,1},{3,4},{4,3},{5,6},{6,5},{7,8},{8,7},{9,10},{10,... | collective-permute-start | bytes 786440 | tf_op jit(solution)/shard_map/ppermute | solution.py:222
  271.4 26.0 %collective-permute-start.46 = (bf16[4160,128]{1,0:T(8,128)(2,1)S(1)}, bf16[4160,128]{1,0:T(8,128)(2,1)S(1)}, u32[]{:S(2)}, u32[]{:S(2)}) collective-permute-start(bf16[4160,128]{1,0:T(8,128)(2,1)S(1)} %broadcast_select_fusion), channel_id=1, source_target_pairs={{0,32},{32,0},{64,96},{96,64},{128,160},{160,128},{192,224},{224,1... | collective-permute-start | bytes 3194888 | tf_op jit(solution)/shard_map/ppermute | solution.py:230
  273.4 15.1 %collective-permute-start.45 = (bf16[1040,128]{1,0:T(8,128)(2,1)S(1)}, bf16[1040,128]{1,0:T(8,128)(2,1)S(1)}, u32[]{:S(2)}, u32[]{:S(2)}) collective-permute-start(bf16[1040,128]{1,0:T(8,128)(2,1)S(1)} %pad_maximum_fusion.16), channel_id=1, source_target_pairs={{0,31},{1,2},{2,1},{3,4},{4,3},{5,6},{6,5},{7,8},{8,7},{9,10},{10,... | collective-permute-start | bytes 798728 | tf_op jit(solution)/shard_map/ppermute | solution.py:210
  278.4 11.2 %collective-permute-start.44 = (bf16[1040,128]{1,0:T(8,128)(2,1)S(1)}, bf16[1040,128]{1,0:T(8,128)(2,1)S(1)}, u32[]{:S(2)}, u32[]{:S(2)}) collective-permute-start(bf16[1040,128]{1,0:T(8,128)(2,1)S(1)} %pad_maximum_fusion.15), channel_id=1, source_target_pairs={{0,1},{1,0},{2,3},{3,2},{4,5},{5,4},{6,7},{7,6},{8,9},{9,8},{10,11... | collective-permute-start | bytes 798728 | tf_op jit(solution)/shard_map/ppermute | solution.py:210
  280.4 14.1 %collective-permute-start.42 = (bf16[512,256]{1,0:T(8,128)(2,1)S(1)}, bf16[512,256]{1,0:T(8,128)(2,1)S(1)}, u32[]{:S(2)}, u32[]{:S(2)}) collective-permute-start(bf16[512,256]{1,0:T(8,128)(2,1)S(1)} %get-tuple-element.93), channel_id=1, source_target_pairs={{0,1},{1,0},{2,3},{3,2},{4,5},{5,4},{6,7},{7,6},{8,9},{9,8},{10,11... | collective-permute-start | bytes 786440 | tf_op jit(solution)/shard_map/ppermute | solution.py:221
  284.3 13.1 %collective-permute-start.43 = (bf16[512,256]{1,0:T(8,128)(2,1)S(1)}, bf16[512,256]{1,0:T(8,128)(2,1)S(1)}, u32[]{:S(2)}, u32[]{:S(2)}) collective-permute-start(bf16[512,256]{1,0:T(8,128)(2,1)S(1)} %get-tuple-element.92), channel_id=1, source_target_pairs={{0,31},{1,2},{2,1},{3,4},{4,3},{5,6},{6,5},{7,8},{8,7},{9,10},{10,... | collective-permute-start | bytes 786440 | tf_op jit(solution)/shard_map/ppermute | solution.py:222
  315.3 15.7 %all-to-all-start.1 = ((f32[32,8,256]{2,1,0:T(8,128)}), f32[32,8,256]{2,1,0:T(8,128)S(1)}, u32[]{:S(2)}, u32[]{:S(2)}) async-start(f32[32,8,256]{2,1,0:T(8,128)} %broadcast_in_dim.31), calls=%async_computation.1 | async-start | bytes 524288 | tf_op jit(solution)/shard_map/all_to_all | solution.py:166
  (2 other events, 30.4 us)

commit v4 on v3

--- a/solution.py
+++ b/solution.py
@@ -1,3 +1,5 @@
+import functools
+
 import jax
 import jax.numpy as jnp
 from jax import lax
@@ -11,13 +13,13 @@
 HALF = 4 * TILE
 DEAD = 7
 
-
-def visit_kernel(cur, ra, rb, rim_a, rim_b, first, second, out, wide, mid):
+def visit_kernel(cur_a, cur_b, ra, rb, rim_a, rim_b, first, second, out_a, out_b, wide, mid):
     for n in range(4):
         wide[(3 - n) * TILE : (4 - n) * TILE, :] = ra[n * TILE : (n + 1) * TILE, :]
         wide[(15 - n) * TILE : (16 - n) * TILE, :] = rb[n * TILE : (n + 1) * TILE, :]
-    wide[4 * TILE : 12 * TILE, :] = cur[...]
-    zero = jnp.zeros((TILE, cur.shape[1]), cur.dtype)
+    wide[4 * TILE : 8 * TILE, :] = cur_a[...]
+    wide[8 * TILE : 12 * TILE, :] = cur_b[...]
+    zero = jnp.zeros((TILE, cur_a.shape[1]), cur_a.dtype)
     wide[16 * TILE :, :] = zero
     mid[12 * TILE :, :] = zero
 
@@ -41,7 +43,7 @@
             right = jnp.concatenate([block(j), block(j + 1)], axis=0)
             part = jnp.dot(left, right, preferred_element_type=jnp.float32)
             total = part if total is None else total + part
-        return total.astype(out.dtype)
+        return total.astype(out_a.dtype)
 
     for n in range(2):
         c = 1 - n
@@ -51,31 +53,96 @@
     for c in range(8):
         mid[(c + 2) * TILE : (c + 3) * TILE, :] = row(first, c, wide, c + 4, 1, 16)
     for c in range(8):
-        out[c * TILE : (c + 1) * TILE, :] = row(second, c, mid, c + 2, 1, 12)
-
-
-def visit(cur, ra, rb, rim_a, rim_b, first, second):
+        half = out_a if c < 4 else out_b
+        half[c % 4 * TILE : (c % 4 + 1) * TILE, :] = row(second, c, mid, c + 2, 1, 12)
+
+def visit(halves, ra, rb, rim_a, rim_b, first, second):
     vmem = pl.BlockSpec(memory_space=pltpu.VMEM)
-    columns = cur.shape[1]
+    shape = jax.ShapeDtypeStruct(halves[0].shape, halves[0].dtype)
+    columns = shape.shape[1]
     return pl.pallas_call(
         visit_kernel,
-        out_shape=jax.ShapeDtypeStruct(cur.shape, cur.dtype),
-        in_specs=[vmem] * 7,
-        out_specs=vmem,
+        out_shape=(shape, shape),
+        in_specs=[vmem] * 8,
+        out_specs=(vmem, vmem),
         scratch_shapes=[
-            pltpu.VMEM((17 * TILE, columns), cur.dtype),
-            pltpu.VMEM((13 * TILE, columns), cur.dtype),
+            pltpu.VMEM((17 * TILE, columns), shape.dtype),
+            pltpu.VMEM((13 * TILE, columns), shape.dtype),
         ],
         compiler_params=pltpu.CompilerParams(vmem_limit_bytes=24 * 1024 * 1024),
         cost_estimate=pl.CostEstimate(flops=700_000_000, bytes_accessed=4_000_000, transcendentals=0),
         name="two_steps",
-    )(cur, ra, rb, rim_a, rim_b, first, second)
+    )(*halves, ra, rb, rim_a, rim_b, first, second)
+
+def pack_kernel(total, info, cols, counts, blocks, packed, rim_a, rim_b):
+    even = info[0]
+    block_rows, slots = cols.shape
+    span = slots * TILE
+    lines = block_rows * span
+    line = lax.broadcasted_iota(jnp.int32, (8, TILE), 0)
+    for c in range(0, block_rows, 2):
+        tables = []
+        for i in range(2):
+            source = jnp.where(even == 1, block_rows - 1 - (c + i), c + i)
+            packed[(c + i) * span : (c + i + 1) * span, :] = blocks[
+                pl.ds(pl.multiple_of(source * span, span), span), :
+            ]
+            table = jnp.full((8, TILE), DEAD, jnp.int32)
+            for j in range(slots):
+                offset = lax.rem(cols[source, j] - info[1] - source + HB + total, total)
+                offset = jnp.where(even == 1, 2 * HB - offset, offset)
+                value = jnp.where(j < counts[source], offset, DEAD)
+                table = jnp.where(line == j, value, table)
+            tables.append(table.astype(jnp.float32))
+        both = jnp.concatenate(tables, axis=0).astype(packed.dtype)
+        packed[lines + c * 8 : lines + c * 8 + 16, :] = both
+    edge = HB * span
+    rim_a[:edge, :] = packed[:edge, :]
+    rim_a[edge:, :] = packed[lines : lines + 8 * HB, :]
+    rim_b[:edge, :] = packed[lines - edge : lines, :]
+    rim_b[edge:, :] = packed[lines + 8 * (block_rows - HB) :, :]
+
+def pack(total, info, cols, counts, blocks):
+    block_rows, slots, tile, _ = blocks.shape
+    lines = block_rows * slots * tile
+    vmem = pl.BlockSpec(memory_space=pltpu.VMEM)
+    smem = pl.BlockSpec(memory_space=pltpu.SMEM)
+    rim = jax.ShapeDtypeStruct((HB * slots * tile + 8 * HB, tile), blocks.dtype)
+    whole = jax.ShapeDtypeStruct((lines + 8 * block_rows, tile), blocks.dtype)
+    return pl.pallas_call(
+        functools.partial(pack_kernel, total),
+        out_shape=(whole, rim, rim),
+        in_specs=[smem, smem, smem, vmem],
+        out_specs=(vmem, vmem, vmem),
+        compiler_params=pltpu.CompilerParams(vmem_limit_bytes=16 * 1024 * 1024),
+        name="pack_operator",
+    )(info, cols, counts, blocks.reshape(lines, tile))
+
+def halve_kernel(info, start, half_a, half_b):
+    block_rows = start.shape[0] // TILE
+    for c in range(block_rows):
+        source = jnp.where(info[0] == 1, block_rows - 1 - c, c)
+        half = half_a if c < 4 else half_b
+        half[c % 4 * TILE : (c % 4 + 1) * TILE, :] = start[
+            pl.ds(pl.multiple_of(source * TILE, TILE), TILE), :
+        ]
+
+def halve(info, start):
+    vmem = pl.BlockSpec(memory_space=pltpu.VMEM)
+    half = jax.ShapeDtypeStruct((HALF, start.shape[1]), start.dtype)
+    return pl.pallas_call(
+        halve_kernel,
+        out_shape=(half, half),
+        in_specs=[pl.BlockSpec(memory_space=pltpu.SMEM), vmem],
+        out_specs=(vmem, vmem),
+        compiler_params=pltpu.CompilerParams(vmem_limit_bytes=8 * 1024 * 1024),
+        name="halve_start",
+    )(info, start)
 
 
 NB = 16
 
-
-def factor_kernel(gram_ref, arrived_ref, basis_ref, factor_ref, a_ref, w_ref):
+def factor_kernel(info, gram_ref, half_a, half_b, basis_ref, factor_ref, a_ref, w_ref):
     size = gram_ref.shape[0]
     a_ref[...] = gram_ref[...]
     row_i = lax.broadcasted_iota(jnp.int32, (size, size), 0)
@@ -130,30 +197,28 @@
     high = w.astype(jnp.bfloat16)
     low = (w - high.astype(jnp.float32)).astype(jnp.bfloat16)
     dims = (((1,), (1,)), ((), ()))
-
-    @pl.loop(0, arrived_ref.shape[0], step=256)
-    def _(piece):
-        at = pl.ds(pl.multiple_of(piece, 256), 256)
-        rows = arrived_ref[at, :]
-        basis_ref[at, :] = lax.dot_general(
+    for c in range(8):
+        half = half_a if c < 4 else half_b
+        rows = half[c % 4 * TILE : (c % 4 + 1) * TILE, :]
+        place = jnp.where(info[0] == 1, 7 - c, c)
+        basis_ref[pl.ds(pl.multiple_of(place * TILE, TILE), TILE), :] = lax.dot_general(
             rows, high, dims, preferred_element_type=jnp.float32
         ) + lax.dot_general(rows, low, dims, preferred_element_type=jnp.float32)
 
-
-def finish(gram, arrived):
+def finish(info, gram, halves):
     size = gram.shape[0]
     vmem = pl.BlockSpec(memory_space=pltpu.VMEM)
     return pl.pallas_call(
         factor_kernel,
         out_shape=(
-            jax.ShapeDtypeStruct(arrived.shape, jnp.float32),
+            jax.ShapeDtypeStruct((2 * HALF, size), jnp.float32),
             jax.ShapeDtypeStruct((size, size), jnp.float32),
         ),
-        in_specs=[vmem, vmem],
+        in_specs=[pl.BlockSpec(memory_space=pltpu.SMEM), vmem, vmem, vmem],
         out_specs=(vmem, vmem),
         scratch_shapes=[pltpu.VMEM((size, size), jnp.float32), pltpu.VMEM((size, size), jnp.float32)],
         name="factor_solve",
-    )(gram, arrived)
+    )(info, gram, *halves)
 
 
 def sum_over_rows(term):
@@ -166,31 +231,13 @@
     return lax.all_to_all(copies, "rows", 0, 0, tiled=True).reshape(size, size)
 
 
-def packed_operator(blocks, cols, counts, even):
-    block_rows, slots, tile, _ = blocks.shape
-    owners = lax.axis_size("rows")
-    total = block_rows * owners
-    index = lax.axis_index("rows") * block_rows + jnp.arange(block_rows, dtype=jnp.int32)
-    offset = jnp.mod(cols - index[:, None] + HB, total) - HB
-    offset = jnp.where(even, -offset, offset) + HB
-    live = jnp.arange(slots, dtype=jnp.int32)[None, :] < counts[:, None]
-    place = jnp.where(live, offset, DEAD)
-    place = jnp.where(even, place[::-1], place)
-    place = jnp.pad(place, ((0, 0), (0, 8 - slots)), constant_values=DEAD)
-    table = jnp.broadcast_to(
-        place.reshape(block_rows * 8, 1).astype(jnp.bfloat16), (block_rows * 8, tile)
-    )
-    blocks = jnp.where(even, blocks[::-1], blocks)
-    return jnp.concatenate([blocks.reshape(block_rows * slots * tile, tile), table], axis=0)
-
-
 def body(start, blocks, cols, counts):
     block_rows, slots, tile = blocks.shape[1:4]
     rows_here = start.shape[1]
-    columns = start.shape[2]
     owners = lax.axis_size("rows")
     sections = lax.axis_size("phase")
-    even = lax.axis_index("rows") % 2 == 0
+    place = lax.axis_index("rows")
+    info = jnp.stack([1 - place % 2, place * block_rows]).astype(jnp.int32)
     first_core = lax.axis_index("phase") % 2 == 0
     to_a = [(i, i ^ 1) for i in range(owners)]
     to_b = [(i, (i + 1) % owners if i % 2 else (i - 1) % owners) for i in range(owners)]
@@ -200,44 +247,47 @@
     lines = block_rows * slots * tile
     edge = HB * slots * tile
 
-    def mirrored(rows):
-        tiles = rows.reshape(rows_here // tile, tile, columns)
-        return jnp.where(even, tiles[::-1], tiles).reshape(rows_here, columns)
-
-    def rims(operator):
+    def rims(a_side, b_side):
+        return (lax.ppermute(a_side, "rows", to_a), lax.ppermute(b_side, "rows", to_b))
+
+    def rims_of(operator):
         a_side = jnp.concatenate([operator[:edge], operator[lines : lines + 8 * HB]], axis=0)
         b_side = jnp.concatenate([operator[lines - edge : lines], operator[-8 * HB :]], axis=0)
-        return (lax.ppermute(a_side, "rows", to_a), lax.ppermute(b_side, "rows", to_b))
+        return a_side, b_side
 
     visits = sections // 2
     far = visits // 2
-    home = packed_operator(blocks[0], cols[0], counts[0], even)
+    home, home_a, home_b = pack(block_rows * owners, info, cols[0], counts[0], blocks[0])
     held = {0: home, visits: home}
     held[1] = lax.ppermute(home, "phase", back)
     held[visits - 1] = lax.ppermute(home, "phase", ahead)
-    travel = mirrored(start[0])
-    rim = rims(home)
+    halves = halve(info, start[0])
+    rim = rims(home_a, home_b)
     for turn in range(visits):
-        from_a = lax.ppermute(travel[:HALF], "rows", to_a)
-        from_b = lax.ppermute(travel[HALF:], "rows", to_b)
-        here, later, travel = lax.optimization_barrier((held[turn], held[turn + 1], travel))
+        from_a = lax.ppermute(halves[0], "rows", to_a)
+        from_b = lax.ppermute(halves[1], "rows", to_b)
+        here, later = held[turn], held[turn + 1]
+        if 0 < turn < far:
+            here, later, from_a, from_b = lax.optimization_barrier((here, later, from_a, from_b))
+        else:
+            here, later, halves = lax.optimization_barrier((here, later, halves))
         if turn + 2 <= far:
             held[turn + 2] = lax.ppermute(later, "phase", back)
         end = visits - 1 - turn
         if turn > 0 and end > far:
-            nearer, travel = lax.optimization_barrier((held[end + 1], travel))
+            nearer, from_a = lax.optimization_barrier((held[end + 1], from_a))
             held[end] = lax.ppermute(nearer, "phase", ahead)
         other = lax.ppermute(jnp.where(first_core, later, here), "phase", mates)
-        next_rim = rims(later) if turn + 1 < visits else None
-        travel = visit(travel, from_a, from_b, *rim, here, other)
+        next_rim = rims(*rims_of(later)) if turn + 1 < visits else None
+        halves = visit(halves, from_a, from_b, *rim, here, other)
         rim = next_rim
 
-    arrived = mirrored(travel)
+    arrived = jnp.concatenate(halves, axis=0)
     gram_term = lax.dot_general(
         arrived, arrived, (((0,), (0,)), ((), ())), preferred_element_type=jnp.float32
     )
     gram_total = sum_over_rows(gram_term.astype(jnp.bfloat16)) / (rows_here * owners)
-    basis_out, upper_factor = finish(gram_total, arrived)
+    basis_out, upper_factor = finish(info, gram_total, halves)
     return (basis_out[None], upper_factor[None])
 
 

time: 348 us -> 336 us (0.966)
  the two profiles are of different devices: /device:TPU:64 before, /device:TPU:8 now
where the time goes in v4:
time: 336 us; the launch traced here: 334 us
  starting transfers between devices  164 us (49%)
  waiting for transfers between devices  96.7 us (29%)
  blocking collectives  38.6 us (11%)
  Pallas kernels  27.2 us (8%)
  local copies, waits for them, and re-layouts  3.65 us (1%)
    ppermute x8, starting transfers between devices, body(): from_b = lax.ppermute(halves[1], 'rows', to_b)  42.2 us
    ppermute x8, starting transfers between devices, rims(): lax.ppermute(b_side, 'rows', to_b)  37.4 us
    ppermute x8, starting transfers between devices, body(): from_a = lax.ppermute(halves[0], 'rows', to_a)  26.1 us
    ppermute x8, waiting for transfers between devices, body(): from_b = lax.ppermute(halves[1], 'rows', to_b)  26 us
    all_to_all x1, blocking collectives, sum_over_rows(): pieces = lax.all_to_all(pieces, 'rows', 0, 0, tiled=True)  23.6 us
    ppermute x1, waiting for transfers between devices, body(): held[1] = lax.ppermute(home, 'phase', back)  22.1 us
    ppermute x8, waiting for transfers between devices, body(): from_a = lax.ppermute(halves[0], 'rows', to_a)  18.6 us
    ppermute x8, starting transfers between devices, rims(): lax.ppermute(a_side, 'rows', to_a)  15.9 us
  transfers between devices with their start and end apart: 47, of which 22 were waited for; matrix products, arithmetic and copies ran while one was open for 0% of the time, Pallas kernels for 2%

profile of v4, /device:TPU:8, one launch (start us, length us, event | category | flops | bytes accessed | tf_op | source)
XLA Modules:
  0.0 334.0 jit_solution(18406119902052720997)
XLA Ops:
  4.8 10.9 %collective-permute-start.1 = (bf16[4160,128]{1,0:T(8,128)(2,1)S(1)}, bf16[4160,128]{1,0:T(8,128)(2,1)S(1)}, u32[]{:S(2)}, u32[]{:S(2)}) collective-permute-start(bf16[4160,128]{1,0:T(8,128)(2,1)S(1)} %get-tuple-element.115.first), channel_id=1, source_target_pairs={{0,448},{32,480},{64,0},{96,32},{128,64},{160,96},{192,128},{224,1... | collective-permute-start | bytes 3194888 | tf_op jit(solution)/shard_map/ppermute | solution.py:262
  16.4 22.1 %collective-permute-done.1.first = bf16[4160,128]{1,0:T(8,128)(2,1)S(1)} collective-permute-done((bf16[4160,128]{1,0:T(8,128)(2,1)S(1)}, bf16[4160,128]{1,0:T(8,128)(2,1)S(1)}, u32[]{:S(2)}, u32[]{:S(2)}) %collective-permute-start.1) | collective-permute-done | bytes 1064992 | tf_op jit(solution)/shard_map/ppermute | solution.py:262
  40.6 5.6 %collective-permute-start.2 = (bf16[4160,128]{1,0:T(8,128)(2,1)S(1)}, bf16[4160,128]{1,0:T(8,128)(2,1)S(1)}, u32[]{:S(2)}, u32[]{:S(2)}) collective-permute-start(bf16[4160,128]{1,0:T(8,128)(2,1)S(1)} %collective-permute-done.1.first), channel_id=1, source_target_pairs={{0,448},{32,480},{64,0},{96,32},{128,64},{160,96},{192,128},{224,1... | collective-permute-start | bytes 3194888 | tf_op jit(solution)/shard_map/ppermute | solution.py:275
  46.2 3.4 %collective-permute-start.3 = (bf16[512,256]{1,0:T(8,128)(2,1)S(1)}, bf16[512,256]{1,0:T(8,128)(2,1)S(1)}, u32[]{:S(2)}, u32[]{:S(2)}) collective-permute-start(bf16[512,256]{1,0:T(8,128)(2,1)S(1)} %get-tuple-element.65.cur_a), channel_id=1, source_target_pairs={{0,1},{1,0},{2,3},{3,2},{4,5},{5,4},{6,7},{7,6},{8,9},{9,8},{10,11... | collective-permute-start | bytes 786440 | tf_op jit(solution)/shard_map/ppermute | solution.py:267
  49.6 2.4 collective-permute-start.5
  52.1 4.6 %collective-permute-start.6 = (bf16[1040,128]{1,0:T(8,128)(2,1)S(1)}, bf16[1040,128]{1,0:T(8,128)(2,1)S(1)}, u32[]{:S(2)}, u32[]{:S(2)}) collective-permute-start(bf16[1040,128]{1,0:T(8,128)(2,1)S(1)} %get-tuple-element.68), channel_id=1, source_target_pairs={{0,31},{1,2},{2,1},{3,4},{4,3},{5,6},{6,5},{7,8},{8,7},{9,10},{10,... | collective-permute-start | bytes 798728 | tf_op jit(solution)/shard_map/ppermute | solution.py:251
  57.3 4.5 %collective-permute-start.4 = (bf16[512,256]{1,0:T(8,128)(2,1)S(1)}, bf16[512,256]{1,0:T(8,128)(2,1)S(1)}, u32[]{:S(2)}, u32[]{:S(2)}) collective-permute-start(bf16[512,256]{1,0:T(8,128)(2,1)S(1)} %get-tuple-element.66.cur_b), channel_id=1, source_target_pairs={{0,31},{1,2},{2,1},{3,4},{4,3},{5,6},{6,5},{7,8},{8,7},{9,10},{10,... | collective-permute-start | bytes 786440 | tf_op jit(solution)/shard_map/ppermute | solution.py:268
  61.8 7.8 %collective-permute-done.4.rb = bf16[512,256]{1,0:T(8,128)(2,1)S(1)} collective-permute-done((bf16[512,256]{1,0:T(8,128)(2,1)S(1)}, bf16[512,256]{1,0:T(8,128)(2,1)S(1)}, u32[]{:S(2)}, u32[]{:S(2)}) %collective-permute-start.4) | collective-permute-done | bytes 262176 | tf_op jit(solution)/shard_map/ppermute | solution.py:268
  73.0 4.6 %collective-permute-start.9 = (bf16[512,256]{1,0:T(8,128)(2,1)S(1)}, bf16[512,256]{1,0:T(8,128)(2,1)S(1)}, u32[]{:S(2)}, u32[]{:S(2)}) collective-permute-start(bf16[512,256]{1,0:T(8,128)(2,1)S(1)} %get-tuple-element.71.cur_b), channel_id=1, source_target_pairs={{0,31},{1,2},{2,1},{3,4},{4,3},{5,6},{6,5},{7,8},{8,7},{9,10},{10,... | collective-permute-start | bytes 786440 | tf_op jit(solution)/shard_map/ppermute | solution.py:268
  77.5 1.9 collective-permute-start
  80.0 4.0 %collective-permute-done.9.rb = bf16[512,256]{1,0:T(8,128)(2,1)S(1)} collective-permute-done((bf16[512,256]{1,0:T(8,128)(2,1)S(1)}, bf16[512,256]{1,0:T(8,128)(2,1)S(1)}, u32[]{:S(2)}, u32[]{:S(2)}) %collective-permute-start.9) | collective-permute-done | bytes 262176 | tf_op jit(solution)/shard_map/ppermute | solution.py:268
  86.1 2.5 collective-permute-start.11
  88.6 2.0 collective-permute-start.12
  90.6 4.8 %collective-permute-start.13 = (bf16[1040,128]{1,0:T(8,128)(2,1)S(1)}, bf16[1040,128]{1,0:T(8,128)(2,1)S(1)}, u32[]{:S(2)}, u32[]{:S(2)}) collective-permute-start(bf16[1040,128]{1,0:T(8,128)(2,1)S(1)} %pad_maximum_fusion.1), channel_id=1, source_target_pairs={{0,31},{1,2},{2,1},{3,4},{4,3},{5,6},{6,5},{7,8},{8,7},{9,10},{10,... | collective-permute-start | bytes 798728 | tf_op jit(solution)/shard_map/ppermute | solution.py:251
  95.4 9.1 %collective-permute-done.first = bf16[4160,128]{1,0:T(8,128)(2,1)S(1)} collective-permute-done((bf16[4160,128]{1,0:T(8,128)(2,1)S(1)}, bf16[4160,128]{1,0:T(8,128)(2,1)S(1)}, u32[]{:S(2)}, u32[]{:S(2)}) %collective-permute-start) | collective-permute-done | bytes 1064992 | tf_op jit(solution)/shard_map/ppermute | solution.py:263
  106.0 3.2 collective-permute-start.15
  109.2 4.8 %collective-permute-start.16 = (bf16[512,256]{1,0:T(8,128)(2,1)S(1)}, bf16[512,256]{1,0:T(8,128)(2,1)S(1)}, u32[]{:S(2)}, u32[]{:S(2)}) collective-permute-start(bf16[512,256]{1,0:T(8,128)(2,1)S(1)} %get-tuple-element.79.cur_b), channel_id=1, source_target_pairs={{0,31},{1,2},{2,1},{3,4},{4,3},{5,6},{6,5},{7,8},{8,7},{9,10},{10,... | collective-permute-start | bytes 786440 | tf_op jit(solution)/shard_map/ppermute | solution.py:268
  116.0 3.6 %collective-permute-done.16.rb = bf16[512,256]{1,0:T(8,128)(2,1)S(1)} collective-permute-done((bf16[512,256]{1,0:T(8,128)(2,1)S(1)}, bf16[512,256]{1,0:T(8,128)(2,1)S(1)}, u32[]{:S(2)}, u32[]{:S(2)}) %collective-permute-start.16) | collective-permute-done | bytes 262176 | tf_op jit(solution)/shard_map/ppermute | solution.py:268
  123.6 4.8 %collective-permute-start.20 = (bf16[1040,128]{1,0:T(8,128)(2,1)S(1)}, bf16[1040,128]{1,0:T(8,128)(2,1)S(1)}, u32[]{:S(2)}, u32[]{:S(2)}) collective-permute-start(bf16[1040,128]{1,0:T(8,128)(2,1)S(1)} %pad_maximum_fusion.3), channel_id=1, source_target_pairs={{0,31},{1,2},{2,1},{3,4},{4,3},{5,6},{6,5},{7,8},{8,7},{9,10},{10,... | collective-permute-start | bytes 798728 | tf_op jit(solution)/shard_map/ppermute | solution.py:251
  130.4 9.5 %collective-permute-done.10.first = bf16[4160,128]{1,0:T(8,128)(2,1)S(1)} collective-permute-done((bf16[4160,128]{1,0:T(8,128)(2,1)S(1)}, bf16[4160,128]{1,0:T(8,128)(2,1)S(1)}, u32[]{:S(2)}, u32[]{:S(2)}) %collective-permute-start.10) | collective-permute-done | bytes 1064992 | tf_op jit(solution)/shard_map/ppermute | solution.py:279
  141.3 1.9 collective-permute-start.22
  143.3 7.2 %collective-permute-start.23 = (bf16[512,256]{1,0:T(8,128)(2,1)S(1)}, bf16[512,256]{1,0:T(8,128)(2,1)S(1)}, u32[]{:S(2)}, u32[]{:S(2)}) collective-permute-start(bf16[512,256]{1,0:T(8,128)(2,1)S(1)} %get-tuple-element.87.cur_b), channel_id=1, source_target_pairs={{0,31},{1,2},{2,1},{3,4},{4,3},{5,6},{6,5},{7,8},{8,7},{9,10},{10,... | collective-permute-start | bytes 786440 | tf_op jit(solution)/shard_map/ppermute | solution.py:268
  150.5 2.1 collective-permute-start.17
  152.7 2.2 collective-permute-done.23.rb
  157.0 6.0 %collective-permute-start.25 = (bf16[1040,128]{1,0:T(8,128)(2,1)S(1)}, bf16[1040,128]{1,0:T(8,128)(2,1)S(1)}, u32[]{:S(2)}, u32[]{:S(2)}) collective-permute-start(bf16[1040,128]{1,0:T(8,128)(2,1)S(1)} %pad_maximum_fusion.5), channel_id=1, source_target_pairs={{0,31},{1,2},{2,1},{3,4},{4,3},{5,6},{6,5},{7,8},{8,7},{9,10},{10,... | collective-permute-start | bytes 798728 | tf_op jit(solution)/shard_map/ppermute | solution.py:251
  165.0 5.1 %collective-permute-done.25.rim_b = bf16[1040,128]{1,0:T(8,128)(2,1)S(1)} collective-permute-done((bf16[1040,128]{1,0:T(8,128)(2,1)S(1)}, bf16[1040,128]{1,0:T(8,128)(2,1)S(1)}, u32[]{:S(2)}, u32[]{:S(2)}) %collective-permute-start.25) | collective-permute-done | bytes 266272 | tf_op jit(solution)/shard_map/ppermute | solution.py:251
  170.1 3.4 %collective-permute-done.24.rim_a = bf16[1040,128]{1,0:T(8,128)(2,1)S(1)} collective-permute-done((bf16[1040,128]{1,0:T(8,128)(2,1)S(1)}, bf16[1040,128]{1,0:T(8,128)(2,1)S(1)}, u32[]{:S(2)}, u32[]{:S(2)}) %collective-permute-start.24) | collective-permute-done | bytes 266272 | tf_op jit(solution)/shard_map/ppermute | solution.py:251
  177.8 2.6 collective-permute-start.30
  182.3 3.9 %collective-permute-start.27 = (bf16[512,256]{1,0:T(8,128)(2,1)S(1)}, bf16[512,256]{1,0:T(8,128)(2,1)S(1)}, u32[]{:S(2)}, u32[]{:S(2)}) collective-permute-start(bf16[512,256]{1,0:T(8,128)(2,1)S(1)} %get-tuple-element.94.cur_a), channel_id=1, source_target_pairs={{0,1},{1,0},{2,3},{3,2},{4,5},{5,4},{6,7},{7,6},{8,9},{9,8},{10,11... | collective-permute-start | bytes 786440 | tf_op jit(solution)/shard_map/ppermute | solution.py:267
  186.2 6.0 %collective-permute-start.28 = (bf16[512,256]{1,0:T(8,128)(2,1)S(1)}, bf16[512,256]{1,0:T(8,128)(2,1)S(1)}, u32[]{:S(2)}, u32[]{:S(2)}) collective-permute-start(bf16[512,256]{1,0:T(8,128)(2,1)S(1)} %get-tuple-element.95.cur_b), channel_id=1, source_target_pairs={{0,31},{1,2},{2,1},{3,4},{4,3},{5,6},{6,5},{7,8},{8,7},{9,10},{10,... | collective-permute-start | bytes 786440 | tf_op jit(solution)/shard_map/ppermute | solution.py:268
  192.3 4.1 %collective-permute-done.27.ra = bf16[512,256]{1,0:T(8,128)(2,1)S(1)} collective-permute-done((bf16[512,256]{1,0:T(8,128)(2,1)S(1)}, bf16[512,256]{1,0:T(8,128)(2,1)S(1)}, u32[]{:S(2)}, u32[]{:S(2)}) %collective-permute-start.27) | collective-permute-done | bytes 262176 | tf_op jit(solution)/shard_map/ppermute | solution.py:267
  196.4 2.2 collective-permute-done.28.rb
  202.3 5.8 %collective-permute-start.35 = (bf16[1040,128]{1,0:T(8,128)(2,1)S(1)}, bf16[1040,128]{1,0:T(8,128)(2,1)S(1)}, u32[]{:S(2)}, u32[]{:S(2)}) collective-permute-start(bf16[1040,128]{1,0:T(8,128)(2,1)S(1)} %pad_maximum_fusion.9), channel_id=1, source_target_pairs={{0,31},{1,2},{2,1},{3,4},{4,3},{5,6},{6,5},{7,8},{8,7},{9,10},{10,... | collective-permute-start | bytes 798728 | tf_op jit(solution)/shard_map/ppermute | solution.py:251
  210.0 3.9 %collective-permute-start.32 = (bf16[512,256]{1,0:T(8,128)(2,1)S(1)}, bf16[512,256]{1,0:T(8,128)(2,1)S(1)}, u32[]{:S(2)}, u32[]{:S(2)}) collective-permute-start(bf16[512,256]{1,0:T(8,128)(2,1)S(1)} %get-tuple-element.100.cur_a), channel_id=1, source_target_pairs={{0,1},{1,0},{2,3},{3,2},{4,5},{5,4},{6,7},{7,6},{8,9},{9,8},{10,11... | collective-permute-start | bytes 786440 | tf_op jit(solution)/shard_map/ppermute | solution.py:267
  213.9 4.0 %collective-permute-start.33 = (bf16[512,256]{1,0:T(8,128)(2,1)S(1)}, bf16[512,256]{1,0:T(8,128)(2,1)S(1)}, u32[]{:S(2)}, u32[]{:S(2)}) collective-permute-start(bf16[512,256]{1,0:T(8,128)(2,1)S(1)} %get-tuple-element.101.cur_b), channel_id=1, source_target_pairs={{0,31},{1,2},{2,1},{3,4},{4,3},{5,6},{6,5},{7,8},{8,7},{9,10},{10,... | collective-permute-start | bytes 786440 | tf_op jit(solution)/shard_map/ppermute | solution.py:268
  219.2 4.9 %collective-permute-done.32.ra = bf16[512,256]{1,0:T(8,128)(2,1)S(1)} collective-permute-done((bf16[512,256]{1,0:T(8,128)(2,1)S(1)}, bf16[512,256]{1,0:T(8,128)(2,1)S(1)}, u32[]{:S(2)}, u32[]{:S(2)}) %collective-permute-start.32) | collective-permute-done | bytes 262176 | tf_op jit(solution)/shard_map/ppermute | solution.py:267
  229.4 4.1 %collective-permute-start.40 = (bf16[1040,128]{1,0:T(8,128)(2,1)S(1)}, bf16[1040,128]{1,0:T(8,128)(2,1)S(1)}, u32[]{:S(2)}, u32[]{:S(2)}) collective-permute-start(bf16[1040,128]{1,0:T(8,128)(2,1)S(1)} %pad_maximum_fusion.11), channel_id=1, source_target_pairs={{0,31},{1,2},{2,1},{3,4},{4,3},{5,6},{6,5},{7,8},{8,7},{9,10},{10,... | collective-permute-start | bytes 798728 | tf_op jit(solution)/shard_map/ppermute | solution.py:251
  235.5 3.9 %collective-permute-start.37 = (bf16[512,256]{1,0:T(8,128)(2,1)S(1)}, bf16[512,256]{1,0:T(8,128)(2,1)S(1)}, u32[]{:S(2)}, u32[]{:S(2)}) collective-permute-start(bf16[512,256]{1,0:T(8,128)(2,1)S(1)} %get-tuple-element.106.cur_a), channel_id=1, source_target_pairs={{0,1},{1,0},{2,3},{3,2},{4,5},{5,4},{6,7},{7,6},{8,9},{9,8},{10,11... | collective-permute-start | bytes 786440 | tf_op jit(solution)/shard_map/ppermute | solution.py:267
  239.4 4.5 %collective-permute-start.38 = (bf16[512,256]{1,0:T(8,128)(2,1)S(1)}, bf16[512,256]{1,0:T(8,128)(2,1)S(1)}, u32[]{:S(2)}, u32[]{:S(2)}) collective-permute-start(bf16[512,256]{1,0:T(8,128)(2,1)S(1)} %get-tuple-element.107.cur_b), channel_id=1, source_target_pairs={{0,31},{1,2},{2,1},{3,4},{4,3},{5,6},{6,5},{7,8},{8,7},{9,10},{10,... | collective-permute-start | bytes 786440 | tf_op jit(solution)/shard_map/ppermute | solution.py:268
  244.7 4.9 %collective-permute-done.37.ra = bf16[512,256]{1,0:T(8,128)(2,1)S(1)} collective-permute-done((bf16[512,256]{1,0:T(8,128)(2,1)S(1)}, bf16[512,256]{1,0:T(8,128)(2,1)S(1)}, u32[]{:S(2)}, u32[]{:S(2)}) %collective-permute-start.37) | collective-permute-done | bytes 262176 | tf_op jit(solution)/shard_map/ppermute | solution.py:267
  254.9 4.8 %collective-permute-start.45 = (bf16[1040,128]{1,0:T(8,128)(2,1)S(1)}, bf16[1040,128]{1,0:T(8,128)(2,1)S(1)}, u32[]{:S(2)}, u32[]{:S(2)}) collective-permute-start(bf16[1040,128]{1,0:T(8,128)(2,1)S(1)} %pad_maximum_fusion.13), channel_id=1, source_target_pairs={{0,31},{1,2},{2,1},{3,4},{4,3},{5,6},{6,5},{7,8},{8,7},{9,10},{10,... | collective-permute-start | bytes 798728 | tf_op jit(solution)/shard_map/ppermute | solution.py:251
  261.6 3.9 %collective-permute-start.42 = (bf16[512,256]{1,0:T(8,128)(2,1)S(1)}, bf16[512,256]{1,0:T(8,128)(2,1)S(1)}, u32[]{:S(2)}, u32[]{:S(2)}) collective-permute-start(bf16[512,256]{1,0:T(8,128)(2,1)S(1)} %get-tuple-element.112.cur_a), channel_id=1, source_target_pairs={{0,1},{1,0},{2,3},{3,2},{4,5},{5,4},{6,7},{7,6},{8,9},{9,8},{10,11... | collective-permute-start | bytes 786440 | tf_op jit(solution)/shard_map/ppermute | solution.py:267
  265.5 6.5 %collective-permute-start.43 = (bf16[512,256]{1,0:T(8,128)(2,1)S(1)}, bf16[512,256]{1,0:T(8,128)(2,1)S(1)}, u32[]{:S(2)}, u32[]{:S(2)}) collective-permute-start(bf16[512,256]{1,0:T(8,128)(2,1)S(1)} %get-tuple-element.113.cur_b), channel_id=1, source_target_pairs={{0,31},{1,2},{2,1},{3,4},{4,3},{5,6},{6,5},{7,8},{8,7},{9,10},{10,... | collective-permute-start | bytes 786440 | tf_op jit(solution)/shard_map/ppermute | solution.py:268
  272.1 3.6 %collective-permute-done.42.ra = bf16[512,256]{1,0:T(8,128)(2,1)S(1)} collective-permute-done((bf16[512,256]{1,0:T(8,128)(2,1)S(1)}, bf16[512,256]{1,0:T(8,128)(2,1)S(1)}, u32[]{:S(2)}, u32[]{:S(2)}) %collective-permute-start.42) | collective-permute-done | bytes 262176 | tf_op jit(solution)/shard_map/ppermute | solution.py:267
  275.7 2.8 collective-permute-done.43.rb
  280.3 23.6 %all_to_all.10 = bf16[32,8,256]{2,1,0:T(8,128)(2,1)S(1)} all-to-all(bf16[32,8,256]{2,1,0:T(8,128)(2,1)S(1)} %fusion), channel_id=1, replica_groups=mesh['phase'=16,'rows'=32] {'rows'}, dimensions={0} | all-to-all | bytes 262144 | tf_op jit(solution)/shard_map/all_to_all | solution.py:228
  304.0 15.0 %all_to_all.11 = f32[32,8,256]{2,1,0:T(8,128)S(1)} all-to-all(f32[32,8,256]{2,1,0:T(8,128)S(1)} %broadcast_in_dim.12), channel_id=1, replica_groups=mesh['phase'=16,'rows'=32] {'rows'}, dimensions={0} | all-to-all | bytes 524288 | tf_op jit(solution)/shard_map/all_to_all | solution.py:231
  319.8 14.2 %factor_solve.1 = (f32[1024,256]{1,0:T(8,128)}, f32[256,256]{1,0:T(8,128)}) custom-call(s32[2]{0:T(128)} %copy-done.4, f32[256,256]{1,0:T(8,128)} %multiply_bitcast_fusion.gram_ref, bf16[512,256]{1,0:T(8,128)(2,1)} %copy-done.2, bf16[512,256]{1,0:T(8,128)(2,1)} %copy-done.3), custom_call_target="tpu_custom_call" | custom-call | tf_op jit(solution)/shard_map/factor_solve/pallas_call | solution.py:211
  (117 shorter events, 59.1 us)
Async XLA Ops:
  1.5 37.2 %copy-start.4 = (s32[2]{0:T(128)}, s32[2]{0:T(128)S(1)}, u32[]{:S(2)}) copy-start(s32[2]{0:T(128)S(1)} %pad_add_fusion.info) | copy-start | bytes 28
  4.8 33.7 %collective-permute-start.1 = (bf16[4160,128]{1,0:T(8,128)(2,1)S(1)}, bf16[4160,128]{1,0:T(8,128)(2,1)S(1)}, u32[]{:S(2)}, u32[]{:S(2)}) collective-permute-start(bf16[4160,128]{1,0:T(8,128)(2,1)S(1)} %get-tuple-element.115.first), channel_id=1, source_target_pairs={{0,448},{32,480},{64,0},{96,32},{128,64},{160,96},{192,128},{224,1... | collective-permute-start | bytes 3194888 | tf_op jit(solution)/shard_map/ppermute | solution.py:262
  38.7 31.0 %collective-permute-start.7 = (bf16[4160,128]{1,0:T(8,128)(2,1)S(1)}, bf16[4160,128]{1,0:T(8,128)(2,1)S(1)}, u32[]{:S(2)}, u32[]{:S(2)}) collective-permute-start(bf16[4160,128]{1,0:T(8,128)(2,1)S(1)} %broadcast_select_fusion.7), channel_id=1, source_target_pairs={{0,32},{32,0},{64,96},{96,64},{128,160},{160,128},{192,224},{224,1... | collective-permute-start | bytes 3194888 | tf_op jit(solution)/shard_map/ppermute | solution.py:280
  40.6 38.9 %collective-permute-start.2 = (bf16[4160,128]{1,0:T(8,128)(2,1)S(1)}, bf16[4160,128]{1,0:T(8,128)(2,1)S(1)}, u32[]{:S(2)}, u32[]{:S(2)}) collective-permute-start(bf16[4160,128]{1,0:T(8,128)(2,1)S(1)} %collective-permute-done.1.first), channel_id=1, source_target_pairs={{0,448},{32,480},{64,0},{96,32},{128,64},{160,96},{192,128},{224,1... | collective-permute-start | bytes 3194888 | tf_op jit(solution)/shard_map/ppermute | solution.py:275
  46.2 11.1 %collective-permute-start.3 = (bf16[512,256]{1,0:T(8,128)(2,1)S(1)}, bf16[512,256]{1,0:T(8,128)(2,1)S(1)}, u32[]{:S(2)}, u32[]{:S(2)}) collective-permute-start(bf16[512,256]{1,0:T(8,128)(2,1)S(1)} %get-tuple-element.65.cur_a), channel_id=1, source_target_pairs={{0,1},{1,0},{2,3},{3,2},{4,5},{5,4},{6,7},{7,6},{8,9},{9,8},{10,11... | collective-permute-start | bytes 786440 | tf_op jit(solution)/shard_map/ppermute | solution.py:267
  49.6 20.0 %collective-permute-start.5 = (bf16[1040,128]{1,0:T(8,128)(2,1)S(1)}, bf16[1040,128]{1,0:T(8,128)(2,1)S(1)}, u32[]{:S(2)}, u32[]{:S(2)}) collective-permute-start(bf16[1040,128]{1,0:T(8,128)(2,1)S(1)} %copy-done.7), channel_id=1, source_target_pairs={{0,1},{1,0},{2,3},{3,2},{4,5},{5,4},{6,7},{7,6},{8,9},{9,8},{10,11... | collective-permute-start | bytes 798728 | tf_op jit(solution)/shard_map/ppermute | solution.py:251
  52.1 17.6 %collective-permute-start.6 = (bf16[1040,128]{1,0:T(8,128)(2,1)S(1)}, bf16[1040,128]{1,0:T(8,128)(2,1)S(1)}, u32[]{:S(2)}, u32[]{:S(2)}) collective-permute-start(bf16[1040,128]{1,0:T(8,128)(2,1)S(1)} %get-tuple-element.68), channel_id=1, source_target_pairs={{0,31},{1,2},{2,1},{3,4},{4,3},{5,6},{6,5},{7,8},{8,7},{9,10},{10,... | collective-permute-start | bytes 798728 | tf_op jit(solution)/shard_map/ppermute | solution.py:251
  57.3 12.4 %collective-permute-start.4 = (bf16[512,256]{1,0:T(8,128)(2,1)S(1)}, bf16[512,256]{1,0:T(8,128)(2,1)S(1)}, u32[]{:S(2)}, u32[]{:S(2)}) collective-permute-start(bf16[512,256]{1,0:T(8,128)(2,1)S(1)} %get-tuple-element.66.cur_b), channel_id=1, source_target_pairs={{0,31},{1,2},{2,1},{3,4},{4,3},{5,6},{6,5},{7,8},{8,7},{9,10},{10,... | collective-permute-start | bytes 786440 | tf_op jit(solution)/shard_map/ppermute | solution.py:268
  71.1 8.9 %collective-permute-start.8 = (bf16[512,256]{1,0:T(8,128)(2,1)S(1)}, bf16[512,256]{1,0:T(8,128)(2,1)S(1)}, u32[]{:S(2)}, u32[]{:S(2)}) collective-permute-start(bf16[512,256]{1,0:T(8,128)(2,1)S(1)} %get-tuple-element.70.cur_a), channel_id=1, source_target_pairs={{0,1},{1,0},{2,3},{3,2},{4,5},{5,4},{6,7},{7,6},{8,9},{9,8},{10,11... | collective-permute-start | bytes 786440 | tf_op jit(solution)/shard_map/ppermute | solution.py:267
  73.0 11.0 %collective-permute-start.9 = (bf16[512,256]{1,0:T(8,128)(2,1)S(1)}, bf16[512,256]{1,0:T(8,128)(2,1)S(1)}, u32[]{:S(2)}, u32[]{:S(2)}) collective-permute-start(bf16[512,256]{1,0:T(8,128)(2,1)S(1)} %get-tuple-element.71.cur_b), channel_id=1, source_target_pairs={{0,31},{1,2},{2,1},{3,4},{4,3},{5,6},{6,5},{7,8},{8,7},{9,10},{10,... | collective-permute-start | bytes 786440 | tf_op jit(solution)/shard_map/ppermute | solution.py:268
  77.5 27.0 %collective-permute-start = (bf16[4160,128]{1,0:T(8,128)(2,1)S(1)}, bf16[4160,128]{1,0:T(8,128)(2,1)S(1)}, u32[]{:S(2)}, u32[]{:S(2)}) collective-permute-start(bf16[4160,128]{1,0:T(8,128)(2,1)S(1)} %get-tuple-element.115.first), channel_id=1, source_target_pairs={{0,64},{32,96},{64,128},{96,160},{128,192},{160,224},{192,256},{22... | collective-permute-start | bytes 3194888 | tf_op jit(solution)/shard_map/ppermute | solution.py:263
  84.1 20.5 %collective-permute-start.14 = (bf16[4160,128]{1,0:T(8,128)(2,1)S(1)}, bf16[4160,128]{1,0:T(8,128)(2,1)S(1)}, u32[]{:S(2)}, u32[]{:S(2)}) collective-permute-start(bf16[4160,128]{1,0:T(8,128)(2,1)S(1)} %broadcast_select_fusion.6), channel_id=1, source_target_pairs={{0,32},{32,0},{64,96},{96,64},{128,160},{160,128},{192,224},{224,1... | collective-permute-start | bytes 3194888 | tf_op jit(solution)/shard_map/ppermute | solution.py:280
  86.1 29.8 %collective-permute-start.11 = (bf16[4160,128]{1,0:T(8,128)(2,1)S(1)}, bf16[4160,128]{1,0:T(8,128)(2,1)S(1)}, u32[]{:S(2)}, u32[]{:S(2)}) collective-permute-start(bf16[4160,128]{1,0:T(8,128)(2,1)S(1)} %collective-permute-done.2.first), channel_id=1, source_target_pairs={{0,448},{32,480},{64,0},{96,32},{128,64},{160,96},{192,128},{224,1... | collective-permute-start | bytes 3194888 | tf_op jit(solution)/shard_map/ppermute | solution.py:275
  88.6 15.9 %collective-permute-start.12 = (bf16[1040,128]{1,0:T(8,128)(2,1)S(1)}, bf16[1040,128]{1,0:T(8,128)(2,1)S(1)}, u32[]{:S(2)}, u32[]{:S(2)}) collective-permute-start(bf16[1040,128]{1,0:T(8,128)(2,1)S(1)} %pad_maximum_fusion), channel_id=1, source_target_pairs={{0,1},{1,0},{2,3},{3,2},{4,5},{5,4},{6,7},{7,6},{8,9},{9,8},{10,11... | collective-permute-start | bytes 798728 | tf_op jit(solution)/shard_map/ppermute | solution.py:251
  90.6 14.0 %collective-permute-start.13 = (bf16[1040,128]{1,0:T(8,128)(2,1)S(1)}, bf16[1040,128]{1,0:T(8,128)(2,1)S(1)}, u32[]{:S(2)}, u32[]{:S(2)}) collective-permute-start(bf16[1040,128]{1,0:T(8,128)(2,1)S(1)} %pad_maximum_fusion.1), channel_id=1, source_target_pairs={{0,31},{1,2},{2,1},{3,4},{4,3},{5,6},{6,5},{7,8},{8,7},{9,10},{10,... | collective-permute-start | bytes 798728 | tf_op jit(solution)/shard_map/ppermute | solution.py:251
  106.0 9.9 %collective-permute-start.15 = (bf16[512,256]{1,0:T(8,128)(2,1)S(1)}, bf16[512,256]{1,0:T(8,128)(2,1)S(1)}, u32[]{:S(2)}, u32[]{:S(2)}) collective-permute-start(bf16[512,256]{1,0:T(8,128)(2,1)S(1)} %get-tuple-element.78.cur_a), channel_id=1, source_target_pairs={{0,1},{1,0},{2,3},{3,2},{4,5},{5,4},{6,7},{7,6},{8,9},{9,8},{10,11... | collective-permute-start | bytes 786440 | tf_op jit(solution)/shard_map/ppermute | solution.py:267
  109.2 10.4 %collective-permute-start.16 = (bf16[512,256]{1,0:T(8,128)(2,1)S(1)}, bf16[512,256]{1,0:T(8,128)(2,1)S(1)}, u32[]{:S(2)}, u32[]{:S(2)}) collective-permute-start(bf16[512,256]{1,0:T(8,128)(2,1)S(1)} %get-tuple-element.79.cur_b), channel_id=1, source_target_pairs={{0,31},{1,2},{2,1},{3,4},{4,3},{5,6},{6,5},{7,8},{8,7},{9,10},{10,... | collective-permute-start | bytes 786440 | tf_op jit(solution)/shard_map/ppermute | solution.py:268
  114.0 25.8 %collective-permute-start.10 = (bf16[4160,128]{1,0:T(8,128)(2,1)S(1)}, bf16[4160,128]{1,0:T(8,128)(2,1)S(1)}, u32[]{:S(2)}, u32[]{:S(2)}) collective-permute-start(bf16[4160,128]{1,0:T(8,128)(2,1)S(1)} %collective-permute-done.first), channel_id=1, source_target_pairs={{0,64},{32,96},{64,128},{96,160},{128,192},{160,224},{192,256},{22... | collective-permute-start | bytes 3194888 | tf_op jit(solution)/shard_map/ppermute | solution.py:279
  119.7 20.2 %collective-permute-start.21 = (bf16[4160,128]{1,0:T(8,128)(2,1)S(1)}, bf16[4160,128]{1,0:T(8,128)(2,1)S(1)}, u32[]{:S(2)}, u32[]{:S(2)}) collective-permute-start(bf16[4160,128]{1,0:T(8,128)(2,1)S(1)} %broadcast_select_fusion.5), channel_id=1, source_target_pairs={{0,32},{32,0},{64,96},{96,64},{128,160},{160,128},{192,224},{224,1... | collective-permute-start | bytes 3194888 | tf_op jit(solution)/shard_map/ppermute | solution.py:280
  121.7 31.0 %collective-permute-start.18 = (bf16[4160,128]{1,0:T(8,128)(2,1)S(1)}, bf16[4160,128]{1,0:T(8,128)(2,1)S(1)}, u32[]{:S(2)}, u32[]{:S(2)}) collective-permute-start(bf16[4160,128]{1,0:T(8,128)(2,1)S(1)} %collective-permute-done.11.first), channel_id=1, source_target_pairs={{0,448},{32,480},{64,0},{96,32},{128,64},{160,96},{192,128},{224,1... | collective-permute-start | bytes 3194888 | tf_op jit(solution)/shard_map/ppermute | solution.py:275
  123.6 16.2 %collective-permute-start.20 = (bf16[1040,128]{1,0:T(8,128)(2,1)S(1)}, bf16[1040,128]{1,0:T(8,128)(2,1)S(1)}, u32[]{:S(2)}, u32[]{:S(2)}) collective-permute-start(bf16[1040,128]{1,0:T(8,128)(2,1)S(1)} %pad_maximum_fusion.3), channel_id=1, source_target_pairs={{0,31},{1,2},{2,1},{3,4},{4,3},{5,6},{6,5},{7,8},{8,7},{9,10},{10,... | collective-permute-start | bytes 798728 | tf_op jit(solution)/shard_map/ppermute | solution.py:251
  128.5 11.4 %collective-permute-start.19 = (bf16[1040,128]{1,0:T(8,128)(2,1)S(1)}, bf16[1040,128]{1,0:T(8,128)(2,1)S(1)}, u32[]{:S(2)}, u32[]{:S(2)}) collective-permute-start(bf16[1040,128]{1,0:T(8,128)(2,1)S(1)} %pad_maximum_fusion.2), channel_id=1, source_target_pairs={{0,1},{1,0},{2,3},{3,2},{4,5},{5,4},{6,7},{7,6},{8,9},{9,8},{10,11... | collective-permute-start | bytes 798728 | tf_op jit(solution)/shard_map/ppermute | solution.py:251
  141.3 11.3 %collective-permute-start.22 = (bf16[512,256]{1,0:T(8,128)(2,1)S(1)}, bf16[512,256]{1,0:T(8,128)(2,1)S(1)}, u32[]{:S(2)}, u32[]{:S(2)}) collective-permute-start(bf16[512,256]{1,0:T(8,128)(2,1)S(1)} %get-tuple-element.86.cur_a), channel_id=1, source_target_pairs={{0,1},{1,0},{2,3},{3,2},{4,5},{5,4},{6,7},{7,6},{8,9},{9,8},{10,11... | collective-permute-start | bytes 786440 | tf_op jit(solution)/shard_map/ppermute | solution.py:267
  143.3 11.6 %collective-permute-start.23 = (bf16[512,256]{1,0:T(8,128)(2,1)S(1)}, bf16[512,256]{1,0:T(8,128)(2,1)S(1)}, u32[]{:S(2)}, u32[]{:S(2)}) collective-permute-start(bf16[512,256]{1,0:T(8,128)(2,1)S(1)} %get-tuple-element.87.cur_b), channel_id=1, source_target_pairs={{0,31},{1,2},{2,1},{3,4},{4,3},{5,6},{6,5},{7,8},{8,7},{9,10},{10,... | collective-permute-start | bytes 786440 | tf_op jit(solution)/shard_map/ppermute | solution.py:268
  150.5 25.1 %collective-permute-start.17 = (bf16[4160,128]{1,0:T(8,128)(2,1)S(1)}, bf16[4160,128]{1,0:T(8,128)(2,1)S(1)}, u32[]{:S(2)}, u32[]{:S(2)}) collective-permute-start(bf16[4160,128]{1,0:T(8,128)(2,1)S(1)} %collective-permute-done.10.first), channel_id=1, source_target_pairs={{0,64},{32,96},{64,128},{96,160},{128,192},{160,224},{192,256},{22... | collective-permute-start | bytes 3194888 | tf_op jit(solution)/shard_map/ppermute | solution.py:279
  155.0 18.5 %collective-permute-start.26 = (bf16[4160,128]{1,0:T(8,128)(2,1)S(1)}, bf16[4160,128]{1,0:T(8,128)(2,1)S(1)}, u32[]{:S(2)}, u32[]{:S(2)}) collective-permute-start(bf16[4160,128]{1,0:T(8,128)(2,1)S(1)} %broadcast_select_fusion.4), channel_id=1, source_target_pairs={{0,32},{32,0},{64,96},{96,64},{128,160},{160,128},{192,224},{224,1... | collective-permute-start | bytes 3194888 | tf_op jit(solution)/shard_map/ppermute | solution.py:280
  157.0 13.1 %collective-permute-start.25 = (bf16[1040,128]{1,0:T(8,128)(2,1)S(1)}, bf16[1040,128]{1,0:T(8,128)(2,1)S(1)}, u32[]{:S(2)}, u32[]{:S(2)}) collective-permute-start(bf16[1040,128]{1,0:T(8,128)(2,1)S(1)} %pad_maximum_fusion.5), channel_id=1, source_target_pairs={{0,31},{1,2},{2,1},{3,4},{4,3},{5,6},{6,5},{7,8},{8,7},{9,10},{10,... | collective-permute-start | bytes 798728 | tf_op jit(solution)/shard_map/ppermute | solution.py:251
  163.1 10.4 %collective-permute-start.24 = (bf16[1040,128]{1,0:T(8,128)(2,1)S(1)}, bf16[1040,128]{1,0:T(8,128)(2,1)S(1)}, u32[]{:S(2)}, u32[]{:S(2)}) collective-permute-start(bf16[1040,128]{1,0:T(8,128)(2,1)S(1)} %pad_maximum_fusion.4), channel_id=1, source_target_pairs={{0,1},{1,0},{2,3},{3,2},{4,5},{5,4},{6,7},{7,6},{8,9},{9,8},{10,11... | collective-permute-start | bytes 798728 | tf_op jit(solution)/shard_map/ppermute | solution.py:251
  175.8 22.9 %collective-permute-start.31 = (bf16[4160,128]{1,0:T(8,128)(2,1)S(1)}, bf16[4160,128]{1,0:T(8,128)(2,1)S(1)}, u32[]{:S(2)}, u32[]{:S(2)}) collective-permute-start(bf16[4160,128]{1,0:T(8,128)(2,1)S(1)} %broadcast_select_fusion.3), channel_id=1, source_target_pairs={{0,32},{32,0},{64,96},{96,64},{128,160},{160,128},{192,224},{224,1... | collective-permute-start | bytes 3194888 | tf_op jit(solution)/shard_map/ppermute | solution.py:280
  177.8 14.5 %collective-permute-start.30 = (bf16[1040,128]{1,0:T(8,128)(2,1)S(1)}, bf16[1040,128]{1,0:T(8,128)(2,1)S(1)}, u32[]{:S(2)}, u32[]{:S(2)}) collective-permute-start(bf16[1040,128]{1,0:T(8,128)(2,1)S(1)} %pad_maximum_fusion.7), channel_id=1, source_target_pairs={{0,31},{1,2},{2,1},{3,4},{4,3},{5,6},{6,5},{7,8},{8,7},{9,10},{10,... | collective-permute-start | bytes 798728 | tf_op jit(solution)/shard_map/ppermute | solution.py:251
  180.4 11.9 %collective-permute-start.29 = (bf16[1040,128]{1,0:T(8,128)(2,1)S(1)}, bf16[1040,128]{1,0:T(8,128)(2,1)S(1)}, u32[]{:S(2)}, u32[]{:S(2)}) collective-permute-start(bf16[1040,128]{1,0:T(8,128)(2,1)S(1)} %pad_maximum_fusion.6), channel_id=1, source_target_pairs={{0,1},{1,0},{2,3},{3,2},{4,5},{5,4},{6,7},{7,6},{8,9},{9,8},{10,11... | collective-permute-start | bytes 798728 | tf_op jit(solution)/shard_map/ppermute | solution.py:251
  182.3 14.1 %collective-permute-start.27 = (bf16[512,256]{1,0:T(8,128)(2,1)S(1)}, bf16[512,256]{1,0:T(8,128)(2,1)S(1)}, u32[]{:S(2)}, u32[]{:S(2)}) collective-permute-start(bf16[512,256]{1,0:T(8,128)(2,1)S(1)} %get-tuple-element.94.cur_a), channel_id=1, source_target_pairs={{0,1},{1,0},{2,3},{3,2},{4,5},{5,4},{6,7},{7,6},{8,9},{9,8},{10,11... | collective-permute-start | bytes 786440 | tf_op jit(solution)/shard_map/ppermute | solution.py:267
  186.2 12.4 %collective-permute-start.28 = (bf16[512,256]{1,0:T(8,128)(2,1)S(1)}, bf16[512,256]{1,0:T(8,128)(2,1)S(1)}, u32[]{:S(2)}, u32[]{:S(2)}) collective-permute-start(bf16[512,256]{1,0:T(8,128)(2,1)S(1)} %get-tuple-element.95.cur_b), channel_id=1, source_target_pairs={{0,31},{1,2},{2,1},{3,4},{4,3},{5,6},{6,5},{7,8},{8,7},{9,10},{10,... | collective-permute-start | bytes 786440 | tf_op jit(solution)/shard_map/ppermute | solution.py:268
  200.2 25.5 %collective-permute-start.36 = (bf16[4160,128]{1,0:T(8,128)(2,1)S(1)}, bf16[4160,128]{1,0:T(8,128)(2,1)S(1)}, u32[]{:S(2)}, u32[]{:S(2)}) collective-permute-start(bf16[4160,128]{1,0:T(8,128)(2,1)S(1)} %broadcast_select_fusion.2), channel_id=1, source_target_pairs={{0,32},{32,0},{64,96},{96,64},{128,160},{160,128},{192,224},{224,1... | collective-permute-start | bytes 3194888 | tf_op jit(solution)/shard_map/ppermute | solution.py:280
  202.3 15.7 %collective-permute-start.35 = (bf16[1040,128]{1,0:T(8,128)(2,1)S(1)}, bf16[1040,128]{1,0:T(8,128)(2,1)S(1)}, u32[]{:S(2)}, u32[]{:S(2)}) collective-permute-start(bf16[1040,128]{1,0:T(8,128)(2,1)S(1)} %pad_maximum_fusion.9), channel_id=1, source_target_pairs={{0,31},{1,2},{2,1},{3,4},{4,3},{5,6},{6,5},{7,8},{8,7},{9,10},{10,... | collective-permute-start | bytes 798728 | tf_op jit(solution)/shard_map/ppermute | solution.py:251
  208.0 11.2 %collective-permute-start.34 = (bf16[1040,128]{1,0:T(8,128)(2,1)S(1)}, bf16[1040,128]{1,0:T(8,128)(2,1)S(1)}, u32[]{:S(2)}, u32[]{:S(2)}) collective-permute-start(bf16[1040,128]{1,0:T(8,128)(2,1)S(1)} %pad_maximum_fusion.8), channel_id=1, source_target_pairs={{0,1},{1,0},{2,3},{3,2},{4,5},{5,4},{6,7},{7,6},{8,9},{9,8},{10,11... | collective-permute-start | bytes 798728 | tf_op jit(solution)/shard_map/ppermute | solution.py:251
  210.0 14.1 %collective-permute-start.32 = (bf16[512,256]{1,0:T(8,128)(2,1)S(1)}, bf16[512,256]{1,0:T(8,128)(2,1)S(1)}, u32[]{:S(2)}, u32[]{:S(2)}) collective-permute-start(bf16[512,256]{1,0:T(8,128)(2,1)S(1)} %get-tuple-element.100.cur_a), channel_id=1, source_target_pairs={{0,1},{1,0},{2,3},{3,2},{4,5},{5,4},{6,7},{7,6},{8,9},{9,8},{10,11... | collective-permute-start | bytes 786440 | tf_op jit(solution)/shard_map/ppermute | solution.py:267
  213.9 11.9 %collective-permute-start.33 = (bf16[512,256]{1,0:T(8,128)(2,1)S(1)}, bf16[512,256]{1,0:T(8,128)(2,1)S(1)}, u32[]{:S(2)}, u32[]{:S(2)}) collective-permute-start(bf16[512,256]{1,0:T(8,128)(2,1)S(1)} %get-tuple-element.101.cur_b), channel_id=1, source_target_pairs={{0,31},{1,2},{2,1},{3,4},{4,3},{5,6},{6,5},{7,8},{8,7},{9,10},{10,... | collective-permute-start | bytes 786440 | tf_op jit(solution)/shard_map/ppermute | solution.py:268
  227.4 23.9 %collective-permute-start.41 = (bf16[4160,128]{1,0:T(8,128)(2,1)S(1)}, bf16[4160,128]{1,0:T(8,128)(2,1)S(1)}, u32[]{:S(2)}, u32[]{:S(2)}) collective-permute-start(bf16[4160,128]{1,0:T(8,128)(2,1)S(1)} %broadcast_select_fusion.1), channel_id=1, source_target_pairs={{0,32},{32,0},{64,96},{96,64},{128,160},{160,128},{192,224},{224,1... | collective-permute-start | bytes 3194888 | tf_op jit(solution)/shard_map/ppermute | solution.py:280
  229.4 14.5 %collective-permute-start.40 = (bf16[1040,128]{1,0:T(8,128)(2,1)S(1)}, bf16[1040,128]{1,0:T(8,128)(2,1)S(1)}, u32[]{:S(2)}, u32[]{:S(2)}) collective-permute-start(bf16[1040,128]{1,0:T(8,128)(2,1)S(1)} %pad_maximum_fusion.11), channel_id=1, source_target_pairs={{0,31},{1,2},{2,1},{3,4},{4,3},{5,6},{6,5},{7,8},{8,7},{9,10},{10,... | collective-permute-start | bytes 798728 | tf_op jit(solution)/shard_map/ppermute | solution.py:251
  233.5 11.2 %collective-permute-start.39 = (bf16[1040,128]{1,0:T(8,128)(2,1)S(1)}, bf16[1040,128]{1,0:T(8,128)(2,1)S(1)}, u32[]{:S(2)}, u32[]{:S(2)}) collective-permute-start(bf16[1040,128]{1,0:T(8,128)(2,1)S(1)} %pad_maximum_fusion.10), channel_id=1, source_target_pairs={{0,1},{1,0},{2,3},{3,2},{4,5},{5,4},{6,7},{7,6},{8,9},{9,8},{10,11... | collective-permute-start | bytes 798728 | tf_op jit(solution)/shard_map/ppermute | solution.py:251
  235.5 14.1 %collective-permute-start.37 = (bf16[512,256]{1,0:T(8,128)(2,1)S(1)}, bf16[512,256]{1,0:T(8,128)(2,1)S(1)}, u32[]{:S(2)}, u32[]{:S(2)}) collective-permute-start(bf16[512,256]{1,0:T(8,128)(2,1)S(1)} %get-tuple-element.106.cur_a), channel_id=1, source_target_pairs={{0,1},{1,0},{2,3},{3,2},{4,5},{5,4},{6,7},{7,6},{8,9},{9,8},{10,11... | collective-permute-start | bytes 786440 | tf_op jit(solution)/shard_map/ppermute | solution.py:267
  239.4 11.9 %collective-permute-start.38 = (bf16[512,256]{1,0:T(8,128)(2,1)S(1)}, bf16[512,256]{1,0:T(8,128)(2,1)S(1)}, u32[]{:S(2)}, u32[]{:S(2)}) collective-permute-start(bf16[512,256]{1,0:T(8,128)(2,1)S(1)} %get-tuple-element.107.cur_b), channel_id=1, source_target_pairs={{0,31},{1,2},{2,1},{3,4},{4,3},{5,6},{6,5},{7,8},{8,7},{9,10},{10,... | collective-permute-start | bytes 786440 | tf_op jit(solution)/shard_map/ppermute | solution.py:268
  252.9 25.6 %collective-permute-start.46 = (bf16[4160,128]{1,0:T(8,128)(2,1)S(1)}, bf16[4160,128]{1,0:T(8,128)(2,1)S(1)}, u32[]{:S(2)}, u32[]{:S(2)}) collective-permute-start(bf16[4160,128]{1,0:T(8,128)(2,1)S(1)} %broadcast_select_fusion), channel_id=1, source_target_pairs={{0,32},{32,0},{64,96},{96,64},{128,160},{160,128},{192,224},{224,1... | collective-permute-start | bytes 3194888 | tf_op jit(solution)/shard_map/ppermute | solution.py:280
  254.9 17.2 %collective-permute-start.45 = (bf16[1040,128]{1,0:T(8,128)(2,1)S(1)}, bf16[1040,128]{1,0:T(8,128)(2,1)S(1)}, u32[]{:S(2)}, u32[]{:S(2)}) collective-permute-start(bf16[1040,128]{1,0:T(8,128)(2,1)S(1)} %pad_maximum_fusion.13), channel_id=1, source_target_pairs={{0,31},{1,2},{2,1},{3,4},{4,3},{5,6},{6,5},{7,8},{8,7},{9,10},{10,... | collective-permute-start | bytes 798728 | tf_op jit(solution)/shard_map/ppermute | solution.py:251
  259.7 12.4 %collective-permute-start.44 = (bf16[1040,128]{1,0:T(8,128)(2,1)S(1)}, bf16[1040,128]{1,0:T(8,128)(2,1)S(1)}, u32[]{:S(2)}, u32[]{:S(2)}) collective-permute-start(bf16[1040,128]{1,0:T(8,128)(2,1)S(1)} %pad_maximum_fusion.12), channel_id=1, source_target_pairs={{0,1},{1,0},{2,3},{3,2},{4,5},{5,4},{6,7},{7,6},{8,9},{9,8},{10,11... | collective-permute-start | bytes 798728 | tf_op jit(solution)/shard_map/ppermute | solution.py:251
  261.6 14.1 %collective-permute-start.42 = (bf16[512,256]{1,0:T(8,128)(2,1)S(1)}, bf16[512,256]{1,0:T(8,128)(2,1)S(1)}, u32[]{:S(2)}, u32[]{:S(2)}) collective-permute-start(bf16[512,256]{1,0:T(8,128)(2,1)S(1)} %get-tuple-element.112.cur_a), channel_id=1, source_target_pairs={{0,1},{1,0},{2,3},{3,2},{4,5},{5,4},{6,7},{7,6},{8,9},{9,8},{10,11... | collective-permute-start | bytes 786440 | tf_op jit(solution)/shard_map/ppermute | solution.py:267
  265.5 12.9 %collective-permute-start.43 = (bf16[512,256]{1,0:T(8,128)(2,1)S(1)}, bf16[512,256]{1,0:T(8,128)(2,1)S(1)}, u32[]{:S(2)}, u32[]{:S(2)}) collective-permute-start(bf16[512,256]{1,0:T(8,128)(2,1)S(1)} %get-tuple-element.113.cur_b), channel_id=1, source_target_pairs={{0,31},{1,2},{2,1},{3,4},{4,3},{5,6},{6,5},{7,8},{8,7},{9,10},{10,... | collective-permute-start | bytes 786440 | tf_op jit(solution)/shard_map/ppermute | solution.py:268
  (7 other events, 74.2 us)

commit v5 on v4

--- a/solution.py
+++ b/solution.py
@@ -13,7 +13,7 @@
 HALF = 4 * TILE
 DEAD = 7
 
-def visit_kernel(cur_a, cur_b, ra, rb, rim_a, rim_b, first, second, out_a, out_b, wide, mid):
+def visit_kernel(rim_at, second_at, cur_a, cur_b, ra, rb, rim_a, rim_b, first, second, out_a, out_b, wide, mid):
     for n in range(4):
         wide[(3 - n) * TILE : (4 - n) * TILE, :] = ra[n * TILE : (n + 1) * TILE, :]
         wide[(15 - n) * TILE : (16 - n) * TILE, :] = rb[n * TILE : (n + 1) * TILE, :]
@@ -23,8 +23,8 @@
     wide[16 * TILE :, :] = zero
     mid[12 * TILE :, :] = zero
 
-    def row(ops, n, source, centre, sign, nothing):
-        line = ops.shape[0] // (4 * TILE + 8) * 4 * TILE + n * 8
+    def row(ops, at, count, n, source, centre, sign, nothing):
+        line = at + count * 4 * TILE + n * 8
         table = ops[line : line + 8, :].astype(jnp.float32).astype(jnp.int32)
 
         def block(j):
@@ -35,7 +35,7 @@
             return source[pl.ds(pl.multiple_of(place * TILE, TILE), TILE), :]
 
         def slot(j):
-            return ops[(n * 4 + j) * TILE : (n * 4 + j + 1) * TILE, :]
+            return ops[at + (n * 4 + j) * TILE : at + (n * 4 + j + 1) * TILE, :]
 
         total = None
         for j in (0, 2):
@@ -47,21 +47,21 @@
 
     for n in range(2):
         c = 1 - n
-        mid[c * TILE : (c + 1) * TILE, :] = row(rim_a, n, wide, c + 2, -1, 16)
+        mid[c * TILE : (c + 1) * TILE, :] = row(rim_a, rim_at, 2, n, wide, c + 2, -1, 16)
         c = 11 - n
-        mid[c * TILE : (c + 1) * TILE, :] = row(rim_b, n, wide, c + 2, -1, 16)
+        mid[c * TILE : (c + 1) * TILE, :] = row(rim_b, rim_at, 2, n, wide, c + 2, -1, 16)
     for c in range(8):
-        mid[(c + 2) * TILE : (c + 3) * TILE, :] = row(first, c, wide, c + 4, 1, 16)
+        mid[(c + 2) * TILE : (c + 3) * TILE, :] = row(first, 0, 8, c, wide, c + 4, 1, 16)
     for c in range(8):
         half = out_a if c < 4 else out_b
-        half[c % 4 * TILE : (c % 4 + 1) * TILE, :] = row(second, c, mid, c + 2, 1, 12)
-
-def visit(halves, ra, rb, rim_a, rim_b, first, second):
+        half[c % 4 * TILE : (c % 4 + 1) * TILE, :] = row(second, second_at, 8, c, mid, c + 2, 1, 12)
+
+def visit(halves, ra, rb, rim_a, rim_b, first, second, rim_at=0, second_at=0):
     vmem = pl.BlockSpec(memory_space=pltpu.VMEM)
     shape = jax.ShapeDtypeStruct(halves[0].shape, halves[0].dtype)
     columns = shape.shape[1]
     return pl.pallas_call(
-        visit_kernel,
+        functools.partial(visit_kernel, rim_at, second_at),
         out_shape=(shape, shape),
         in_specs=[vmem] * 8,
         out_specs=(vmem, vmem),
@@ -138,6 +138,48 @@
         compiler_params=pltpu.CompilerParams(vmem_limit_bytes=8 * 1024 * 1024),
         name="halve_start",
     )(info, start)
+
+def gather_kernel(info, *refs):
+    operators, (side_a, side_b, swapped) = refs[:-3], refs[-3:]
+    span = operators[0].shape[0]
+    rim = side_a.shape[0] // (len(operators) - 1)
+    tables = 8 * HB
+
+    for n, (operator, following) in enumerate(zip(operators[:-1], operators[1:])):
+        @pl.loop(0, span, step=160)
+        def _(line):
+            at = pl.ds(pl.multiple_of(line, 32), 160)
+            to = pl.ds(pl.multiple_of(n * span + line, 32), 160)
+            swapped[to, :] = jnp.where(info[2] == 0, following[at, :], operator[at, :])
+
+        edge = rim - tables
+        body = span - span // (4 * TILE + 8) * 8
+
+        @pl.loop(0, edge, step=TILE)
+        def _(line):
+            at = pl.multiple_of(line, TILE)
+            to = pl.ds(pl.multiple_of(n * rim + line, 16), TILE)
+            side_a[to, :] = operator[pl.ds(at, TILE), :]
+            side_b[to, :] = operator[pl.ds(body - edge + at, TILE), :]
+
+        at = n * rim + edge
+        side_a[at : at + tables, :] = operator[body : body + tables, :]
+        side_b[at : at + tables, :] = operator[span - tables :, :]
+
+def gather_last(info, rim_rows, operators):
+    vmem = pl.BlockSpec(memory_space=pltpu.VMEM)
+    kind = operators[0].dtype
+    count = len(operators) - 1
+    side = jax.ShapeDtypeStruct((count * rim_rows, TILE), kind)
+    swapped = jax.ShapeDtypeStruct((count * operators[0].shape[0], TILE), kind)
+    return pl.pallas_call(
+        gather_kernel,
+        out_shape=(side, side, swapped),
+        in_specs=[pl.BlockSpec(memory_space=pltpu.SMEM)] + [vmem] * len(operators),
+        out_specs=(vmem, vmem, vmem),
+        compiler_params=pltpu.CompilerParams(vmem_limit_bytes=24 * 1024 * 1024),
+        name="gather_last",
+    )(info, *operators)
 
 
 NB = 16
@@ -237,8 +279,9 @@
     owners = lax.axis_size("rows")
     sections = lax.axis_size("phase")
     place = lax.axis_index("rows")
-    info = jnp.stack([1 - place % 2, place * block_rows]).astype(jnp.int32)
-    first_core = lax.axis_index("phase") % 2 == 0
+    core = lax.axis_index("phase") % 2
+    info = jnp.stack([1 - place % 2, place * block_rows, core]).astype(jnp.int32)
+    first_core = core == 0
     to_a = [(i, i ^ 1) for i in range(owners)]
     to_b = [(i, (i + 1) % owners if i % 2 else (i - 1) % owners) for i in range(owners)]
     back = [(i, (i - 2) % sections) for i in range(sections)]
@@ -263,24 +306,33 @@
     held[visits - 1] = lax.ppermute(home, "phase", ahead)
     halves = halve(info, start[0])
     rim = rims(home_a, home_b)
+    span = home.shape[0]
+    rim_span = home_a.shape[0]
     for turn in range(visits):
         from_a = lax.ppermute(halves[0], "rows", to_a)
         from_b = lax.ppermute(halves[1], "rows", to_b)
-        here, later = held[turn], held[turn + 1]
-        if 0 < turn < far:
-            here, later, from_a, from_b = lax.optimization_barrier((here, later, from_a, from_b))
+        if turn <= far:
+            here, later, halves = lax.optimization_barrier((held[turn], held[turn + 1], halves))
+            if turn + 2 <= far:
+                held[turn + 2] = lax.ppermute(later, "phase", back)
+            end = visits - 1 - turn
+            if turn > 0 and end > far:
+                nearer, halves = lax.optimization_barrier((held[end + 1], halves))
+                held[end] = lax.ppermute(nearer, "phase", ahead)
+            picked = jnp.where(first_core, later, here)
+            other, other_at, rim_at = lax.ppermute(picked, "phase", mates), 0, 0
+        if turn < far:
+            next_rim = rims(*rims_of(later))
+        elif turn == far:
+            last = [later] + [held[n] for n in range(turn + 2, visits)] + [home]
+            side_a, side_b, swapped = gather_last(info, rim_span, last)
+            next_rim = rims(side_a, side_b)
+            others = lax.ppermute(swapped, "phase", mates)
         else:
-            here, later, halves = lax.optimization_barrier((here, later, halves))
-        if turn + 2 <= far:
-            held[turn + 2] = lax.ppermute(later, "phase", back)
-        end = visits - 1 - turn
-        if turn > 0 and end > far:
-            nearer, from_a = lax.optimization_barrier((held[end + 1], from_a))
-            held[end] = lax.ppermute(nearer, "phase", ahead)
-        other = lax.ppermute(jnp.where(first_core, later, here), "phase", mates)
-        next_rim = rims(*rims_of(later)) if turn + 1 < visits else None
-        halves = visit(halves, from_a, from_b, *rim, here, other)
-        rim = next_rim
+            other, other_at, rim_at = others, (turn - far - 1) * span, (turn - far - 1) * rim_span
+        halves = visit(halves, from_a, from_b, *rim, held[turn], other, rim_at, other_at)
+        if turn <= far:
+            rim = next_rim
 
     arrived = jnp.concatenate(halves, axis=0)
     gram_term = lax.dot_general(

time: 336 us -> 319 us (0.949)
  the two profiles are of different devices: /device:TPU:8 before, /device:TPU:64 now
where the time goes in v5:
time: 319 us; the launch traced here: 317 us
  starting transfers between devices  158 us (50%)
  waiting for transfers between devices  92.5 us (29%)
  blocking collectives  31.2 us (10%)
  Pallas kernels  29.2 us (9%)
    ppermute x8, waiting for transfers between devices, body(): from_b = lax.ppermute(halves[1], 'rows', to_b)  57.2 us
    ppermute x8, starting transfers between devices, body(): from_b = lax.ppermute(halves[1], 'rows', to_b)  46.1 us
    ppermute x6, starting transfers between devices, rims(): lax.ppermute(b_side, 'rows', to_b)  38.4 us
    ppermute x1, waiting for transfers between devices, body(): held[1] = lax.ppermute(home, 'phase', back)  20.3 us
    ppermute x3, starting transfers between devices, body(): held[turn + 2] = lax.ppermute(later, 'phase', back)  17.9 us
    ppermute x8, starting transfers between devices, body(): from_a = lax.ppermute(halves[0], 'rows', to_a)  17.1 us
    all_to_all x1, blocking collectives, sum_over_rows(): pieces = lax.all_to_all(pieces, 'rows', 0, 0, tiled=True)  16.4 us
    all_to_all x1, blocking collectives, sum_over_rows(): return lax.all_to_all(copies, 'rows', 0, 0, tiled=True).reshape(size, size)  14.8 us
  transfers between devices with their start and end apart: 41, of which 18 were waited for; matrix products, arithmetic and copies ran while one was open for 0% of the time, Pallas kernels for 2%

profile of v5, /device:TPU:64, one launch (start us, length us, event | category | flops | bytes accessed | tf_op | source)
XLA Modules:
  0.0 317.3 jit_solution(14677856413726440321)
XLA Ops:
  4.1 6.9 %collective-permute-start = (bf16[4160,128]{1,0:T(8,128)(2,1)S(1)}, bf16[4160,128]{1,0:T(8,128)(2,1)S(1)}, u32[]{:S(2)}, u32[]{:S(2)}) collective-permute-start(bf16[4160,128]{1,0:T(8,128)(2,1)S(1)} %get-tuple-element.62.first.refs_3_), channel_id=1, source_target_pairs={{0,448},{32,480},{64,0},{96,32},{128,64},{160,96},{192,128},{224,1... | collective-permute-start | bytes 3194888 | tf_op jit(solution)/shard_map/ppermute | solution.py:305
  11.7 20.3 %collective-permute-done.first = bf16[4160,128]{1,0:T(8,128)(2,1)S(1)} collective-permute-done((bf16[4160,128]{1,0:T(8,128)(2,1)S(1)}, bf16[4160,128]{1,0:T(8,128)(2,1)S(1)}, u32[]{:S(2)}, u32[]{:S(2)}) %collective-permute-start) | collective-permute-done | bytes 1064992 | tf_op jit(solution)/shard_map/ppermute | solution.py:305
  32.0 1.9 collective-permute-start.6
  34.0 7.5 %collective-permute-start.1 = (bf16[4160,128]{1,0:T(8,128)(2,1)S(1)}, bf16[4160,128]{1,0:T(8,128)(2,1)S(1)}, u32[]{:S(2)}, u32[]{:S(2)}) collective-permute-start(bf16[4160,128]{1,0:T(8,128)(2,1)S(1)} %collective-permute-done.first), channel_id=1, source_target_pairs={{0,448},{32,480},{64,0},{96,32},{128,64},{160,96},{192,128},{224,1... | collective-permute-start | bytes 3194888 | tf_op jit(solution)/shard_map/ppermute | solution.py:317
  41.5 3.4 %collective-permute-start.2 = (bf16[512,256]{1,0:T(8,128)(2,1)S(1)}, bf16[512,256]{1,0:T(8,128)(2,1)S(1)}, u32[]{:S(2)}, u32[]{:S(2)}) collective-permute-start(bf16[512,256]{1,0:T(8,128)(2,1)S(1)} %get-tuple-element.58.cur_a), channel_id=1, source_target_pairs={{0,1},{1,0},{2,3},{3,2},{4,5},{5,4},{6,7},{7,6},{8,9},{9,8},{10,11... | collective-permute-start | bytes 786440 | tf_op jit(solution)/shard_map/ppermute | solution.py:312
  44.9 2.4 collective-permute-start.4
  47.3 7.6 %collective-permute-start.5 = (bf16[1040,128]{1,0:T(8,128)(2,1)S(1)}, bf16[1040,128]{1,0:T(8,128)(2,1)S(1)}, u32[]{:S(2)}, u32[]{:S(2)}) collective-permute-start(bf16[1040,128]{1,0:T(8,128)(2,1)S(1)} %get-tuple-element.61), channel_id=1, source_target_pairs={{0,31},{1,2},{2,1},{3,4},{4,3},{5,6},{6,5},{7,8},{8,7},{9,10},{10,... | collective-permute-start | bytes 798728 | tf_op jit(solution)/shard_map/ppermute | solution.py:294
  54.9 5.2 %collective-permute-start.3 = (bf16[512,256]{1,0:T(8,128)(2,1)S(1)}, bf16[512,256]{1,0:T(8,128)(2,1)S(1)}, u32[]{:S(2)}, u32[]{:S(2)}) collective-permute-start(bf16[512,256]{1,0:T(8,128)(2,1)S(1)} %get-tuple-element.59.cur_b), channel_id=1, source_target_pairs={{0,31},{1,2},{2,1},{3,4},{4,3},{5,6},{6,5},{7,8},{8,7},{9,10},{10,... | collective-permute-start | bytes 786440 | tf_op jit(solution)/shard_map/ppermute | solution.py:313
  60.1 7.6 %collective-permute-done.3.rb = bf16[512,256]{1,0:T(8,128)(2,1)S(1)} collective-permute-done((bf16[512,256]{1,0:T(8,128)(2,1)S(1)}, bf16[512,256]{1,0:T(8,128)(2,1)S(1)}, u32[]{:S(2)}, u32[]{:S(2)}) %collective-permute-start.3) | collective-permute-done | bytes 262176 | tf_op jit(solution)/shard_map/ppermute | solution.py:313
  71.1 5.6 %collective-permute-start.7 = (bf16[4160,128]{1,0:T(8,128)(2,1)S(1)}, bf16[4160,128]{1,0:T(8,128)(2,1)S(1)}, u32[]{:S(2)}, u32[]{:S(2)}) collective-permute-start(bf16[4160,128]{1,0:T(8,128)(2,1)S(1)} %collective-permute-done.1.first), channel_id=1, source_target_pairs={{0,448},{32,480},{64,0},{96,32},{128,64},{160,96},{192,128},{224,1... | collective-permute-start | bytes 3194888 | tf_op jit(solution)/shard_map/ppermute | solution.py:317
  76.8 1.9 collective-permute-start.13
  78.8 1.9 collective-permute-start.11
  80.8 6.0 %collective-permute-start.12 = (bf16[1040,128]{1,0:T(8,128)(2,1)S(1)}, bf16[1040,128]{1,0:T(8,128)(2,1)S(1)}, u32[]{:S(2)}, u32[]{:S(2)}) collective-permute-start(bf16[1040,128]{1,0:T(8,128)(2,1)S(1)} %pad_maximum_fusion.1), channel_id=1, source_target_pairs={{0,31},{1,2},{2,1},{3,4},{4,3},{5,6},{6,5},{7,8},{8,7},{9,10},{10,... | collective-permute-start | bytes 798728 | tf_op jit(solution)/shard_map/ppermute | solution.py:294
  86.8 8.7 %collective-permute-done.8.refs_2_.first = bf16[4160,128]{1,0:T(8,128)(2,1)S(1)} collective-permute-done((bf16[4160,128]{1,0:T(8,128)(2,1)S(1)}, bf16[4160,128]{1,0:T(8,128)(2,1)S(1)}, u32[]{:S(2)}, u32[]{:S(2)}) %collective-permute-start.8) | collective-permute-done | bytes 1064992 | tf_op jit(solution)/shard_map/ppermute | solution.py:306
  97.4 6.2 %collective-permute-start.10 = (bf16[512,256]{1,0:T(8,128)(2,1)S(1)}, bf16[512,256]{1,0:T(8,128)(2,1)S(1)}, u32[]{:S(2)}, u32[]{:S(2)}) collective-permute-start(bf16[512,256]{1,0:T(8,128)(2,1)S(1)} %get-tuple-element.69.cur_b), channel_id=1, source_target_pairs={{0,31},{1,2},{2,1},{3,4},{4,3},{5,6},{6,5},{7,8},{8,7},{9,10},{10,... | collective-permute-start | bytes 786440 | tf_op jit(solution)/shard_map/ppermute | solution.py:313
  103.7 1.9 collective-permute-start.15
  105.6 3.4 %collective-permute-done.10.rb = bf16[512,256]{1,0:T(8,128)(2,1)S(1)} collective-permute-done((bf16[512,256]{1,0:T(8,128)(2,1)S(1)}, bf16[512,256]{1,0:T(8,128)(2,1)S(1)}, u32[]{:S(2)}, u32[]{:S(2)}) %collective-permute-start.10) | collective-permute-done | bytes 262176 | tf_op jit(solution)/shard_map/ppermute | solution.py:313
  110.4 4.9 %collective-permute-start.14 = (bf16[4160,128]{1,0:T(8,128)(2,1)S(1)}, bf16[4160,128]{1,0:T(8,128)(2,1)S(1)}, u32[]{:S(2)}, u32[]{:S(2)}) collective-permute-start(bf16[4160,128]{1,0:T(8,128)(2,1)S(1)} %collective-permute-done.7.first), channel_id=1, source_target_pairs={{0,448},{32,480},{64,0},{96,32},{128,64},{160,96},{192,128},{224,1... | collective-permute-start | bytes 3194888 | tf_op jit(solution)/shard_map/ppermute | solution.py:317
  115.4 1.9 collective-permute-start.21
  119.4 6.2 %collective-permute-start.20 = (bf16[1040,128]{1,0:T(8,128)(2,1)S(1)}, bf16[1040,128]{1,0:T(8,128)(2,1)S(1)}, u32[]{:S(2)}, u32[]{:S(2)}) collective-permute-start(bf16[1040,128]{1,0:T(8,128)(2,1)S(1)} %pad_maximum_fusion.3), channel_id=1, source_target_pairs={{0,31},{1,2},{2,1},{3,4},{4,3},{5,6},{6,5},{7,8},{8,7},{9,10},{10,... | collective-permute-start | bytes 798728 | tf_op jit(solution)/shard_map/ppermute | solution.py:294
  125.7 2.5 collective-permute-done.19.rim_a
  128.1 2.2 collective-permute-start.17
  130.3 6.2 %collective-permute-start.18 = (bf16[512,256]{1,0:T(8,128)(2,1)S(1)}, bf16[512,256]{1,0:T(8,128)(2,1)S(1)}, u32[]{:S(2)}, u32[]{:S(2)}) collective-permute-start(bf16[512,256]{1,0:T(8,128)(2,1)S(1)} %get-tuple-element.79.cur_b), channel_id=1, source_target_pairs={{0,31},{1,2},{2,1},{3,4},{4,3},{5,6},{6,5},{7,8},{8,7},{9,10},{10,... | collective-permute-start | bytes 786440 | tf_op jit(solution)/shard_map/ppermute | solution.py:313
  136.6 1.9 collective-permute-start.16
  138.5 4.9 %collective-permute-done.18.rb = bf16[512,256]{1,0:T(8,128)(2,1)S(1)} collective-permute-done((bf16[512,256]{1,0:T(8,128)(2,1)S(1)}, bf16[512,256]{1,0:T(8,128)(2,1)S(1)}, u32[]{:S(2)}, u32[]{:S(2)}) %collective-permute-start.18) | collective-permute-done | bytes 262176 | tf_op jit(solution)/shard_map/ppermute | solution.py:313
  145.0 1.9 collective-permute-start.26
  147.0 1.9 collective-permute-start.24
  149.0 6.2 %collective-permute-start.25 = (bf16[1040,128]{1,0:T(8,128)(2,1)S(1)}, bf16[1040,128]{1,0:T(8,128)(2,1)S(1)}, u32[]{:S(2)}, u32[]{:S(2)}) collective-permute-start(bf16[1040,128]{1,0:T(8,128)(2,1)S(1)} %pad_maximum_fusion.5), channel_id=1, source_target_pairs={{0,31},{1,2},{2,1},{3,4},{4,3},{5,6},{6,5},{7,8},{8,7},{9,10},{10,... | collective-permute-start | bytes 798728 | tf_op jit(solution)/shard_map/ppermute | solution.py:294
  157.7 6.7 %collective-permute-start.23 = (bf16[512,256]{1,0:T(8,128)(2,1)S(1)}, bf16[512,256]{1,0:T(8,128)(2,1)S(1)}, u32[]{:S(2)}, u32[]{:S(2)}) collective-permute-start(bf16[512,256]{1,0:T(8,128)(2,1)S(1)} %get-tuple-element.84.cur_b), channel_id=1, source_target_pairs={{0,31},{1,2},{2,1},{3,4},{4,3},{5,6},{6,5},{7,8},{8,7},{9,10},{10,... | collective-permute-start | bytes 786440 | tf_op jit(solution)/shard_map/ppermute | solution.py:313
  165.6 5.3 %collective-permute-done.23.rb = bf16[512,256]{1,0:T(8,128)(2,1)S(1)} collective-permute-done((bf16[512,256]{1,0:T(8,128)(2,1)S(1)}, bf16[512,256]{1,0:T(8,128)(2,1)S(1)}, u32[]{:S(2)}, u32[]{:S(2)}) %collective-permute-start.23) | collective-permute-done | bytes 262176 | tf_op jit(solution)/shard_map/ppermute | solution.py:313
  172.3 2.1 gather_last.1
  176.5 2.4 collective-permute-start.31
  178.9 1.9 collective-permute-start.29
  180.9 6.2 %collective-permute-start.30 = (bf16[1040,128]{1,0:T(8,128)(2,1)S(1)}, bf16[1040,128]{1,0:T(8,128)(2,1)S(1)}, u32[]{:S(2)}, u32[]{:S(2)}) collective-permute-start(bf16[1040,128]{1,0:T(8,128)(2,1)S(1)} %pad_maximum_fusion.7), channel_id=1, source_target_pairs={{0,31},{1,2},{2,1},{3,4},{4,3},{5,6},{6,5},{7,8},{8,7},{9,10},{10,... | collective-permute-start | bytes 798728 | tf_op jit(solution)/shard_map/ppermute | solution.py:294
  189.1 3.8 %collective-permute-start.34 = (bf16[3120,128]{1,0:T(8,128)(2,1)S(1)}, bf16[3120,128]{1,0:T(8,128)(2,1)S(1)}, u32[]{:S(2)}, u32[]{:S(2)}) collective-permute-start(bf16[3120,128]{1,0:T(8,128)(2,1)S(1)} %get-tuple-element.95), channel_id=1, source_target_pairs={{0,1},{1,0},{2,3},{3,2},{4,5},{5,4},{6,7},{7,6},{8,9},{9,8},{10,11... | collective-permute-start | bytes 2396168 | tf_op jit(solution)/shard_map/ppermute | solution.py:294
  194.4 6.2 %collective-permute-start.35 = (bf16[3120,128]{1,0:T(8,128)(2,1)S(1)}, bf16[3120,128]{1,0:T(8,128)(2,1)S(1)}, u32[]{:S(2)}, u32[]{:S(2)}) collective-permute-start(bf16[3120,128]{1,0:T(8,128)(2,1)S(1)} %get-tuple-element.96), channel_id=1, source_target_pairs={{0,31},{1,2},{2,1},{3,4},{4,3},{5,6},{6,5},{7,8},{8,7},{9,10},{10,... | collective-permute-start | bytes 2396168 | tf_op jit(solution)/shard_map/ppermute | solution.py:294
  200.6 3.1 collective-permute-start.28
  203.8 20.3 %collective-permute-done.28.rb = bf16[512,256]{1,0:T(8,128)(2,1)S(1)} collective-permute-done((bf16[512,256]{1,0:T(8,128)(2,1)S(1)}, bf16[512,256]{1,0:T(8,128)(2,1)S(1)}, u32[]{:S(2)}, u32[]{:S(2)}) %collective-permute-start.28) | collective-permute-done | bytes 262176 | tf_op jit(solution)/shard_map/ppermute | solution.py:313
  227.5 6.2 %collective-permute-start.33 = (bf16[512,256]{1,0:T(8,128)(2,1)S(1)}, bf16[512,256]{1,0:T(8,128)(2,1)S(1)}, u32[]{:S(2)}, u32[]{:S(2)}) collective-permute-start(bf16[512,256]{1,0:T(8,128)(2,1)S(1)} %get-tuple-element.94.cur_b), channel_id=1, source_target_pairs={{0,31},{1,2},{2,1},{3,4},{4,3},{5,6},{6,5},{7,8},{8,7},{9,10},{10,... | collective-permute-start | bytes 786440 | tf_op jit(solution)/shard_map/ppermute | solution.py:313
  234.0 5.2 %collective-permute-done.33.rb = bf16[512,256]{1,0:T(8,128)(2,1)S(1)} collective-permute-done((bf16[512,256]{1,0:T(8,128)(2,1)S(1)}, bf16[512,256]{1,0:T(8,128)(2,1)S(1)}, u32[]{:S(2)}, u32[]{:S(2)}) %collective-permute-start.33) | collective-permute-done | bytes 262176 | tf_op jit(solution)/shard_map/ppermute | solution.py:313
  242.6 6.2 %collective-permute-start.38 = (bf16[512,256]{1,0:T(8,128)(2,1)S(1)}, bf16[512,256]{1,0:T(8,128)(2,1)S(1)}, u32[]{:S(2)}, u32[]{:S(2)}) collective-permute-start(bf16[512,256]{1,0:T(8,128)(2,1)S(1)} %get-tuple-element.99.cur_b), channel_id=1, source_target_pairs={{0,31},{1,2},{2,1},{3,4},{4,3},{5,6},{6,5},{7,8},{8,7},{9,10},{10,... | collective-permute-start | bytes 786440 | tf_op jit(solution)/shard_map/ppermute | solution.py:313
  248.9 5.2 %collective-permute-done.38.rb = bf16[512,256]{1,0:T(8,128)(2,1)S(1)} collective-permute-done((bf16[512,256]{1,0:T(8,128)(2,1)S(1)}, bf16[512,256]{1,0:T(8,128)(2,1)S(1)}, u32[]{:S(2)}, u32[]{:S(2)}) %collective-permute-start.38) | collective-permute-done | bytes 262176 | tf_op jit(solution)/shard_map/ppermute | solution.py:313
  255.7 1.9 collective-permute-start.39
  257.6 6.2 %collective-permute-start.40 = (bf16[512,256]{1,0:T(8,128)(2,1)S(1)}, bf16[512,256]{1,0:T(8,128)(2,1)S(1)}, u32[]{:S(2)}, u32[]{:S(2)}) collective-permute-start(bf16[512,256]{1,0:T(8,128)(2,1)S(1)} %get-tuple-element.101.cur_b), channel_id=1, source_target_pairs={{0,31},{1,2},{2,1},{3,4},{4,3},{5,6},{6,5},{7,8},{8,7},{9,10},{10,... | collective-permute-start | bytes 786440 | tf_op jit(solution)/shard_map/ppermute | solution.py:313
  263.9 5.2 %collective-permute-done.40.rb = bf16[512,256]{1,0:T(8,128)(2,1)S(1)} collective-permute-done((bf16[512,256]{1,0:T(8,128)(2,1)S(1)}, bf16[512,256]{1,0:T(8,128)(2,1)S(1)}, u32[]{:S(2)}, u32[]{:S(2)}) %collective-permute-start.40) | collective-permute-done | bytes 262176 | tf_op jit(solution)/shard_map/ppermute | solution.py:313
  271.0 16.4 %all_to_all.10 = bf16[32,8,256]{2,1,0:T(8,128)(2,1)S(1)} all-to-all(bf16[32,8,256]{2,1,0:T(8,128)(2,1)S(1)} %fusion), channel_id=1, replica_groups=mesh['phase'=16,'rows'=32] {'rows'}, dimensions={0} | all-to-all | bytes 262144 | tf_op jit(solution)/shard_map/all_to_all | solution.py:270
  287.5 14.8 %all_to_all.11 = f32[32,8,256]{2,1,0:T(8,128)S(1)} all-to-all(f32[32,8,256]{2,1,0:T(8,128)S(1)} %broadcast_in_dim.12), channel_id=1, replica_groups=mesh['phase'=16,'rows'=32] {'rows'}, dimensions={0} | all-to-all | bytes 524288 | tf_op jit(solution)/shard_map/all_to_all | solution.py:273
  303.1 14.2 %factor_solve.1 = (f32[1024,256]{1,0:T(8,128)}, f32[256,256]{1,0:T(8,128)}) custom-call(s32[3]{0:T(128)} %copy-done.4, f32[256,256]{1,0:T(8,128)} %multiply_bitcast_fusion.gram_ref, bf16[512,256]{1,0:T(8,128)(2,1)} %copy-done.2, bf16[512,256]{1,0:T(8,128)(2,1)} %copy-done.3), custom_call_target="tpu_custom_call" | custom-call | tf_op jit(solution)/shard_map/factor_solve/pallas_call | solution.py:253
  (87 shorter events, 36.9 us)
Async XLA Ops:
  1.5 170.8 %copy-start.4 = (s32[3]{0:T(128)}, s32[3]{0:T(128)S(1)}, u32[]{:S(2)}) copy-start(s32[3]{0:T(128)S(1)} %pad_add_fusion.info) | copy-start | bytes 40
  1.5 1.2 copy-start
  2.7 0.7 copy-start.5
  3.4 7.7 %copy-start.1 = (bf16[1,1024,256]{2,1,0:T(8,128)(2,1)S(1)}, bf16[1,1024,256]{2,1,0:T(8,128)(2,1)}, u32[]{:S(2)}) copy-start(bf16[1,1024,256]{2,1,0:T(8,128)(2,1)} %param.4) | copy-start | bytes 1572868
  4.1 27.8 %collective-permute-start = (bf16[4160,128]{1,0:T(8,128)(2,1)S(1)}, bf16[4160,128]{1,0:T(8,128)(2,1)S(1)}, u32[]{:S(2)}, u32[]{:S(2)}) collective-permute-start(bf16[4160,128]{1,0:T(8,128)(2,1)S(1)} %get-tuple-element.62.first.refs_3_), channel_id=1, source_target_pairs={{0,448},{32,480},{64,0},{96,32},{128,64},{160,96},{192,128},{224,1... | collective-permute-start | bytes 3194888 | tf_op jit(solution)/shard_map/ppermute | solution.py:305
  32.0 37.6 %collective-permute-start.6 = (bf16[4160,128]{1,0:T(8,128)(2,1)S(1)}, bf16[4160,128]{1,0:T(8,128)(2,1)S(1)}, u32[]{:S(2)}, u32[]{:S(2)}) collective-permute-start(bf16[4160,128]{1,0:T(8,128)(2,1)S(1)} %broadcast_select_fusion.4), channel_id=1, source_target_pairs={{0,32},{32,0},{64,96},{96,64},{128,160},{160,128},{192,224},{224,1... | collective-permute-start | bytes 3194888 | tf_op jit(solution)/shard_map/ppermute | solution.py:323
  34.0 37.1 %collective-permute-start.1 = (bf16[4160,128]{1,0:T(8,128)(2,1)S(1)}, bf16[4160,128]{1,0:T(8,128)(2,1)S(1)}, u32[]{:S(2)}, u32[]{:S(2)}) collective-permute-start(bf16[4160,128]{1,0:T(8,128)(2,1)S(1)} %collective-permute-done.first), channel_id=1, source_target_pairs={{0,448},{32,480},{64,0},{96,32},{128,64},{160,96},{192,128},{224,1... | collective-permute-start | bytes 3194888 | tf_op jit(solution)/shard_map/ppermute | solution.py:317
  41.5 13.4 %collective-permute-start.2 = (bf16[512,256]{1,0:T(8,128)(2,1)S(1)}, bf16[512,256]{1,0:T(8,128)(2,1)S(1)}, u32[]{:S(2)}, u32[]{:S(2)}) collective-permute-start(bf16[512,256]{1,0:T(8,128)(2,1)S(1)} %get-tuple-element.58.cur_a), channel_id=1, source_target_pairs={{0,1},{1,0},{2,3},{3,2},{4,5},{5,4},{6,7},{7,6},{8,9},{9,8},{10,11... | collective-permute-start | bytes 786440 | tf_op jit(solution)/shard_map/ppermute | solution.py:312
  44.9 24.8 %collective-permute-start.4 = (bf16[1040,128]{1,0:T(8,128)(2,1)S(1)}, bf16[1040,128]{1,0:T(8,128)(2,1)S(1)}, u32[]{:S(2)}, u32[]{:S(2)}) collective-permute-start(bf16[1040,128]{1,0:T(8,128)(2,1)S(1)} %get-tuple-element.60), channel_id=1, source_target_pairs={{0,1},{1,0},{2,3},{3,2},{4,5},{5,4},{6,7},{7,6},{8,9},{9,8},{10,11... | collective-permute-start | bytes 798728 | tf_op jit(solution)/shard_map/ppermute | solution.py:294
  47.3 22.3 %collective-permute-start.5 = (bf16[1040,128]{1,0:T(8,128)(2,1)S(1)}, bf16[1040,128]{1,0:T(8,128)(2,1)S(1)}, u32[]{:S(2)}, u32[]{:S(2)}) collective-permute-start(bf16[1040,128]{1,0:T(8,128)(2,1)S(1)} %get-tuple-element.61), channel_id=1, source_target_pairs={{0,31},{1,2},{2,1},{3,4},{4,3},{5,6},{6,5},{7,8},{8,7},{9,10},{10,... | collective-permute-start | bytes 798728 | tf_op jit(solution)/shard_map/ppermute | solution.py:294
  54.9 12.8 %collective-permute-start.3 = (bf16[512,256]{1,0:T(8,128)(2,1)S(1)}, bf16[512,256]{1,0:T(8,128)(2,1)S(1)}, u32[]{:S(2)}, u32[]{:S(2)}) collective-permute-start(bf16[512,256]{1,0:T(8,128)(2,1)S(1)} %get-tuple-element.59.cur_b), channel_id=1, source_target_pairs={{0,31},{1,2},{2,1},{3,4},{4,3},{5,6},{6,5},{7,8},{8,7},{9,10},{10,... | collective-permute-start | bytes 786440 | tf_op jit(solution)/shard_map/ppermute | solution.py:313
  67.7 27.8 %collective-permute-start.8 = (bf16[4160,128]{1,0:T(8,128)(2,1)S(1)}, bf16[4160,128]{1,0:T(8,128)(2,1)S(1)}, u32[]{:S(2)}, u32[]{:S(2)}) collective-permute-start(bf16[4160,128]{1,0:T(8,128)(2,1)S(1)} %get-tuple-element.62.first.refs_3_), channel_id=1, source_target_pairs={{0,64},{32,96},{64,128},{96,160},{128,192},{160,224},{192,256},{22... | collective-permute-start | bytes 3194888 | tf_op jit(solution)/shard_map/ppermute | solution.py:306
  71.1 39.4 %collective-permute-start.7 = (bf16[4160,128]{1,0:T(8,128)(2,1)S(1)}, bf16[4160,128]{1,0:T(8,128)(2,1)S(1)}, u32[]{:S(2)}, u32[]{:S(2)}) collective-permute-start(bf16[4160,128]{1,0:T(8,128)(2,1)S(1)} %collective-permute-done.1.first), channel_id=1, source_target_pairs={{0,448},{32,480},{64,0},{96,32},{128,64},{160,96},{192,128},{224,1... | collective-permute-start | bytes 3194888 | tf_op jit(solution)/shard_map/ppermute | solution.py:317
  76.8 32.2 %collective-permute-start.13 = (bf16[4160,128]{1,0:T(8,128)(2,1)S(1)}, bf16[4160,128]{1,0:T(8,128)(2,1)S(1)}, u32[]{:S(2)}, u32[]{:S(2)}) collective-permute-start(bf16[4160,128]{1,0:T(8,128)(2,1)S(1)} %broadcast_select_fusion.3), channel_id=1, source_target_pairs={{0,32},{32,0},{64,96},{96,64},{128,160},{160,128},{192,224},{224,1... | collective-permute-start | bytes 3194888 | tf_op jit(solution)/shard_map/ppermute | solution.py:323
  78.8 18.6 %collective-permute-start.11 = (bf16[1040,128]{1,0:T(8,128)(2,1)S(1)}, bf16[1040,128]{1,0:T(8,128)(2,1)S(1)}, u32[]{:S(2)}, u32[]{:S(2)}) collective-permute-start(bf16[1040,128]{1,0:T(8,128)(2,1)S(1)} %pad_maximum_fusion), channel_id=1, source_target_pairs={{0,1},{1,0},{2,3},{3,2},{4,5},{5,4},{6,7},{7,6},{8,9},{9,8},{10,11... | collective-permute-start | bytes 798728 | tf_op jit(solution)/shard_map/ppermute | solution.py:294
  80.8 22.9 %collective-permute-start.12 = (bf16[1040,128]{1,0:T(8,128)(2,1)S(1)}, bf16[1040,128]{1,0:T(8,128)(2,1)S(1)}, u32[]{:S(2)}, u32[]{:S(2)}) collective-permute-start(bf16[1040,128]{1,0:T(8,128)(2,1)S(1)} %pad_maximum_fusion.1), channel_id=1, source_target_pairs={{0,31},{1,2},{2,1},{3,4},{4,3},{5,6},{6,5},{7,8},{8,7},{9,10},{10,... | collective-permute-start | bytes 798728 | tf_op jit(solution)/shard_map/ppermute | solution.py:294
  95.5 10.1 %collective-permute-start.9 = (bf16[512,256]{1,0:T(8,128)(2,1)S(1)}, bf16[512,256]{1,0:T(8,128)(2,1)S(1)}, u32[]{:S(2)}, u32[]{:S(2)}) collective-permute-start(bf16[512,256]{1,0:T(8,128)(2,1)S(1)} %get-tuple-element.68.cur_a), channel_id=1, source_target_pairs={{0,1},{1,0},{2,3},{3,2},{4,5},{5,4},{6,7},{7,6},{8,9},{9,8},{10,11... | collective-permute-start | bytes 786440 | tf_op jit(solution)/shard_map/ppermute | solution.py:312
  97.4 11.6 %collective-permute-start.10 = (bf16[512,256]{1,0:T(8,128)(2,1)S(1)}, bf16[512,256]{1,0:T(8,128)(2,1)S(1)}, u32[]{:S(2)}, u32[]{:S(2)}) collective-permute-start(bf16[512,256]{1,0:T(8,128)(2,1)S(1)} %get-tuple-element.69.cur_b), channel_id=1, source_target_pairs={{0,31},{1,2},{2,1},{3,4},{4,3},{5,6},{6,5},{7,8},{8,7},{9,10},{10,... | collective-permute-start | bytes 786440 | tf_op jit(solution)/shard_map/ppermute | solution.py:313
  103.7 26.7 %collective-permute-start.15 = (bf16[4160,128]{1,0:T(8,128)(2,1)S(1)}, bf16[4160,128]{1,0:T(8,128)(2,1)S(1)}, u32[]{:S(2)}, u32[]{:S(2)}) collective-permute-start(bf16[4160,128]{1,0:T(8,128)(2,1)S(1)} %collective-permute-done.8.refs_2_.first), channel_id=1, source_target_pairs={{0,64},{32,96},{64,128},{96,160},{128,192},{160,224},{192,256},{22... | collective-permute-start | bytes 3194888 | tf_op jit(solution)/shard_map/ppermute | solution.py:321
  110.4 34.4 %collective-permute-start.14 = (bf16[4160,128]{1,0:T(8,128)(2,1)S(1)}, bf16[4160,128]{1,0:T(8,128)(2,1)S(1)}, u32[]{:S(2)}, u32[]{:S(2)}) collective-permute-start(bf16[4160,128]{1,0:T(8,128)(2,1)S(1)} %collective-permute-done.7.first), channel_id=1, source_target_pairs={{0,448},{32,480},{64,0},{96,32},{128,64},{160,96},{192,128},{224,1... | collective-permute-start | bytes 3194888 | tf_op jit(solution)/shard_map/ppermute | solution.py:317
  115.4 28.0 %collective-permute-start.21 = (bf16[4160,128]{1,0:T(8,128)(2,1)S(1)}, bf16[4160,128]{1,0:T(8,128)(2,1)S(1)}, u32[]{:S(2)}, u32[]{:S(2)}) collective-permute-start(bf16[4160,128]{1,0:T(8,128)(2,1)S(1)} %broadcast_select_fusion.2), channel_id=1, source_target_pairs={{0,32},{32,0},{64,96},{96,64},{128,160},{160,128},{192,224},{224,1... | collective-permute-start | bytes 3194888 | tf_op jit(solution)/shard_map/ppermute | solution.py:323
  117.4 10.7 %collective-permute-start.19 = (bf16[1040,128]{1,0:T(8,128)(2,1)S(1)}, bf16[1040,128]{1,0:T(8,128)(2,1)S(1)}, u32[]{:S(2)}, u32[]{:S(2)}) collective-permute-start(bf16[1040,128]{1,0:T(8,128)(2,1)S(1)} %pad_maximum_fusion.2), channel_id=1, source_target_pairs={{0,1},{1,0},{2,3},{3,2},{4,5},{5,4},{6,7},{7,6},{8,9},{9,8},{10,11... | collective-permute-start | bytes 798728 | tf_op jit(solution)/shard_map/ppermute | solution.py:294
  119.4 17.2 %collective-permute-start.20 = (bf16[1040,128]{1,0:T(8,128)(2,1)S(1)}, bf16[1040,128]{1,0:T(8,128)(2,1)S(1)}, u32[]{:S(2)}, u32[]{:S(2)}) collective-permute-start(bf16[1040,128]{1,0:T(8,128)(2,1)S(1)} %pad_maximum_fusion.3), channel_id=1, source_target_pairs={{0,31},{1,2},{2,1},{3,4},{4,3},{5,6},{6,5},{7,8},{8,7},{9,10},{10,... | collective-permute-start | bytes 798728 | tf_op jit(solution)/shard_map/ppermute | solution.py:294
  128.1 10.4 %collective-permute-start.17 = (bf16[512,256]{1,0:T(8,128)(2,1)S(1)}, bf16[512,256]{1,0:T(8,128)(2,1)S(1)}, u32[]{:S(2)}, u32[]{:S(2)}) collective-permute-start(bf16[512,256]{1,0:T(8,128)(2,1)S(1)} %get-tuple-element.78.cur_a), channel_id=1, source_target_pairs={{0,1},{1,0},{2,3},{3,2},{4,5},{5,4},{6,7},{7,6},{8,9},{9,8},{10,11... | collective-permute-start | bytes 786440 | tf_op jit(solution)/shard_map/ppermute | solution.py:312
  130.3 13.1 %collective-permute-start.18 = (bf16[512,256]{1,0:T(8,128)(2,1)S(1)}, bf16[512,256]{1,0:T(8,128)(2,1)S(1)}, u32[]{:S(2)}, u32[]{:S(2)}) collective-permute-start(bf16[512,256]{1,0:T(8,128)(2,1)S(1)} %get-tuple-element.79.cur_b), channel_id=1, source_target_pairs={{0,31},{1,2},{2,1},{3,4},{4,3},{5,6},{6,5},{7,8},{8,7},{9,10},{10,... | collective-permute-start | bytes 786440 | tf_op jit(solution)/shard_map/ppermute | solution.py:313
  136.6 35.7 %collective-permute-start.16 = (bf16[4160,128]{1,0:T(8,128)(2,1)S(1)}, bf16[4160,128]{1,0:T(8,128)(2,1)S(1)}, u32[]{:S(2)}, u32[]{:S(2)}) collective-permute-start(bf16[4160,128]{1,0:T(8,128)(2,1)S(1)} %collective-permute-done.15.refs_1_.first), channel_id=1, source_target_pairs={{0,64},{32,96},{64,128},{96,160},{128,192},{160,224},{192,256},{22... | collective-permute-start | bytes 3194888 | tf_op jit(solution)/shard_map/ppermute | solution.py:321
  145.0 25.8 %collective-permute-start.26 = (bf16[4160,128]{1,0:T(8,128)(2,1)S(1)}, bf16[4160,128]{1,0:T(8,128)(2,1)S(1)}, u32[]{:S(2)}, u32[]{:S(2)}) collective-permute-start(bf16[4160,128]{1,0:T(8,128)(2,1)S(1)} %broadcast_select_fusion.1), channel_id=1, source_target_pairs={{0,32},{32,0},{64,96},{96,64},{128,160},{160,128},{192,224},{224,1... | collective-permute-start | bytes 3194888 | tf_op jit(solution)/shard_map/ppermute | solution.py:323
  147.0 10.7 %collective-permute-start.24 = (bf16[1040,128]{1,0:T(8,128)(2,1)S(1)}, bf16[1040,128]{1,0:T(8,128)(2,1)S(1)}, u32[]{:S(2)}, u32[]{:S(2)}) collective-permute-start(bf16[1040,128]{1,0:T(8,128)(2,1)S(1)} %pad_maximum_fusion.4), channel_id=1, source_target_pairs={{0,1},{1,0},{2,3},{3,2},{4,5},{5,4},{6,7},{7,6},{8,9},{9,8},{10,11... | collective-permute-start | bytes 798728 | tf_op jit(solution)/shard_map/ppermute | solution.py:294
  149.0 15.5 %collective-permute-start.25 = (bf16[1040,128]{1,0:T(8,128)(2,1)S(1)}, bf16[1040,128]{1,0:T(8,128)(2,1)S(1)}, u32[]{:S(2)}, u32[]{:S(2)}) collective-permute-start(bf16[1040,128]{1,0:T(8,128)(2,1)S(1)} %pad_maximum_fusion.5), channel_id=1, source_target_pairs={{0,31},{1,2},{2,1},{3,4},{4,3},{5,6},{6,5},{7,8},{8,7},{9,10},{10,... | collective-permute-start | bytes 798728 | tf_op jit(solution)/shard_map/ppermute | solution.py:294
  155.2 10.3 %collective-permute-start.22 = (bf16[512,256]{1,0:T(8,128)(2,1)S(1)}, bf16[512,256]{1,0:T(8,128)(2,1)S(1)}, u32[]{:S(2)}, u32[]{:S(2)}) collective-permute-start(bf16[512,256]{1,0:T(8,128)(2,1)S(1)} %get-tuple-element.83.cur_a), channel_id=1, source_target_pairs={{0,1},{1,0},{2,3},{3,2},{4,5},{5,4},{6,7},{7,6},{8,9},{9,8},{10,11... | collective-permute-start | bytes 786440 | tf_op jit(solution)/shard_map/ppermute | solution.py:312
  157.7 13.1 %collective-permute-start.23 = (bf16[512,256]{1,0:T(8,128)(2,1)S(1)}, bf16[512,256]{1,0:T(8,128)(2,1)S(1)}, u32[]{:S(2)}, u32[]{:S(2)}) collective-permute-start(bf16[512,256]{1,0:T(8,128)(2,1)S(1)} %get-tuple-element.84.cur_b), channel_id=1, source_target_pairs={{0,31},{1,2},{2,1},{3,4},{4,3},{5,6},{6,5},{7,8},{8,7},{9,10},{10,... | collective-permute-start | bytes 786440 | tf_op jit(solution)/shard_map/ppermute | solution.py:313
  174.4 64.8 %collective-permute-start.36 = (bf16[12480,128]{1,0:T(8,128)(2,1)S(1)}, bf16[12480,128]{1,0:T(8,128)(2,1)S(1)}, u32[]{:S(2)}, u32[]{:S(2)}) collective-permute-start(bf16[12480,128]{1,0:T(8,128)(2,1)S(1)} %get-tuple-element.97), channel_id=1, source_target_pairs={{0,32},{32,0},{64,96},{96,64},{128,160},{160,128},{192,224},{224,1... | collective-permute-start | bytes 9584648 | tf_op jit(solution)/shard_map/ppermute | solution.py:330
  176.5 47.6 %collective-permute-start.31 = (bf16[4160,128]{1,0:T(8,128)(2,1)S(1)}, bf16[4160,128]{1,0:T(8,128)(2,1)S(1)}, u32[]{:S(2)}, u32[]{:S(2)}) collective-permute-start(bf16[4160,128]{1,0:T(8,128)(2,1)S(1)} %broadcast_select_fusion), channel_id=1, source_target_pairs={{0,32},{32,0},{64,96},{96,64},{128,160},{160,128},{192,224},{224,1... | collective-permute-start | bytes 3194888 | tf_op jit(solution)/shard_map/ppermute | solution.py:323
  178.9 10.2 %collective-permute-start.29 = (bf16[1040,128]{1,0:T(8,128)(2,1)S(1)}, bf16[1040,128]{1,0:T(8,128)(2,1)S(1)}, u32[]{:S(2)}, u32[]{:S(2)}) collective-permute-start(bf16[1040,128]{1,0:T(8,128)(2,1)S(1)} %pad_maximum_fusion.6), channel_id=1, source_target_pairs={{0,1},{1,0},{2,3},{3,2},{4,5},{5,4},{6,7},{7,6},{8,9},{9,8},{10,11... | collective-permute-start | bytes 798728 | tf_op jit(solution)/shard_map/ppermute | solution.py:294
  180.9 13.5 %collective-permute-start.30 = (bf16[1040,128]{1,0:T(8,128)(2,1)S(1)}, bf16[1040,128]{1,0:T(8,128)(2,1)S(1)}, u32[]{:S(2)}, u32[]{:S(2)}) collective-permute-start(bf16[1040,128]{1,0:T(8,128)(2,1)S(1)} %pad_maximum_fusion.7), channel_id=1, source_target_pairs={{0,31},{1,2},{2,1},{3,4},{4,3},{5,6},{6,5},{7,8},{8,7},{9,10},{10,... | collective-permute-start | bytes 798728 | tf_op jit(solution)/shard_map/ppermute | solution.py:294
  187.1 13.5 %collective-permute-start.27 = (bf16[512,256]{1,0:T(8,128)(2,1)S(1)}, bf16[512,256]{1,0:T(8,128)(2,1)S(1)}, u32[]{:S(2)}, u32[]{:S(2)}) collective-permute-start(bf16[512,256]{1,0:T(8,128)(2,1)S(1)} %get-tuple-element.89.cur_a), channel_id=1, source_target_pairs={{0,1},{1,0},{2,3},{3,2},{4,5},{5,4},{6,7},{7,6},{8,9},{9,8},{10,11... | collective-permute-start | bytes 786440 | tf_op jit(solution)/shard_map/ppermute | solution.py:312
  189.1 44.6 %collective-permute-start.34 = (bf16[3120,128]{1,0:T(8,128)(2,1)S(1)}, bf16[3120,128]{1,0:T(8,128)(2,1)S(1)}, u32[]{:S(2)}, u32[]{:S(2)}) collective-permute-start(bf16[3120,128]{1,0:T(8,128)(2,1)S(1)} %get-tuple-element.95), channel_id=1, source_target_pairs={{0,1},{1,0},{2,3},{3,2},{4,5},{5,4},{6,7},{7,6},{8,9},{9,8},{10,11... | collective-permute-start | bytes 2396168 | tf_op jit(solution)/shard_map/ppermute | solution.py:294
  194.4 39.3 %collective-permute-start.35 = (bf16[3120,128]{1,0:T(8,128)(2,1)S(1)}, bf16[3120,128]{1,0:T(8,128)(2,1)S(1)}, u32[]{:S(2)}, u32[]{:S(2)}) collective-permute-start(bf16[3120,128]{1,0:T(8,128)(2,1)S(1)} %get-tuple-element.96), channel_id=1, source_target_pairs={{0,31},{1,2},{2,1},{3,4},{4,3},{5,6},{6,5},{7,8},{8,7},{9,10},{10,... | collective-permute-start | bytes 2396168 | tf_op jit(solution)/shard_map/ppermute | solution.py:294
  200.6 23.5 %collective-permute-start.28 = (bf16[512,256]{1,0:T(8,128)(2,1)S(1)}, bf16[512,256]{1,0:T(8,128)(2,1)S(1)}, u32[]{:S(2)}, u32[]{:S(2)}) collective-permute-start(bf16[512,256]{1,0:T(8,128)(2,1)S(1)} %get-tuple-element.90.cur_b), channel_id=1, source_target_pairs={{0,31},{1,2},{2,1},{3,4},{4,3},{5,6},{6,5},{7,8},{8,7},{9,10},{10,... | collective-permute-start | bytes 786440 | tf_op jit(solution)/shard_map/ppermute | solution.py:313
  225.6 8.4 %collective-permute-start.32 = (bf16[512,256]{1,0:T(8,128)(2,1)S(1)}, bf16[512,256]{1,0:T(8,128)(2,1)S(1)}, u32[]{:S(2)}, u32[]{:S(2)}) collective-permute-start(bf16[512,256]{1,0:T(8,128)(2,1)S(1)} %get-tuple-element.93.cur_a), channel_id=1, source_target_pairs={{0,1},{1,0},{2,3},{3,2},{4,5},{5,4},{6,7},{7,6},{8,9},{9,8},{10,11... | collective-permute-start | bytes 786440 | tf_op jit(solution)/shard_map/ppermute | solution.py:312
  227.5 11.7 %collective-permute-start.33 = (bf16[512,256]{1,0:T(8,128)(2,1)S(1)}, bf16[512,256]{1,0:T(8,128)(2,1)S(1)}, u32[]{:S(2)}, u32[]{:S(2)}) collective-permute-start(bf16[512,256]{1,0:T(8,128)(2,1)S(1)} %get-tuple-element.94.cur_b), channel_id=1, source_target_pairs={{0,31},{1,2},{2,1},{3,4},{4,3},{5,6},{6,5},{7,8},{8,7},{9,10},{10,... | collective-permute-start | bytes 786440 | tf_op jit(solution)/shard_map/ppermute | solution.py:313
  240.7 8.3 %collective-permute-start.37 = (bf16[512,256]{1,0:T(8,128)(2,1)S(1)}, bf16[512,256]{1,0:T(8,128)(2,1)S(1)}, u32[]{:S(2)}, u32[]{:S(2)}) collective-permute-start(bf16[512,256]{1,0:T(8,128)(2,1)S(1)} %get-tuple-element.98.cur_a), channel_id=1, source_target_pairs={{0,1},{1,0},{2,3},{3,2},{4,5},{5,4},{6,7},{7,6},{8,9},{9,8},{10,11... | collective-permute-start | bytes 786440 | tf_op jit(solution)/shard_map/ppermute | solution.py:312
  242.6 11.6 %collective-permute-start.38 = (bf16[512,256]{1,0:T(8,128)(2,1)S(1)}, bf16[512,256]{1,0:T(8,128)(2,1)S(1)}, u32[]{:S(2)}, u32[]{:S(2)}) collective-permute-start(bf16[512,256]{1,0:T(8,128)(2,1)S(1)} %get-tuple-element.99.cur_b), channel_id=1, source_target_pairs={{0,31},{1,2},{2,1},{3,4},{4,3},{5,6},{6,5},{7,8},{8,7},{9,10},{10,... | collective-permute-start | bytes 786440 | tf_op jit(solution)/shard_map/ppermute | solution.py:313
  255.7 8.3 %collective-permute-start.39 = (bf16[512,256]{1,0:T(8,128)(2,1)S(1)}, bf16[512,256]{1,0:T(8,128)(2,1)S(1)}, u32[]{:S(2)}, u32[]{:S(2)}) collective-permute-start(bf16[512,256]{1,0:T(8,128)(2,1)S(1)} %get-tuple-element.100.cur_a), channel_id=1, source_target_pairs={{0,1},{1,0},{2,3},{3,2},{4,5},{5,4},{6,7},{7,6},{8,9},{9,8},{10,11... | collective-permute-start | bytes 786440 | tf_op jit(solution)/shard_map/ppermute | solution.py:312
  257.6 11.6 %collective-permute-start.40 = (bf16[512,256]{1,0:T(8,128)(2,1)S(1)}, bf16[512,256]{1,0:T(8,128)(2,1)S(1)}, u32[]{:S(2)}, u32[]{:S(2)}) collective-permute-start(bf16[512,256]{1,0:T(8,128)(2,1)S(1)} %get-tuple-element.101.cur_b), channel_id=1, source_target_pairs={{0,31},{1,2},{2,1},{3,4},{4,3},{5,6},{6,5},{7,8},{8,7},{9,10},{10,... | collective-permute-start | bytes 786440 | tf_op jit(solution)/shard_map/ppermute | solution.py:313
  270.6 16.8 %copy-start.2 = (bf16[512,256]{1,0:T(8,128)(2,1)}, bf16[512,256]{1,0:T(8,128)(2,1)S(1)}, u32[]{:S(2)}) copy-start(bf16[512,256]{1,0:T(8,128)(2,1)S(1)} %get-tuple-element.102.half_a) | copy-start | bytes 786436
  270.7 16.8 %copy-start.3 = (bf16[512,256]{1,0:T(8,128)(2,1)}, bf16[512,256]{1,0:T(8,128)(2,1)S(1)}, u32[]{:S(2)}) copy-start(bf16[512,256]{1,0:T(8,128)(2,1)S(1)} %get-tuple-element.103.half_b) | copy-start | bytes 786436

commit v6 on v5

--- a/solution.py
+++ b/solution.py
@@ -13,13 +13,37 @@
 HALF = 4 * TILE
 DEAD = 7
 
-def visit_kernel(rim_at, second_at, cur_a, cur_b, ra, rb, rim_a, rim_b, first, second, out_a, out_b, wide, mid):
+def copy_rims(operator, side_a, side_b, at):
+    span = operator.shape[0]
+    body = span - span // (4 * TILE + 8) * 8
+    edge = HB * 4 * TILE
+    tables = 8 * HB
+
+    @pl.loop(0, edge, step=TILE)
+    def _(line):
+        line = pl.multiple_of(line, TILE)
+        to = pl.ds(pl.multiple_of(at + line, 16), TILE)
+        side_a[to, :] = operator[pl.ds(line, TILE), :]
+        side_b[to, :] = operator[pl.ds(body - edge + line, TILE), :]
+
+    at = at + edge
+    side_a[at : at + tables, :] = operator[body : body + tables, :]
+    side_b[at : at + tables, :] = operator[span - tables :, :]
+
+def visit_kernel(rim_at, second_at, flat, *refs):
+    cur_a, cur_b, ra, rb, rim_a, rim_b, first, second = refs[:8]
+    out_a, out_b, wide, mid = refs[-4:]
+
+    def pieces(ref, n):
+        for part in range(2):
+            at = part * HALF + n * TILE
+            yield slice(part * TILE, (part + 1) * TILE), ref[at : at + TILE, :]
+
     for n in range(4):
-        wide[(3 - n) * TILE : (4 - n) * TILE, :] = ra[n * TILE : (n + 1) * TILE, :]
-        wide[(15 - n) * TILE : (16 - n) * TILE, :] = rb[n * TILE : (n + 1) * TILE, :]
-    wide[4 * TILE : 8 * TILE, :] = cur_a[...]
-    wide[8 * TILE : 12 * TILE, :] = cur_b[...]
-    zero = jnp.zeros((TILE, cur_a.shape[1]), cur_a.dtype)
+        for place, ref in ((3 - n, ra), (15 - n, rb), (4 + n, cur_a), (8 + n, cur_b)):
+            for lanes, piece in pieces(ref, n):
+                wide[place * TILE : (place + 1) * TILE, lanes] = piece
+    zero = jnp.zeros((TILE, 2 * TILE), wide.dtype)
     wide[16 * TILE :, :] = zero
     mid[12 * TILE :, :] = zero
 
@@ -54,25 +78,39 @@
         mid[(c + 2) * TILE : (c + 3) * TILE, :] = row(first, 0, 8, c, wide, c + 4, 1, 16)
     for c in range(8):
         half = out_a if c < 4 else out_b
-        half[c % 4 * TILE : (c % 4 + 1) * TILE, :] = row(second, second_at, 8, c, mid, c + 2, 1, 12)
-
-def visit(halves, ra, rb, rim_a, rim_b, first, second, rim_at=0, second_at=0):
-    vmem = pl.BlockSpec(memory_space=pltpu.VMEM)
-    shape = jax.ShapeDtypeStruct(halves[0].shape, halves[0].dtype)
-    columns = shape.shape[1]
-    return pl.pallas_call(
-        functools.partial(visit_kernel, rim_at, second_at),
+        value = row(second, second_at, 8, c, mid, c + 2, 1, 12)
+        at = c % 4 * TILE
+        if flat:
+            half[at : at + TILE, :] = value
+        else:
+            half[at : at + TILE, :] = value[:, :TILE]
+            half[HALF + at : HALF + at + TILE, :] = value[:, TILE:]
+    if len(refs) == 13:
+        copy_rims(refs[8], out_a, out_b, 2 * HALF)
+
+def visit(halves, sides, rims, first, second, following, flat, rim_at, second_at):
+    vmem = pl.BlockSpec(memory_space=pltpu.VMEM)
+    kind = halves[0].dtype
+    lines = 2 * HALF
+    if following is not None:
+        lines += HB * (4 * TILE + 8)
+    shape = jax.ShapeDtypeStruct((HALF, 2 * TILE) if flat else (lines, TILE), kind)
+    operands = [*halves, *sides, *rims, first, second]
+    if following is not None:
+        operands.append(following)
+    return pl.pallas_call(
+        functools.partial(visit_kernel, rim_at, second_at, flat),
         out_shape=(shape, shape),
-        in_specs=[vmem] * 8,
+        in_specs=[vmem] * len(operands),
         out_specs=(vmem, vmem),
         scratch_shapes=[
-            pltpu.VMEM((17 * TILE, columns), shape.dtype),
-            pltpu.VMEM((13 * TILE, columns), shape.dtype),
+            pltpu.VMEM((17 * TILE, 2 * TILE), kind),
+            pltpu.VMEM((13 * TILE, 2 * TILE), kind),
         ],
         compiler_params=pltpu.CompilerParams(vmem_limit_bytes=24 * 1024 * 1024),
         cost_estimate=pl.CostEstimate(flops=700_000_000, bytes_accessed=4_000_000, transcendentals=0),
         name="two_steps",
-    )(*halves, ra, rb, rim_a, rim_b, first, second)
+    )(*operands)
 
 def pack_kernel(total, info, cols, counts, blocks, packed, rim_a, rim_b):
     even = info[0]
@@ -123,13 +161,14 @@
     for c in range(block_rows):
         source = jnp.where(info[0] == 1, block_rows - 1 - c, c)
         half = half_a if c < 4 else half_b
-        half[c % 4 * TILE : (c % 4 + 1) * TILE, :] = start[
-            pl.ds(pl.multiple_of(source * TILE, TILE), TILE), :
-        ]
+        value = start[pl.ds(pl.multiple_of(source * TILE, TILE), TILE), :]
+        at = c % 4 * TILE
+        half[at : at + TILE, :] = value[:, :TILE]
+        half[HALF + at : HALF + at + TILE, :] = value[:, TILE:]
 
 def halve(info, start):
     vmem = pl.BlockSpec(memory_space=pltpu.VMEM)
-    half = jax.ShapeDtypeStruct((HALF, start.shape[1]), start.dtype)
+    half = jax.ShapeDtypeStruct((2 * HALF, TILE), start.dtype)
     return pl.pallas_call(
         halve_kernel,
         out_shape=(half, half),
@@ -139,12 +178,9 @@
         name="halve_start",
     )(info, start)
 
-def gather_kernel(info, *refs):
-    operators, (side_a, side_b, swapped) = refs[:-3], refs[-3:]
+def swap_kernel(info, *refs):
+    operators, swapped = refs[:-1], refs[-1]
     span = operators[0].shape[0]
-    rim = side_a.shape[0] // (len(operators) - 1)
-    tables = 8 * HB
-
     for n, (operator, following) in enumerate(zip(operators[:-1], operators[1:])):
         @pl.loop(0, span, step=160)
         def _(line):
@@ -152,34 +188,35 @@
             to = pl.ds(pl.multiple_of(n * span + line, 32), 160)
             swapped[to, :] = jnp.where(info[2] == 0, following[at, :], operator[at, :])
 
-        edge = rim - tables
-        body = span - span // (4 * TILE + 8) * 8
-
-        @pl.loop(0, edge, step=TILE)
-        def _(line):
-            at = pl.multiple_of(line, TILE)
-            to = pl.ds(pl.multiple_of(n * rim + line, 16), TILE)
-            side_a[to, :] = operator[pl.ds(at, TILE), :]
-            side_b[to, :] = operator[pl.ds(body - edge + at, TILE), :]
-
-        at = n * rim + edge
-        side_a[at : at + tables, :] = operator[body : body + tables, :]
-        side_b[at : at + tables, :] = operator[span - tables :, :]
-
-def gather_last(info, rim_rows, operators):
-    vmem = pl.BlockSpec(memory_space=pltpu.VMEM)
-    kind = operators[0].dtype
-    count = len(operators) - 1
-    side = jax.ShapeDtypeStruct((count * rim_rows, TILE), kind)
-    swapped = jax.ShapeDtypeStruct((count * operators[0].shape[0], TILE), kind)
-    return pl.pallas_call(
-        gather_kernel,
-        out_shape=(side, side, swapped),
+def gather_swap(info, operators):
+    vmem = pl.BlockSpec(memory_space=pltpu.VMEM)
+    lines = (len(operators) - 1) * operators[0].shape[0]
+    return pl.pallas_call(
+        swap_kernel,
+        out_shape=jax.ShapeDtypeStruct((lines, TILE), operators[0].dtype),
         in_specs=[pl.BlockSpec(memory_space=pltpu.SMEM)] + [vmem] * len(operators),
-        out_specs=(vmem, vmem, vmem),
+        out_specs=vmem,
         compiler_params=pltpu.CompilerParams(vmem_limit_bytes=24 * 1024 * 1024),
-        name="gather_last",
+        name="gather_swap",
     )(info, *operators)
+
+def rims_kernel(*refs):
+    operators, (side_a, side_b) = refs[:-2], refs[-2:]
+    for n, operator in enumerate(operators):
+        copy_rims(operator, side_a, side_b, n * HB * (4 * TILE + 8))
+
+def gather_rims(operators):
+    vmem = pl.BlockSpec(memory_space=pltpu.VMEM)
+    lines = len(operators) * HB * (4 * TILE + 8)
+    side = jax.ShapeDtypeStruct((lines, TILE), operators[0].dtype)
+    return pl.pallas_call(
+        rims_kernel,
+        out_shape=(side, side),
+        in_specs=[vmem] * len(operators),
+        out_specs=(vmem, vmem),
+        compiler_params=pltpu.CompilerParams(vmem_limit_bytes=24 * 1024 * 1024),
+        name="gather_rims",
+    )(*operators)
 
 
 NB = 16
@@ -274,7 +311,7 @@
 
 
 def body(start, blocks, cols, counts):
-    block_rows, slots, tile = blocks.shape[1:4]
+    block_rows, _, _ = blocks.shape[1:4]
     rows_here = start.shape[1]
     owners = lax.axis_size("rows")
     sections = lax.axis_size("phase")
@@ -287,16 +324,9 @@
     back = [(i, (i - 2) % sections) for i in range(sections)]
     ahead = [(i, (i + 2) % sections) for i in range(sections)]
     mates = [(i, i ^ 1) for i in range(sections)]
-    lines = block_rows * slots * tile
-    edge = HB * slots * tile
 
     def rims(a_side, b_side):
         return (lax.ppermute(a_side, "rows", to_a), lax.ppermute(b_side, "rows", to_b))
-
-    def rims_of(operator):
-        a_side = jnp.concatenate([operator[:edge], operator[lines : lines + 8 * HB]], axis=0)
-        b_side = jnp.concatenate([operator[lines - edge : lines], operator[-8 * HB :]], axis=0)
-        return a_side, b_side
 
     visits = sections // 2
     far = visits // 2
@@ -305,12 +335,15 @@
     held[1] = lax.ppermute(home, "phase", back)
     held[visits - 1] = lax.ppermute(home, "phase", ahead)
     halves = halve(info, start[0])
-    rim = rims(home_a, home_b)
+    first_rims = rims(home_a, home_b)
     span = home.shape[0]
     rim_span = home_a.shape[0]
+    batched = far + 2
     for turn in range(visits):
-        from_a = lax.ppermute(halves[0], "rows", to_a)
-        from_b = lax.ppermute(halves[1], "rows", to_b)
+        sides = (
+            lax.ppermute(halves[0], "rows", to_a), lax.ppermute(halves[1], "rows", to_b)
+        )
+        second_at = 0
         if turn <= far:
             here, later, halves = lax.optimization_barrier((held[turn], held[turn + 1], halves))
             if turn + 2 <= far:
@@ -320,19 +353,28 @@
                 nearer, halves = lax.optimization_barrier((held[end + 1], halves))
                 held[end] = lax.ppermute(nearer, "phase", ahead)
             picked = jnp.where(first_core, later, here)
-            other, other_at, rim_at = lax.ppermute(picked, "phase", mates), 0, 0
-        if turn < far:
-            next_rim = rims(*rims_of(later))
-        elif turn == far:
-            last = [later] + [held[n] for n in range(turn + 2, visits)] + [home]
-            side_a, side_b, swapped = gather_last(info, rim_span, last)
-            next_rim = rims(side_a, side_b)
-            others = lax.ppermute(swapped, "phase", mates)
+            other = lax.ppermute(picked, "phase", mates)
+        if turn == far - 1:
+            last, halves = lax.optimization_barrier(
+                ([held[n] for n in range(batched, visits)], halves)
+            )
+            last_rims = rims(*gather_rims(last))
+        if turn == far:
+            last = [later] + [held[n] for n in range(batched, visits)] + [home]
+            others = lax.ppermute(gather_swap(info, last), "phase", mates)
+        if turn > far:
+            other, second_at = others, (turn - far - 1) * span
+        if turn == 0:
+            rim, rim_at = first_rims, 0
+        elif turn < batched:
+            rim, rim_at = sides, rows_here
         else:
-            other, other_at, rim_at = others, (turn - far - 1) * span, (turn - far - 1) * rim_span
-        halves = visit(halves, from_a, from_b, *rim, held[turn], other, rim_at, other_at)
-        if turn <= far:
-            rim = next_rim
+            rim, rim_at = last_rims, (turn - batched) * rim_span
+        halves = visit(
+            halves, sides, rim, held[turn], other,
+            held[turn + 1] if turn + 1 < batched else None,
+            turn + 1 == visits, rim_at, second_at,
+        )
 
     arrived = jnp.concatenate(halves, axis=0)
     gram_term = lax.dot_general(

time: 319 us -> 298 us (0.934)
  the two profiles are of different devices: /device:TPU:64 before, /device:TPU:8 now
where the time goes in v6:
time: 298 us; the launch traced here: 297 us
  starting transfers between devices  119 us (40%)
  waiting for transfers between devices  107 us (36%)
  blocking collectives  36.6 us (12%)
  Pallas kernels  29.5 us (10%)
    ppermute x8, starting transfers between devices, body(): lax.ppermute(halves[1], 'rows', to_b)  40.4 us
    ppermute x8, waiting for transfers between devices, body(): lax.ppermute(halves[1], 'rows', to_b)  33.5 us
    ppermute x8, waiting for transfers between devices, body(): lax.ppermute(halves[0], 'rows', to_a)  24.1 us
    ppermute x1, waiting for transfers between devices, body(): held[1] = lax.ppermute(home, 'phase', back)  22.1 us
    all_to_all x1, blocking collectives, sum_over_rows(): pieces = lax.all_to_all(pieces, 'rows', 0, 0, tiled=True)  21.6 us
    ppermute x8, starting transfers between devices, body(): lax.ppermute(halves[0], 'rows', to_a)  16.9 us
    ppermute x3, starting transfers between devices, body(): held[turn + 2] = lax.ppermute(later, 'phase', back)  16.3 us
    all_to_all x1, blocking collectives, sum_over_rows(): return lax.all_to_all(copies, 'rows', 0, 0, tiled=True).reshape(size, size)  15 us
  transfers between devices with their start and end apart: 33, of which 21 were waited for; matrix products, arithmetic and copies ran while one was open for 0% of the time, Pallas kernels for 3%

profile of v6, /device:TPU:8, one launch (start us, length us, event | category | flops | bytes accessed | tf_op | source)
XLA Modules:
  0.0 297.2 jit_solution(8103474114377731048)
XLA Ops:
  4.1 10.9 %collective-permute-start = (bf16[4160,128]{1,0:T(8,128)(2,1)S(1)}, bf16[4160,128]{1,0:T(8,128)(2,1)S(1)}, u32[]{:S(2)}, u32[]{:S(2)}) collective-permute-start(bf16[4160,128]{1,0:T(8,128)(2,1)S(1)} %get-tuple-element.65.refs_6_.refs_3_), channel_id=1, source_target_pairs={{0,448},{32,480},{64,0},{96,32},{128,64},{160,96},{192,128},{224,1... | collective-permute-start | bytes 3194888 | tf_op jit(solution)/shard_map/ppermute | solution.py:335
  15.7 22.1 %collective-permute-done.refs_8_.refs_6_ = bf16[4160,128]{1,0:T(8,128)(2,1)S(1)} collective-permute-done((bf16[4160,128]{1,0:T(8,128)(2,1)S(1)}, bf16[4160,128]{1,0:T(8,128)(2,1)S(1)}, u32[]{:S(2)}, u32[]{:S(2)}) %collective-permute-start) | collective-permute-done | bytes 1064992 | tf_op jit(solution)/shard_map/ppermute | solution.py:335
  38.0 1.9 collective-permute-start.6
  39.9 5.6 %collective-permute-start.1 = (bf16[4160,128]{1,0:T(8,128)(2,1)S(1)}, bf16[4160,128]{1,0:T(8,128)(2,1)S(1)}, u32[]{:S(2)}, u32[]{:S(2)}) collective-permute-start(bf16[4160,128]{1,0:T(8,128)(2,1)S(1)} %collective-permute-done.refs_8_.refs_6_), channel_id=1, source_target_pairs={{0,448},{32,480},{64,0},{96,32},{128,64},{160,96},{192,128},{224,1... | collective-permute-start | bytes 3194888 | tf_op jit(solution)/shard_map/ppermute | solution.py:350
  45.5 3.4 %collective-permute-start.2 = (bf16[1024,128]{1,0:T(8,128)(2,1)S(1)}, bf16[1024,128]{1,0:T(8,128)(2,1)S(1)}, u32[]{:S(2)}, u32[]{:S(2)}) collective-permute-start(bf16[1024,128]{1,0:T(8,128)(2,1)S(1)} %get-tuple-element.61.refs_0_), channel_id=1, source_target_pairs={{0,1},{1,0},{2,3},{3,2},{4,5},{5,4},{6,7},{7,6},{8,9},{9,8},{10,11... | collective-permute-start | bytes 786440 | tf_op jit(solution)/shard_map/ppermute | solution.py:344
  48.9 2.4 collective-permute-start.4
  51.4 4.6 %collective-permute-start.5 = (bf16[1040,128]{1,0:T(8,128)(2,1)S(1)}, bf16[1040,128]{1,0:T(8,128)(2,1)S(1)}, u32[]{:S(2)}, u32[]{:S(2)}) collective-permute-start(bf16[1040,128]{1,0:T(8,128)(2,1)S(1)} %get-tuple-element.64), channel_id=1, source_target_pairs={{0,31},{1,2},{2,1},{3,4},{4,3},{5,6},{6,5},{7,8},{8,7},{9,10},{10,... | collective-permute-start | bytes 798728 | tf_op jit(solution)/shard_map/ppermute | solution.py:329
  56.6 4.5 %collective-permute-start.3 = (bf16[1024,128]{1,0:T(8,128)(2,1)S(1)}, bf16[1024,128]{1,0:T(8,128)(2,1)S(1)}, u32[]{:S(2)}, u32[]{:S(2)}) collective-permute-start(bf16[1024,128]{1,0:T(8,128)(2,1)S(1)} %get-tuple-element.62.refs_1_), channel_id=1, source_target_pairs={{0,31},{1,2},{2,1},{3,4},{4,3},{5,6},{6,5},{7,8},{8,7},{9,10},{10,... | collective-permute-start | bytes 786440 | tf_op jit(solution)/shard_map/ppermute | solution.py:344
  61.1 7.8 %collective-permute-done.3.refs_3_ = bf16[1024,128]{1,0:T(8,128)(2,1)S(1)} collective-permute-done((bf16[1024,128]{1,0:T(8,128)(2,1)S(1)}, bf16[1024,128]{1,0:T(8,128)(2,1)S(1)}, u32[]{:S(2)}, u32[]{:S(2)}) %collective-permute-start.3) | collective-permute-done | bytes 262176 | tf_op jit(solution)/shard_map/ppermute | solution.py:344
  72.5 1.9 collective-permute-start.11
  74.5 5.1 %collective-permute-start.7 = (bf16[4160,128]{1,0:T(8,128)(2,1)S(1)}, bf16[4160,128]{1,0:T(8,128)(2,1)S(1)}, u32[]{:S(2)}, u32[]{:S(2)}) collective-permute-start(bf16[4160,128]{1,0:T(8,128)(2,1)S(1)} %collective-permute-done.1.refs_8_.refs_6_), channel_id=1, source_target_pairs={{0,448},{32,480},{64,0},{96,32},{128,64},{160,96},{192,128},{224,1... | collective-permute-start | bytes 3194888 | tf_op jit(solution)/shard_map/ppermute | solution.py:350
  79.6 1.9 collective-permute-start.9
  81.5 4.6 %collective-permute-start.10 = (bf16[2064,128]{1,0:T(8,128)(2,1)S(1)}, bf16[2064,128]{1,0:T(8,128)(2,1)S(1)}, u32[]{:S(2)}, u32[]{:S(2)}) collective-permute-start(bf16[2064,128]{1,0:T(8,128)(2,1)S(1)} %get-tuple-element.72.refs_1_), channel_id=1, source_target_pairs={{0,31},{1,2},{2,1},{3,4},{4,3},{5,6},{6,5},{7,8},{8,7},{9,10},{10,... | collective-permute-start | bytes 1585160 | tf_op jit(solution)/shard_map/ppermute | solution.py:344
  86.1 10.2 %collective-permute-done.8.refs_2_.refs_1_.refs_6_ = bf16[4160,128]{1,0:T(8,128)(2,1)S(1)} collective-permute-done((bf16[4160,128]{1,0:T(8,128)(2,1)S(1)}, bf16[4160,128]{1,0:T(8,128)(2,1)S(1)}, u32[]{:S(2)}, u32[]{:S(2)}) %collective-permute-start.8) | collective-permute-done | bytes 1064992 | tf_op jit(solution)/shard_map/ppermute | solution.py:336
  103.1 1.9 collective-permute-start.17
  105.0 5.6 %collective-permute-start.12 = (bf16[4160,128]{1,0:T(8,128)(2,1)S(1)}, bf16[4160,128]{1,0:T(8,128)(2,1)S(1)}, u32[]{:S(2)}, u32[]{:S(2)}) collective-permute-start(bf16[4160,128]{1,0:T(8,128)(2,1)S(1)} %collective-permute-done.7.refs_8_.refs_6_), channel_id=1, source_target_pairs={{0,448},{32,480},{64,0},{96,32},{128,64},{160,96},{192,128},{224,1... | collective-permute-start | bytes 3194888 | tf_op jit(solution)/shard_map/ppermute | solution.py:350
  110.7 1.9 collective-permute-start.15
  112.6 4.6 %collective-permute-start.16 = (bf16[2064,128]{1,0:T(8,128)(2,1)S(1)}, bf16[2064,128]{1,0:T(8,128)(2,1)S(1)}, u32[]{:S(2)}, u32[]{:S(2)}) collective-permute-start(bf16[2064,128]{1,0:T(8,128)(2,1)S(1)} %get-tuple-element.82.refs_1_), channel_id=1, source_target_pairs={{0,31},{1,2},{2,1},{3,4},{4,3},{5,6},{6,5},{7,8},{8,7},{9,10},{10,... | collective-permute-start | bytes 1585160 | tf_op jit(solution)/shard_map/ppermute | solution.py:344
  117.1 5.5 %collective-permute-done.13.refs_1_.refs_0_.refs_6_ = bf16[4160,128]{1,0:T(8,128)(2,1)S(1)} collective-permute-done((bf16[4160,128]{1,0:T(8,128)(2,1)S(1)}, bf16[4160,128]{1,0:T(8,128)(2,1)S(1)}, u32[]{:S(2)}, u32[]{:S(2)}) %collective-permute-start.13) | collective-permute-done | bytes 1064992 | tf_op jit(solution)/shard_map/ppermute | solution.py:354
  122.7 4.0 %collective-permute-done.15.refs_2_.refs_4_ = bf16[2064,128]{1,0:T(8,128)(2,1)S(1)} collective-permute-done((bf16[2064,128]{1,0:T(8,128)(2,1)S(1)}, bf16[2064,128]{1,0:T(8,128)(2,1)S(1)}, u32[]{:S(2)}, u32[]{:S(2)}) %collective-permute-start.15) | collective-permute-done | bytes 528416 | tf_op jit(solution)/shard_map/ppermute | solution.py:344
  126.7 4.0 %collective-permute-done.16.refs_3_.refs_5_ = bf16[2064,128]{1,0:T(8,128)(2,1)S(1)} collective-permute-done((bf16[2064,128]{1,0:T(8,128)(2,1)S(1)}, bf16[2064,128]{1,0:T(8,128)(2,1)S(1)}, u32[]{:S(2)}, u32[]{:S(2)}) %collective-permute-start.16) | collective-permute-done | bytes 528416 | tf_op jit(solution)/shard_map/ppermute | solution.py:344
  134.2 1.9 collective-permute-start.20
  136.1 1.9 collective-permute-start.14
  138.1 1.9 collective-permute-start.18
  140.0 4.6 %collective-permute-start.19 = (bf16[2064,128]{1,0:T(8,128)(2,1)S(1)}, bf16[2064,128]{1,0:T(8,128)(2,1)S(1)}, u32[]{:S(2)}, u32[]{:S(2)}) collective-permute-start(bf16[2064,128]{1,0:T(8,128)(2,1)S(1)} %get-tuple-element.89.refs_1_), channel_id=1, source_target_pairs={{0,31},{1,2},{2,1},{3,4},{4,3},{5,6},{6,5},{7,8},{8,7},{9,10},{10,... | collective-permute-start | bytes 1585160 | tf_op jit(solution)/shard_map/ppermute | solution.py:344
  144.6 9.8 %collective-permute-done.18.refs_2_.refs_4_ = bf16[2064,128]{1,0:T(8,128)(2,1)S(1)} collective-permute-done((bf16[2064,128]{1,0:T(8,128)(2,1)S(1)}, bf16[2064,128]{1,0:T(8,128)(2,1)S(1)}, u32[]{:S(2)}, u32[]{:S(2)}) %collective-permute-start.18) | collective-permute-done | bytes 528416 | tf_op jit(solution)/shard_map/ppermute | solution.py:344
  154.4 4.0 %collective-permute-done.19.refs_3_.refs_5_ = bf16[2064,128]{1,0:T(8,128)(2,1)S(1)} collective-permute-done((bf16[2064,128]{1,0:T(8,128)(2,1)S(1)}, bf16[2064,128]{1,0:T(8,128)(2,1)S(1)}, u32[]{:S(2)}, u32[]{:S(2)}) %collective-permute-start.19) | collective-permute-done | bytes 528416 | tf_op jit(solution)/shard_map/ppermute | solution.py:344
  159.9 6.0 %collective-permute-done.14.refs_8_.refs_0_.refs_6_ = bf16[4160,128]{1,0:T(8,128)(2,1)S(1)} collective-permute-done((bf16[4160,128]{1,0:T(8,128)(2,1)S(1)}, bf16[4160,128]{1,0:T(8,128)(2,1)S(1)}, u32[]{:S(2)}, u32[]{:S(2)}) %collective-permute-start.14) | collective-permute-done | bytes 1064992 | tf_op jit(solution)/shard_map/ppermute | solution.py:354
  167.8 1.9 collective-permute-start.26
  169.8 2.4 collective-permute-start.23
  172.2 1.9 collective-permute-start.21
  174.2 4.6 %collective-permute-start.22 = (bf16[2064,128]{1,0:T(8,128)(2,1)S(1)}, bf16[2064,128]{1,0:T(8,128)(2,1)S(1)}, u32[]{:S(2)}, u32[]{:S(2)}) collective-permute-start(bf16[2064,128]{1,0:T(8,128)(2,1)S(1)} %get-tuple-element.95.refs_1_), channel_id=1, source_target_pairs={{0,31},{1,2},{2,1},{3,4},{4,3},{5,6},{6,5},{7,8},{8,7},{9,10},{10,... | collective-permute-start | bytes 1585160 | tf_op jit(solution)/shard_map/ppermute | solution.py:344
  178.7 9.3 %collective-permute-done.21.refs_2_.refs_4_ = bf16[2064,128]{1,0:T(8,128)(2,1)S(1)} collective-permute-done((bf16[2064,128]{1,0:T(8,128)(2,1)S(1)}, bf16[2064,128]{1,0:T(8,128)(2,1)S(1)}, u32[]{:S(2)}, u32[]{:S(2)}) %collective-permute-start.21) | collective-permute-done | bytes 528416 | tf_op jit(solution)/shard_map/ppermute | solution.py:344
  188.1 4.0 %collective-permute-done.22.refs_3_.refs_5_ = bf16[2064,128]{1,0:T(8,128)(2,1)S(1)} collective-permute-done((bf16[2064,128]{1,0:T(8,128)(2,1)S(1)}, bf16[2064,128]{1,0:T(8,128)(2,1)S(1)}, u32[]{:S(2)}, u32[]{:S(2)}) %collective-permute-start.22) | collective-permute-done | bytes 528416 | tf_op jit(solution)/shard_map/ppermute | solution.py:344
  193.6 2.0 collective-permute-start.24
  195.6 5.1 %collective-permute-start.25 = (bf16[2064,128]{1,0:T(8,128)(2,1)S(1)}, bf16[2064,128]{1,0:T(8,128)(2,1)S(1)}, u32[]{:S(2)}, u32[]{:S(2)}) collective-permute-start(bf16[2064,128]{1,0:T(8,128)(2,1)S(1)} %get-tuple-element.99.refs_1_), channel_id=1, source_target_pairs={{0,31},{1,2},{2,1},{3,4},{4,3},{5,6},{6,5},{7,8},{8,7},{9,10},{10,... | collective-permute-start | bytes 1585160 | tf_op jit(solution)/shard_map/ppermute | solution.py:344
  200.8 2.9 collective-permute-start.29
  203.7 6.5 %collective-permute-start.30 = (bf16[2080,128]{1,0:T(8,128)(2,1)S(1)}, bf16[2080,128]{1,0:T(8,128)(2,1)S(1)}, u32[]{:S(2)}, u32[]{:S(2)}) collective-permute-start(bf16[2080,128]{1,0:T(8,128)(2,1)S(1)} %get-tuple-element.105), channel_id=1, source_target_pairs={{0,31},{1,2},{2,1},{3,4},{4,3},{5,6},{6,5},{7,8},{8,7},{9,10},{10,... | collective-permute-start | bytes 1597448 | tf_op jit(solution)/shard_map/ppermute | solution.py:329
  210.4 4.1 %collective-permute-done.25.refs_3_.refs_5_ = bf16[2064,128]{1,0:T(8,128)(2,1)S(1)} collective-permute-done((bf16[2064,128]{1,0:T(8,128)(2,1)S(1)}, bf16[2064,128]{1,0:T(8,128)(2,1)S(1)}, u32[]{:S(2)}, u32[]{:S(2)}) %collective-permute-start.25) | collective-permute-done | bytes 528416 | tf_op jit(solution)/shard_map/ppermute | solution.py:344
  215.9 1.9 collective-permute-start.27
  217.8 6.3 %collective-permute-start.28 = (bf16[1024,128]{1,0:T(8,128)(2,1)S(1)}, bf16[1024,128]{1,0:T(8,128)(2,1)S(1)}, u32[]{:S(2)}, u32[]{:S(2)}) collective-permute-start(bf16[1024,128]{1,0:T(8,128)(2,1)S(1)} %get-tuple-element.101.refs_1_), channel_id=1, source_target_pairs={{0,31},{1,2},{2,1},{3,4},{4,3},{5,6},{6,5},{7,8},{8,7},{9,10},{10,... | collective-permute-start | bytes 786440 | tf_op jit(solution)/shard_map/ppermute | solution.py:344
  225.9 3.8 %collective-permute-done.28.refs_3_ = bf16[1024,128]{1,0:T(8,128)(2,1)S(1)} collective-permute-done((bf16[1024,128]{1,0:T(8,128)(2,1)S(1)}, bf16[1024,128]{1,0:T(8,128)(2,1)S(1)}, u32[]{:S(2)}, u32[]{:S(2)}) %collective-permute-start.28) | collective-permute-done | bytes 262176 | tf_op jit(solution)/shard_map/ppermute | solution.py:344
  231.1 2.0 collective-permute-start.31
  233.1 6.3 %collective-permute-start.32 = (bf16[1024,128]{1,0:T(8,128)(2,1)S(1)}, bf16[1024,128]{1,0:T(8,128)(2,1)S(1)}, u32[]{:S(2)}, u32[]{:S(2)}) collective-permute-start(bf16[1024,128]{1,0:T(8,128)(2,1)S(1)} %get-tuple-element.107.refs_1_), channel_id=1, source_target_pairs={{0,31},{1,2},{2,1},{3,4},{4,3},{5,6},{6,5},{7,8},{8,7},{9,10},{10,... | collective-permute-start | bytes 786440 | tf_op jit(solution)/shard_map/ppermute | solution.py:344
  239.5 4.2 %collective-permute-done.32.refs_3_ = bf16[1024,128]{1,0:T(8,128)(2,1)S(1)} collective-permute-done((bf16[1024,128]{1,0:T(8,128)(2,1)S(1)}, bf16[1024,128]{1,0:T(8,128)(2,1)S(1)}, u32[]{:S(2)}, u32[]{:S(2)}) %collective-permute-start.32) | collective-permute-done | bytes 262176 | tf_op jit(solution)/shard_map/ppermute | solution.py:344
  245.5 21.6 %all_to_all.10 = bf16[32,8,256]{2,1,0:T(8,128)(2,1)S(1)} all-to-all(bf16[32,8,256]{2,1,0:T(8,128)(2,1)S(1)} %fusion), channel_id=1, replica_groups=mesh['phase'=16,'rows'=32] {'rows'}, dimensions={0} | all-to-all | bytes 262144 | tf_op jit(solution)/shard_map/all_to_all | solution.py:307
  267.2 15.0 %all_to_all.11 = f32[32,8,256]{2,1,0:T(8,128)S(1)} all-to-all(f32[32,8,256]{2,1,0:T(8,128)S(1)} %broadcast_in_dim.12), channel_id=1, replica_groups=mesh['phase'=16,'rows'=32] {'rows'}, dimensions={0} | all-to-all | bytes 524288 | tf_op jit(solution)/shard_map/all_to_all | solution.py:310
  282.9 14.2 %factor_solve.1 = (f32[1024,256]{1,0:T(8,128)}, f32[256,256]{1,0:T(8,128)}) custom-call(s32[3]{0:T(128)} %copy-done.4, f32[256,256]{1,0:T(8,128)} %multiply_bitcast_fusion.gram_ref, bf16[512,256]{1,0:T(8,128)(2,1)} %copy-done.2, bf16[512,256]{1,0:T(8,128)(2,1)} %copy-done.3), custom_call_target="tpu_custom_call" | custom-call | tf_op jit(solution)/shard_map/factor_solve/pallas_call | solution.py:290
  (56 shorter events, 31.4 us)
Async XLA Ops:
  1.5 164.4 %copy-start.4 = (s32[3]{0:T(128)}, s32[3]{0:T(128)S(1)}, u32[]{:S(2)}) copy-start(s32[3]{0:T(128)S(1)} %pad_add_fusion.info) | copy-start | bytes 40
  1.5 1.2 copy-start
  2.7 0.7 copy-start.5
  3.4 11.7 %copy-start.1 = (bf16[1,1024,256]{2,1,0:T(8,128)(2,1)S(1)}, bf16[1,1024,256]{2,1,0:T(8,128)(2,1)}, u32[]{:S(2)}) copy-start(bf16[1,1024,256]{2,1,0:T(8,128)(2,1)} %param.4) | copy-start | bytes 1572868
  4.1 33.7 %collective-permute-start = (bf16[4160,128]{1,0:T(8,128)(2,1)S(1)}, bf16[4160,128]{1,0:T(8,128)(2,1)S(1)}, u32[]{:S(2)}, u32[]{:S(2)}) collective-permute-start(bf16[4160,128]{1,0:T(8,128)(2,1)S(1)} %get-tuple-element.65.refs_6_.refs_3_), channel_id=1, source_target_pairs={{0,448},{32,480},{64,0},{96,32},{128,64},{160,96},{192,128},{224,1... | collective-permute-start | bytes 3194888 | tf_op jit(solution)/shard_map/ppermute | solution.py:335
  38.0 32.9 %collective-permute-start.6 = (bf16[4160,128]{1,0:T(8,128)(2,1)S(1)}, bf16[4160,128]{1,0:T(8,128)(2,1)S(1)}, u32[]{:S(2)}, u32[]{:S(2)}) collective-permute-start(bf16[4160,128]{1,0:T(8,128)(2,1)S(1)} %broadcast_select_fusion.4), channel_id=1, source_target_pairs={{0,32},{32,0},{64,96},{96,64},{128,160},{160,128},{192,224},{224,1... | collective-permute-start | bytes 3194888 | tf_op jit(solution)/shard_map/ppermute | solution.py:356
  39.9 32.5 %collective-permute-start.1 = (bf16[4160,128]{1,0:T(8,128)(2,1)S(1)}, bf16[4160,128]{1,0:T(8,128)(2,1)S(1)}, u32[]{:S(2)}, u32[]{:S(2)}) collective-permute-start(bf16[4160,128]{1,0:T(8,128)(2,1)S(1)} %collective-permute-done.refs_8_.refs_6_), channel_id=1, source_target_pairs={{0,448},{32,480},{64,0},{96,32},{128,64},{160,96},{192,128},{224,1... | collective-permute-start | bytes 3194888 | tf_op jit(solution)/shard_map/ppermute | solution.py:350
  45.5 11.1 %collective-permute-start.2 = (bf16[1024,128]{1,0:T(8,128)(2,1)S(1)}, bf16[1024,128]{1,0:T(8,128)(2,1)S(1)}, u32[]{:S(2)}, u32[]{:S(2)}) collective-permute-start(bf16[1024,128]{1,0:T(8,128)(2,1)S(1)} %get-tuple-element.61.refs_0_), channel_id=1, source_target_pairs={{0,1},{1,0},{2,3},{3,2},{4,5},{5,4},{6,7},{7,6},{8,9},{9,8},{10,11... | collective-permute-start | bytes 786440 | tf_op jit(solution)/shard_map/ppermute | solution.py:344
  48.9 21.9 %collective-permute-start.4 = (bf16[1040,128]{1,0:T(8,128)(2,1)S(1)}, bf16[1040,128]{1,0:T(8,128)(2,1)S(1)}, u32[]{:S(2)}, u32[]{:S(2)}) collective-permute-start(bf16[1040,128]{1,0:T(8,128)(2,1)S(1)} %get-tuple-element.63), channel_id=1, source_target_pairs={{0,1},{1,0},{2,3},{3,2},{4,5},{5,4},{6,7},{7,6},{8,9},{9,8},{10,11... | collective-permute-start | bytes 798728 | tf_op jit(solution)/shard_map/ppermute | solution.py:329
  51.4 19.5 %collective-permute-start.5 = (bf16[1040,128]{1,0:T(8,128)(2,1)S(1)}, bf16[1040,128]{1,0:T(8,128)(2,1)S(1)}, u32[]{:S(2)}, u32[]{:S(2)}) collective-permute-start(bf16[1040,128]{1,0:T(8,128)(2,1)S(1)} %get-tuple-element.64), channel_id=1, source_target_pairs={{0,31},{1,2},{2,1},{3,4},{4,3},{5,6},{6,5},{7,8},{8,7},{9,10},{10,... | collective-permute-start | bytes 798728 | tf_op jit(solution)/shard_map/ppermute | solution.py:329
  56.6 12.4 %collective-permute-start.3 = (bf16[1024,128]{1,0:T(8,128)(2,1)S(1)}, bf16[1024,128]{1,0:T(8,128)(2,1)S(1)}, u32[]{:S(2)}, u32[]{:S(2)}) collective-permute-start(bf16[1024,128]{1,0:T(8,128)(2,1)S(1)} %get-tuple-element.62.refs_1_), channel_id=1, source_target_pairs={{0,31},{1,2},{2,1},{3,4},{4,3},{5,6},{6,5},{7,8},{8,7},{9,10},{10,... | collective-permute-start | bytes 786440 | tf_op jit(solution)/shard_map/ppermute | solution.py:344
  68.9 27.3 %collective-permute-start.8 = (bf16[4160,128]{1,0:T(8,128)(2,1)S(1)}, bf16[4160,128]{1,0:T(8,128)(2,1)S(1)}, u32[]{:S(2)}, u32[]{:S(2)}) collective-permute-start(bf16[4160,128]{1,0:T(8,128)(2,1)S(1)} %get-tuple-element.65.refs_6_.refs_3_), channel_id=1, source_target_pairs={{0,64},{32,96},{64,128},{96,160},{128,192},{160,224},{192,256},{22... | collective-permute-start | bytes 3194888 | tf_op jit(solution)/shard_map/ppermute | solution.py:336
  72.5 27.1 %collective-permute-start.11 = (bf16[4160,128]{1,0:T(8,128)(2,1)S(1)}, bf16[4160,128]{1,0:T(8,128)(2,1)S(1)}, u32[]{:S(2)}, u32[]{:S(2)}) collective-permute-start(bf16[4160,128]{1,0:T(8,128)(2,1)S(1)} %broadcast_select_fusion.3), channel_id=1, source_target_pairs={{0,32},{32,0},{64,96},{96,64},{128,160},{160,128},{192,224},{224,1... | collective-permute-start | bytes 3194888 | tf_op jit(solution)/shard_map/ppermute | solution.py:356
  74.5 28.5 %collective-permute-start.7 = (bf16[4160,128]{1,0:T(8,128)(2,1)S(1)}, bf16[4160,128]{1,0:T(8,128)(2,1)S(1)}, u32[]{:S(2)}, u32[]{:S(2)}) collective-permute-start(bf16[4160,128]{1,0:T(8,128)(2,1)S(1)} %collective-permute-done.1.refs_8_.refs_6_), channel_id=1, source_target_pairs={{0,448},{32,480},{64,0},{96,32},{128,64},{160,96},{192,128},{224,1... | collective-permute-start | bytes 3194888 | tf_op jit(solution)/shard_map/ppermute | solution.py:350
  79.6 18.6 %collective-permute-start.9 = (bf16[2064,128]{1,0:T(8,128)(2,1)S(1)}, bf16[2064,128]{1,0:T(8,128)(2,1)S(1)}, u32[]{:S(2)}, u32[]{:S(2)}) collective-permute-start(bf16[2064,128]{1,0:T(8,128)(2,1)S(1)} %get-tuple-element.71.refs_0_), channel_id=1, source_target_pairs={{0,1},{1,0},{2,3},{3,2},{4,5},{5,4},{6,7},{7,6},{8,9},{9,8},{10,11... | collective-permute-start | bytes 1585160 | tf_op jit(solution)/shard_map/ppermute | solution.py:344
  81.5 18.1 %collective-permute-start.10 = (bf16[2064,128]{1,0:T(8,128)(2,1)S(1)}, bf16[2064,128]{1,0:T(8,128)(2,1)S(1)}, u32[]{:S(2)}, u32[]{:S(2)}) collective-permute-start(bf16[2064,128]{1,0:T(8,128)(2,1)S(1)} %get-tuple-element.72.refs_1_), channel_id=1, source_target_pairs={{0,31},{1,2},{2,1},{3,4},{4,3},{5,6},{6,5},{7,8},{8,7},{9,10},{10,... | collective-permute-start | bytes 1585160 | tf_op jit(solution)/shard_map/ppermute | solution.py:344
  96.2 26.5 %collective-permute-start.13 = (bf16[4160,128]{1,0:T(8,128)(2,1)S(1)}, bf16[4160,128]{1,0:T(8,128)(2,1)S(1)}, u32[]{:S(2)}, u32[]{:S(2)}) collective-permute-start(bf16[4160,128]{1,0:T(8,128)(2,1)S(1)} %collective-permute-done.8.refs_2_.refs_1_.refs_6_), channel_id=1, source_target_pairs={{0,64},{32,96},{64,128},{96,160},{128,192},{160,224},{192,256},{22... | collective-permute-start | bytes 3194888 | tf_op jit(solution)/shard_map/ppermute | solution.py:354
  103.1 27.6 %collective-permute-start.17 = (bf16[4160,128]{1,0:T(8,128)(2,1)S(1)}, bf16[4160,128]{1,0:T(8,128)(2,1)S(1)}, u32[]{:S(2)}, u32[]{:S(2)}) collective-permute-start(bf16[4160,128]{1,0:T(8,128)(2,1)S(1)} %broadcast_select_fusion.2), channel_id=1, source_target_pairs={{0,32},{32,0},{64,96},{96,64},{128,160},{160,128},{192,224},{224,1... | collective-permute-start | bytes 3194888 | tf_op jit(solution)/shard_map/ppermute | solution.py:356
  105.0 29.0 %collective-permute-start.12 = (bf16[4160,128]{1,0:T(8,128)(2,1)S(1)}, bf16[4160,128]{1,0:T(8,128)(2,1)S(1)}, u32[]{:S(2)}, u32[]{:S(2)}) collective-permute-start(bf16[4160,128]{1,0:T(8,128)(2,1)S(1)} %collective-permute-done.7.refs_8_.refs_6_), channel_id=1, source_target_pairs={{0,448},{32,480},{64,0},{96,32},{128,64},{160,96},{192,128},{224,1... | collective-permute-start | bytes 3194888 | tf_op jit(solution)/shard_map/ppermute | solution.py:350
  110.7 16.0 %collective-permute-start.15 = (bf16[2064,128]{1,0:T(8,128)(2,1)S(1)}, bf16[2064,128]{1,0:T(8,128)(2,1)S(1)}, u32[]{:S(2)}, u32[]{:S(2)}) collective-permute-start(bf16[2064,128]{1,0:T(8,128)(2,1)S(1)} %get-tuple-element.81.refs_0_), channel_id=1, source_target_pairs={{0,1},{1,0},{2,3},{3,2},{4,5},{5,4},{6,7},{7,6},{8,9},{9,8},{10,11... | collective-permute-start | bytes 1585160 | tf_op jit(solution)/shard_map/ppermute | solution.py:344
  112.6 18.1 %collective-permute-start.16 = (bf16[2064,128]{1,0:T(8,128)(2,1)S(1)}, bf16[2064,128]{1,0:T(8,128)(2,1)S(1)}, u32[]{:S(2)}, u32[]{:S(2)}) collective-permute-start(bf16[2064,128]{1,0:T(8,128)(2,1)S(1)} %get-tuple-element.82.refs_1_), channel_id=1, source_target_pairs={{0,31},{1,2},{2,1},{3,4},{4,3},{5,6},{6,5},{7,8},{8,7},{9,10},{10,... | collective-permute-start | bytes 1585160 | tf_op jit(solution)/shard_map/ppermute | solution.py:344
  134.2 24.2 %collective-permute-start.20 = (bf16[4160,128]{1,0:T(8,128)(2,1)S(1)}, bf16[4160,128]{1,0:T(8,128)(2,1)S(1)}, u32[]{:S(2)}, u32[]{:S(2)}) collective-permute-start(bf16[4160,128]{1,0:T(8,128)(2,1)S(1)} %broadcast_select_fusion.1), channel_id=1, source_target_pairs={{0,32},{32,0},{64,96},{96,64},{128,160},{160,128},{192,224},{224,1... | collective-permute-start | bytes 3194888 | tf_op jit(solution)/shard_map/ppermute | solution.py:356
  136.1 29.8 %collective-permute-start.14 = (bf16[4160,128]{1,0:T(8,128)(2,1)S(1)}, bf16[4160,128]{1,0:T(8,128)(2,1)S(1)}, u32[]{:S(2)}, u32[]{:S(2)}) collective-permute-start(bf16[4160,128]{1,0:T(8,128)(2,1)S(1)} %collective-permute-done.13.refs_1_.refs_0_.refs_6_), channel_id=1, source_target_pairs={{0,64},{32,96},{64,128},{96,160},{128,192},{160,224},{192,256},{22... | collective-permute-start | bytes 3194888 | tf_op jit(solution)/shard_map/ppermute | solution.py:354
  138.1 16.3 %collective-permute-start.18 = (bf16[2064,128]{1,0:T(8,128)(2,1)S(1)}, bf16[2064,128]{1,0:T(8,128)(2,1)S(1)}, u32[]{:S(2)}, u32[]{:S(2)}) collective-permute-start(bf16[2064,128]{1,0:T(8,128)(2,1)S(1)} %get-tuple-element.88.refs_0_), channel_id=1, source_target_pairs={{0,1},{1,0},{2,3},{3,2},{4,5},{5,4},{6,7},{7,6},{8,9},{9,8},{10,11... | collective-permute-start | bytes 1585160 | tf_op jit(solution)/shard_map/ppermute | solution.py:344
  140.0 18.4 %collective-permute-start.19 = (bf16[2064,128]{1,0:T(8,128)(2,1)S(1)}, bf16[2064,128]{1,0:T(8,128)(2,1)S(1)}, u32[]{:S(2)}, u32[]{:S(2)}) collective-permute-start(bf16[2064,128]{1,0:T(8,128)(2,1)S(1)} %get-tuple-element.89.refs_1_), channel_id=1, source_target_pairs={{0,31},{1,2},{2,1},{3,4},{4,3},{5,6},{6,5},{7,8},{8,7},{9,10},{10,... | collective-permute-start | bytes 1585160 | tf_op jit(solution)/shard_map/ppermute | solution.py:344
  167.8 46.7 %collective-permute-start.26 = (bf16[12480,128]{1,0:T(8,128)(2,1)S(1)}, bf16[12480,128]{1,0:T(8,128)(2,1)S(1)}, u32[]{:S(2)}, u32[]{:S(2)}) collective-permute-start(bf16[12480,128]{1,0:T(8,128)(2,1)S(1)} %gather_swap.1), channel_id=1, source_target_pairs={{0,32},{32,0},{64,96},{96,64},{128,160},{160,128},{192,224},{224,1... | collective-permute-start | bytes 9584648 | tf_op jit(solution)/shard_map/ppermute | solution.py:364
  169.8 22.3 %collective-permute-start.23 = (bf16[4160,128]{1,0:T(8,128)(2,1)S(1)}, bf16[4160,128]{1,0:T(8,128)(2,1)S(1)}, u32[]{:S(2)}, u32[]{:S(2)}) collective-permute-start(bf16[4160,128]{1,0:T(8,128)(2,1)S(1)} %broadcast_select_fusion), channel_id=1, source_target_pairs={{0,32},{32,0},{64,96},{96,64},{128,160},{160,128},{192,224},{224,1... | collective-permute-start | bytes 3194888 | tf_op jit(solution)/shard_map/ppermute | solution.py:356
  172.2 15.8 %collective-permute-start.21 = (bf16[2064,128]{1,0:T(8,128)(2,1)S(1)}, bf16[2064,128]{1,0:T(8,128)(2,1)S(1)}, u32[]{:S(2)}, u32[]{:S(2)}) collective-permute-start(bf16[2064,128]{1,0:T(8,128)(2,1)S(1)} %get-tuple-element.94.refs_0_), channel_id=1, source_target_pairs={{0,1},{1,0},{2,3},{3,2},{4,5},{5,4},{6,7},{7,6},{8,9},{9,8},{10,11... | collective-permute-start | bytes 1585160 | tf_op jit(solution)/shard_map/ppermute | solution.py:344
  174.2 17.9 %collective-permute-start.22 = (bf16[2064,128]{1,0:T(8,128)(2,1)S(1)}, bf16[2064,128]{1,0:T(8,128)(2,1)S(1)}, u32[]{:S(2)}, u32[]{:S(2)}) collective-permute-start(bf16[2064,128]{1,0:T(8,128)(2,1)S(1)} %get-tuple-element.95.refs_1_), channel_id=1, source_target_pairs={{0,31},{1,2},{2,1},{3,4},{4,3},{5,6},{6,5},{7,8},{8,7},{9,10},{10,... | collective-permute-start | bytes 1585160 | tf_op jit(solution)/shard_map/ppermute | solution.py:344
  193.6 16.8 %collective-permute-start.24 = (bf16[2064,128]{1,0:T(8,128)(2,1)S(1)}, bf16[2064,128]{1,0:T(8,128)(2,1)S(1)}, u32[]{:S(2)}, u32[]{:S(2)}) collective-permute-start(bf16[2064,128]{1,0:T(8,128)(2,1)S(1)} %get-tuple-element.98.refs_0_), channel_id=1, source_target_pairs={{0,1},{1,0},{2,3},{3,2},{4,5},{5,4},{6,7},{7,6},{8,9},{9,8},{10,11... | collective-permute-start | bytes 1585160 | tf_op jit(solution)/shard_map/ppermute | solution.py:344
  195.6 18.9 %collective-permute-start.25 = (bf16[2064,128]{1,0:T(8,128)(2,1)S(1)}, bf16[2064,128]{1,0:T(8,128)(2,1)S(1)}, u32[]{:S(2)}, u32[]{:S(2)}) collective-permute-start(bf16[2064,128]{1,0:T(8,128)(2,1)S(1)} %get-tuple-element.99.refs_1_), channel_id=1, source_target_pairs={{0,31},{1,2},{2,1},{3,4},{4,3},{5,6},{6,5},{7,8},{8,7},{9,10},{10,... | collective-permute-start | bytes 1585160 | tf_op jit(solution)/shard_map/ppermute | solution.py:344
  200.8 23.3 %collective-permute-start.29 = (bf16[2080,128]{1,0:T(8,128)(2,1)S(1)}, bf16[2080,128]{1,0:T(8,128)(2,1)S(1)}, u32[]{:S(2)}, u32[]{:S(2)}) collective-permute-start(bf16[2080,128]{1,0:T(8,128)(2,1)S(1)} %get-tuple-element.104), channel_id=1, source_target_pairs={{0,1},{1,0},{2,3},{3,2},{4,5},{5,4},{6,7},{7,6},{8,9},{9,8},{10,11... | collective-permute-start | bytes 1597448 | tf_op jit(solution)/shard_map/ppermute | solution.py:329
  203.7 22.2 %collective-permute-start.30 = (bf16[2080,128]{1,0:T(8,128)(2,1)S(1)}, bf16[2080,128]{1,0:T(8,128)(2,1)S(1)}, u32[]{:S(2)}, u32[]{:S(2)}) collective-permute-start(bf16[2080,128]{1,0:T(8,128)(2,1)S(1)} %get-tuple-element.105), channel_id=1, source_target_pairs={{0,31},{1,2},{2,1},{3,4},{4,3},{5,6},{6,5},{7,8},{8,7},{9,10},{10,... | collective-permute-start | bytes 1597448 | tf_op jit(solution)/shard_map/ppermute | solution.py:329
  215.9 10.0 %collective-permute-start.27 = (bf16[1024,128]{1,0:T(8,128)(2,1)S(1)}, bf16[1024,128]{1,0:T(8,128)(2,1)S(1)}, u32[]{:S(2)}, u32[]{:S(2)}) collective-permute-start(bf16[1024,128]{1,0:T(8,128)(2,1)S(1)} %get-tuple-element.100.refs_0_), channel_id=1, source_target_pairs={{0,1},{1,0},{2,3},{3,2},{4,5},{5,4},{6,7},{7,6},{8,9},{9,8},{10,11... | collective-permute-start | bytes 786440 | tf_op jit(solution)/shard_map/ppermute | solution.py:344
  217.8 11.8 %collective-permute-start.28 = (bf16[1024,128]{1,0:T(8,128)(2,1)S(1)}, bf16[1024,128]{1,0:T(8,128)(2,1)S(1)}, u32[]{:S(2)}, u32[]{:S(2)}) collective-permute-start(bf16[1024,128]{1,0:T(8,128)(2,1)S(1)} %get-tuple-element.101.refs_1_), channel_id=1, source_target_pairs={{0,31},{1,2},{2,1},{3,4},{4,3},{5,6},{6,5},{7,8},{8,7},{9,10},{10,... | collective-permute-start | bytes 786440 | tf_op jit(solution)/shard_map/ppermute | solution.py:344
  231.1 8.4 %collective-permute-start.31 = (bf16[1024,128]{1,0:T(8,128)(2,1)S(1)}, bf16[1024,128]{1,0:T(8,128)(2,1)S(1)}, u32[]{:S(2)}, u32[]{:S(2)}) collective-permute-start(bf16[1024,128]{1,0:T(8,128)(2,1)S(1)} %get-tuple-element.106.refs_0_), channel_id=1, source_target_pairs={{0,1},{1,0},{2,3},{3,2},{4,5},{5,4},{6,7},{7,6},{8,9},{9,8},{10,11... | collective-permute-start | bytes 786440 | tf_op jit(solution)/shard_map/ppermute | solution.py:344
  233.1 10.6 %collective-permute-start.32 = (bf16[1024,128]{1,0:T(8,128)(2,1)S(1)}, bf16[1024,128]{1,0:T(8,128)(2,1)S(1)}, u32[]{:S(2)}, u32[]{:S(2)}) collective-permute-start(bf16[1024,128]{1,0:T(8,128)(2,1)S(1)} %get-tuple-element.107.refs_1_), channel_id=1, source_target_pairs={{0,31},{1,2},{2,1},{3,4},{4,3},{5,6},{6,5},{7,8},{8,7},{9,10},{10,... | collective-permute-start | bytes 786440 | tf_op jit(solution)/shard_map/ppermute | solution.py:344
  245.1 22.0 %copy-start.2 = (bf16[512,256]{1,0:T(8,128)(2,1)}, bf16[512,256]{1,0:T(8,128)(2,1)S(1)}, u32[]{:S(2)}) copy-start(bf16[512,256]{1,0:T(8,128)(2,1)S(1)} %get-tuple-element.108.half_a) | copy-start | bytes 786436
  245.2 22.0 %copy-start.3 = (bf16[512,256]{1,0:T(8,128)(2,1)}, bf16[512,256]{1,0:T(8,128)(2,1)S(1)}, u32[]{:S(2)}) copy-start(bf16[512,256]{1,0:T(8,128)(2,1)S(1)} %get-tuple-element.109.half_b) | copy-start | bytes 786436

commit v7 on v6

--- a/solution.py
+++ b/solution.py
@@ -85,19 +85,16 @@
         else:
             half[at : at + TILE, :] = value[:, :TILE]
             half[HALF + at : HALF + at + TILE, :] = value[:, TILE:]
-    if len(refs) == 13:
-        copy_rims(refs[8], out_a, out_b, 2 * HALF)
+    for n, operator in enumerate(refs[8:-4]):
+        copy_rims(operator, out_a, out_b, 2 * HALF + n * HB * (4 * TILE + 8))
 
 def visit(halves, sides, rims, first, second, following, flat, rim_at, second_at):
     vmem = pl.BlockSpec(memory_space=pltpu.VMEM)
     kind = halves[0].dtype
     lines = 2 * HALF
-    if following is not None:
-        lines += HB * (4 * TILE + 8)
+    lines += len(following) * HB * (4 * TILE + 8)
     shape = jax.ShapeDtypeStruct((HALF, 2 * TILE) if flat else (lines, TILE), kind)
-    operands = [*halves, *sides, *rims, first, second]
-    if following is not None:
-        operands.append(following)
+    operands = [*halves, *sides, *rims, first, second, *following]
     return pl.pallas_call(
         functools.partial(visit_kernel, rim_at, second_at, flat),
         out_shape=(shape, shape),
@@ -199,24 +196,6 @@
         compiler_params=pltpu.CompilerParams(vmem_limit_bytes=24 * 1024 * 1024),
         name="gather_swap",
     )(info, *operators)
-
-def rims_kernel(*refs):
-    operators, (side_a, side_b) = refs[:-2], refs[-2:]
-    for n, operator in enumerate(operators):
-        copy_rims(operator, side_a, side_b, n * HB * (4 * TILE + 8))
-
-def gather_rims(operators):
-    vmem = pl.BlockSpec(memory_space=pltpu.VMEM)
-    lines = len(operators) * HB * (4 * TILE + 8)
-    side = jax.ShapeDtypeStruct((lines, TILE), operators[0].dtype)
-    return pl.pallas_call(
-        rims_kernel,
-        out_shape=(side, side),
-        in_specs=[vmem] * len(operators),
-        out_specs=(vmem, vmem),
-        compiler_params=pltpu.CompilerParams(vmem_limit_bytes=24 * 1024 * 1024),
-        name="gather_rims",
-    )(*operators)
 
 
 NB = 16
@@ -338,11 +317,12 @@
     first_rims = rims(home_a, home_b)
     span = home.shape[0]
     rim_span = home_a.shape[0]
-    batched = far + 2
+    riders = {n: [n] for n in range(1, far + 2)}
+    for n in range(far + 2, visits):
+        riders[visits + 1 - n].append(n)
+    rim_of = {0: (first_rims, 0)}
     for turn in range(visits):
-        sides = (
-            lax.ppermute(halves[0], "rows", to_a), lax.ppermute(halves[1], "rows", to_b)
-        )
+        sides = (lax.ppermute(halves[0], "rows", to_a), lax.ppermute(halves[1], "rows", to_b))
         second_at = 0
         if turn <= far:
             here, later, halves = lax.optimization_barrier((held[turn], held[turn + 1], halves))
@@ -354,25 +334,17 @@
                 held[end] = lax.ppermute(nearer, "phase", ahead)
             picked = jnp.where(first_core, later, here)
             other = lax.ppermute(picked, "phase", mates)
-        if turn == far - 1:
-            last, halves = lax.optimization_barrier(
-                ([held[n] for n in range(batched, visits)], halves)
-            )
-            last_rims = rims(*gather_rims(last))
         if turn == far:
-            last = [later] + [held[n] for n in range(batched, visits)] + [home]
+            last = [later] + [held[n] for n in range(turn + 2, visits)] + [home]
             others = lax.ppermute(gather_swap(info, last), "phase", mates)
         if turn > far:
             other, second_at = others, (turn - far - 1) * span
-        if turn == 0:
-            rim, rim_at = first_rims, 0
-        elif turn < batched:
-            rim, rim_at = sides, rows_here
-        else:
-            rim, rim_at = last_rims, (turn - batched) * rim_span
+        for n, operator in enumerate(riders.get(turn, [])):
+            rim_of[operator] = (sides, rows_here + n * rim_span)
+        rim, rim_at = rim_of[turn]
+        following = [held[n] for n in riders.get(turn + 1, [])]
         halves = visit(
-            halves, sides, rim, held[turn], other,
-            held[turn + 1] if turn + 1 < batched else None,
+            halves, sides, rim, held[turn], other, following,
             turn + 1 == visits, rim_at, second_at,
         )
 

time: 298 us -> 302 us (1.013)
  waiting for transfers between devices: 107 us -> 114 us
    ppermute x8, waiting for transfers between devices: 24.1 us -> 38.5 us  [body(): lax.ppermute(halves[0], 'rows', to_a)]
    ppermute x8, starting transfers between devices: 40.4 us -> 46.9 us  [body(): lax.ppermute(halves[1], 'rows', to_b)]
    ppermute x2 -> x1, starting transfers between devices: 11 us -> 4.55 us  [rims(): lax.ppermute(b_side, 'rows', to_b)]
    ppermute x2, waiting for transfers between devices: 11.5 us -> 5.57 us  [body(): held[end] = lax.ppermute(nearer, 'phase', ahead)]
  transfers between devices with their start and end apart: 33 -> 31, of which waited for: 21 -> 17; matrix products, arithmetic and copies ran while one was open for 0% -> 0% of each run, Pallas kernels for 3% -> 3%
where the time goes in v7:
time: 302 us; the launch traced here: 301 us
  starting transfers between devices  116 us (38%)
  waiting for transfers between devices  114 us (38%)
  blocking collectives  36.6 us (12%)
  Pallas kernels  29.4 us (10%)
    ppermute x8, starting transfers between devices, body(): lax.ppermute(halves[1], 'rows', to_b)  46.9 us
    ppermute x8, waiting for transfers between devices, body(): lax.ppermute(halves[0], 'rows', to_a)  38.5 us
    ppermute x8, waiting for transfers between devices, body(): lax.ppermute(halves[1], 'rows', to_b)  35.7 us
    ppermute x1, waiting for transfers between devices, body(): held[1] = lax.ppermute(home, 'phase', back)  22.1 us
    all_to_all x1, blocking collectives, sum_over_rows(): pieces = lax.all_to_all(pieces, 'rows', 0, 0, tiled=True)  21.6 us
    ppermute x8, starting transfers between devices, body(): lax.ppermute(halves[0], 'rows', to_a)  16.9 us
    ppermute x3, starting transfers between devices, body(): held[turn + 2] = lax.ppermute(later, 'phase', back)  16.3 us
    all_to_all x1, blocking collectives, sum_over_rows(): return lax.all_to_all(copies, 'rows', 0, 0, tiled=True).reshape(size, size)  15 us
  transfers between devices with their start and end apart: 31, of which 17 were waited for; matrix products, arithmetic and copies ran while one was open for 0% of the time, Pallas kernels for 3%

profile of v7, /device:TPU:8, one launch (start us, length us, event | category | flops | bytes accessed | tf_op | source)
XLA Modules:
  0.0 301.3 jit_solution(2500048977542354659)
XLA Ops:
  4.1 10.9 %collective-permute-start = (bf16[4160,128]{1,0:T(8,128)(2,1)S(1)}, bf16[4160,128]{1,0:T(8,128)(2,1)S(1)}, u32[]{:S(2)}, u32[]{:S(2)}) collective-permute-start(bf16[4160,128]{1,0:T(8,128)(2,1)S(1)} %get-tuple-element.59.refs_6_.refs_3_), channel_id=1, source_target_pairs={{0,448},{32,480},{64,0},{96,32},{128,64},{160,96},{192,128},{224,1... | collective-permute-start | bytes 3194888 | tf_op jit(solution)/shard_map/ppermute | solution.py:314
  15.7 22.1 %collective-permute-done.refs_8_.refs_6_ = bf16[4160,128]{1,0:T(8,128)(2,1)S(1)} collective-permute-done((bf16[4160,128]{1,0:T(8,128)(2,1)S(1)}, bf16[4160,128]{1,0:T(8,128)(2,1)S(1)}, u32[]{:S(2)}, u32[]{:S(2)}) %collective-permute-start) | collective-permute-done | bytes 1064992 | tf_op jit(solution)/shard_map/ppermute | solution.py:314
  38.0 1.9 collective-permute-start.6
  39.9 5.6 %collective-permute-start.1 = (bf16[4160,128]{1,0:T(8,128)(2,1)S(1)}, bf16[4160,128]{1,0:T(8,128)(2,1)S(1)}, u32[]{:S(2)}, u32[]{:S(2)}) collective-permute-start(bf16[4160,128]{1,0:T(8,128)(2,1)S(1)} %collective-permute-done.refs_8_.refs_6_), channel_id=1, source_target_pairs={{0,448},{32,480},{64,0},{96,32},{128,64},{160,96},{192,128},{224,1... | collective-permute-start | bytes 3194888 | tf_op jit(solution)/shard_map/ppermute | solution.py:330
  45.5 3.4 %collective-permute-start.2 = (bf16[1024,128]{1,0:T(8,128)(2,1)S(1)}, bf16[1024,128]{1,0:T(8,128)(2,1)S(1)}, u32[]{:S(2)}, u32[]{:S(2)}) collective-permute-start(bf16[1024,128]{1,0:T(8,128)(2,1)S(1)} %get-tuple-element.55.refs_0_), channel_id=1, source_target_pairs={{0,1},{1,0},{2,3},{3,2},{4,5},{5,4},{6,7},{7,6},{8,9},{9,8},{10,11... | collective-permute-start | bytes 786440 | tf_op jit(solution)/shard_map/ppermute | solution.py:325
  48.9 2.4 collective-permute-start.4
  51.4 4.6 %collective-permute-start.5 = (bf16[1040,128]{1,0:T(8,128)(2,1)S(1)}, bf16[1040,128]{1,0:T(8,128)(2,1)S(1)}, u32[]{:S(2)}, u32[]{:S(2)}) collective-permute-start(bf16[1040,128]{1,0:T(8,128)(2,1)S(1)} %get-tuple-element.58), channel_id=1, source_target_pairs={{0,31},{1,2},{2,1},{3,4},{4,3},{5,6},{6,5},{7,8},{8,7},{9,10},{10,... | collective-permute-start | bytes 798728 | tf_op jit(solution)/shard_map/ppermute | solution.py:308
  56.6 4.5 %collective-permute-start.3 = (bf16[1024,128]{1,0:T(8,128)(2,1)S(1)}, bf16[1024,128]{1,0:T(8,128)(2,1)S(1)}, u32[]{:S(2)}, u32[]{:S(2)}) collective-permute-start(bf16[1024,128]{1,0:T(8,128)(2,1)S(1)} %get-tuple-element.56.refs_1_), channel_id=1, source_target_pairs={{0,31},{1,2},{2,1},{3,4},{4,3},{5,6},{6,5},{7,8},{8,7},{9,10},{10,... | collective-permute-start | bytes 786440 | tf_op jit(solution)/shard_map/ppermute | solution.py:325
  61.1 7.8 %collective-permute-done.3.refs_3_ = bf16[1024,128]{1,0:T(8,128)(2,1)S(1)} collective-permute-done((bf16[1024,128]{1,0:T(8,128)(2,1)S(1)}, bf16[1024,128]{1,0:T(8,128)(2,1)S(1)}, u32[]{:S(2)}, u32[]{:S(2)}) %collective-permute-start.3) | collective-permute-done | bytes 262176 | tf_op jit(solution)/shard_map/ppermute | solution.py:325
  68.9 1.9 collective-permute-start.8
  72.5 1.9 collective-permute-start.11
  74.4 5.1 %collective-permute-start.7 = (bf16[4160,128]{1,0:T(8,128)(2,1)S(1)}, bf16[4160,128]{1,0:T(8,128)(2,1)S(1)}, u32[]{:S(2)}, u32[]{:S(2)}) collective-permute-start(bf16[4160,128]{1,0:T(8,128)(2,1)S(1)} %collective-permute-done.1.refs_8_.refs_6_), channel_id=1, source_target_pairs={{0,448},{32,480},{64,0},{96,32},{128,64},{160,96},{192,128},{224,1... | collective-permute-start | bytes 3194888 | tf_op jit(solution)/shard_map/ppermute | solution.py:330
  79.6 1.9 collective-permute-start.9
  81.5 4.6 %collective-permute-start.10 = (bf16[2064,128]{1,0:T(8,128)(2,1)S(1)}, bf16[2064,128]{1,0:T(8,128)(2,1)S(1)}, u32[]{:S(2)}, u32[]{:S(2)}) collective-permute-start(bf16[2064,128]{1,0:T(8,128)(2,1)S(1)} %get-tuple-element.66.refs_1_), channel_id=1, source_target_pairs={{0,31},{1,2},{2,1},{3,4},{4,3},{5,6},{6,5},{7,8},{8,7},{9,10},{10,... | collective-permute-start | bytes 1585160 | tf_op jit(solution)/shard_map/ppermute | solution.py:325
  86.1 10.2 %collective-permute-done.8.refs_9_.refs_2_.refs_6_ = bf16[4160,128]{1,0:T(8,128)(2,1)S(1)} collective-permute-done((bf16[4160,128]{1,0:T(8,128)(2,1)S(1)}, bf16[4160,128]{1,0:T(8,128)(2,1)S(1)}, u32[]{:S(2)}, u32[]{:S(2)}) %collective-permute-start.8) | collective-permute-done | bytes 1064992 | tf_op jit(solution)/shard_map/ppermute | solution.py:315
  96.2 1.9 collective-permute-start.13
  103.1 1.9 collective-permute-start.17
  105.0 5.6 %collective-permute-start.12 = (bf16[4160,128]{1,0:T(8,128)(2,1)S(1)}, bf16[4160,128]{1,0:T(8,128)(2,1)S(1)}, u32[]{:S(2)}, u32[]{:S(2)}) collective-permute-start(bf16[4160,128]{1,0:T(8,128)(2,1)S(1)} %collective-permute-done.7.refs_8_.refs_6_), channel_id=1, source_target_pairs={{0,448},{32,480},{64,0},{96,32},{128,64},{160,96},{192,128},{224,1... | collective-permute-start | bytes 3194888 | tf_op jit(solution)/shard_map/ppermute | solution.py:330
  110.6 1.9 collective-permute-start.15
  112.6 4.6 %collective-permute-start.16 = (bf16[3104,128]{1,0:T(8,128)(2,1)S(1)}, bf16[3104,128]{1,0:T(8,128)(2,1)S(1)}, u32[]{:S(2)}, u32[]{:S(2)}) collective-permute-start(bf16[3104,128]{1,0:T(8,128)(2,1)S(1)} %get-tuple-element.76.refs_1_), channel_id=1, source_target_pairs={{0,31},{1,2},{2,1},{3,4},{4,3},{5,6},{6,5},{7,8},{8,7},{9,10},{10,... | collective-permute-start | bytes 2383880 | tf_op jit(solution)/shard_map/ppermute | solution.py:325
  117.1 5.6 %collective-permute-done.13.refs_9_.refs_1_.refs_6_ = bf16[4160,128]{1,0:T(8,128)(2,1)S(1)} collective-permute-done((bf16[4160,128]{1,0:T(8,128)(2,1)S(1)}, bf16[4160,128]{1,0:T(8,128)(2,1)S(1)}, u32[]{:S(2)}, u32[]{:S(2)}) %collective-permute-start.13) | collective-permute-done | bytes 1064992 | tf_op jit(solution)/shard_map/ppermute | solution.py:334
  122.7 9.7 %collective-permute-done.15.refs_2_.refs_4_ = bf16[3104,128]{1,0:T(8,128)(2,1)S(1)} collective-permute-done((bf16[3104,128]{1,0:T(8,128)(2,1)S(1)}, bf16[3104,128]{1,0:T(8,128)(2,1)S(1)}, u32[]{:S(2)}, u32[]{:S(2)}) %collective-permute-start.15) | collective-permute-done | bytes 794656 | tf_op jit(solution)/shard_map/ppermute | solution.py:325
  132.4 4.0 %collective-permute-done.16.refs_3_.refs_5_ = bf16[3104,128]{1,0:T(8,128)(2,1)S(1)} collective-permute-done((bf16[3104,128]{1,0:T(8,128)(2,1)S(1)}, bf16[3104,128]{1,0:T(8,128)(2,1)S(1)}, u32[]{:S(2)}, u32[]{:S(2)}) %collective-permute-start.16) | collective-permute-done | bytes 794656 | tf_op jit(solution)/shard_map/ppermute | solution.py:325
  138.1 1.9 collective-permute-start.20
  140.0 1.9 collective-permute-start.14
  142.0 2.0 collective-permute-start.18
  143.9 5.1 %collective-permute-start.19 = (bf16[3104,128]{1,0:T(8,128)(2,1)S(1)}, bf16[3104,128]{1,0:T(8,128)(2,1)S(1)}, u32[]{:S(2)}, u32[]{:S(2)}) collective-permute-start(bf16[3104,128]{1,0:T(8,128)(2,1)S(1)} %get-tuple-element.81.refs_1_), channel_id=1, source_target_pairs={{0,31},{1,2},{2,1},{3,4},{4,3},{5,6},{6,5},{7,8},{8,7},{9,10},{10,... | collective-permute-start | bytes 2383880 | tf_op jit(solution)/shard_map/ppermute | solution.py:325
  149.0 15.0 %collective-permute-done.18.refs_2_.refs_4_ = bf16[3104,128]{1,0:T(8,128)(2,1)S(1)} collective-permute-done((bf16[3104,128]{1,0:T(8,128)(2,1)S(1)}, bf16[3104,128]{1,0:T(8,128)(2,1)S(1)}, u32[]{:S(2)}, u32[]{:S(2)}) %collective-permute-start.18) | collective-permute-done | bytes 794656 | tf_op jit(solution)/shard_map/ppermute | solution.py:325
  164.0 4.0 %collective-permute-done.19.refs_3_.refs_5_ = bf16[3104,128]{1,0:T(8,128)(2,1)S(1)} collective-permute-done((bf16[3104,128]{1,0:T(8,128)(2,1)S(1)}, bf16[3104,128]{1,0:T(8,128)(2,1)S(1)}, u32[]{:S(2)}, u32[]{:S(2)}) %collective-permute-start.19) | collective-permute-done | bytes 794656 | tf_op jit(solution)/shard_map/ppermute | solution.py:325
  171.4 1.9 collective-permute-start.26
  173.5 2.4 collective-permute-start.23
  175.9 1.9 collective-permute-start.21
  177.8 6.3 %collective-permute-start.22 = (bf16[2064,128]{1,0:T(8,128)(2,1)S(1)}, bf16[2064,128]{1,0:T(8,128)(2,1)S(1)}, u32[]{:S(2)}, u32[]{:S(2)}) collective-permute-start(bf16[2064,128]{1,0:T(8,128)(2,1)S(1)} %get-tuple-element.87.refs_1_), channel_id=1, source_target_pairs={{0,31},{1,2},{2,1},{3,4},{4,3},{5,6},{6,5},{7,8},{8,7},{9,10},{10,... | collective-permute-start | bytes 1585160 | tf_op jit(solution)/shard_map/ppermute | solution.py:325
  184.1 7.6 %collective-permute-done.21.refs_2_.refs_4_ = bf16[2064,128]{1,0:T(8,128)(2,1)S(1)} collective-permute-done((bf16[2064,128]{1,0:T(8,128)(2,1)S(1)}, bf16[2064,128]{1,0:T(8,128)(2,1)S(1)}, u32[]{:S(2)}, u32[]{:S(2)}) %collective-permute-start.21) | collective-permute-done | bytes 528416 | tf_op jit(solution)/shard_map/ppermute | solution.py:325
  191.7 4.3 %collective-permute-done.22.refs_3_.refs_5_ = bf16[2064,128]{1,0:T(8,128)(2,1)S(1)} collective-permute-done((bf16[2064,128]{1,0:T(8,128)(2,1)S(1)}, bf16[2064,128]{1,0:T(8,128)(2,1)S(1)}, u32[]{:S(2)}, u32[]{:S(2)}) %collective-permute-start.22) | collective-permute-done | bytes 528416 | tf_op jit(solution)/shard_map/ppermute | solution.py:325
  197.6 1.9 collective-permute-start.24
  199.5 7.4 %collective-permute-start.25 = (bf16[2064,128]{1,0:T(8,128)(2,1)S(1)}, bf16[2064,128]{1,0:T(8,128)(2,1)S(1)}, u32[]{:S(2)}, u32[]{:S(2)}) collective-permute-start(bf16[2064,128]{1,0:T(8,128)(2,1)S(1)} %get-tuple-element.91.refs_1_), channel_id=1, source_target_pairs={{0,31},{1,2},{2,1},{3,4},{4,3},{5,6},{6,5},{7,8},{8,7},{9,10},{10,... | collective-permute-start | bytes 1585160 | tf_op jit(solution)/shard_map/ppermute | solution.py:325
  206.9 5.6 %collective-permute-done.24.refs_2_.refs_4_ = bf16[2064,128]{1,0:T(8,128)(2,1)S(1)} collective-permute-done((bf16[2064,128]{1,0:T(8,128)(2,1)S(1)}, bf16[2064,128]{1,0:T(8,128)(2,1)S(1)}, u32[]{:S(2)}, u32[]{:S(2)}) %collective-permute-start.24) | collective-permute-done | bytes 528416 | tf_op jit(solution)/shard_map/ppermute | solution.py:325
  212.5 5.3 %collective-permute-done.25.refs_3_.refs_5_ = bf16[2064,128]{1,0:T(8,128)(2,1)S(1)} collective-permute-done((bf16[2064,128]{1,0:T(8,128)(2,1)S(1)}, bf16[2064,128]{1,0:T(8,128)(2,1)S(1)}, u32[]{:S(2)}, u32[]{:S(2)}) %collective-permute-start.25) | collective-permute-done | bytes 528416 | tf_op jit(solution)/shard_map/ppermute | solution.py:325
  219.2 1.9 collective-permute-start.27
  221.2 7.2 %collective-permute-start.28 = (bf16[1024,128]{1,0:T(8,128)(2,1)S(1)}, bf16[1024,128]{1,0:T(8,128)(2,1)S(1)}, u32[]{:S(2)}, u32[]{:S(2)}) collective-permute-start(bf16[1024,128]{1,0:T(8,128)(2,1)S(1)} %get-tuple-element.93.refs_1_), channel_id=1, source_target_pairs={{0,31},{1,2},{2,1},{3,4},{4,3},{5,6},{6,5},{7,8},{8,7},{9,10},{10,... | collective-permute-start | bytes 786440 | tf_op jit(solution)/shard_map/ppermute | solution.py:325
  228.4 4.5 %collective-permute-done.28.refs_3_ = bf16[1024,128]{1,0:T(8,128)(2,1)S(1)} collective-permute-done((bf16[1024,128]{1,0:T(8,128)(2,1)S(1)}, bf16[1024,128]{1,0:T(8,128)(2,1)S(1)}, u32[]{:S(2)}, u32[]{:S(2)}) %collective-permute-start.28) | collective-permute-done | bytes 262176 | tf_op jit(solution)/shard_map/ppermute | solution.py:325
  234.3 1.9 collective-permute-start.29
  236.3 7.2 %collective-permute-start.30 = (bf16[1024,128]{1,0:T(8,128)(2,1)S(1)}, bf16[1024,128]{1,0:T(8,128)(2,1)S(1)}, u32[]{:S(2)}, u32[]{:S(2)}) collective-permute-start(bf16[1024,128]{1,0:T(8,128)(2,1)S(1)} %get-tuple-element.95.refs_1_), channel_id=1, source_target_pairs={{0,31},{1,2},{2,1},{3,4},{4,3},{5,6},{6,5},{7,8},{8,7},{9,10},{10,... | collective-permute-start | bytes 786440 | tf_op jit(solution)/shard_map/ppermute | solution.py:325
  243.5 4.3 %collective-permute-done.30.refs_3_ = bf16[1024,128]{1,0:T(8,128)(2,1)S(1)} collective-permute-done((bf16[1024,128]{1,0:T(8,128)(2,1)S(1)}, bf16[1024,128]{1,0:T(8,128)(2,1)S(1)}, u32[]{:S(2)}, u32[]{:S(2)}) %collective-permute-start.30) | collective-permute-done | bytes 262176 | tf_op jit(solution)/shard_map/ppermute | solution.py:325
  249.6 21.6 %all_to_all.10 = bf16[32,8,256]{2,1,0:T(8,128)(2,1)S(1)} all-to-all(bf16[32,8,256]{2,1,0:T(8,128)(2,1)S(1)} %fusion), channel_id=1, replica_groups=mesh['phase'=16,'rows'=32] {'rows'}, dimensions={0} | all-to-all | bytes 262144 | tf_op jit(solution)/shard_map/all_to_all | solution.py:286
  271.3 15.0 %all_to_all.11 = f32[32,8,256]{2,1,0:T(8,128)S(1)} all-to-all(f32[32,8,256]{2,1,0:T(8,128)S(1)} %broadcast_in_dim.12), channel_id=1, replica_groups=mesh['phase'=16,'rows'=32] {'rows'}, dimensions={0} | all-to-all | bytes 524288 | tf_op jit(solution)/shard_map/all_to_all | solution.py:289
  287.1 14.2 %factor_solve.1 = (f32[1024,256]{1,0:T(8,128)}, f32[256,256]{1,0:T(8,128)}) custom-call(s32[3]{0:T(128)} %copy-done.4, f32[256,256]{1,0:T(8,128)} %multiply_bitcast_fusion.gram_ref, bf16[512,256]{1,0:T(8,128)(2,1)} %copy-done.2, bf16[512,256]{1,0:T(8,128)(2,1)} %copy-done.3), custom_call_target="tpu_custom_call" | custom-call | tf_op jit(solution)/shard_map/factor_solve/pallas_call | solution.py:269
  (51 shorter events, 23.5 us)
Async XLA Ops:
  1.5 168.1 %copy-start.4 = (s32[3]{0:T(128)}, s32[3]{0:T(128)S(1)}, u32[]{:S(2)}) copy-start(s32[3]{0:T(128)S(1)} %pad_add_fusion.info) | copy-start | bytes 40
  1.5 1.2 copy-start
  2.7 0.7 copy-start.5
  3.4 11.7 %copy-start.1 = (bf16[1,1024,256]{2,1,0:T(8,128)(2,1)S(1)}, bf16[1,1024,256]{2,1,0:T(8,128)(2,1)}, u32[]{:S(2)}) copy-start(bf16[1,1024,256]{2,1,0:T(8,128)(2,1)} %param.4) | copy-start | bytes 1572868
  4.1 33.7 %collective-permute-start = (bf16[4160,128]{1,0:T(8,128)(2,1)S(1)}, bf16[4160,128]{1,0:T(8,128)(2,1)S(1)}, u32[]{:S(2)}, u32[]{:S(2)}) collective-permute-start(bf16[4160,128]{1,0:T(8,128)(2,1)S(1)} %get-tuple-element.59.refs_6_.refs_3_), channel_id=1, source_target_pairs={{0,448},{32,480},{64,0},{96,32},{128,64},{160,96},{192,128},{224,1... | collective-permute-start | bytes 3194888 | tf_op jit(solution)/shard_map/ppermute | solution.py:314
  38.0 32.9 %collective-permute-start.6 = (bf16[4160,128]{1,0:T(8,128)(2,1)S(1)}, bf16[4160,128]{1,0:T(8,128)(2,1)S(1)}, u32[]{:S(2)}, u32[]{:S(2)}) collective-permute-start(bf16[4160,128]{1,0:T(8,128)(2,1)S(1)} %broadcast_select_fusion.4), channel_id=1, source_target_pairs={{0,32},{32,0},{64,96},{96,64},{128,160},{160,128},{192,224},{224,1... | collective-permute-start | bytes 3194888 | tf_op jit(solution)/shard_map/ppermute | solution.py:336
  39.9 32.5 %collective-permute-start.1 = (bf16[4160,128]{1,0:T(8,128)(2,1)S(1)}, bf16[4160,128]{1,0:T(8,128)(2,1)S(1)}, u32[]{:S(2)}, u32[]{:S(2)}) collective-permute-start(bf16[4160,128]{1,0:T(8,128)(2,1)S(1)} %collective-permute-done.refs_8_.refs_6_), channel_id=1, source_target_pairs={{0,448},{32,480},{64,0},{96,32},{128,64},{160,96},{192,128},{224,1... | collective-permute-start | bytes 3194888 | tf_op jit(solution)/shard_map/ppermute | solution.py:330
  45.5 11.1 %collective-permute-start.2 = (bf16[1024,128]{1,0:T(8,128)(2,1)S(1)}, bf16[1024,128]{1,0:T(8,128)(2,1)S(1)}, u32[]{:S(2)}, u32[]{:S(2)}) collective-permute-start(bf16[1024,128]{1,0:T(8,128)(2,1)S(1)} %get-tuple-element.55.refs_0_), channel_id=1, source_target_pairs={{0,1},{1,0},{2,3},{3,2},{4,5},{5,4},{6,7},{7,6},{8,9},{9,8},{10,11... | collective-permute-start | bytes 786440 | tf_op jit(solution)/shard_map/ppermute | solution.py:325
  48.9 21.9 %collective-permute-start.4 = (bf16[1040,128]{1,0:T(8,128)(2,1)S(1)}, bf16[1040,128]{1,0:T(8,128)(2,1)S(1)}, u32[]{:S(2)}, u32[]{:S(2)}) collective-permute-start(bf16[1040,128]{1,0:T(8,128)(2,1)S(1)} %get-tuple-element.57), channel_id=1, source_target_pairs={{0,1},{1,0},{2,3},{3,2},{4,5},{5,4},{6,7},{7,6},{8,9},{9,8},{10,11... | collective-permute-start | bytes 798728 | tf_op jit(solution)/shard_map/ppermute | solution.py:308
  51.4 19.5 %collective-permute-start.5 = (bf16[1040,128]{1,0:T(8,128)(2,1)S(1)}, bf16[1040,128]{1,0:T(8,128)(2,1)S(1)}, u32[]{:S(2)}, u32[]{:S(2)}) collective-permute-start(bf16[1040,128]{1,0:T(8,128)(2,1)S(1)} %get-tuple-element.58), channel_id=1, source_target_pairs={{0,31},{1,2},{2,1},{3,4},{4,3},{5,6},{6,5},{7,8},{8,7},{9,10},{10,... | collective-permute-start | bytes 798728 | tf_op jit(solution)/shard_map/ppermute | solution.py:308
  56.6 12.4 %collective-permute-start.3 = (bf16[1024,128]{1,0:T(8,128)(2,1)S(1)}, bf16[1024,128]{1,0:T(8,128)(2,1)S(1)}, u32[]{:S(2)}, u32[]{:S(2)}) collective-permute-start(bf16[1024,128]{1,0:T(8,128)(2,1)S(1)} %get-tuple-element.56.refs_1_), channel_id=1, source_target_pairs={{0,31},{1,2},{2,1},{3,4},{4,3},{5,6},{6,5},{7,8},{8,7},{9,10},{10,... | collective-permute-start | bytes 786440 | tf_op jit(solution)/shard_map/ppermute | solution.py:325
  68.9 27.3 %collective-permute-start.8 = (bf16[4160,128]{1,0:T(8,128)(2,1)S(1)}, bf16[4160,128]{1,0:T(8,128)(2,1)S(1)}, u32[]{:S(2)}, u32[]{:S(2)}) collective-permute-start(bf16[4160,128]{1,0:T(8,128)(2,1)S(1)} %get-tuple-element.59.refs_6_.refs_3_), channel_id=1, source_target_pairs={{0,64},{32,96},{64,128},{96,160},{128,192},{160,224},{192,256},{22... | collective-permute-start | bytes 3194888 | tf_op jit(solution)/shard_map/ppermute | solution.py:315
  72.5 27.1 %collective-permute-start.11 = (bf16[4160,128]{1,0:T(8,128)(2,1)S(1)}, bf16[4160,128]{1,0:T(8,128)(2,1)S(1)}, u32[]{:S(2)}, u32[]{:S(2)}) collective-permute-start(bf16[4160,128]{1,0:T(8,128)(2,1)S(1)} %broadcast_select_fusion.3), channel_id=1, source_target_pairs={{0,32},{32,0},{64,96},{96,64},{128,160},{160,128},{192,224},{224,1... | collective-permute-start | bytes 3194888 | tf_op jit(solution)/shard_map/ppermute | solution.py:336
  74.4 28.5 %collective-permute-start.7 = (bf16[4160,128]{1,0:T(8,128)(2,1)S(1)}, bf16[4160,128]{1,0:T(8,128)(2,1)S(1)}, u32[]{:S(2)}, u32[]{:S(2)}) collective-permute-start(bf16[4160,128]{1,0:T(8,128)(2,1)S(1)} %collective-permute-done.1.refs_8_.refs_6_), channel_id=1, source_target_pairs={{0,448},{32,480},{64,0},{96,32},{128,64},{160,96},{192,128},{224,1... | collective-permute-start | bytes 3194888 | tf_op jit(solution)/shard_map/ppermute | solution.py:330
  79.6 18.6 %collective-permute-start.9 = (bf16[2064,128]{1,0:T(8,128)(2,1)S(1)}, bf16[2064,128]{1,0:T(8,128)(2,1)S(1)}, u32[]{:S(2)}, u32[]{:S(2)}) collective-permute-start(bf16[2064,128]{1,0:T(8,128)(2,1)S(1)} %get-tuple-element.65.refs_0_), channel_id=1, source_target_pairs={{0,1},{1,0},{2,3},{3,2},{4,5},{5,4},{6,7},{7,6},{8,9},{9,8},{10,11... | collective-permute-start | bytes 1585160 | tf_op jit(solution)/shard_map/ppermute | solution.py:325
  81.5 18.1 %collective-permute-start.10 = (bf16[2064,128]{1,0:T(8,128)(2,1)S(1)}, bf16[2064,128]{1,0:T(8,128)(2,1)S(1)}, u32[]{:S(2)}, u32[]{:S(2)}) collective-permute-start(bf16[2064,128]{1,0:T(8,128)(2,1)S(1)} %get-tuple-element.66.refs_1_), channel_id=1, source_target_pairs={{0,31},{1,2},{2,1},{3,4},{4,3},{5,6},{6,5},{7,8},{8,7},{9,10},{10,... | collective-permute-start | bytes 1585160 | tf_op jit(solution)/shard_map/ppermute | solution.py:325
  96.2 26.5 %collective-permute-start.13 = (bf16[4160,128]{1,0:T(8,128)(2,1)S(1)}, bf16[4160,128]{1,0:T(8,128)(2,1)S(1)}, u32[]{:S(2)}, u32[]{:S(2)}) collective-permute-start(bf16[4160,128]{1,0:T(8,128)(2,1)S(1)} %collective-permute-done.8.refs_9_.refs_2_.refs_6_), channel_id=1, source_target_pairs={{0,64},{32,96},{64,128},{96,160},{128,192},{160,224},{192,256},{22... | collective-permute-start | bytes 3194888 | tf_op jit(solution)/shard_map/ppermute | solution.py:334
  103.1 33.3 %collective-permute-start.17 = (bf16[4160,128]{1,0:T(8,128)(2,1)S(1)}, bf16[4160,128]{1,0:T(8,128)(2,1)S(1)}, u32[]{:S(2)}, u32[]{:S(2)}) collective-permute-start(bf16[4160,128]{1,0:T(8,128)(2,1)S(1)} %broadcast_select_fusion.2), channel_id=1, source_target_pairs={{0,32},{32,0},{64,96},{96,64},{128,160},{160,128},{192,224},{224,1... | collective-permute-start | bytes 3194888 | tf_op jit(solution)/shard_map/ppermute | solution.py:336
  105.0 33.0 %collective-permute-start.12 = (bf16[4160,128]{1,0:T(8,128)(2,1)S(1)}, bf16[4160,128]{1,0:T(8,128)(2,1)S(1)}, u32[]{:S(2)}, u32[]{:S(2)}) collective-permute-start(bf16[4160,128]{1,0:T(8,128)(2,1)S(1)} %collective-permute-done.7.refs_8_.refs_6_), channel_id=1, source_target_pairs={{0,448},{32,480},{64,0},{96,32},{128,64},{160,96},{192,128},{224,1... | collective-permute-start | bytes 3194888 | tf_op jit(solution)/shard_map/ppermute | solution.py:330
  110.6 21.7 %collective-permute-start.15 = (bf16[3104,128]{1,0:T(8,128)(2,1)S(1)}, bf16[3104,128]{1,0:T(8,128)(2,1)S(1)}, u32[]{:S(2)}, u32[]{:S(2)}) collective-permute-start(bf16[3104,128]{1,0:T(8,128)(2,1)S(1)} %get-tuple-element.75.refs_0_), channel_id=1, source_target_pairs={{0,1},{1,0},{2,3},{3,2},{4,5},{5,4},{6,7},{7,6},{8,9},{9,8},{10,11... | collective-permute-start | bytes 2383880 | tf_op jit(solution)/shard_map/ppermute | solution.py:325
  112.6 23.8 %collective-permute-start.16 = (bf16[3104,128]{1,0:T(8,128)(2,1)S(1)}, bf16[3104,128]{1,0:T(8,128)(2,1)S(1)}, u32[]{:S(2)}, u32[]{:S(2)}) collective-permute-start(bf16[3104,128]{1,0:T(8,128)(2,1)S(1)} %get-tuple-element.76.refs_1_), channel_id=1, source_target_pairs={{0,31},{1,2},{2,1},{3,4},{4,3},{5,6},{6,5},{7,8},{8,7},{9,10},{10,... | collective-permute-start | bytes 2383880 | tf_op jit(solution)/shard_map/ppermute | solution.py:325
  138.1 29.9 %collective-permute-start.20 = (bf16[4160,128]{1,0:T(8,128)(2,1)S(1)}, bf16[4160,128]{1,0:T(8,128)(2,1)S(1)}, u32[]{:S(2)}, u32[]{:S(2)}) collective-permute-start(bf16[4160,128]{1,0:T(8,128)(2,1)S(1)} %broadcast_select_fusion.1), channel_id=1, source_target_pairs={{0,32},{32,0},{64,96},{96,64},{128,160},{160,128},{192,224},{224,1... | collective-permute-start | bytes 3194888 | tf_op jit(solution)/shard_map/ppermute | solution.py:336
  140.0 29.5 %collective-permute-start.14 = (bf16[4160,128]{1,0:T(8,128)(2,1)S(1)}, bf16[4160,128]{1,0:T(8,128)(2,1)S(1)}, u32[]{:S(2)}, u32[]{:S(2)}) collective-permute-start(bf16[4160,128]{1,0:T(8,128)(2,1)S(1)} %collective-permute-done.13.refs_9_.refs_1_.refs_6_), channel_id=1, source_target_pairs={{0,64},{32,96},{64,128},{96,160},{128,192},{160,224},{192,256},{22... | collective-permute-start | bytes 3194888 | tf_op jit(solution)/shard_map/ppermute | solution.py:334
  142.0 22.0 %collective-permute-start.18 = (bf16[3104,128]{1,0:T(8,128)(2,1)S(1)}, bf16[3104,128]{1,0:T(8,128)(2,1)S(1)}, u32[]{:S(2)}, u32[]{:S(2)}) collective-permute-start(bf16[3104,128]{1,0:T(8,128)(2,1)S(1)} %get-tuple-element.80.refs_0_), channel_id=1, source_target_pairs={{0,1},{1,0},{2,3},{3,2},{4,5},{5,4},{6,7},{7,6},{8,9},{9,8},{10,11... | collective-permute-start | bytes 2383880 | tf_op jit(solution)/shard_map/ppermute | solution.py:325
  143.9 24.1 %collective-permute-start.19 = (bf16[3104,128]{1,0:T(8,128)(2,1)S(1)}, bf16[3104,128]{1,0:T(8,128)(2,1)S(1)}, u32[]{:S(2)}, u32[]{:S(2)}) collective-permute-start(bf16[3104,128]{1,0:T(8,128)(2,1)S(1)} %get-tuple-element.81.refs_1_), channel_id=1, source_target_pairs={{0,31},{1,2},{2,1},{3,4},{4,3},{5,6},{6,5},{7,8},{8,7},{9,10},{10,... | collective-permute-start | bytes 2383880 | tf_op jit(solution)/shard_map/ppermute | solution.py:325
  171.4 46.4 %collective-permute-start.26 = (bf16[12480,128]{1,0:T(8,128)(2,1)S(1)}, bf16[12480,128]{1,0:T(8,128)(2,1)S(1)}, u32[]{:S(2)}, u32[]{:S(2)}) collective-permute-start(bf16[12480,128]{1,0:T(8,128)(2,1)S(1)} %gather_swap.1), channel_id=1, source_target_pairs={{0,32},{32,0},{64,96},{96,64},{128,160},{160,128},{192,224},{224,1... | collective-permute-start | bytes 9584648 | tf_op jit(solution)/shard_map/ppermute | solution.py:339
  173.5 22.6 %collective-permute-start.23 = (bf16[4160,128]{1,0:T(8,128)(2,1)S(1)}, bf16[4160,128]{1,0:T(8,128)(2,1)S(1)}, u32[]{:S(2)}, u32[]{:S(2)}) collective-permute-start(bf16[4160,128]{1,0:T(8,128)(2,1)S(1)} %broadcast_select_fusion), channel_id=1, source_target_pairs={{0,32},{32,0},{64,96},{96,64},{128,160},{160,128},{192,224},{224,1... | collective-permute-start | bytes 3194888 | tf_op jit(solution)/shard_map/ppermute | solution.py:336
  175.9 15.8 %collective-permute-start.21 = (bf16[2064,128]{1,0:T(8,128)(2,1)S(1)}, bf16[2064,128]{1,0:T(8,128)(2,1)S(1)}, u32[]{:S(2)}, u32[]{:S(2)}) collective-permute-start(bf16[2064,128]{1,0:T(8,128)(2,1)S(1)} %get-tuple-element.86.refs_0_), channel_id=1, source_target_pairs={{0,1},{1,0},{2,3},{3,2},{4,5},{5,4},{6,7},{7,6},{8,9},{9,8},{10,11... | collective-permute-start | bytes 1585160 | tf_op jit(solution)/shard_map/ppermute | solution.py:325
  177.8 18.2 %collective-permute-start.22 = (bf16[2064,128]{1,0:T(8,128)(2,1)S(1)}, bf16[2064,128]{1,0:T(8,128)(2,1)S(1)}, u32[]{:S(2)}, u32[]{:S(2)}) collective-permute-start(bf16[2064,128]{1,0:T(8,128)(2,1)S(1)} %get-tuple-element.87.refs_1_), channel_id=1, source_target_pairs={{0,31},{1,2},{2,1},{3,4},{4,3},{5,6},{6,5},{7,8},{8,7},{9,10},{10,... | collective-permute-start | bytes 1585160 | tf_op jit(solution)/shard_map/ppermute | solution.py:325
  197.6 15.0 %collective-permute-start.24 = (bf16[2064,128]{1,0:T(8,128)(2,1)S(1)}, bf16[2064,128]{1,0:T(8,128)(2,1)S(1)}, u32[]{:S(2)}, u32[]{:S(2)}) collective-permute-start(bf16[2064,128]{1,0:T(8,128)(2,1)S(1)} %get-tuple-element.90.refs_0_), channel_id=1, source_target_pairs={{0,1},{1,0},{2,3},{3,2},{4,5},{5,4},{6,7},{7,6},{8,9},{9,8},{10,11... | collective-permute-start | bytes 1585160 | tf_op jit(solution)/shard_map/ppermute | solution.py:325
  199.5 18.3 %collective-permute-start.25 = (bf16[2064,128]{1,0:T(8,128)(2,1)S(1)}, bf16[2064,128]{1,0:T(8,128)(2,1)S(1)}, u32[]{:S(2)}, u32[]{:S(2)}) collective-permute-start(bf16[2064,128]{1,0:T(8,128)(2,1)S(1)} %get-tuple-element.91.refs_1_), channel_id=1, source_target_pairs={{0,31},{1,2},{2,1},{3,4},{4,3},{5,6},{6,5},{7,8},{8,7},{9,10},{10,... | collective-permute-start | bytes 1585160 | tf_op jit(solution)/shard_map/ppermute | solution.py:325
  219.2 9.2 %collective-permute-start.27 = (bf16[1024,128]{1,0:T(8,128)(2,1)S(1)}, bf16[1024,128]{1,0:T(8,128)(2,1)S(1)}, u32[]{:S(2)}, u32[]{:S(2)}) collective-permute-start(bf16[1024,128]{1,0:T(8,128)(2,1)S(1)} %get-tuple-element.92.refs_0_), channel_id=1, source_target_pairs={{0,1},{1,0},{2,3},{3,2},{4,5},{5,4},{6,7},{7,6},{8,9},{9,8},{10,11... | collective-permute-start | bytes 786440 | tf_op jit(solution)/shard_map/ppermute | solution.py:325
  221.2 11.7 %collective-permute-start.28 = (bf16[1024,128]{1,0:T(8,128)(2,1)S(1)}, bf16[1024,128]{1,0:T(8,128)(2,1)S(1)}, u32[]{:S(2)}, u32[]{:S(2)}) collective-permute-start(bf16[1024,128]{1,0:T(8,128)(2,1)S(1)} %get-tuple-element.93.refs_1_), channel_id=1, source_target_pairs={{0,31},{1,2},{2,1},{3,4},{4,3},{5,6},{6,5},{7,8},{8,7},{9,10},{10,... | collective-permute-start | bytes 786440 | tf_op jit(solution)/shard_map/ppermute | solution.py:325
  234.3 9.2 %collective-permute-start.29 = (bf16[1024,128]{1,0:T(8,128)(2,1)S(1)}, bf16[1024,128]{1,0:T(8,128)(2,1)S(1)}, u32[]{:S(2)}, u32[]{:S(2)}) collective-permute-start(bf16[1024,128]{1,0:T(8,128)(2,1)S(1)} %get-tuple-element.94.refs_0_), channel_id=1, source_target_pairs={{0,1},{1,0},{2,3},{3,2},{4,5},{5,4},{6,7},{7,6},{8,9},{9,8},{10,11... | collective-permute-start | bytes 786440 | tf_op jit(solution)/shard_map/ppermute | solution.py:325
  236.3 11.6 %collective-permute-start.30 = (bf16[1024,128]{1,0:T(8,128)(2,1)S(1)}, bf16[1024,128]{1,0:T(8,128)(2,1)S(1)}, u32[]{:S(2)}, u32[]{:S(2)}) collective-permute-start(bf16[1024,128]{1,0:T(8,128)(2,1)S(1)} %get-tuple-element.95.refs_1_), channel_id=1, source_target_pairs={{0,31},{1,2},{2,1},{3,4},{4,3},{5,6},{6,5},{7,8},{8,7},{9,10},{10,... | collective-permute-start | bytes 786440 | tf_op jit(solution)/shard_map/ppermute | solution.py:325
  249.3 22.1 %copy-start.2 = (bf16[512,256]{1,0:T(8,128)(2,1)}, bf16[512,256]{1,0:T(8,128)(2,1)S(1)}, u32[]{:S(2)}) copy-start(bf16[512,256]{1,0:T(8,128)(2,1)S(1)} %get-tuple-element.96.half_a) | copy-start | bytes 786436
  249.3 22.1 %copy-start.3 = (bf16[512,256]{1,0:T(8,128)(2,1)}, bf16[512,256]{1,0:T(8,128)(2,1)S(1)}, u32[]{:S(2)}) copy-start(bf16[512,256]{1,0:T(8,128)(2,1)S(1)} %get-tuple-element.97.half_b) | copy-start | bytes 786436

commit v8 on v7

--- a/solution.py
+++ b/solution.py
@@ -198,7 +198,7 @@
     )(info, *operators)
 
 
-NB = 16
+NB = 32
 
 def factor_kernel(info, gram_ref, half_a, half_b, basis_ref, factor_ref, a_ref, w_ref):
     size = gram_ref.shape[0]
@@ -319,7 +319,7 @@
     rim_span = home_a.shape[0]
     riders = {n: [n] for n in range(1, far + 2)}
     for n in range(far + 2, visits):
-        riders[visits + 1 - n].append(n)
+        riders[visits - n].append(n)
     rim_of = {0: (first_rims, 0)}
     for turn in range(visits):
         sides = (lax.ppermute(halves[0], "rows", to_a), lax.ppermute(halves[1], "rows", to_b))
@@ -328,8 +328,8 @@
             here, later, halves = lax.optimization_barrier((held[turn], held[turn + 1], halves))
             if turn + 2 <= far:
                 held[turn + 2] = lax.ppermute(later, "phase", back)
-            end = visits - 1 - turn
-            if turn > 0 and end > far:
+            end = visits - 2 - turn
+            if end > far:
                 nearer, halves = lax.optimization_barrier((held[end + 1], halves))
                 held[end] = lax.ppermute(nearer, "phase", ahead)
             picked = jnp.where(first_core, later, here)

time: 302 us -> 304 us (level)
  waiting for transfers between devices: 114 us -> 118 us
    ppermute x1, waiting for transfers between devices: 10.2 us -> 0.01 us  [body(): held[visits - 1] = lax.ppermute(home, 'phase', ahead)]
    ppermute x2, waiting for transfers between devices: 5.57 us -> 13.4 us  [body(): held[end] = lax.ppermute(nearer, 'phase', ahead)]
    ppermute x8, waiting for transfers between devices: 38.5 us -> 46 us  [body(): lax.ppermute(halves[0], 'rows', to_a)]
    ppermute x8, waiting for transfers between devices: 35.7 us -> 39.3 us  [body(): lax.ppermute(halves[1], 'rows', to_b)]
    ppermute x3, starting transfers between devices: 16.3 us -> 12.9 us  [body(): held[turn + 2] = lax.ppermute(later, 'phase', back)]
where the time goes in v8:
time: 304 us; the launch traced here: 303 us
  waiting for transfers between devices  118 us (39%)
  starting transfers between devices  115 us (38%)
  blocking collectives  36.6 us (12%)
  Pallas kernels  26.5 us (9%)
  local copies, waits for them, and re-layouts  4.41 us (1%)
    ppermute x8, starting transfers between devices, body(): lax.ppermute(halves[1], 'rows', to_b)  47.5 us
    ppermute x8, waiting for transfers between devices, body(): lax.ppermute(halves[0], 'rows', to_a)  46 us
    ppermute x8, waiting for transfers between devices, body(): lax.ppermute(halves[1], 'rows', to_b)  39.3 us
    all_to_all x1, blocking collectives, sum_over_rows(): pieces = lax.all_to_all(pieces, 'rows', 0, 0, tiled=True)  21.6 us
    ppermute x1, waiting for transfers between devices, body(): held[1] = lax.ppermute(home, 'phase', back)  19.1 us
    ppermute x8, starting transfers between devices, body(): lax.ppermute(halves[0], 'rows', to_a)  16.9 us
    all_to_all x1, blocking collectives, sum_over_rows(): return lax.all_to_all(copies, 'rows', 0, 0, tiled=True).reshape(size, size)  15 us
    ppermute x2, waiting for transfers between devices, body(): held[end] = lax.ppermute(nearer, 'phase', ahead)  13.4 us
  transfers between devices with their start and end apart: 31, of which 17 were waited for; matrix products, arithmetic and copies ran while one was open for 0% of the time, Pallas kernels for 3%

profile of v8, /device:TPU:8, one launch (start us, length us, event | category | flops | bytes accessed | tf_op | source)
XLA Modules:
  0.0 303.3 jit_solution(18241756320249120261)
XLA Ops:
  4.8 10.9 %collective-permute-start = (bf16[4160,128]{1,0:T(8,128)(2,1)S(1)}, bf16[4160,128]{1,0:T(8,128)(2,1)S(1)}, u32[]{:S(2)}, u32[]{:S(2)}) collective-permute-start(bf16[4160,128]{1,0:T(8,128)(2,1)S(1)} %get-tuple-element.61.refs_6_.refs_3_), channel_id=1, source_target_pairs={{0,448},{32,480},{64,0},{96,32},{128,64},{160,96},{192,128},{224,1... | collective-permute-start | bytes 3194888 | tf_op jit(solution)/shard_map/ppermute | solution.py:314
  15.8 1.9 collective-permute-start.2
  19.4 19.1 %collective-permute-done.refs_8_.refs_6_ = bf16[4160,128]{1,0:T(8,128)(2,1)S(1)} collective-permute-done((bf16[4160,128]{1,0:T(8,128)(2,1)S(1)}, bf16[4160,128]{1,0:T(8,128)(2,1)S(1)}, u32[]{:S(2)}, u32[]{:S(2)}) %collective-permute-start) | collective-permute-done | bytes 1064992 | tf_op jit(solution)/shard_map/ppermute | solution.py:314
  38.7 1.9 collective-permute-start.7
  40.6 5.6 %collective-permute-start.1 = (bf16[4160,128]{1,0:T(8,128)(2,1)S(1)}, bf16[4160,128]{1,0:T(8,128)(2,1)S(1)}, u32[]{:S(2)}, u32[]{:S(2)}) collective-permute-start(bf16[4160,128]{1,0:T(8,128)(2,1)S(1)} %collective-permute-done.refs_8_.refs_6_), channel_id=1, source_target_pairs={{0,448},{32,480},{64,0},{96,32},{128,64},{160,96},{192,128},{224,1... | collective-permute-start | bytes 3194888 | tf_op jit(solution)/shard_map/ppermute | solution.py:330
  46.2 3.4 %collective-permute-start.3 = (bf16[1024,128]{1,0:T(8,128)(2,1)S(1)}, bf16[1024,128]{1,0:T(8,128)(2,1)S(1)}, u32[]{:S(2)}, u32[]{:S(2)}) collective-permute-start(bf16[1024,128]{1,0:T(8,128)(2,1)S(1)} %get-tuple-element.57.refs_0_), channel_id=1, source_target_pairs={{0,1},{1,0},{2,3},{3,2},{4,5},{5,4},{6,7},{7,6},{8,9},{9,8},{10,11... | collective-permute-start | bytes 786440 | tf_op jit(solution)/shard_map/ppermute | solution.py:325
  49.6 2.4 collective-permute-start.5
  52.1 5.2 %collective-permute-done.3.refs_2_ = bf16[1024,128]{1,0:T(8,128)(2,1)S(1)} collective-permute-done((bf16[1024,128]{1,0:T(8,128)(2,1)S(1)}, bf16[1024,128]{1,0:T(8,128)(2,1)S(1)}, u32[]{:S(2)}, u32[]{:S(2)}) %collective-permute-start.3) | collective-permute-done | bytes 262176 | tf_op jit(solution)/shard_map/ppermute | solution.py:325
  57.3 4.5 %collective-permute-start.6 = (bf16[1040,128]{1,0:T(8,128)(2,1)S(1)}, bf16[1040,128]{1,0:T(8,128)(2,1)S(1)}, u32[]{:S(2)}, u32[]{:S(2)}) collective-permute-start(bf16[1040,128]{1,0:T(8,128)(2,1)S(1)} %get-tuple-element.60), channel_id=1, source_target_pairs={{0,31},{1,2},{2,1},{3,4},{4,3},{5,6},{6,5},{7,8},{8,7},{9,10},{10,... | collective-permute-start | bytes 798728 | tf_op jit(solution)/shard_map/ppermute | solution.py:308
  61.8 3.4 %collective-permute-start.4 = (bf16[1024,128]{1,0:T(8,128)(2,1)S(1)}, bf16[1024,128]{1,0:T(8,128)(2,1)S(1)}, u32[]{:S(2)}, u32[]{:S(2)}) collective-permute-start(bf16[1024,128]{1,0:T(8,128)(2,1)S(1)} %get-tuple-element.58.refs_1_), channel_id=1, source_target_pairs={{0,31},{1,2},{2,1},{3,4},{4,3},{5,6},{6,5},{7,8},{8,7},{9,10},{10,... | collective-permute-start | bytes 786440 | tf_op jit(solution)/shard_map/ppermute | solution.py:325
  65.2 8.5 %collective-permute-done.4.refs_3_ = bf16[1024,128]{1,0:T(8,128)(2,1)S(1)} collective-permute-done((bf16[1024,128]{1,0:T(8,128)(2,1)S(1)}, bf16[1024,128]{1,0:T(8,128)(2,1)S(1)}, u32[]{:S(2)}, u32[]{:S(2)}) %collective-permute-start.4) | collective-permute-done | bytes 262176 | tf_op jit(solution)/shard_map/ppermute | solution.py:325
  77.4 1.9 collective-permute-start.12
  79.4 5.1 %collective-permute-start.8 = (bf16[4160,128]{1,0:T(8,128)(2,1)S(1)}, bf16[4160,128]{1,0:T(8,128)(2,1)S(1)}, u32[]{:S(2)}, u32[]{:S(2)}) collective-permute-start(bf16[4160,128]{1,0:T(8,128)(2,1)S(1)} %collective-permute-done.1.refs_8_.refs_6_), channel_id=1, source_target_pairs={{0,448},{32,480},{64,0},{96,32},{128,64},{160,96},{192,128},{224,1... | collective-permute-start | bytes 3194888 | tf_op jit(solution)/shard_map/ppermute | solution.py:330
  84.5 1.9 collective-permute-start.10
  86.4 4.6 %collective-permute-start.11 = (bf16[3104,128]{1,0:T(8,128)(2,1)S(1)}, bf16[3104,128]{1,0:T(8,128)(2,1)S(1)}, u32[]{:S(2)}, u32[]{:S(2)}) collective-permute-start(bf16[3104,128]{1,0:T(8,128)(2,1)S(1)} %get-tuple-element.69.refs_1_), channel_id=1, source_target_pairs={{0,31},{1,2},{2,1},{3,4},{4,3},{5,6},{6,5},{7,8},{8,7},{9,10},{10,... | collective-permute-start | bytes 2383880 | tf_op jit(solution)/shard_map/ppermute | solution.py:325
  91.0 10.0 %collective-permute-done.9.refs_9_.refs_1_.refs_6_ = bf16[4160,128]{1,0:T(8,128)(2,1)S(1)} collective-permute-done((bf16[4160,128]{1,0:T(8,128)(2,1)S(1)}, bf16[4160,128]{1,0:T(8,128)(2,1)S(1)}, u32[]{:S(2)}, u32[]{:S(2)}) %collective-permute-start.9) | collective-permute-done | bytes 1064992 | tf_op jit(solution)/shard_map/ppermute | solution.py:334
  101.0 5.2 %collective-permute-done.10.refs_2_.refs_4_ = bf16[3104,128]{1,0:T(8,128)(2,1)S(1)} collective-permute-done((bf16[3104,128]{1,0:T(8,128)(2,1)S(1)}, bf16[3104,128]{1,0:T(8,128)(2,1)S(1)}, u32[]{:S(2)}, u32[]{:S(2)}) %collective-permute-start.10) | collective-permute-done | bytes 794656 | tf_op jit(solution)/shard_map/ppermute | solution.py:325
  106.2 4.0 %collective-permute-done.11.refs_3_.refs_5_ = bf16[3104,128]{1,0:T(8,128)(2,1)S(1)} collective-permute-done((bf16[3104,128]{1,0:T(8,128)(2,1)S(1)}, bf16[3104,128]{1,0:T(8,128)(2,1)S(1)}, u32[]{:S(2)}, u32[]{:S(2)}) %collective-permute-start.11) | collective-permute-done | bytes 794656 | tf_op jit(solution)/shard_map/ppermute | solution.py:325
  112.0 1.9 collective-permute-start.17
  113.9 2.2 collective-permute-start.13
  116.1 2.0 collective-permute-start.15
  118.1 5.1 %collective-permute-start.16 = (bf16[3104,128]{1,0:T(8,128)(2,1)S(1)}, bf16[3104,128]{1,0:T(8,128)(2,1)S(1)}, u32[]{:S(2)}, u32[]{:S(2)}) collective-permute-start(bf16[3104,128]{1,0:T(8,128)(2,1)S(1)} %get-tuple-element.76.refs_1_), channel_id=1, source_target_pairs={{0,31},{1,2},{2,1},{3,4},{4,3},{5,6},{6,5},{7,8},{8,7},{9,10},{10,... | collective-permute-start | bytes 2383880 | tf_op jit(solution)/shard_map/ppermute | solution.py:325
  123.2 14.7 %collective-permute-done.15.refs_2_.refs_4_ = bf16[3104,128]{1,0:T(8,128)(2,1)S(1)} collective-permute-done((bf16[3104,128]{1,0:T(8,128)(2,1)S(1)}, bf16[3104,128]{1,0:T(8,128)(2,1)S(1)}, u32[]{:S(2)}, u32[]{:S(2)}) %collective-permute-start.15) | collective-permute-done | bytes 794656 | tf_op jit(solution)/shard_map/ppermute | solution.py:325
  137.8 4.0 %collective-permute-done.16.refs_3_.refs_5_ = bf16[3104,128]{1,0:T(8,128)(2,1)S(1)} collective-permute-done((bf16[3104,128]{1,0:T(8,128)(2,1)S(1)}, bf16[3104,128]{1,0:T(8,128)(2,1)S(1)}, u32[]{:S(2)}, u32[]{:S(2)}) %collective-permute-start.16) | collective-permute-done | bytes 794656 | tf_op jit(solution)/shard_map/ppermute | solution.py:325
  143.5 1.9 collective-permute-start.20
  145.4 3.6 %collective-permute-start.14 = (bf16[4160,128]{1,0:T(8,128)(2,1)S(1)}, bf16[4160,128]{1,0:T(8,128)(2,1)S(1)}, u32[]{:S(2)}, u32[]{:S(2)}) collective-permute-start(bf16[4160,128]{1,0:T(8,128)(2,1)S(1)} %collective-permute-done.9.refs_9_.refs_1_.refs_6_), channel_id=1, source_target_pairs={{0,64},{32,96},{64,128},{96,160},{128,192},{160,224},{192,256},{22... | collective-permute-start | bytes 3194888 | tf_op jit(solution)/shard_map/ppermute | solution.py:334
  149.1 2.0 collective-permute-start.18
  151.1 6.3 %collective-permute-start.19 = (bf16[2064,128]{1,0:T(8,128)(2,1)S(1)}, bf16[2064,128]{1,0:T(8,128)(2,1)S(1)}, u32[]{:S(2)}, u32[]{:S(2)}) collective-permute-start(bf16[2064,128]{1,0:T(8,128)(2,1)S(1)} %get-tuple-element.81.refs_1_), channel_id=1, source_target_pairs={{0,31},{1,2},{2,1},{3,4},{4,3},{5,6},{6,5},{7,8},{8,7},{9,10},{10,... | collective-permute-start | bytes 1585160 | tf_op jit(solution)/shard_map/ppermute | solution.py:325
  157.4 7.8 %collective-permute-done.18.refs_2_.refs_4_ = bf16[2064,128]{1,0:T(8,128)(2,1)S(1)} collective-permute-done((bf16[2064,128]{1,0:T(8,128)(2,1)S(1)}, bf16[2064,128]{1,0:T(8,128)(2,1)S(1)}, u32[]{:S(2)}, u32[]{:S(2)}) %collective-permute-start.18) | collective-permute-done | bytes 528416 | tf_op jit(solution)/shard_map/ppermute | solution.py:325
  165.1 4.3 %collective-permute-done.19.refs_3_.refs_5_ = bf16[2064,128]{1,0:T(8,128)(2,1)S(1)} collective-permute-done((bf16[2064,128]{1,0:T(8,128)(2,1)S(1)}, bf16[2064,128]{1,0:T(8,128)(2,1)S(1)}, u32[]{:S(2)}, u32[]{:S(2)}) %collective-permute-start.19) | collective-permute-done | bytes 528416 | tf_op jit(solution)/shard_map/ppermute | solution.py:325
  171.0 3.4 %collective-permute-done.14.refs_8_.refs_0_.refs_6_ = bf16[4160,128]{1,0:T(8,128)(2,1)S(1)} collective-permute-done((bf16[4160,128]{1,0:T(8,128)(2,1)S(1)}, bf16[4160,128]{1,0:T(8,128)(2,1)S(1)}, u32[]{:S(2)}, u32[]{:S(2)}) %collective-permute-start.14) | collective-permute-done | bytes 1064992 | tf_op jit(solution)/shard_map/ppermute | solution.py:334
  176.3 1.9 collective-permute-start.26
  178.4 2.4 collective-permute-start.23
  180.8 2.0 collective-permute-start.21
  182.8 6.3 %collective-permute-start.22 = (bf16[2064,128]{1,0:T(8,128)(2,1)S(1)}, bf16[2064,128]{1,0:T(8,128)(2,1)S(1)}, u32[]{:S(2)}, u32[]{:S(2)}) collective-permute-start(bf16[2064,128]{1,0:T(8,128)(2,1)S(1)} %get-tuple-element.87.refs_1_), channel_id=1, source_target_pairs={{0,31},{1,2},{2,1},{3,4},{4,3},{5,6},{6,5},{7,8},{8,7},{9,10},{10,... | collective-permute-start | bytes 1585160 | tf_op jit(solution)/shard_map/ppermute | solution.py:325
  189.1 7.6 %collective-permute-done.21.refs_2_.refs_4_ = bf16[2064,128]{1,0:T(8,128)(2,1)S(1)} collective-permute-done((bf16[2064,128]{1,0:T(8,128)(2,1)S(1)}, bf16[2064,128]{1,0:T(8,128)(2,1)S(1)}, u32[]{:S(2)}, u32[]{:S(2)}) %collective-permute-start.21) | collective-permute-done | bytes 528416 | tf_op jit(solution)/shard_map/ppermute | solution.py:325
  196.6 4.3 %collective-permute-done.22.refs_3_.refs_5_ = bf16[2064,128]{1,0:T(8,128)(2,1)S(1)} collective-permute-done((bf16[2064,128]{1,0:T(8,128)(2,1)S(1)}, bf16[2064,128]{1,0:T(8,128)(2,1)S(1)}, u32[]{:S(2)}, u32[]{:S(2)}) %collective-permute-start.22) | collective-permute-done | bytes 528416 | tf_op jit(solution)/shard_map/ppermute | solution.py:325
  202.5 1.9 collective-permute-start.24
  204.4 7.4 %collective-permute-start.25 = (bf16[2064,128]{1,0:T(8,128)(2,1)S(1)}, bf16[2064,128]{1,0:T(8,128)(2,1)S(1)}, u32[]{:S(2)}, u32[]{:S(2)}) collective-permute-start(bf16[2064,128]{1,0:T(8,128)(2,1)S(1)} %get-tuple-element.91.refs_1_), channel_id=1, source_target_pairs={{0,31},{1,2},{2,1},{3,4},{4,3},{5,6},{6,5},{7,8},{8,7},{9,10},{10,... | collective-permute-start | bytes 1585160 | tf_op jit(solution)/shard_map/ppermute | solution.py:325
  211.8 5.6 %collective-permute-done.24.refs_2_.refs_4_ = bf16[2064,128]{1,0:T(8,128)(2,1)S(1)} collective-permute-done((bf16[2064,128]{1,0:T(8,128)(2,1)S(1)}, bf16[2064,128]{1,0:T(8,128)(2,1)S(1)}, u32[]{:S(2)}, u32[]{:S(2)}) %collective-permute-start.24) | collective-permute-done | bytes 528416 | tf_op jit(solution)/shard_map/ppermute | solution.py:325
  217.4 5.3 %collective-permute-done.25.refs_3_.refs_5_ = bf16[2064,128]{1,0:T(8,128)(2,1)S(1)} collective-permute-done((bf16[2064,128]{1,0:T(8,128)(2,1)S(1)}, bf16[2064,128]{1,0:T(8,128)(2,1)S(1)}, u32[]{:S(2)}, u32[]{:S(2)}) %collective-permute-start.25) | collective-permute-done | bytes 528416 | tf_op jit(solution)/shard_map/ppermute | solution.py:325
  226.1 7.2 %collective-permute-start.28 = (bf16[1024,128]{1,0:T(8,128)(2,1)S(1)}, bf16[1024,128]{1,0:T(8,128)(2,1)S(1)}, u32[]{:S(2)}, u32[]{:S(2)}) collective-permute-start(bf16[1024,128]{1,0:T(8,128)(2,1)S(1)} %get-tuple-element.93.refs_1_), channel_id=1, source_target_pairs={{0,31},{1,2},{2,1},{3,4},{4,3},{5,6},{6,5},{7,8},{8,7},{9,10},{10,... | collective-permute-start | bytes 786440 | tf_op jit(solution)/shard_map/ppermute | solution.py:325
  233.3 4.5 %collective-permute-done.28.refs_3_ = bf16[1024,128]{1,0:T(8,128)(2,1)S(1)} collective-permute-done((bf16[1024,128]{1,0:T(8,128)(2,1)S(1)}, bf16[1024,128]{1,0:T(8,128)(2,1)S(1)}, u32[]{:S(2)}, u32[]{:S(2)}) %collective-permute-start.28) | collective-permute-done | bytes 262176 | tf_op jit(solution)/shard_map/ppermute | solution.py:325
  241.2 7.2 %collective-permute-start.30 = (bf16[1024,128]{1,0:T(8,128)(2,1)S(1)}, bf16[1024,128]{1,0:T(8,128)(2,1)S(1)}, u32[]{:S(2)}, u32[]{:S(2)}) collective-permute-start(bf16[1024,128]{1,0:T(8,128)(2,1)S(1)} %get-tuple-element.95.refs_1_), channel_id=1, source_target_pairs={{0,31},{1,2},{2,1},{3,4},{4,3},{5,6},{6,5},{7,8},{8,7},{9,10},{10,... | collective-permute-start | bytes 786440 | tf_op jit(solution)/shard_map/ppermute | solution.py:325
  248.4 4.3 %collective-permute-done.30.refs_3_ = bf16[1024,128]{1,0:T(8,128)(2,1)S(1)} collective-permute-done((bf16[1024,128]{1,0:T(8,128)(2,1)S(1)}, bf16[1024,128]{1,0:T(8,128)(2,1)S(1)}, u32[]{:S(2)}, u32[]{:S(2)}) %collective-permute-start.30) | collective-permute-done | bytes 262176 | tf_op jit(solution)/shard_map/ppermute | solution.py:325
  254.5 21.6 %all_to_all.10 = bf16[32,8,256]{2,1,0:T(8,128)(2,1)S(1)} all-to-all(bf16[32,8,256]{2,1,0:T(8,128)(2,1)S(1)} %fusion), channel_id=1, replica_groups=mesh['phase'=16,'rows'=32] {'rows'}, dimensions={0} | all-to-all | bytes 262144 | tf_op jit(solution)/shard_map/all_to_all | solution.py:286
  276.2 15.0 %all_to_all.11 = f32[32,8,256]{2,1,0:T(8,128)S(1)} all-to-all(f32[32,8,256]{2,1,0:T(8,128)S(1)} %broadcast_in_dim.12), channel_id=1, replica_groups=mesh['phase'=16,'rows'=32] {'rows'}, dimensions={0} | all-to-all | bytes 524288 | tf_op jit(solution)/shard_map/all_to_all | solution.py:289
  292.0 11.3 %factor_solve.1 = (f32[1024,256]{1,0:T(8,128)}, f32[256,256]{1,0:T(8,128)}) custom-call(s32[3]{0:T(128)} %copy-done.4, f32[256,256]{1,0:T(8,128)} %multiply_bitcast_fusion.gram_ref, bf16[512,256]{1,0:T(8,128)(2,1)} %copy-done.2, bf16[512,256]{1,0:T(8,128)(2,1)} %copy-done.3), custom_call_target="tpu_custom_call" | custom-call | tf_op jit(solution)/shard_map/factor_solve/pallas_call | solution.py:269
  (55 shorter events, 27.1 us)
Async XLA Ops:
  1.5 173.0 %copy-start.4 = (s32[3]{0:T(128)}, s32[3]{0:T(128)S(1)}, u32[]{:S(2)}) copy-start(s32[3]{0:T(128)S(1)} %pad_add_fusion.info) | copy-start | bytes 40
  1.5 1.2 copy-start
  2.7 0.7 copy-start.5
  4.1 0.7 copy-start.6
  4.8 33.7 %collective-permute-start = (bf16[4160,128]{1,0:T(8,128)(2,1)S(1)}, bf16[4160,128]{1,0:T(8,128)(2,1)S(1)}, u32[]{:S(2)}, u32[]{:S(2)}) collective-permute-start(bf16[4160,128]{1,0:T(8,128)(2,1)S(1)} %get-tuple-element.61.refs_6_.refs_3_), channel_id=1, source_target_pairs={{0,448},{32,480},{64,0},{96,32},{128,64},{160,96},{192,128},{224,1... | collective-permute-start | bytes 3194888 | tf_op jit(solution)/shard_map/ppermute | solution.py:314
  15.8 46.0 %collective-permute-start.2 = (bf16[4160,128]{1,0:T(8,128)(2,1)S(1)}, bf16[4160,128]{1,0:T(8,128)(2,1)S(1)}, u32[]{:S(2)}, u32[]{:S(2)}) collective-permute-start(bf16[4160,128]{1,0:T(8,128)(2,1)S(1)} %get-tuple-element.61.refs_6_.refs_3_), channel_id=1, source_target_pairs={{0,64},{32,96},{64,128},{96,160},{128,192},{160,224},{192,256},{22... | collective-permute-start | bytes 3194888 | tf_op jit(solution)/shard_map/ppermute | solution.py:315
  17.7 1.0 copy-start.1
  38.5 11.1 %copy-start.7 = (bf16[1040,128]{1,0:T(8,128)(2,1)S(1)}, bf16[1040,128]{1,0:T(8,128)(2,1)}, u32[]{:S(2)}) copy-start(bf16[1040,128]{1,0:T(8,128)(2,1)} %copy-done.6) | copy-start | bytes 798724
  38.7 37.1 %collective-permute-start.7 = (bf16[4160,128]{1,0:T(8,128)(2,1)S(1)}, bf16[4160,128]{1,0:T(8,128)(2,1)S(1)}, u32[]{:S(2)}, u32[]{:S(2)}) collective-permute-start(bf16[4160,128]{1,0:T(8,128)(2,1)S(1)} %broadcast_select_fusion.4), channel_id=1, source_target_pairs={{0,32},{32,0},{64,96},{96,64},{128,160},{160,128},{192,224},{224,1... | collective-permute-start | bytes 3194888 | tf_op jit(solution)/shard_map/ppermute | solution.py:336
  40.6 36.7 %collective-permute-start.1 = (bf16[4160,128]{1,0:T(8,128)(2,1)S(1)}, bf16[4160,128]{1,0:T(8,128)(2,1)S(1)}, u32[]{:S(2)}, u32[]{:S(2)}) collective-permute-start(bf16[4160,128]{1,0:T(8,128)(2,1)S(1)} %collective-permute-done.refs_8_.refs_6_), channel_id=1, source_target_pairs={{0,448},{32,480},{64,0},{96,32},{128,64},{160,96},{192,128},{224,1... | collective-permute-start | bytes 3194888 | tf_op jit(solution)/shard_map/ppermute | solution.py:330
  46.2 11.1 %collective-permute-start.3 = (bf16[1024,128]{1,0:T(8,128)(2,1)S(1)}, bf16[1024,128]{1,0:T(8,128)(2,1)S(1)}, u32[]{:S(2)}, u32[]{:S(2)}) collective-permute-start(bf16[1024,128]{1,0:T(8,128)(2,1)S(1)} %get-tuple-element.57.refs_0_), channel_id=1, source_target_pairs={{0,1},{1,0},{2,3},{3,2},{4,5},{5,4},{6,7},{7,6},{8,9},{9,8},{10,11... | collective-permute-start | bytes 786440 | tf_op jit(solution)/shard_map/ppermute | solution.py:325
  49.6 26.1 %collective-permute-start.5 = (bf16[1040,128]{1,0:T(8,128)(2,1)S(1)}, bf16[1040,128]{1,0:T(8,128)(2,1)S(1)}, u32[]{:S(2)}, u32[]{:S(2)}) collective-permute-start(bf16[1040,128]{1,0:T(8,128)(2,1)S(1)} %copy-done.7), channel_id=1, source_target_pairs={{0,1},{1,0},{2,3},{3,2},{4,5},{5,4},{6,7},{7,6},{8,9},{9,8},{10,11... | collective-permute-start | bytes 798728 | tf_op jit(solution)/shard_map/ppermute | solution.py:308
  57.3 18.4 %collective-permute-start.6 = (bf16[1040,128]{1,0:T(8,128)(2,1)S(1)}, bf16[1040,128]{1,0:T(8,128)(2,1)S(1)}, u32[]{:S(2)}, u32[]{:S(2)}) collective-permute-start(bf16[1040,128]{1,0:T(8,128)(2,1)S(1)} %get-tuple-element.60), channel_id=1, source_target_pairs={{0,31},{1,2},{2,1},{3,4},{4,3},{5,6},{6,5},{7,8},{8,7},{9,10},{10,... | collective-permute-start | bytes 798728 | tf_op jit(solution)/shard_map/ppermute | solution.py:308
  61.8 12.0 %collective-permute-start.4 = (bf16[1024,128]{1,0:T(8,128)(2,1)S(1)}, bf16[1024,128]{1,0:T(8,128)(2,1)S(1)}, u32[]{:S(2)}, u32[]{:S(2)}) collective-permute-start(bf16[1024,128]{1,0:T(8,128)(2,1)S(1)} %get-tuple-element.58.refs_1_), channel_id=1, source_target_pairs={{0,31},{1,2},{2,1},{3,4},{4,3},{5,6},{6,5},{7,8},{8,7},{9,10},{10,... | collective-permute-start | bytes 786440 | tf_op jit(solution)/shard_map/ppermute | solution.py:325
  73.8 27.2 %collective-permute-start.9 = (bf16[4160,128]{1,0:T(8,128)(2,1)S(1)}, bf16[4160,128]{1,0:T(8,128)(2,1)S(1)}, u32[]{:S(2)}, u32[]{:S(2)}) collective-permute-start(bf16[4160,128]{1,0:T(8,128)(2,1)S(1)} %collective-permute-done.2.refs_9_.refs_2_.refs_6_), channel_id=1, source_target_pairs={{0,64},{32,96},{64,128},{96,160},{128,192},{160,224},{192,256},{22... | collective-permute-start | bytes 3194888 | tf_op jit(solution)/shard_map/ppermute | solution.py:334
  77.4 32.8 %collective-permute-start.12 = (bf16[4160,128]{1,0:T(8,128)(2,1)S(1)}, bf16[4160,128]{1,0:T(8,128)(2,1)S(1)}, u32[]{:S(2)}, u32[]{:S(2)}) collective-permute-start(bf16[4160,128]{1,0:T(8,128)(2,1)S(1)} %broadcast_select_fusion.3), channel_id=1, source_target_pairs={{0,32},{32,0},{64,96},{96,64},{128,160},{160,128},{192,224},{224,1... | collective-permute-start | bytes 3194888 | tf_op jit(solution)/shard_map/ppermute | solution.py:336
  79.4 32.5 %collective-permute-start.8 = (bf16[4160,128]{1,0:T(8,128)(2,1)S(1)}, bf16[4160,128]{1,0:T(8,128)(2,1)S(1)}, u32[]{:S(2)}, u32[]{:S(2)}) collective-permute-start(bf16[4160,128]{1,0:T(8,128)(2,1)S(1)} %collective-permute-done.1.refs_8_.refs_6_), channel_id=1, source_target_pairs={{0,448},{32,480},{64,0},{96,32},{128,64},{160,96},{192,128},{224,1... | collective-permute-start | bytes 3194888 | tf_op jit(solution)/shard_map/ppermute | solution.py:330
  84.5 21.7 %collective-permute-start.10 = (bf16[3104,128]{1,0:T(8,128)(2,1)S(1)}, bf16[3104,128]{1,0:T(8,128)(2,1)S(1)}, u32[]{:S(2)}, u32[]{:S(2)}) collective-permute-start(bf16[3104,128]{1,0:T(8,128)(2,1)S(1)} %get-tuple-element.68.refs_0_), channel_id=1, source_target_pairs={{0,1},{1,0},{2,3},{3,2},{4,5},{5,4},{6,7},{7,6},{8,9},{9,8},{10,11... | collective-permute-start | bytes 2383880 | tf_op jit(solution)/shard_map/ppermute | solution.py:325
  86.4 23.8 %collective-permute-start.11 = (bf16[3104,128]{1,0:T(8,128)(2,1)S(1)}, bf16[3104,128]{1,0:T(8,128)(2,1)S(1)}, u32[]{:S(2)}, u32[]{:S(2)}) collective-permute-start(bf16[3104,128]{1,0:T(8,128)(2,1)S(1)} %get-tuple-element.69.refs_1_), channel_id=1, source_target_pairs={{0,31},{1,2},{2,1},{3,4},{4,3},{5,6},{6,5},{7,8},{8,7},{9,10},{10,... | collective-permute-start | bytes 2383880 | tf_op jit(solution)/shard_map/ppermute | solution.py:325
  112.0 29.9 %collective-permute-start.17 = (bf16[4160,128]{1,0:T(8,128)(2,1)S(1)}, bf16[4160,128]{1,0:T(8,128)(2,1)S(1)}, u32[]{:S(2)}, u32[]{:S(2)}) collective-permute-start(bf16[4160,128]{1,0:T(8,128)(2,1)S(1)} %broadcast_select_fusion.2), channel_id=1, source_target_pairs={{0,32},{32,0},{64,96},{96,64},{128,160},{160,128},{192,224},{224,1... | collective-permute-start | bytes 3194888 | tf_op jit(solution)/shard_map/ppermute | solution.py:336
  113.9 29.5 %collective-permute-start.13 = (bf16[4160,128]{1,0:T(8,128)(2,1)S(1)}, bf16[4160,128]{1,0:T(8,128)(2,1)S(1)}, u32[]{:S(2)}, u32[]{:S(2)}) collective-permute-start(bf16[4160,128]{1,0:T(8,128)(2,1)S(1)} %collective-permute-done.8.refs_8_.refs_6_), channel_id=1, source_target_pairs={{0,448},{32,480},{64,0},{96,32},{128,64},{160,96},{192,128},{224,1... | collective-permute-start | bytes 3194888 | tf_op jit(solution)/shard_map/ppermute | solution.py:330
  116.1 21.7 %collective-permute-start.15 = (bf16[3104,128]{1,0:T(8,128)(2,1)S(1)}, bf16[3104,128]{1,0:T(8,128)(2,1)S(1)}, u32[]{:S(2)}, u32[]{:S(2)}) collective-permute-start(bf16[3104,128]{1,0:T(8,128)(2,1)S(1)} %get-tuple-element.75.refs_0_), channel_id=1, source_target_pairs={{0,1},{1,0},{2,3},{3,2},{4,5},{5,4},{6,7},{7,6},{8,9},{9,8},{10,11... | collective-permute-start | bytes 2383880 | tf_op jit(solution)/shard_map/ppermute | solution.py:325
  118.1 23.8 %collective-permute-start.16 = (bf16[3104,128]{1,0:T(8,128)(2,1)S(1)}, bf16[3104,128]{1,0:T(8,128)(2,1)S(1)}, u32[]{:S(2)}, u32[]{:S(2)}) collective-permute-start(bf16[3104,128]{1,0:T(8,128)(2,1)S(1)} %get-tuple-element.76.refs_1_), channel_id=1, source_target_pairs={{0,31},{1,2},{2,1},{3,4},{4,3},{5,6},{6,5},{7,8},{8,7},{9,10},{10,... | collective-permute-start | bytes 2383880 | tf_op jit(solution)/shard_map/ppermute | solution.py:325
  143.5 26.0 %collective-permute-start.20 = (bf16[4160,128]{1,0:T(8,128)(2,1)S(1)}, bf16[4160,128]{1,0:T(8,128)(2,1)S(1)}, u32[]{:S(2)}, u32[]{:S(2)}) collective-permute-start(bf16[4160,128]{1,0:T(8,128)(2,1)S(1)} %broadcast_select_fusion.1), channel_id=1, source_target_pairs={{0,32},{32,0},{64,96},{96,64},{128,160},{160,128},{192,224},{224,1... | collective-permute-start | bytes 3194888 | tf_op jit(solution)/shard_map/ppermute | solution.py:336
  145.4 29.0 %collective-permute-start.14 = (bf16[4160,128]{1,0:T(8,128)(2,1)S(1)}, bf16[4160,128]{1,0:T(8,128)(2,1)S(1)}, u32[]{:S(2)}, u32[]{:S(2)}) collective-permute-start(bf16[4160,128]{1,0:T(8,128)(2,1)S(1)} %collective-permute-done.9.refs_9_.refs_1_.refs_6_), channel_id=1, source_target_pairs={{0,64},{32,96},{64,128},{96,160},{128,192},{160,224},{192,256},{22... | collective-permute-start | bytes 3194888 | tf_op jit(solution)/shard_map/ppermute | solution.py:334
  149.1 16.0 %collective-permute-start.18 = (bf16[2064,128]{1,0:T(8,128)(2,1)S(1)}, bf16[2064,128]{1,0:T(8,128)(2,1)S(1)}, u32[]{:S(2)}, u32[]{:S(2)}) collective-permute-start(bf16[2064,128]{1,0:T(8,128)(2,1)S(1)} %get-tuple-element.80.refs_0_), channel_id=1, source_target_pairs={{0,1},{1,0},{2,3},{3,2},{4,5},{5,4},{6,7},{7,6},{8,9},{9,8},{10,11... | collective-permute-start | bytes 1585160 | tf_op jit(solution)/shard_map/ppermute | solution.py:325
  151.1 18.4 %collective-permute-start.19 = (bf16[2064,128]{1,0:T(8,128)(2,1)S(1)}, bf16[2064,128]{1,0:T(8,128)(2,1)S(1)}, u32[]{:S(2)}, u32[]{:S(2)}) collective-permute-start(bf16[2064,128]{1,0:T(8,128)(2,1)S(1)} %get-tuple-element.81.refs_1_), channel_id=1, source_target_pairs={{0,31},{1,2},{2,1},{3,4},{4,3},{5,6},{6,5},{7,8},{8,7},{9,10},{10,... | collective-permute-start | bytes 1585160 | tf_op jit(solution)/shard_map/ppermute | solution.py:325
  176.3 46.4 %collective-permute-start.26 = (bf16[12480,128]{1,0:T(8,128)(2,1)S(1)}, bf16[12480,128]{1,0:T(8,128)(2,1)S(1)}, u32[]{:S(2)}, u32[]{:S(2)}) collective-permute-start(bf16[12480,128]{1,0:T(8,128)(2,1)S(1)} %gather_swap.1), channel_id=1, source_target_pairs={{0,32},{32,0},{64,96},{96,64},{128,160},{160,128},{192,224},{224,1... | collective-permute-start | bytes 9584648 | tf_op jit(solution)/shard_map/ppermute | solution.py:339
  178.4 22.6 %collective-permute-start.23 = (bf16[4160,128]{1,0:T(8,128)(2,1)S(1)}, bf16[4160,128]{1,0:T(8,128)(2,1)S(1)}, u32[]{:S(2)}, u32[]{:S(2)}) collective-permute-start(bf16[4160,128]{1,0:T(8,128)(2,1)S(1)} %broadcast_select_fusion), channel_id=1, source_target_pairs={{0,32},{32,0},{64,96},{96,64},{128,160},{160,128},{192,224},{224,1... | collective-permute-start | bytes 3194888 | tf_op jit(solution)/shard_map/ppermute | solution.py:336
  180.8 15.8 %collective-permute-start.21 = (bf16[2064,128]{1,0:T(8,128)(2,1)S(1)}, bf16[2064,128]{1,0:T(8,128)(2,1)S(1)}, u32[]{:S(2)}, u32[]{:S(2)}) collective-permute-start(bf16[2064,128]{1,0:T(8,128)(2,1)S(1)} %get-tuple-element.86.refs_0_), channel_id=1, source_target_pairs={{0,1},{1,0},{2,3},{3,2},{4,5},{5,4},{6,7},{7,6},{8,9},{9,8},{10,11... | collective-permute-start | bytes 1585160 | tf_op jit(solution)/shard_map/ppermute | solution.py:325
  182.8 18.2 %collective-permute-start.22 = (bf16[2064,128]{1,0:T(8,128)(2,1)S(1)}, bf16[2064,128]{1,0:T(8,128)(2,1)S(1)}, u32[]{:S(2)}, u32[]{:S(2)}) collective-permute-start(bf16[2064,128]{1,0:T(8,128)(2,1)S(1)} %get-tuple-element.87.refs_1_), channel_id=1, source_target_pairs={{0,31},{1,2},{2,1},{3,4},{4,3},{5,6},{6,5},{7,8},{8,7},{9,10},{10,... | collective-permute-start | bytes 1585160 | tf_op jit(solution)/shard_map/ppermute | solution.py:325
  202.5 15.0 %collective-permute-start.24 = (bf16[2064,128]{1,0:T(8,128)(2,1)S(1)}, bf16[2064,128]{1,0:T(8,128)(2,1)S(1)}, u32[]{:S(2)}, u32[]{:S(2)}) collective-permute-start(bf16[2064,128]{1,0:T(8,128)(2,1)S(1)} %get-tuple-element.90.refs_0_), channel_id=1, source_target_pairs={{0,1},{1,0},{2,3},{3,2},{4,5},{5,4},{6,7},{7,6},{8,9},{9,8},{10,11... | collective-permute-start | bytes 1585160 | tf_op jit(solution)/shard_map/ppermute | solution.py:325
  204.4 18.3 %collective-permute-start.25 = (bf16[2064,128]{1,0:T(8,128)(2,1)S(1)}, bf16[2064,128]{1,0:T(8,128)(2,1)S(1)}, u32[]{:S(2)}, u32[]{:S(2)}) collective-permute-start(bf16[2064,128]{1,0:T(8,128)(2,1)S(1)} %get-tuple-element.91.refs_1_), channel_id=1, source_target_pairs={{0,31},{1,2},{2,1},{3,4},{4,3},{5,6},{6,5},{7,8},{8,7},{9,10},{10,... | collective-permute-start | bytes 1585160 | tf_op jit(solution)/shard_map/ppermute | solution.py:325
  224.1 9.2 %collective-permute-start.27 = (bf16[1024,128]{1,0:T(8,128)(2,1)S(1)}, bf16[1024,128]{1,0:T(8,128)(2,1)S(1)}, u32[]{:S(2)}, u32[]{:S(2)}) collective-permute-start(bf16[1024,128]{1,0:T(8,128)(2,1)S(1)} %get-tuple-element.92.refs_0_), channel_id=1, source_target_pairs={{0,1},{1,0},{2,3},{3,2},{4,5},{5,4},{6,7},{7,6},{8,9},{9,8},{10,11... | collective-permute-start | bytes 786440 | tf_op jit(solution)/shard_map/ppermute | solution.py:325
  226.1 11.7 %collective-permute-start.28 = (bf16[1024,128]{1,0:T(8,128)(2,1)S(1)}, bf16[1024,128]{1,0:T(8,128)(2,1)S(1)}, u32[]{:S(2)}, u32[]{:S(2)}) collective-permute-start(bf16[1024,128]{1,0:T(8,128)(2,1)S(1)} %get-tuple-element.93.refs_1_), channel_id=1, source_target_pairs={{0,31},{1,2},{2,1},{3,4},{4,3},{5,6},{6,5},{7,8},{8,7},{9,10},{10,... | collective-permute-start | bytes 786440 | tf_op jit(solution)/shard_map/ppermute | solution.py:325
  239.2 9.2 %collective-permute-start.29 = (bf16[1024,128]{1,0:T(8,128)(2,1)S(1)}, bf16[1024,128]{1,0:T(8,128)(2,1)S(1)}, u32[]{:S(2)}, u32[]{:S(2)}) collective-permute-start(bf16[1024,128]{1,0:T(8,128)(2,1)S(1)} %get-tuple-element.94.refs_0_), channel_id=1, source_target_pairs={{0,1},{1,0},{2,3},{3,2},{4,5},{5,4},{6,7},{7,6},{8,9},{9,8},{10,11... | collective-permute-start | bytes 786440 | tf_op jit(solution)/shard_map/ppermute | solution.py:325
  241.2 11.6 %collective-permute-start.30 = (bf16[1024,128]{1,0:T(8,128)(2,1)S(1)}, bf16[1024,128]{1,0:T(8,128)(2,1)S(1)}, u32[]{:S(2)}, u32[]{:S(2)}) collective-permute-start(bf16[1024,128]{1,0:T(8,128)(2,1)S(1)} %get-tuple-element.95.refs_1_), channel_id=1, source_target_pairs={{0,31},{1,2},{2,1},{3,4},{4,3},{5,6},{6,5},{7,8},{8,7},{9,10},{10,... | collective-permute-start | bytes 786440 | tf_op jit(solution)/shard_map/ppermute | solution.py:325
  254.2 22.0 %copy-start.2 = (bf16[512,256]{1,0:T(8,128)(2,1)}, bf16[512,256]{1,0:T(8,128)(2,1)S(1)}, u32[]{:S(2)}) copy-start(bf16[512,256]{1,0:T(8,128)(2,1)S(1)} %get-tuple-element.96.half_a) | copy-start | bytes 786436
  254.2 22.0 %copy-start.3 = (bf16[512,256]{1,0:T(8,128)(2,1)}, bf16[512,256]{1,0:T(8,128)(2,1)S(1)}, u32[]{:S(2)}) copy-start(bf16[512,256]{1,0:T(8,128)(2,1)S(1)} %get-tuple-element.97.half_b) | copy-start | bytes 786436
